TPU v7x, 32 devices: a whole 2x2x4 slice. The times are simulated.
32 devices in a mesh: fsdp: 2 (over x), ctx: 4 (over z), tp: 4 (over y, core).
Axes of the slice: x: 2, y: 2, z: 4, core: 2. Of those that a mesh axis runs over, the one named last changes fastest.
Arguments:
- layer_input: bfloat16 [2048, 8, 1536], P(('ctx', 'tp'), 'fsdp'), may hold values from -6 to 6
- lengths: int32 [8], P('fsdp'), may hold values from 512 to 2048, as said below
- attn_gain: bfloat16 [1536], P(('fsdp', 'ctx')), may hold values from 0.5 to 1.5
- w_query: bfloat16 [1536, 1536], P(('fsdp', 'ctx'), 'tp'), may hold values from -0.15625 to 0.15625
- w_key: bfloat16 [1536, 1536], P(('fsdp', 'ctx'), 'tp'), may hold values from -0.15625 to 0.15625
- w_value: bfloat16 [1536, 1536], P(('fsdp', 'ctx'), 'tp'), may hold values from -0.15625 to 0.15625
- w_forget: bfloat16 [1536, 24], P(('fsdp', 'ctx'), 'tp'), may hold values from -0.15625 to 0.15625
- forget_bias: bfloat16 [24], P('tp'), may hold values from 2 to 9
- w_gate_out: bfloat16 [1536, 1536], P(('fsdp', 'ctx'), 'tp'), may hold values from -0.15625 to 0.15625
- w_out: bfloat16 [1536, 1536], P(('fsdp', 'ctx'), 'tp'), may hold values from -0.625 to 0.625
- mlp_gain: bfloat16 [1536], P(('fsdp', 'ctx')), may hold values from 0.5 to 1.5
- w_gate: bfloat16 [1536, 4096], P(('fsdp', 'ctx'), 'tp'), may hold values from -0.15625 to 0.15625
- w_up: bfloat16 [1536, 4096], P(('fsdp', 'ctx'), 'tp'), may hold values from -0.15625 to 0.15625
- w_down: bfloat16 [1536, 4096], P(('fsdp', 'ctx'), 'tp'), may hold values from -0.09375 to 0.09375
- cotangent: bfloat16 [2048, 8, 1536], P(('ctx', 'tp'), 'fsdp'), may hold values from -6 to 6
Outputs:
- output: bfloat16 [2048, 8, 1536], P(('ctx', 'tp'), 'fsdp')
- input_grad: bfloat16 [2048, 8, 1536], P(('ctx', 'tp'), 'fsdp')
- attn_gain_grad: float32 [1536], P(('fsdp', 'ctx'))
- w_query_grad: float32 [1536, 1536], P(('fsdp', 'ctx'), 'tp')
- w_key_grad: float32 [1536, 1536], P(('fsdp', 'ctx'), 'tp')
- w_value_grad: float32 [1536, 1536], P(('fsdp', 'ctx'), 'tp')
- w_forget_grad: float32 [1536, 24], P(('fsdp', 'ctx'), 'tp')
- forget_bias_grad: float32 [24], P('tp')
- w_gate_out_grad: float32 [1536, 1536], P(('fsdp', 'ctx'), 'tp')
- w_out_grad: float32 [1536, 1536], P(('fsdp', 'ctx'), 'tp')
- mlp_gain_grad: float32 [1536], P(('fsdp', 'ctx'))
- w_gate_grad: float32 [1536, 4096], P(('fsdp', 'ctx'), 'tp')
- w_up_grad: float32 [1536, 4096], P(('fsdp', 'ctx'), 'tp')
- w_down_grad: float32 [1536, 4096], P(('fsdp', 'ctx'), 'tp')
Inputs may be any that keep to these rules, and one draw needn't show every extreme that they name: Slots l < lengths[b] of sequence b are valid; in every draw one sequence has 2048 valid slots and one has 512.
All inputs are finite; a program needn't handle non-finite values.
Results may differ from a plain program's by a relative error of at most 0.017.
Values may be sent and summed in bfloat16 or wider, within the bound.
A program may use at most 256 MiB of HBM per device.

v0:
```python
import jax
import jax.numpy as jnp
from jax import lax
from jax.sharding import PartitionSpec as P

QB = 512


epsilon = 1e-06
masked_score = -1e30


def row_norm(values):
    inverse = lax.rsqrt(jnp.mean(values * values, axis=-1, keepdims=True) + epsilon)
    return (values * inverse, inverse)


def norm_back(grad_normed, unit_rows, inverse, gain_vec):
    scaled = grad_normed * gain_vec
    inner_mean = jnp.mean(scaled * unit_rows, axis=-1, keepdims=True)
    return inverse * (scaled - unit_rows * inner_mean)


def spread_rows(row_values):
    return lax.all_gather(row_values, "tp", axis=0, tiled=True)


def summed_row_values(term_pairs):
    summed = None
    for operand, weight, pattern, axis_pos in term_pairs:
        product = jnp.einsum(pattern, operand, weight, preferred_element_type=jnp.float32)
        summed = product if summed is None else summed + product
    return lax.psum_scatter(summed, "tp", scatter_dimension=0, tiled=True)


def per_device(
    layer_input,
    lengths,
    attn_gain,
    w_query,
    w_key,
    w_value,
    w_forget,
    forget_bias,
    w_gate_out,
    w_out,
    mlp_gain,
    w_gate,
    w_up,
    w_down,
    cotangent,
):
    local_rows, seq_count, model_width = layer_input.shape
    head_count = forget_bias.shape[0]
    head_size = w_query.shape[1] // head_count
    tp_size = lax.axis_size("tp")
    ctx_size = lax.axis_size("ctx")
    shard_count = lax.axis_size("fsdp") * ctx_size
    ctx_rows = local_rows * tp_size
    seq_len = ctx_rows * ctx_size
    item_count = seq_count * head_count // ctx_size
    item_total = seq_count * head_count
    score_scale = head_size ** (-0.5)
    ctx_index = lax.axis_index("ctx")
    tp_index = lax.axis_index("tp")
    shard_index = lax.axis_index("fsdp") * ctx_size + ctx_index
    (
        gain_one,
        query_w,
        key_w,
        value_w,
        forget_w,
        outgate_w,
        out_w,
        gain_two,
        gate_matrix,
        up_matrix,
        down_matrix,
    ) = (
        lax.all_gather(attn_gain, ("fsdp", "ctx"), axis=0, tiled=True),
        lax.all_gather(w_query, ("fsdp", "ctx"), axis=0, tiled=True),
        lax.all_gather(w_key, ("fsdp", "ctx"), axis=0, tiled=True),
        lax.all_gather(w_value, ("fsdp", "ctx"), axis=0, tiled=True),
        lax.all_gather(w_forget, ("fsdp", "ctx"), axis=0, tiled=True),
        lax.all_gather(w_gate_out, ("fsdp", "ctx"), axis=0, tiled=True),
        lax.all_gather(w_out, ("fsdp", "ctx"), axis=0, tiled=True),
        lax.all_gather(mlp_gain, ("fsdp", "ctx"), axis=0, tiled=True),
        lax.all_gather(w_gate, ("fsdp", "ctx"), axis=0, tiled=True),
        lax.all_gather(w_up, ("fsdp", "ctx"), axis=0, tiled=True),
        lax.all_gather(w_down, ("fsdp", "ctx"), axis=0, tiled=True),
    )

    def cube_of(weight):
        return weight.reshape(model_width, head_count, head_size)

    local_pos = (ctx_index * tp_size + tp_index) * local_rows + jnp.arange(
        local_rows, dtype=jnp.int32
    )
    valid_rows = (local_pos[:, None] < lengths[None, :]).astype(jnp.float32)
    ctx_pos = ctx_index * ctx_rows + jnp.arange(ctx_rows, dtype=jnp.int32)
    ctx_valid = (ctx_pos[None, :] < lengths[:, None]).astype(jnp.float32)
    item_seq = (ctx_index * item_count + jnp.arange(item_count, dtype=jnp.int32)) // head_count
    seq_ids = jnp.arange(seq_count, dtype=jnp.int32)
    item_len = jnp.sum(
        jnp.where(item_seq[:, None] == seq_ids[None, :], lengths[None, :], 0), axis=1
    )
    key_pos = jnp.arange(seq_len, dtype=jnp.int32)
    key_ok = key_pos[None, :] < item_len[:, None]
    input_f = layer_input.astype(jnp.float32)
    unit_one, inverse_one = row_norm(input_f)
    gain_one_f = gain_one.astype(jnp.float32)
    normed_one = spread_rows((unit_one * gain_one_f).astype(jnp.bfloat16))

    def head_rows(weight_cube):
        return jnp.einsum(
            "lsd,dhe->shel", normed_one, weight_cube, preferred_element_type=jnp.float32
        )

    query_rows = (
        head_rows(cube_of(query_w)).astype(jnp.bfloat16).reshape(item_total, head_size, ctx_rows)
    )
    key_rows = (
        head_rows(cube_of(key_w)).astype(jnp.bfloat16).reshape(item_total, head_size, ctx_rows)
    )
    value_rows = (
        head_rows(cube_of(value_w)).astype(jnp.bfloat16).reshape(item_total, head_size, ctx_rows)
    )
    forget_logit = jnp.einsum(
        "lsd,dh->shl", normed_one, forget_w, preferred_element_type=jnp.float32
    )
    forget_logit = forget_logit + forget_bias.astype(jnp.float32)[None, :, None]
    log_forget = (
        (ctx_valid[:, None, :] * jax.nn.log_sigmoid(forget_logit))
        .astype(jnp.bfloat16)
        .reshape(item_total, 1, ctx_rows)
    )
    query_items, key_items, value_items, forget_items = (
        lax.all_to_all(query_rows, "ctx", split_axis=0, concat_axis=2, tiled=True),
        lax.all_to_all(key_rows, "ctx", split_axis=0, concat_axis=2, tiled=True),
        lax.all_to_all(value_rows, "ctx", split_axis=0, concat_axis=2, tiled=True),
        lax.all_to_all(log_forget, "ctx", split_axis=0, concat_axis=2, tiled=True),
    )
    decay_sum = jnp.cumsum(forget_items[:, 0, :].astype(jnp.float32), axis=1)
    block_total = seq_len // QB

    def block_scores(block_index):
        row_start = block_index * QB
        query_block = lax.dynamic_slice_in_dim(query_items, row_start, QB, 2)
        decay_here = lax.dynamic_slice_in_dim(decay_sum, row_start, QB, 1)
        scores = (
            jnp.einsum("iek,iel->ikl", query_block, key_items, preferred_element_type=jnp.float32)
            * score_scale
        )
        scores = scores + decay_here[:, :, None] - decay_sum[:, None, :]
        query_pos = row_start + jnp.arange(QB, dtype=jnp.int32)
        allowed = (key_pos[None, None, :] <= query_pos[None, :, None]) & key_ok[:, None, :]
        return (jnp.where(allowed, scores, masked_score), query_block)

    def forward_block(block_index):
        scores, query_block = block_scores(block_index)
        row_top = jnp.max(scores, axis=2, keepdims=True)
        weight = jnp.exp(scores - row_top)
        row_total = jnp.sum(weight, axis=2, keepdims=True)
        prob_rows = (weight / row_total).astype(jnp.bfloat16)
        attended = jnp.einsum(
            "ikl,iel->iek", prob_rows, value_items, preferred_element_type=jnp.float32
        )
        return (attended.astype(jnp.bfloat16), (row_top + jnp.log(row_total))[:, :, 0])

    att_blocks, lse_blocks = lax.map(forward_block, jnp.arange(block_total, dtype=jnp.int32))
    attended_items = att_blocks.transpose(1, 2, 0, 3).reshape(item_count, head_size, seq_len)
    log_total = lse_blocks.transpose(1, 0, 2).reshape(item_count, seq_len)
    attended_rows = lax.all_to_all(
        attended_items, "ctx", split_axis=2, concat_axis=0, tiled=True
    ).reshape(seq_count, head_count, head_size, ctx_rows)
    attended_f = attended_rows.astype(jnp.float32)
    out_gate = jax.nn.sigmoid(head_rows(cube_of(outgate_w)))
    mixed_out = (attended_f * out_gate).astype(jnp.bfloat16)
    attn_branch = summed_row_values([(mixed_out, cube_of(out_w), "shel,dhe->lsd", 3)])
    hidden_state = input_f + attn_branch
    unit_two, inverse_two = row_norm(hidden_state)
    gain_two_f = gain_two.astype(jnp.float32)
    second_normed_input = spread_rows((unit_two * gain_two_f).astype(jnp.bfloat16))
    gate_preactivation = jnp.einsum(
        "kag,gr->kar", second_normed_input, gate_matrix, preferred_element_type=jnp.float32
    )
    up_projection = jnp.einsum(
        "kag,gr->kar", second_normed_input, up_matrix, preferred_element_type=jnp.float32
    )
    gate_sig = jax.nn.sigmoid(gate_preactivation)
    silu_gate = gate_preactivation * gate_sig
    inner_activation = (silu_gate * up_projection).astype(jnp.bfloat16)
    feedforward_branch = summed_row_values([(inner_activation, down_matrix, "gex,rx->ger", 0)])
    output = (valid_rows[:, :, None] * (hidden_state + feedforward_branch)).astype(jnp.bfloat16)
    grad_out = valid_rows[:, :, None] * cotangent.astype(jnp.float32)
    gradient_row_values = spread_rows(grad_out.astype(jnp.bfloat16))
    gradient_inner_act = jnp.einsum(
        "kag,gr->kar", gradient_row_values, down_matrix, preferred_element_type=jnp.float32
    )
    gradient_gate_branch = (
        gradient_inner_act
        * up_projection
        * gate_sig
        * (1.0 + gate_preactivation * (1.0 - gate_sig))
    ).astype(jnp.bfloat16)
    gradient_up_branch = (gradient_inner_act * silu_gate).astype(jnp.bfloat16)
    down_weight_gradient = jnp.einsum(
        "yqv,yqi->vi", gradient_row_values, inner_activation, preferred_element_type=jnp.float32
    )
    gate_weight_gradient = jnp.einsum(
        "yqv,yqi->vi", second_normed_input, gradient_gate_branch, preferred_element_type=jnp.float32
    )
    up_weight_gradient = jnp.einsum(
        "yqv,yqi->vi", second_normed_input, gradient_up_branch, preferred_element_type=jnp.float32
    )
    grad_normed_two = summed_row_values(
        [
            (gradient_gate_branch, gate_matrix, "gex,rx->ger", 0),
            (gradient_up_branch, up_matrix, "gex,rx->ger", 0),
        ]
    )
    mlp_gain_part = jnp.sum(grad_normed_two * unit_two, axis=(0, 1))
    grad_hidden = grad_out + norm_back(grad_normed_two, unit_two, inverse_two, gain_two_f)
    branch_rows = spread_rows(grad_hidden.astype(jnp.bfloat16))
    grad_mixed = jnp.einsum(
        "lsd,dhe->shel", branch_rows, cube_of(out_w), preferred_element_type=jnp.float32
    )
    out_grad = jnp.einsum(
        "lsd,shel->dhe", branch_rows, mixed_out, preferred_element_type=jnp.float32
    ).reshape(model_width, head_count * head_size)
    grad_attended = (
        (grad_mixed * out_gate).astype(jnp.bfloat16).reshape(item_total, head_size, ctx_rows)
    )
    grad_gate_logit = (grad_mixed * attended_f * out_gate * (1.0 - out_gate)).astype(jnp.bfloat16)
    outgate_grad = jnp.einsum(
        "lsd,shel->dhe", normed_one, grad_gate_logit, preferred_element_type=jnp.float32
    ).reshape(model_width, head_count * head_size)
    grad_items = lax.all_to_all(grad_attended, "ctx", split_axis=0, concat_axis=2, tiled=True)

    def backward_block(totals, block_index):
        key_acc, value_acc, column_acc = totals
        scores, query_block = block_scores(block_index)
        row_start = block_index * QB
        lse_here = lax.dynamic_slice_in_dim(log_total, row_start, QB, 1)
        prob_f = jnp.exp(scores - lse_here[:, :, None])
        grad_block = lax.dynamic_slice_in_dim(grad_items, row_start, QB, 2)
        grad_prob = jnp.einsum(
            "iek,iel->ikl", grad_block, value_items, preferred_element_type=jnp.float32
        )
        row_inner = jnp.sum(prob_f * grad_prob, axis=2, keepdims=True)
        grad_score = (prob_f * (grad_prob - row_inner)).astype(jnp.bfloat16)
        grad_score_f = grad_score.astype(jnp.float32)
        query_grad_block = (
            jnp.einsum("ikl,iel->iek", grad_score, key_items, preferred_element_type=jnp.float32)
            * score_scale
        )
        key_acc = (
            key_acc
            + jnp.einsum(
                "ikl,iek->iel", grad_score, query_block, preferred_element_type=jnp.float32
            )
            * score_scale
        )
        value_acc = value_acc + jnp.einsum(
            "ikl,iek->iel",
            prob_f.astype(jnp.bfloat16),
            grad_block,
            preferred_element_type=jnp.float32,
        )
        column_acc = column_acc + jnp.sum(grad_score_f, axis=1)
        return ((key_acc, value_acc, column_acc), (query_grad_block, jnp.sum(grad_score_f, axis=2)))

    zero_grad = jnp.zeros((item_count, head_size, seq_len), jnp.float32)
    zero_decay = jnp.zeros((item_count, seq_len), jnp.float32)
    (key_grad_items, value_grad_items, column_sum), (query_blocks, row_blocks) = lax.scan(
        backward_block, (zero_grad, zero_grad, zero_decay), jnp.arange(block_total, dtype=jnp.int32)
    )
    query_grad_items = query_blocks.transpose(1, 2, 0, 3).reshape(item_count, head_size, seq_len)
    decay_grad = row_blocks.transpose(1, 0, 2).reshape(item_count, seq_len) - column_sum
    forget_grad_items = jnp.flip(jnp.cumsum(jnp.flip(decay_grad, 1), axis=1), 1)
    grad_query, grad_key, grad_value, grad_forget = (
        lax.all_to_all(
            query_grad_items.astype(jnp.bfloat16), "ctx", split_axis=2, concat_axis=0, tiled=True
        ),
        lax.all_to_all(
            key_grad_items.astype(jnp.bfloat16), "ctx", split_axis=2, concat_axis=0, tiled=True
        ),
        lax.all_to_all(
            value_grad_items.astype(jnp.bfloat16), "ctx", split_axis=2, concat_axis=0, tiled=True
        ),
        lax.all_to_all(
            forget_grad_items.astype(jnp.bfloat16)[:, None, :],
            "ctx",
            split_axis=2,
            concat_axis=0,
            tiled=True,
        ),
    )
    grad_query = grad_query.reshape(seq_count, head_count, head_size, ctx_rows)
    grad_key = grad_key.reshape(seq_count, head_count, head_size, ctx_rows)
    grad_value = grad_value.reshape(seq_count, head_count, head_size, ctx_rows)
    grad_forget_logit = (
        grad_forget.reshape(seq_count, head_count, ctx_rows).astype(jnp.float32)
        * ctx_valid[:, None, :]
        * jax.nn.sigmoid(-forget_logit)
    ).astype(jnp.bfloat16)
    forget_grad = jnp.einsum(
        "lsd,shl->dh", normed_one, grad_forget_logit, preferred_element_type=jnp.float32
    )
    bias_part = jnp.sum(grad_forget_logit.astype(jnp.float32), axis=(0, 2))
    query_grad = jnp.einsum(
        "lsd,shel->dhe", normed_one, grad_query, preferred_element_type=jnp.float32
    ).reshape(model_width, head_count * head_size)
    key_grad = jnp.einsum(
        "lsd,shel->dhe", normed_one, grad_key, preferred_element_type=jnp.float32
    ).reshape(model_width, head_count * head_size)
    value_grad = jnp.einsum(
        "lsd,shel->dhe", normed_one, grad_value, preferred_element_type=jnp.float32
    ).reshape(model_width, head_count * head_size)
    grad_normed_one = summed_row_values(
        [
            (grad_query, cube_of(query_w), "shel,dhe->lsd", 3),
            (grad_key, cube_of(key_w), "shel,dhe->lsd", 3),
            (grad_value, cube_of(value_w), "shel,dhe->lsd", 3),
            (grad_gate_logit, cube_of(outgate_w), "shel,dhe->lsd", 3),
            (grad_forget_logit, forget_w, "shl,dh->lsd", 2),
        ]
    )
    attn_gain_part = jnp.sum(grad_normed_one * unit_one, axis=(0, 1))
    input_grad = (
        grad_hidden + norm_back(grad_normed_one, unit_one, inverse_one, gain_one_f)
    ).astype(jnp.bfloat16)
    bias_full = lax.dynamic_update_slice(
        jnp.zeros((head_count * tp_size,), jnp.float32), bias_part, (tp_index * head_count,)
    )
    gain_one_sum, gain_two_sum, bias_sum = lax.psum(
        (attn_gain_part, mlp_gain_part, bias_full), ("fsdp", "ctx", "tp")
    )
    shard_rows = model_width // shard_count
    attn_gain_grad = lax.dynamic_slice_in_dim(gain_one_sum, shard_index * shard_rows, shard_rows, 0)
    mlp_gain_grad = lax.dynamic_slice_in_dim(gain_two_sum, shard_index * shard_rows, shard_rows, 0)
    forget_bias_grad = lax.dynamic_slice_in_dim(bias_sum, tp_index * head_count, head_count, 0)
    query_sum, key_sum, value_sum, forget_sum, outgate_sum, out_sum, gate_sum, up_sum, down_sum = (
        lax.psum_scatter(query_grad, ("fsdp", "ctx"), scatter_dimension=0, tiled=True),
        lax.psum_scatter(key_grad, ("fsdp", "ctx"), scatter_dimension=0, tiled=True),
        lax.psum_scatter(value_grad, ("fsdp", "ctx"), scatter_dimension=0, tiled=True),
        lax.psum_scatter(forget_grad, ("fsdp", "ctx"), scatter_dimension=0, tiled=True),
        lax.psum_scatter(outgate_grad, ("fsdp", "ctx"), scatter_dimension=0, tiled=True),
        lax.psum_scatter(out_grad, ("fsdp", "ctx"), scatter_dimension=0, tiled=True),
        lax.psum_scatter(gate_weight_gradient, ("fsdp", "ctx"), scatter_dimension=0, tiled=True),
        lax.psum_scatter(up_weight_gradient, ("fsdp", "ctx"), scatter_dimension=0, tiled=True),
        lax.psum_scatter(down_weight_gradient, ("fsdp", "ctx"), scatter_dimension=0, tiled=True),
    )
    return (
        output,
        input_grad,
        attn_gain_grad,
        query_sum,
        key_sum,
        value_sum,
        forget_sum,
        forget_bias_grad,
        outgate_sum,
        out_sum,
        mlp_gain_grad,
        gate_sum,
        up_sum,
        down_sum,
    )


def solution(mesh):
    return jax.shard_map(
        per_device,
        mesh=mesh,
        in_specs=(
            P(("ctx", "tp"), "fsdp", None),
            P("fsdp"),
            P(("fsdp", "ctx")),
            P(("fsdp", "ctx"), "tp"),
            P(("fsdp", "ctx"), "tp"),
            P(("fsdp", "ctx"), "tp"),
            P(("fsdp", "ctx"), "tp"),
            P("tp"),
            P(("fsdp", "ctx"), "tp"),
            P(("fsdp", "ctx"), "tp"),
            P(("fsdp", "ctx")),
            P(("fsdp", "ctx"), "tp"),
            P(("fsdp", "ctx"), "tp"),
            P(("fsdp", "ctx"), "tp"),
            P(("ctx", "tp"), "fsdp", None),
        ),
        out_specs=(
            P(("ctx", "tp"), "fsdp", None),
            P(("ctx", "tp"), "fsdp", None),
            P(("fsdp", "ctx")),
            P(("fsdp", "ctx"), "tp"),
            P(("fsdp", "ctx"), "tp"),
            P(("fsdp", "ctx"), "tp"),
            P(("fsdp", "ctx"), "tp"),
            P("tp"),
            P(("fsdp", "ctx"), "tp"),
            P(("fsdp", "ctx"), "tp"),
            P(("fsdp", "ctx")),
            P(("fsdp", "ctx"), "tp"),
            P(("fsdp", "ctx"), "tp"),
            P(("fsdp", "ctx"), "tp"),
        ),
        check_vma=False,
    )
```

profile of v0, /device:TPU:0, one launch (start us, length us, event | category | flops | bytes accessed | tf_op | source)
XLA Modules:
  0.0 2689.2 jit_solution(9009633147254347707)
XLA Ops:
  11.6 24.4 all-reduce.3
  42.3 30.5 %all-gather = bf16[8,192,6]{1,2,0:T(8,128)(2,1)S(1)} all-gather(bf16[1,192,6]{1,2,0:T(8,128)(2,1)S(1)} %bitcast.433), channel_id=1, replica_groups=mesh['fsdp'=2,'ctx'=4,'tp'=4] {'fsdp','ctx'}, dimensions={0}, use_global_device_ids=true | all-gather | bytes 20736 | tf_op jit(solution)/shard_map/all_gather | solution.py:84
  74.6 27.0 %all-gather.14.cloned.1.call-done = bf16[512,4,1536]{2,0,1:T(8,128)(2,1)} async-done(((bf16[128,4,1536]{2,0,1:T(8,128)(2,1)}), bf16[512,4,1536]{2,0,1:T(8,128)(2,1)}) %all-gather.14.cloned.1.call-update) | async-done | bytes 6291472 | tf_op jit(solution)/shard_map/all_gather | solution.py:25
  127.0 26.8 all-gather.20.cloned.1.call-done
  177.9 46.6 %all-gather.16.cloned.1.call-done = bf16[1536,384]{1,0:T(8,128)(2,1)} async-done(((bf16[192,384]{1,0:T(8,128)(2,1)}), bf16[1536,384]{1,0:T(8,128)(2,1)}) %all-gather.16.cloned.1.call-update) | async-done | bytes 1179664 | tf_op jit(solution)/shard_map/all_gather | solution.py:81
  252.5 27.9 %all-to-all-done = bf16[24,64,512]{2,1,0:T(8,128)(2,1)} async-done(((bf16[24,64,512]{2,1,0:T(8,128)(2,1)}), bf16[24,64,512]{2,1,0:T(8,128)(2,1)}, u32[]{:S(2)}, u32[]{:S(2)}) %all-to-all-start) | async-done | bytes 1572896 | tf_op jit(solution)/shard_map/all_to_all | solution.py:138
  287.0 168.2 %while.32 = (s32[]{:T(128)}, bf16[4,6,64,512]{3,2,1,0:T(8,128)(2,1)}, f32[4,6,512]{2,1,0:T(8,128)S(1)}, s32[4]{0:T(128)S(1)}, bf16[6,64,2048]{2,1,0:T(8,128)(2,1...) while((s32[]{:T(128)}, ...), condition=%wide.region_7.8_spmd.clone, body=%wide.region_4.7_spmd.clone.sunk | while | flops 1743988224 | bytes 184684784 | solution.py:170
  472.6 54.2 %all-gather.24.cloned.1.call-done = bf16[1536,384]{1,0:T(8,128)(2,1)} async-done(((bf16[192,384]{1,0:T(8,128)(2,1)}), bf16[1536,384]{1,0:T(8,128)(2,1)}) %all-gather.24.cloned.1.call-update) | async-done | bytes 1179664 | tf_op jit(solution)/shard_map/all_gather | solution.py:86
  554.5 97.2 %reduce-scatter.16.cloned.1.call-done = f32[128,4,1536]{2,0,1:T(8,128)} async-done(((f32[512,4,1536]{2,0,1:T(8,128)}), f32[128,4,1536]{2,0,1:T(8,128)}) %reduce-scatter.16.cloned.1.call-update) | async-done | bytes 3145744 | tf_op jit(solution)/shard_map/reduce_scatter | solution.py:33
  660.8 53.4 %all-gather.30.cloned.1.call-done = bf16[1536,1024]{1,0:T(8,128)(2,1)} async-done(((bf16[192,1024]{1,0:T(8,128)(2,1)}), bf16[1536,1024]{1,0:T(8,128)(2,1)}) %all-gather.30.cloned.1.call-update) | async-done | bytes 3145744 | tf_op jit(solution)/shard_map/all_gather | solution.py:89
  714.2 47.2 %all-gather.26.cloned.1.call-done = bf16[512,4,1536]{2,0,1:T(8,128)(2,1)} async-done(((bf16[128,4,1536]{2,0,1:T(8,128)(2,1)}), bf16[512,4,1536]{2,0,1:T(8,128)(2,1)}) %all-gather.26.cloned.1.call-update) | async-done | bytes 6291472 | tf_op jit(solution)/shard_map/all_gather | solution.py:25
  773.5 50.3 %all-gather.28.cloned.1.call-done = bf16[1536,1024]{1,0:T(8,128)(2,1)} async-done(((bf16[192,1024]{1,0:T(8,128)(2,1)}), bf16[1536,1024]{1,0:T(8,128)(2,1)}) %all-gather.28.cloned.1.call-update) | async-done | bytes 3145744 | tf_op jit(solution)/shard_map/all_gather | solution.py:88
  835.4 49.6 %all-gather.32.cloned.1.call-done = bf16[1536,1024]{1,0:T(8,128)(2,1)} async-done(((bf16[192,1024]{1,0:T(8,128)(2,1)}), bf16[1536,1024]{1,0:T(8,128)(2,1)}) %all-gather.32.cloned.1.call-update) | async-done | bytes 3145744 | tf_op jit(solution)/shard_map/all_gather | solution.py:90
  885.0 47.0 %all-gather.34.cloned.1.call-done = bf16[512,4,1536]{2,0,1:T(8,128)(2,1)} async-done(((bf16[128,4,1536]{2,0,1:T(8,128)(2,1)}), bf16[512,4,1536]{2,0,1:T(8,128)(2,1)}) %all-gather.34.cloned.1.call-update) | async-done | bytes 6291472 | tf_op jit(solution)/shard_map/all_gather | solution.py:25
  975.4 99.2 %reduce-scatter.20.cloned.1.call-done = f32[128,4,1536]{2,0,1:T(8,128)} async-done(((f32[512,4,1536]{2,0,1:T(8,128)}), f32[128,4,1536]{2,0,1:T(8,128)}) %reduce-scatter.20.cloned.1.call-update) | async-done | bytes 3145744 | tf_op jit(solution)/shard_map/reduce_scatter | solution.py:33
  1080.3 46.5 %all-gather.36.cloned.1.call-done = bf16[512,4,1536]{2,0,1:T(8,128)(2,1)} async-done(((bf16[128,4,1536]{2,0,1:T(8,128)(2,1)}), bf16[512,4,1536]{2,0,1:T(8,128)(2,1)}) %all-gather.36.cloned.1.call-update) | async-done | bytes 6291472 | tf_op jit(solution)/shard_map/all_gather | solution.py:25
  1140.8 37.5 %all-to-all-done.5 = bf16[24,64,512]{2,1,0:T(8,128)(2,1)} async-done(((bf16[24,64,512]{2,1,0:T(8,128)(2,1)}), bf16[24,64,512]{2,1,0:T(8,128)(2,1)}, u32[]{:S(2)}, u32[]{:S(2)}) %all-to-all-start.5) | async-done | bytes 1572896 | tf_op jit(solution)/shard_map/all_to_all | solution.py:238
  1185.9 355.5 %while.33 = (s32[]{:T(128)}, f32[6,64,2048]{2,1,0:T(8,128)}, f32[6,64,2048]{2,1,0:T(8,128)S(1)}, f32[6,2048]{1,0:T(8,128)S(1)}, bf16[4,6,64,512]{3,2,1,0:T(8,128...) while((s32[]{:T(128)}, f32[6,64,2048]{2,1,0:T(8,128)}, ...), condition=%wide.region_17.18_spmd.clone, body=%wide.region_13.17_spmd.clone.sunk | while | flops 4126099968 | bytes 210919728 | solution.py:275
  1223.6 21.3 convert_reduce_fusion.5
  1311.6 21.3 convert_reduce_fusion.5
  1597.1 23.6 all-to-all-done.8
  1634.0 26.8 all-to-all-done.7
  1855.4 40.1 %all-reduce.2 = (f32[1536]{0:T(1024)S(1)}, f32[24]{0:T(128)S(1)}, f32[1536]{0:T(1024)S(1)}) all-reduce(f32[1536]{0:T(1024)S(1)} %get-tuple-element.329, f32[24]{0:T(128)S(1)} %dynamic_update_slice.18, f32[1536]{0:T(1024)S(1)} %copy-done.28), channel_id=1, replica_groups=mesh['fsdp'=2,'ctx'=4,'tp'=4] {'fsdp','ctx','tp'}, use_global_device_ids=true, to_apply=%region_23.24 | all-reduce | flops 3096 | bytes 24768 | tf_op jit(solution)/shard_map/psum | solution.py:336
  1897.4 57.0 %reduce-scatter.18.cloned.1.call-done = f32[128,4,1536]{2,0,1:T(8,128)} async-done(((f32[512,4,1536]{2,0,1:T(8,128)}), f32[128,4,1536]{2,0,1:T(8,128)}) %reduce-scatter.18.cloned.1.call-update) | async-done | bytes 3145744 | tf_op jit(solution)/shard_map/reduce_scatter | solution.py:33
  1965.0 111.8 %reduce-scatter.38.cloned.1.call-done = f32[192,1024]{1,0:T(8,128)} async-done(((f32[1536,1024]{1,0:T(8,128)}), f32[192,1024]{1,0:T(8,128)}) %reduce-scatter.38.cloned.1.call-update) | async-done | bytes 786448 | tf_op jit(solution)/shard_map/reduce_scatter | solution.py:352
  2076.8 121.7 %reduce-scatter.34.cloned.1.call-done = f32[192,1024]{1,0:T(8,128)} async-done(((f32[1536,1024]{1,0:T(8,128)}), f32[192,1024]{1,0:T(8,128)}) %reduce-scatter.34.cloned.1.call-update) | async-done | bytes 786448 | tf_op jit(solution)/shard_map/reduce_scatter | solution.py:350
  2198.5 121.5 %reduce-scatter.36.cloned.1.call-done = f32[192,1024]{1,0:T(8,128)} async-done(((f32[1536,1024]{1,0:T(8,128)}), f32[192,1024]{1,0:T(8,128)}) %reduce-scatter.36.cloned.1.call-update) | async-done | bytes 786448 | tf_op jit(solution)/shard_map/reduce_scatter | solution.py:351
  2320.0 72.6 %reduce-scatter.32.cloned.1.call-done = f32[192,384]{1,0:T(8,128)} async-done(((f32[1536,384]{1,0:T(8,128)}), f32[192,384]{1,0:T(8,128)}) %reduce-scatter.32.cloned.1.call-update) | async-done | bytes 294928 | tf_op jit(solution)/shard_map/reduce_scatter | solution.py:349
  2392.6 72.5 %reduce-scatter.30.cloned.1.call-done = f32[192,384]{1,0:T(8,128)} async-done(((f32[1536,384]{1,0:T(8,128)}), f32[192,384]{1,0:T(8,128)}) %reduce-scatter.30.cloned.1.call-update) | async-done | bytes 294928 | tf_op jit(solution)/shard_map/reduce_scatter | solution.py:348
  2465.1 72.5 %reduce-scatter.28.cloned.1.call-done = f32[192,384]{1,0:T(8,128)} async-done(((f32[1536,384]{1,0:T(8,128)}), f32[192,384]{1,0:T(8,128)}) %reduce-scatter.28.cloned.1.call-update) | async-done | bytes 294928 | tf_op jit(solution)/shard_map/reduce_scatter | solution.py:346
  2537.5 72.4 %reduce-scatter.26.cloned.1.call-done = f32[192,384]{1,0:T(8,128)} async-done(((f32[1536,384]{1,0:T(8,128)}), f32[192,384]{1,0:T(8,128)}) %reduce-scatter.26.cloned.1.call-update) | async-done | bytes 294928 | tf_op jit(solution)/shard_map/reduce_scatter | solution.py:345
  2609.9 72.5 %reduce-scatter.24.cloned.1.call-done = f32[192,384]{1,0:T(8,128)} async-done(((f32[1536,384]{1,0:T(8,128)}), f32[192,384]{1,0:T(8,128)}) %reduce-scatter.24.cloned.1.call-update) | async-done | bytes 294928 | tf_op jit(solution)/shard_map/reduce_scatter | solution.py:344
  (400 shorter events, 994.1 us)
Async XLA Ops:
  7.2 65.8 %all-gather.18.cloned.1.call-start = ((), (), s32[]{:S(2)}) async-start(), calls=%async_computation.25 | async-start | bytes 1327104 | tf_op jit(solution)/shard_map/all_gather | solution.py:82
  7.9 93.7 %all-gather.14.cloned.1.call-start = ((), (), s32[]{:S(2)}) async-start(), calls=%async_computation.23 | async-start | bytes 7864320 | tf_op jit(solution)/shard_map/all_gather | solution.py:25
  41.5 112.2 %all-gather.20.cloned.1.call-start = ((), (), s32[]{:S(2)}) async-start(), calls=%async_computation.26 | async-start | bytes 1327104 | tf_op jit(solution)/shard_map/all_gather | solution.py:83
  121.3 51.4 %all-to-all-start.1 = ((bf16[24,64,512]{2,1,0:T(8,128)(2,1)}), bf16[24,64,512]{2,1,0:T(8,128)(2,1)S(1)}, u32[]{:S(2)}, u32[]{:S(2)}) async-start(bf16[24,64,512]{2,1,0:T(8,128)(2,1)} %bitcast.13), calls=%async_computation.1 | async-start | bytes 3145728 | tf_op jit(solution)/shard_map/all_to_all | solution.py:139
  126.4 98.0 %all-gather.16.cloned.1.call-start = ((), (), s32[]{:S(2)}) async-start(), calls=%async_computation.24 | async-start | bytes 1327104 | tf_op jit(solution)/shard_map/all_gather | solution.py:81
  172.7 61.0 %all-to-all-start.3 = ((bf16[24,64,512]{2,1,0:T(8,128)(2,1)}), bf16[24,64,512]{2,1,0:T(8,128)(2,1)S(1)}, u32[]{:S(2)}, u32[]{:S(2)}) async-start(bf16[24,64,512]{2,1,0:T(8,128)(2,1)} %bitcast.410), calls=%async_computation.3 | async-start | bytes 3145728 | tf_op jit(solution)/shard_map/all_to_all | solution.py:140
  233.7 46.7 %all-to-all-start = ((bf16[24,64,512]{2,1,0:T(8,128)(2,1)}), bf16[24,64,512]{2,1,0:T(8,128)(2,1)}, u32[]{:S(2)}, u32[]{:S(2)}) async-start(bf16[24,64,512]{2,1,0:T(8,128)(2,1)} %bitcast.409), calls=%async_computation | async-start | bytes 3145728 | tf_op jit(solution)/shard_map/all_to_all | solution.py:138
  238.1 232.9 %all-gather.22.cloned.1.call-start = ((), (), s32[]{:S(2)}) async-start(), calls=%async_computation.27 | async-start | bytes 1327104 | tf_op jit(solution)/shard_map/all_gather | solution.py:85
  466.8 62.5 %all-to-all-start.4 = ((bf16[4,2,98304]{2,1,0:T(2,128)(2,1)}), bf16[4,2,98304]{2,1,0:T(2,128)(2,1)S(1)}, u32[]{:S(2)}, u32[]{:S(2)}) async-start(bf16[4,2,98304]{2,1,0:T(2,128)(2,1)} %reshape.409), calls=%async_computation.4 | async-start | bytes 3145728 | tf_op jit(solution)/shard_map/all_to_all | solution.py:173
  470.3 56.5 %all-gather.24.cloned.1.call-start = ((), (), s32[]{:S(2)}) async-start(), calls=%async_computation.28 | async-start | bytes 1327104 | tf_op jit(solution)/shard_map/all_gather | solution.py:86
  470.9 180.7 %reduce-scatter.16.cloned.1.call-start = ((), (), s32[]{:S(2)}) async-start(), calls=%async_computation.29 | async-start | bytes 15728640 | tf_op jit(solution)/shard_map/reduce_scatter | solution.py:33
  553.6 160.6 %all-gather.30.cloned.1.call-start = ((), (), s32[]{:S(2)}) async-start(), calls=%async_computation.32 | async-start | bytes 3538944 | tf_op jit(solution)/shard_map/all_gather | solution.py:89
  554.4 207.0 %all-gather.26.cloned.1.call-start = ((), (), s32[]{:S(2)}) async-start(), calls=%async_computation.30 | async-start | bytes 7864320 | tf_op jit(solution)/shard_map/all_gather | solution.py:25
  656.3 167.5 %all-gather.28.cloned.1.call-start = ((), (), s32[]{:S(2)}) async-start(), calls=%async_computation.31 | async-start | bytes 3538944 | tf_op jit(solution)/shard_map/all_gather | solution.py:88
  656.9 228.1 %all-gather.32.cloned.1.call-start = ((), (), s32[]{:S(2)}) async-start(), calls=%async_computation.33 | async-start | bytes 3538944 | tf_op jit(solution)/shard_map/all_gather | solution.py:90
  657.6 274.4 %all-gather.34.cloned.1.call-start = ((), (), s32[]{:S(2)}) async-start(), calls=%async_computation.35 | async-start | bytes 7864320 | tf_op jit(solution)/shard_map/all_gather | solution.py:25
  660.7 413.9 %reduce-scatter.20.cloned.1.call-start = ((), (), s32[]{:S(2)}) async-start(), calls=%async_computation.36 | async-start | bytes 15728640 | tf_op jit(solution)/shard_map/reduce_scatter | solution.py:33
  975.4 151.5 %all-gather.36.cloned.1.call-start = ((), (), s32[]{:S(2)}) async-start(), calls=%async_computation.37 | async-start | bytes 7864320 | tf_op jit(solution)/shard_map/all_gather | solution.py:25
  1136.2 42.1 %all-to-all-start.5 = ((bf16[24,64,512]{2,1,0:T(8,128)(2,1)}), bf16[24,64,512]{2,1,0:T(8,128)(2,1)}, u32[]{:S(2)}, u32[]{:S(2)}) async-start(bf16[24,64,512]{2,1,0:T(8,128)(2,1)} %bitcast.46), calls=%async_computation.8 | async-start | bytes 3145728 | tf_op jit(solution)/shard_map/all_to_all | solution.py:238
  1579.6 41.2 %all-to-all-start.8 = ((bf16[4,2,98304]{2,1,0:T(2,128)(2,1)}), bf16[4,2,98304]{2,1,0:T(2,128)(2,1)}, u32[]{:S(2)}, u32[]{:S(2)}) async-start(bf16[4,2,98304]{2,1,0:T(2,128)(2,1)} %reshape.411), calls=%async_computation.11 | async-start | bytes 3145728 | tf_op jit(solution)/shard_map/all_to_all | solution.py:288
  1660.7 43.7 %all-to-all-start.6 = ((bf16[4,2,98304]{2,1,0:T(2,128)(2,1)}), bf16[4,2,98304]{2,1,0:T(2,128)(2,1)S(1)}, u32[]{:S(2)}, u32[]{:S(2)}) async-start(bf16[4,2,98304]{2,1,0:T(2,128)(2,1)} %reshape.415), calls=%async_computation.9 | async-start | bytes 3145728 | tf_op jit(solution)/shard_map/all_to_all | solution.py:282
  1664.3 180.9 %reduce-scatter.40.cloned.1.call-start = ((), (), s32[]{:S(2)}) async-start(), calls=%async_computation.47 | async-start | bytes 884736
  1685.5 166.6 %reduce-scatter.22.cloned.1.call-start = ((), (), s32[]{:S(2)}) async-start(), calls=%async_computation.38 | async-start | bytes 15728640 | tf_op jit(solution)/shard_map/reduce_scatter | solution.py:33
  1752.4 202.0 %reduce-scatter.18.cloned.1.call-start = ((), (), s32[]{:S(2)}) async-start(), calls=%async_computation.34 | async-start | bytes 15728640 | tf_op jit(solution)/shard_map/reduce_scatter | solution.py:33
  1766.4 310.4 %reduce-scatter.38.cloned.1.call-start = ((), (), s32[]{:S(2)}) async-start(), calls=%async_computation.46 | async-start | bytes 7077888 | tf_op jit(solution)/shard_map/reduce_scatter | solution.py:352
  1780.2 418.2 %reduce-scatter.34.cloned.1.call-start = ((), (), s32[]{:S(2)}) async-start(), calls=%async_computation.44 | async-start | bytes 7077888 | tf_op jit(solution)/shard_map/reduce_scatter | solution.py:350
  1793.0 527.0 %reduce-scatter.36.cloned.1.call-start = ((), (), s32[]{:S(2)}) async-start(), calls=%async_computation.45 | async-start | bytes 7077888 | tf_op jit(solution)/shard_map/reduce_scatter | solution.py:351
  1805.0 587.6 %reduce-scatter.32.cloned.1.call-start = ((), (), s32[]{:S(2)}) async-start(), calls=%async_computation.43 | async-start | bytes 2654208 | tf_op jit(solution)/shard_map/reduce_scatter | solution.py:349
  1812.2 652.9 %reduce-scatter.30.cloned.1.call-start = ((), (), s32[]{:S(2)}) async-start(), calls=%async_computation.42 | async-start | bytes 2654208 | tf_op jit(solution)/shard_map/reduce_scatter | solution.py:348
  1819.6 717.9 %reduce-scatter.28.cloned.1.call-start = ((), (), s32[]{:S(2)}) async-start(), calls=%async_computation.41 | async-start | bytes 2654208 | tf_op jit(solution)/shard_map/reduce_scatter | solution.py:346
  1828.0 781.8 %reduce-scatter.26.cloned.1.call-start = ((), (), s32[]{:S(2)}) async-start(), calls=%async_computation.40 | async-start | bytes 2654208 | tf_op jit(solution)/shard_map/reduce_scatter | solution.py:345
  1836.5 845.9 %reduce-scatter.24.cloned.1.call-start = ((), (), s32[]{:S(2)}) async-start(), calls=%async_computation.39 | async-start | bytes 2654208 | tf_op jit(solution)/shard_map/reduce_scatter | solution.py:344
  (55 other events, 2969.6 us)
Sparse Core Ops, SparseCore 0:
  10.1 44.0 all-gather.17
  56.4 45.1 all-gather.13
  103.7 50.0 all-gather.19
  155.7 68.6 all-gather.15
  240.7 54.4 all-gather.21
  473.0 53.8 all-gather.23
  553.8 97.8 reduce-scatter.15
  653.7 60.4 all-gather.29
  716.3 45.0 all-gather.25
  763.3 60.4 all-gather.27
  825.9 59.0 all-gather.31
  887.0 45.0 all-gather.33
  975.5 99.0 reduce-scatter.19
  1080.5 46.3 all-gather.35
  1685.6 63.2 reduce-scatter.39
  1752.5 99.5 reduce-scatter.21
  1854.7 99.6 reduce-scatter.17
  1958.8 117.8 reduce-scatter.37
  2081.4 117.0 reduce-scatter.33
  2202.9 117.0 reduce-scatter.35
  2324.5 68.0 reduce-scatter.31
  2397.1 67.9 reduce-scatter.29
  2469.5 67.9 reduce-scatter.27
  2541.8 67.9 reduce-scatter.25
  2614.4 67.9 reduce-scatter.23
where the time goes:
time: 2700 us; the launch traced here: 2690 us
  waiting for transfers between devices  1550 us (57%)
  matrix products  610 us (23%)
  other arithmetic  203 us (8%)
  local copies, waits for them, and re-layouts  160 us (6%)
  blocking collectives  95 us (4%)
  starting transfers between devices  44.8 us (2%)
    reduce_scatter x4, waiting for transfers between devices, summed_row_values(): return lax.psum_scatter(summed, 'tp', scatter_dimension=0, tiled=True)  258 us
    all_gather x4, waiting for transfers between devices, spread_rows(): return lax.all_gather(row_values, 'tp', axis=0, tiled=True)  168 us
    dot_general x8, matrix products, block_scores(): jnp.einsum('iek,iel->ikl', query_block, key_items, preferred_element_type...  139 us
    reduce_scatter x1, waiting for transfers between devices, per_device(): lax.psum_scatter(gate_weight_gradient, ('fsdp', 'ctx'), scatter_dimension...  122 us
    reduce_scatter x1, waiting for transfers between devices, per_device(): lax.psum_scatter(up_weight_gradient, ('fsdp', 'ctx'), scatter_dimension=0...  122 us
    reduce_scatter x1, waiting for transfers between devices, per_device(): lax.psum_scatter(down_weight_gradient, ('fsdp', 'ctx'), scatter_dimension...  112 us
    dot_general x9, matrix products, summed_row_values(): jnp.einsum(pattern, operand, weight, preferred_element_type=jnp.float32)  94.3 us
    reduce_sum x4, other arithmetic, backward_block(): jnp.sum(grad_score_f, axis=2)  85.1 us
  transfers between devices with their start and end apart: 35, of which 27 were waited for; matrix products, arithmetic and copies ran while one was open for 18% of the time, Pallas kernels for 0%

commit v1 on v0

v1 whole, which is shorter than its diff:
```python
import functools

import jax
import jax.numpy as jnp
from jax import lax
from jax.experimental import pallas as pl
from jax.experimental.pallas import tpu as pltpu
from jax.sharding import PartitionSpec as P

F32 = jnp.float32
BF16 = jnp.bfloat16
LANES = 128
epsilon = 1e-06
masked_score = -1e30
NT = (((1,), (1,)), ((), ()))
NN = (((1,), (0,)), ((), ()))
TN = (((0,), (0,)), ((), ()))


def dot(left, right, dims):
    return lax.dot_general(left, right, dims, preferred_element_type=F32)


def of_head(block, head, head_size, ones_at=None):
    lane = lax.broadcasted_iota(jnp.int32, block.shape, 1)
    out = jnp.where(lane // head_size == head, block, jnp.zeros_like(block))
    if ones_at is not None:
        out = jnp.where(lane == ones_at, jnp.ones_like(block), out)
    return out


def spare_lane(head, head_size):
    return ((head + 1) % 2) * head_size


def attend_forward(len_ref, qkv_ref, decay_ref, out_ref, exact_ref, lse_ref, *, heads, head_size):
    count, _, block, width = qkv_ref.shape
    scale = head_size**-0.5
    live = pl.cdiv(len_ref[0], block)
    out_ref[...] = jnp.zeros_like(out_ref)
    exact_ref[...] = jnp.zeros_like(exact_ref)
    lse_ref[...] = jnp.zeros_like(lse_ref)
    row = lax.broadcasted_iota(jnp.int32, (block, block), 0)
    column = lax.broadcasted_iota(jnp.int32, (block, block), 1)
    causal = column <= row

    def query_block(i, _):
        query = qkv_ref[i, 0]
        lanes = pl.ds(pl.multiple_of(i * block, block), block)
        result = jnp.zeros((block, width), F32)
        for head in range(heads):
            query_head = of_head(query, head, head_size)

            def step(j, carry, masked):
                top, total, acc = carry
                keys = pl.ds(pl.multiple_of(j * block, block), block)
                score = dot(query_head, qkv_ref[j, 1], NT) * scale
                score = score - decay_ref[head : head + 1, keys]
                if masked:
                    score = jnp.where(causal, score, masked_score)
                new_top = jnp.maximum(top, jnp.max(score, axis=1, keepdims=True))
                prob = jnp.exp(score - new_top)
                shrink = jnp.exp(top - new_top)
                total = total * shrink + jnp.sum(prob, axis=1, keepdims=True)
                acc = acc * shrink + dot(prob.astype(BF16), qkv_ref[j, 2], NN)
                return new_top, total, acc

            carry = (
                jnp.full((block, 1), masked_score, F32),
                jnp.zeros((block, 1), F32),
                jnp.zeros((block, width), F32),
            )
            carry = lax.fori_loop(0, i, lambda j, c: step(j, c, False), carry)
            top, total, acc = step(i, carry, True)
            lane = lax.broadcasted_iota(jnp.int32, acc.shape, 1)
            result = jnp.where(lane // head_size == head, acc / total, result)
            stat = jnp.broadcast_to(top + jnp.log(total), (block, LANES)).T
            lse_ref[head : head + 1, lanes] = stat[0:1]
        exact_ref[i] = result
        out_ref[i] = result.astype(BF16)
        return 0

    lax.fori_loop(0, live, query_block, 0)


def attend_backward(
    len_ref,
    qkv_ref,
    grad_ref,
    exact_ref,
    lse_ref,
    decay_ref,
    dqkv_ref,
    row_ref,
    column_ref,
    dq_acc,
    delta,
    *,
    heads,
    head_size,
):
    count, _, block, width = qkv_ref.shape
    scale = head_size**-0.5
    live = pl.cdiv(len_ref[0], block)
    for ref in (dqkv_ref, row_ref, column_ref, dq_acc):
        ref[...] = jnp.zeros_like(ref)
    row = lax.broadcasted_iota(jnp.int32, (block, block), 0)
    column = lax.broadcasted_iota(jnp.int32, (block, block), 1)
    causal = row <= column

    def prepare(i, _):
        lanes = pl.ds(pl.multiple_of(i * block, block), block)
        product = grad_ref[i].astype(F32) * exact_ref[i]
        lane = lax.broadcasted_iota(jnp.int32, product.shape, 1)
        for head in range(heads):
            part = jnp.where(lane // head_size == head, product, 0.0)
            part = jnp.sum(part, axis=1, keepdims=True)
            delta[head : head + 1, lanes] = jnp.broadcast_to(part, (block, LANES)).T[0:1]
        return 0

    lax.fori_loop(0, live, prepare, 0)

    def key_block(j, _):
        keys = pl.ds(pl.multiple_of(j * block, block), block)
        key = qkv_ref[j, 1]
        value = qkv_ref[j, 2]
        value_total = jnp.zeros((block, width), F32)
        key_total = jnp.zeros((block, width), F32)
        for head in range(heads):
            spare = spare_lane(head, head_size)
            key_ones = of_head(key, head, head_size, spare)
            decay = jnp.broadcast_to(decay_ref[head : head + 1, keys], (LANES, block)).T[:, 0:1]

            def step(i, carry, masked):
                value_acc, key_acc = carry
                lanes = pl.ds(pl.multiple_of(i * block, block), block)
                query = qkv_ref[i, 0]
                grad = of_head(grad_ref[i], head, head_size)
                score = dot(key, of_head(query, head, head_size), NT) * scale
                score = score - decay - lse_ref[head : head + 1, lanes]
                if masked:
                    score = jnp.where(causal, score, masked_score)
                prob = jnp.exp(score)
                grad_prob = dot(value, grad, NT)
                grad_score = prob * (grad_prob - delta[head : head + 1, lanes])
                grad_score = grad_score.astype(BF16)
                value_acc = value_acc + dot(prob.astype(BF16), grad, NN)
                query_ones = of_head(query, head, head_size, spare)
                key_acc = key_acc + dot(grad_score, query_ones, NN)
                dq_acc[head, i] += dot(grad_score, key_ones, TN)
                return value_acc, key_acc

            zero = jnp.zeros((block, width), F32)
            carry = step(j, (zero, zero), True)
            carry = lax.fori_loop(j + 1, live, lambda i, c: step(i, c, False), carry)
            value_acc, key_acc = carry
            value_total = value_total + value_acc
            lane = lax.broadcasted_iota(jnp.int32, key_acc.shape, 1)
            key_total = jnp.where(lane // head_size == head, key_acc, key_total)
            column_ref[head : head + 1, keys] = key_acc.T[spare : spare + 1]
        dqkv_ref[j, 1] = (key_total * scale).astype(BF16)
        dqkv_ref[j, 2] = value_total.astype(BF16)
        return 0

    lax.fori_loop(0, live, key_block, 0)

    def finish(i, _):
        lanes = pl.ds(pl.multiple_of(i * block, block), block)
        total = jnp.zeros((block, width), F32)
        for head in range(heads):
            spare = spare_lane(head, head_size)
            part = dq_acc[head, i]
            lane = lax.broadcasted_iota(jnp.int32, part.shape, 1)
            total = jnp.where(lane // head_size == head, part, total)
            row_ref[head : head + 1, lanes] = part.T[spare : spare + 1]
        dqkv_ref[i, 0] = (total * scale).astype(BF16)
        return 0

    lax.fori_loop(0, live, finish, 0)


def attend_specs(count):
    smem = pl.BlockSpec(memory_space=pltpu.SMEM)
    return [smem] + [pl.BlockSpec(memory_space=pltpu.VMEM)] * count


def attend_cost(qkv, decay, products):
    count, _, block, width = qkv.shape
    heads = decay.shape[0]
    pairs = heads * (count * block) ** 2 // 3
    return pl.CostEstimate(
        flops=2 * products * pairs * 256, bytes_accessed=2 * qkv.size * 2, transcendentals=pairs
    )


def attend(length, qkv, decay, head_size):
    count, _, block, width = qkv.shape
    return pl.pallas_call(
        functools.partial(attend_forward, heads=decay.shape[0], head_size=head_size),
        out_shape=[
            jax.ShapeDtypeStruct((count, block, width), BF16),
            jax.ShapeDtypeStruct((count, block, width), F32),
            jax.ShapeDtypeStruct(decay.shape, F32),
        ],
        in_specs=attend_specs(2),
        out_specs=attend_specs(3)[1:],
        compiler_params=pltpu.CompilerParams(vmem_limit_bytes=40 << 20),
        cost_estimate=attend_cost(qkv, decay, 2),
        name="attend_forward",
    )(length, qkv, decay)


def attend_grad(length, qkv, grad, exact, lse, decay, head_size):
    count, _, block, width = qkv.shape
    heads = decay.shape[0]
    return pl.pallas_call(
        functools.partial(attend_backward, heads=heads, head_size=head_size),
        out_shape=[
            jax.ShapeDtypeStruct(qkv.shape, BF16),
            jax.ShapeDtypeStruct(decay.shape, F32),
            jax.ShapeDtypeStruct(decay.shape, F32),
        ],
        in_specs=attend_specs(5),
        out_specs=attend_specs(3)[1:],
        scratch_shapes=[
            pltpu.VMEM((heads, count, block, width), F32),
            pltpu.VMEM((8, count * block), F32),
        ],
        compiler_params=pltpu.CompilerParams(vmem_limit_bytes=40 << 20),
        cost_estimate=attend_cost(qkv, decay, 5),
        name="attend_backward",
    )(length, qkv, grad, exact, lse, decay)


MESH = pl.DeviceIdType.MESH
CHUNKS = 4


def tp_places():
    me = lax.axis_index("tp")
    sibling = me + 1 - 2 * lax.rem(me, 2)
    across = lax.rem(me + 2, 4)
    diagonal = lax.rem(sibling + 2, 4)
    return me, sibling, across, diagonal


def greet(peers):
    barrier = pltpu.get_barrier_semaphore()
    for peer in peers:
        pl.semaphore_signal(barrier, inc=1, device_id={"tp": peer}, device_id_type=MESH)
    pl.semaphore_wait(barrier, len(peers))


def sending(source, target, send_sem, recv_sem, peer):
    return pltpu.make_async_remote_copy(
        src_ref=source,
        dst_ref=target,
        send_sem=send_sem,
        recv_sem=recv_sem,
        device_id={"tp": peer},
        device_id_type=MESH,
    )


def pick(step, chunks, places):
    me, sibling, across, diagonal = places
    late = step - 2 * chunks
    far = jnp.where(lax.rem(late, 2) == 0, across, diagonal)
    slot = jnp.where(step < chunks, me, jnp.where(step < 2 * chunks, sibling, far))
    chunk = jnp.where(step < 2 * chunks, lax.rem(step, chunks), late // 2)
    return slot, chunk


def gather_loop(table, sems, compute):
    near_send, near_recv, far_send, far_recv, pass_send, pass_recv = sems
    me, sibling, across, diagonal = places = tp_places()
    rows = table.shape[1] // CHUNKS

    def part(slot, chunk):
        return table.at[slot, pl.ds(pl.multiple_of(chunk * rows, rows), rows)]

    def far(chunk):
        return sending(
            part(me, chunk), part(me, chunk), far_send.at[chunk], far_recv.at[chunk], across
        )

    def far_arrival(chunk):
        spot = part(across, chunk)
        return sending(spot, spot, far_send.at[chunk], far_recv.at[chunk], across)

    def passing(chunk):
        spot = part(across, chunk)
        return sending(spot, spot, pass_send.at[chunk], pass_recv.at[chunk], sibling)

    def pass_arrival(chunk):
        spot = part(diagonal, chunk)
        return sending(spot, spot, pass_send.at[chunk], pass_recv.at[chunk], sibling)

    for chunk in range(CHUNKS):
        far(chunk).start()
    near = sending(table.at[me], table.at[me], near_send, near_recv, sibling)
    near.start()

    def body(step, _):
        slot, chunk = pick(step, CHUNKS, places)
        late = step - 2 * CHUNKS

        @pl.when(step == CHUNKS)
        def _():
            spot = table.at[sibling]
            sending(spot, spot, near_send, near_recv, sibling).wait_recv()

        @pl.when((late >= 0) & (lax.rem(late, 2) == 0))
        def _():
            far_arrival(chunk).wait_recv()
            passing(chunk).start()

        @pl.when((late >= 0) & (lax.rem(late, 2) == 1))
        def _():
            pass_arrival(chunk).wait_recv()

        compute(slot, chunk)
        return 0

    lax.fori_loop(0, 4 * CHUNKS, body, 0)
    near.wait_send()
    for chunk in range(CHUNKS):
        far(chunk).wait_send()
        passing(chunk).wait_send()


GATHER_SEMS = [pltpu.SemaphoreType.DMA] * 2 + [pltpu.SemaphoreType.DMA((CHUNKS,))] * 4


def scatter_loop(buffers, sems, partial, finish):
    near_out, near_in, far_out, far_in = buffers
    near_send, near_recv, far_send, far_recv = sems
    me, sibling, across, diagonal = tp_places()
    rows = far_out.shape[0] // CHUNKS

    def span(chunk):
        return pl.ds(pl.multiple_of(chunk * rows, rows), rows)

    def near(half, chunk):
        return sending(
            near_out.at[half, span(chunk)],
            near_in.at[half, span(chunk)],
            near_send.at[half, chunk],
            near_recv.at[half, chunk],
            sibling,
        )

    def far(chunk):
        return sending(
            far_out.at[span(chunk)],
            far_in.at[span(chunk)],
            far_send.at[chunk],
            far_recv.at[chunk],
            across,
        )

    def body(step, _):
        phase, chunk = step // CHUNKS, lax.rem(step, CHUNKS)
        slot = jnp.where(
            phase == 0, diagonal, jnp.where(phase == 1, across, jnp.where(phase == 2, sibling, me))
        )
        value = partial(slot, chunk)
        spot = span(chunk)

        @pl.when(lax.rem(phase, 2) == 0)
        def _():
            half = phase // 2
            near_out[half, spot] = value.astype(BF16)
            near(half, chunk).start()

        @pl.when(phase == 1)
        def _():
            near(0, chunk).wait_recv()
            far_out[spot] = (value + near_in[0, spot].astype(F32)).astype(BF16)
            far(chunk).start()

        @pl.when(phase == 3)
        def _():
            near(1, chunk).wait_recv()
            far(chunk).wait_recv()
            finish(chunk, value + near_in[1, spot].astype(F32) + far_in[spot].astype(F32))

        return 0

    lax.fori_loop(0, 4 * CHUNKS, body, 0)
    for chunk in range(CHUNKS):
        near(0, chunk).wait_send()
        near(1, chunk).wait_send()
        far(chunk).wait_send()


SCATTER_SEMS = [pltpu.SemaphoreType.DMA((2, CHUNKS))] * 2 + [pltpu.SemaphoreType.DMA((CHUNKS,))] * 2


def scatter_buffers(rows, width):
    return [
        pltpu.VMEM((2, rows, width), BF16),
        pltpu.VMEM((2, rows, width), BF16),
        pltpu.VMEM((rows, width), BF16),
        pltpu.VMEM((rows, width), BF16),
    ]


def gather_two_kernel(first_ref, second_ref, first_all, second_all, near_send, near_recv, far_send, far_recv, pass_send, pass_recv, own_sem):
    me, sibling, across, diagonal = tp_places()
    greet((sibling, across))
    pairs = ((first_ref, first_all), (second_ref, second_all))
    rows = first_ref.shape[0] // CHUNKS
    started = []
    for n, (source, table) in enumerate(pairs):
        own = pltpu.make_async_copy(source, table.at[me], own_sem.at[n])
        own.start()
        started.append(own)
    fars, nears, passes = [], [], []
    for n, (source, table) in enumerate(pairs):
        for chunk in range(CHUNKS):
            spot = pl.ds(chunk * rows, rows)
            copy = sending(source.at[spot], table.at[me, spot], far_send.at[n, chunk], far_recv.at[n, chunk], across)
            copy.start()
            fars.append(copy)
        near = sending(source, table.at[me], near_send.at[n], near_recv.at[n], sibling)
        near.start()
        nears.append(near)
    for n, (source, table) in enumerate(pairs):
        for chunk in range(CHUNKS):
            spot = pl.ds(chunk * rows, rows)
            fars[n * CHUNKS + chunk].wait_recv()
            copy = sending(table.at[across, spot], table.at[across, spot], pass_send.at[n, chunk], pass_recv.at[n, chunk], sibling)
            copy.start()
            passes.append(copy)
    for copy in passes + nears:
        copy.wait()
    for copy in fars:
        copy.wait_send()
    for copy in started:
        copy.wait()


def gather_two(first, second, ident):
    rows, width = first.shape
    many = pltpu.SemaphoreType.DMA((2, CHUNKS))
    return pl.pallas_call(
        gather_two_kernel,
        out_shape=[jax.ShapeDtypeStruct((4, rows, width), BF16)] * 2,
        in_specs=[pl.BlockSpec(memory_space=pl.ANY)] * 2,
        out_specs=[pl.BlockSpec(memory_space=pl.ANY)] * 2,
        scratch_shapes=[pltpu.SemaphoreType.DMA((2,))] * 2 + [many] * 4 + [pltpu.SemaphoreType.DMA((2,))],
        compiler_params=pltpu.CompilerParams(collective_id=ident, has_side_effects=True),
        name="gather_rows",
    )(first, second)


def whole(shape, column=None):
    zeros = (0,) * (len(shape) - 1)
    return pl.BlockSpec(shape, lambda i: zeros + (column or 0,), pipeline_mode=pl.Buffered(1))


def remote_params(ident, megabytes):
    return pltpu.CompilerParams(
        collective_id=ident, has_side_effects=True, vmem_limit_bytes=megabytes << 20, dimension_semantics=("arbitrary",)
    )


def project_kernel(layout, x_ref, gain_ref, w_ref, normed_ref, forget_ref, *item_refs):
    seq_count, groups, width, places = layout
    x = x_ref[0].astype(F32)
    normed = (x * lax.rsqrt(jnp.mean(x * x, axis=1, keepdims=True) + epsilon) * gain_ref[...]).astype(BF16)
    normed_ref[0] = normed
    inner = groups * width
    rows = x.shape[0] // seq_count
    count = len(item_refs)
    for kind in range(3):
        value = dot(normed, w_ref[:, kind * inner : (kind + 1) * inner], NN).astype(BF16)
        for slot, (s, g) in enumerate(places):
            piece = value[s * rows : (s + 1) * rows, g * width : (g + 1) * width]
            item_refs[slot % count][slot // count, kind] = piece
    forget_ref[0] = dot(normed, w_ref[:, 3 * inner :], NN)


def project(x_all, gain, full_one, layout, item_count, ctx_size):
    seq_count, groups, width, places = layout
    tp_size, rows, model_width = x_all.shape
    local = rows // seq_count
    item = jax.ShapeDtypeStruct((ctx_size, 3, tp_size * local, width), BF16)
    columns = full_one.shape[1]
    block = pl.BlockSpec((1, rows, model_width), lambda t: (t, 0, 0))
    return pl.pallas_call(
        functools.partial(project_kernel, layout),
        grid=(tp_size,),
        out_shape=[
            jax.ShapeDtypeStruct(x_all.shape, BF16),
            jax.ShapeDtypeStruct((tp_size, rows, LANES), F32),
        ]
        + [item] * item_count,
        in_specs=[
            block,
            pl.BlockSpec((1, model_width), lambda t: (0, 0)),
            pl.BlockSpec((model_width, columns), lambda t: (0, 0), pipeline_mode=pl.Buffered(1)),
        ],
        out_specs=[block, pl.BlockSpec((1, rows, LANES), lambda t: (t, 0, 0))]
        + [pl.BlockSpec((ctx_size, 3, local, width), lambda t: (0, 0, t, 0))] * item_count,
        compiler_params=pltpu.CompilerParams(vmem_limit_bytes=48 << 20, dimension_semantics=("arbitrary",)),
        cost_estimate=pl.CostEstimate(
            flops=2 * x_all.size * columns, bytes_accessed=4 * x_all.size, transcendentals=0
        ),
        name="project",
    )(x_all, gain, full_one)


def out_kernel(layout, count, x_ref, gate_ref, w_ref, gain_ref, *refs):
    seq_count, groups, width, places = layout
    items, (hidden_ref, normed_ref, attended_ref, mixed_ref) = refs[:count], refs[count : count + 4]
    buffers, sems = refs[count + 4 : count + 8], refs[count + 8 :]
    me, sibling, across, diagonal = tp_places()
    greet((sibling, across))
    tp_size, rows, _ = gate_ref.shape
    local = rows // seq_count

    def mix(t, _):
        here = pl.ds(pl.multiple_of(t * local, local), local)
        for slot, (s, g) in enumerate(places[: seq_count * groups]):
            there = (t, pl.ds(s * local, local), pl.ds(g * width, width))
            value = items[slot % count][slot // count, here]
            attended_ref[there] = value
            mixed_ref[there] = (value.astype(F32) * gate_ref[there]).astype(BF16)
        return 0

    lax.fori_loop(0, tp_size, mix, 0)
    size = rows // CHUNKS

    def span(chunk):
        return pl.ds(pl.multiple_of(chunk * size, size), size)

    def partial(slot, chunk):
        return dot(mixed_ref[slot, span(chunk)], w_ref[...], NT)

    def finish(chunk, total):
        hidden = x_ref[span(chunk)].astype(F32) + total
        hidden_ref[span(chunk)] = hidden
        inverse = lax.rsqrt(jnp.mean(hidden * hidden, axis=1, keepdims=True) + epsilon)
        normed_ref[span(chunk)] = (hidden * inverse * gain_ref[...]).astype(BF16)

    scatter_loop(buffers, sems, partial, finish)


def out_project(x, gate, full_two, column, gain, items, layout, ident):
    seq_count, groups, width, places = layout
    rows, model_width = x.shape
    inner = groups * width
    tp_size = gate.shape[0]
    return pl.pallas_call(
        functools.partial(out_kernel, layout, len(items)),
        grid=(1,),
        out_shape=[
            jax.ShapeDtypeStruct(x.shape, F32),
            jax.ShapeDtypeStruct(x.shape, BF16),
            jax.ShapeDtypeStruct(gate.shape, BF16),
            jax.ShapeDtypeStruct(gate.shape, BF16),
        ],
        in_specs=[
            whole(x.shape),
            whole(gate.shape),
            whole((model_width, inner), column),
            whole(gain.shape),
        ]
        + [whole(item.shape) for item in items],
        out_specs=[whole(x.shape), whole(x.shape), whole(gate.shape), whole(gate.shape)],
        scratch_shapes=scatter_buffers(rows, model_width) + SCATTER_SEMS,
        compiler_params=remote_params(ident, 48),
        cost_estimate=pl.CostEstimate(
            flops=2 * gate.size * model_width, bytes_accessed=100 << 20, transcendentals=0
        ),
        name="out_project",
    )(x, gate, full_two, gain, *items)


def mlp_kernel(normed_ref, grad_ref, gate_w, up_w, down_w, all_ref, inner_ref, pair_ref, table, own_sem, *sems):
    me, sibling, across, diagonal = tp_places()
    greet((sibling, across))
    table[me] = normed_ref[...]
    rows, hidden = table.shape[1] // CHUNKS, gate_w.shape[1]
    tile = min(hidden, 512)

    def compute(slot, chunk):
        spot = pl.ds(pl.multiple_of(chunk * rows, rows), rows)
        normed, grad = table[slot, spot], grad_ref[slot, spot]
        for start in range(0, hidden, tile):
            columns = pl.ds(start, tile)
            gate = dot(normed, gate_w[:, columns], NN)
            up = dot(normed, up_w[:, columns], NN)
            back = dot(grad, down_w[:, columns], NN)
            sig = 1.0 / (1.0 + jnp.exp(-gate))
            silu = gate * sig
            inner_ref[slot, spot, columns] = (silu * up).astype(BF16)
            pair_ref[slot, spot, columns] = (back * up * sig * (1.0 + gate * (1.0 - sig))).astype(BF16)
            pair_ref[slot, spot, pl.ds(hidden + start, tile)] = (back * silu).astype(BF16)

    gather_loop(table, sems, compute)
    copy = pltpu.make_async_copy(table, all_ref, own_sem)
    copy.start()
    copy.wait()


def mlp(normed, grad_all, full_two, hidden, ident):
    tp_size, rows, model_width = grad_all.shape
    total = tp_size * rows
    return pl.pallas_call(
        mlp_kernel,
        grid=(1,),
        out_shape=[
            jax.ShapeDtypeStruct(grad_all.shape, BF16),
            jax.ShapeDtypeStruct((tp_size, rows, hidden), BF16),
            jax.ShapeDtypeStruct((tp_size, rows, 2 * hidden), BF16),
        ],
        in_specs=[whole(normed.shape), whole(grad_all.shape)]
        + [whole((model_width, hidden), column) for column in range(3)],
        out_specs=[
            pl.BlockSpec(memory_space=pl.ANY),
            whole((tp_size, rows, hidden)),
            whole((tp_size, rows, 2 * hidden)),
        ],
        scratch_shapes=[pltpu.VMEM(grad_all.shape, BF16), pltpu.SemaphoreType.DMA] + GATHER_SEMS,
        compiler_params=remote_params(ident, 56),
        cost_estimate=pl.CostEstimate(
            flops=6 * total * model_width * hidden, bytes_accessed=100 << 20, transcendentals=total * hidden
        ),
        name="mlp",
    )(normed, grad_all, full_two, full_two, full_two)


def mlp_back_kernel(pair_ref, w_ref, hidden_ref, grad_ref, gain_ref, out_ref, branch_ref, part_ref, *refs):
    buffers, sems = refs[:4], refs[4:]
    me, sibling, across, diagonal = tp_places()
    greet((sibling, across))
    part_ref[...] = jnp.zeros_like(part_ref)
    size = hidden_ref.shape[0] // CHUNKS

    def span(chunk):
        return pl.ds(pl.multiple_of(chunk * size, size), size)

    def partial(slot, chunk):
        return dot(pair_ref[slot, span(chunk)], w_ref[...], NT)

    def finish(chunk, total):
        hidden = hidden_ref[span(chunk)]
        inverse = lax.rsqrt(jnp.mean(hidden * hidden, axis=1, keepdims=True) + epsilon)
        unit = hidden * inverse
        part_ref[...] += jnp.sum(total * unit, axis=0, keepdims=True)
        scaled = total * gain_ref[...]
        middle = jnp.mean(scaled * unit, axis=1, keepdims=True)
        grad = grad_ref[span(chunk)].astype(F32) + inverse * (scaled - unit * middle)
        out_ref[span(chunk)] = grad
        branch_ref[span(chunk)] = grad.astype(BF16)

    scatter_loop(buffers, sems, partial, finish)


def mlp_back(pair, full_two, hidden_state, grad_out, gain, ident):
    tp_size, rows, wide = pair.shape
    model_width = hidden_state.shape[1]
    return pl.pallas_call(
        mlp_back_kernel,
        grid=(1,),
        out_shape=[
            jax.ShapeDtypeStruct(hidden_state.shape, F32),
            jax.ShapeDtypeStruct(hidden_state.shape, BF16),
            jax.ShapeDtypeStruct(gain.shape, F32),
        ],
        in_specs=[
            whole(pair.shape),
            whole((model_width, wide), 0),
            whole(hidden_state.shape),
            whole(grad_out.shape),
            whole(gain.shape),
        ],
        out_specs=[whole(hidden_state.shape), whole(hidden_state.shape), whole(gain.shape)],
        scratch_shapes=scatter_buffers(rows, model_width) + SCATTER_SEMS,
        compiler_params=remote_params(ident, 56),
        cost_estimate=pl.CostEstimate(
            flops=2 * pair.size * model_width, bytes_accessed=100 << 20, transcendentals=0
        ),
        name="mlp_back",
    )(pair, full_two, hidden_state, grad_out, gain)


def out_back_kernel(layout, count, branch_ref, w_ref, gate_ref, attended_ref, *refs):
    seq_count, groups, width, places = layout
    all_ref, logit_ref, items = refs[0], refs[1], refs[2 : 2 + count]
    table, grads, own_sem = refs[2 + count : 5 + count]
    sems = refs[5 + count :]
    me, sibling, across, diagonal = tp_places()
    greet((sibling, across))
    table[me] = branch_ref[...]
    tp_size, rows, _ = gate_ref.shape
    local, size = rows // seq_count, rows // CHUNKS

    def compute(slot, chunk):
        spot = pl.ds(pl.multiple_of(chunk * size, size), size)
        mixed = dot(table[slot, spot], w_ref[...], NN)
        gate = gate_ref[slot, spot]
        scaled = mixed * gate
        grads[slot, spot] = scaled.astype(BF16)
        attended = attended_ref[slot, spot].astype(F32)
        logit_ref[slot, spot] = (scaled * attended * (1.0 - gate)).astype(BF16)

    gather_loop(table, sems, compute)
    copy = pltpu.make_async_copy(table, all_ref, own_sem)
    copy.start()

    def deal(t, _):
        here = pl.ds(pl.multiple_of(t * local, local), local)
        for slot, (s, g) in enumerate(places):
            items[slot % count][slot // count, here] = grads[t, pl.ds(s * local, local), pl.ds(g * width, width)]
        return 0

    lax.fori_loop(0, tp_size, deal, 0)
    copy.wait()


def out_back(branch, full_two, column, gate, attended, layout, item_count, ctx_size, ident):
    seq_count, groups, width, places = layout
    rows, model_width = branch.shape
    tp_size, _, inner = gate.shape
    item = (ctx_size, tp_size * rows // seq_count, width)
    table = (tp_size, rows, model_width)
    return pl.pallas_call(
        functools.partial(out_back_kernel, layout, item_count),
        grid=(1,),
        out_shape=[jax.ShapeDtypeStruct(table, BF16), jax.ShapeDtypeStruct(gate.shape, BF16)]
        + [jax.ShapeDtypeStruct(item, BF16)] * item_count,
        in_specs=[
            whole(branch.shape),
            whole((model_width, inner), column),
            whole(gate.shape),
            whole(attended.shape),
        ],
        out_specs=[pl.BlockSpec(memory_space=pl.ANY), whole(gate.shape)] + [whole(item)] * item_count,
        scratch_shapes=[pltpu.VMEM(table, BF16), pltpu.VMEM(gate.shape, BF16), pltpu.SemaphoreType.DMA]
        + GATHER_SEMS,
        compiler_params=remote_params(ident, 48),
        cost_estimate=pl.CostEstimate(
            flops=2 * gate.size * model_width, bytes_accessed=100 << 20, transcendentals=0
        ),
        name="out_back",
    )(branch, full_two, gate, attended)


def assemble_kernel(layout, count, *refs):
    seq_count, groups, width, places = layout
    items, out_ref = refs[:count], refs[count]
    local = items[0].shape[2]
    inner = groups * width
    for slot, (s, g) in enumerate(places[: seq_count * groups]):
        for kind in range(3):
            columns = pl.ds(kind * inner + g * width, width)
            out_ref[0, pl.ds(s * local, local), columns] = items[slot % count][slot // count, kind]


def assemble(items, layout, tp_size):
    seq_count, groups, width, places = layout
    ctx_size, kinds, ctx_rows, _ = items[0].shape
    local = ctx_rows // tp_size
    shape = (tp_size, seq_count * local, kinds * groups * width)
    return pl.pallas_call(
        functools.partial(assemble_kernel, layout, len(items)),
        grid=(tp_size,),
        out_shape=jax.ShapeDtypeStruct(shape, BF16),
        in_specs=[pl.BlockSpec((ctx_size, kinds, local, width), lambda t: (0, 0, t, 0))] * len(items),
        out_specs=pl.BlockSpec((1,) + shape[1:], lambda t: (t, 0, 0)),
        compiler_params=pltpu.CompilerParams(vmem_limit_bytes=32 << 20, dimension_semantics=("arbitrary",)),
        cost_estimate=pl.CostEstimate(flops=0, bytes_accessed=16 << 20, transcendentals=0),
        name="assemble",
    )(*items)


def input_kernel(qkv_ref, logit_ref, forget_ref, qkv_w, forget_w, gate_w, x_ref, grad_ref, gain_ref, out_ref, part_ref, *refs):
    buffers, sems = refs[:4], refs[4:]
    me, sibling, across, diagonal = tp_places()
    greet((sibling, across))
    part_ref[...] = jnp.zeros_like(part_ref)
    size = x_ref.shape[0] // CHUNKS

    def span(chunk):
        return pl.ds(pl.multiple_of(chunk * size, size), size)

    def partial(slot, chunk):
        value = dot(qkv_ref[slot, span(chunk)], qkv_w[...], NT)
        value = value + dot(logit_ref[slot, span(chunk)], gate_w[...], NT)
        return value + dot(forget_ref[slot, span(chunk)], forget_w[...], NT)

    def finish(chunk, total):
        x = x_ref[span(chunk)].astype(F32)
        inverse = lax.rsqrt(jnp.mean(x * x, axis=1, keepdims=True) + epsilon)
        unit = x * inverse
        part_ref[...] += jnp.sum(total * unit, axis=0, keepdims=True)
        scaled = total * gain_ref[...]
        middle = jnp.mean(scaled * unit, axis=1, keepdims=True)
        out_ref[span(chunk)] = (grad_ref[span(chunk)] + inverse * (scaled - unit * middle)).astype(BF16)

    scatter_loop(buffers, sems, partial, finish)


def input_back(grad_qkv, grad_logit, grad_forget, full_one, full_two, column, x, grad_hidden, gain, ident):
    rows, model_width = x.shape
    wide, inner = grad_qkv.shape[2], grad_logit.shape[2]
    return pl.pallas_call(
        input_kernel,
        grid=(1,),
        out_shape=[jax.ShapeDtypeStruct(x.shape, BF16), jax.ShapeDtypeStruct(gain.shape, F32)],
        in_specs=[
            whole(grad_qkv.shape),
            whole(grad_logit.shape),
            whole(grad_forget.shape),
            whole((model_width, wide), 0),
            whole((model_width, LANES), wide // LANES),
            whole((model_width, inner), column),
            whole(x.shape),
            whole(x.shape),
            whole(gain.shape),
        ],
        out_specs=[whole(x.shape), whole(gain.shape)],
        scratch_shapes=scatter_buffers(rows, model_width) + SCATTER_SEMS,
        compiler_params=remote_params(ident, 56),
        cost_estimate=pl.CostEstimate(
            flops=8 * rows * model_width * (wide + inner + LANES), bytes_accessed=100 << 20, transcendentals=0
        ),
        name="input_back",
    )(grad_qkv, grad_logit, grad_forget, full_one, full_one, full_two, x, grad_hidden, gain)


def running_sum(values):
    length = values.shape[-1]
    cut = values.reshape(values.shape[:-1] + (length // LANES, LANES))
    lower = jnp.tril(jnp.ones((LANES, LANES), F32))
    inside = jnp.einsum("...bk,jk->...bj", cut, lower, precision=lax.Precision.HIGHEST)
    ahead = jnp.tril(jnp.ones((length // LANES, length // LANES), F32), -1)
    before = jnp.sum(jnp.sum(cut, axis=-1)[..., None, :] * ahead, axis=-1)
    return (inside + before[..., None]).reshape(values.shape)


def row_norm(values):
    inverse = lax.rsqrt(jnp.mean(values * values, axis=-1, keepdims=True) + epsilon)
    return (values * inverse, inverse)


def norm_back(grad_normed, unit_rows, inverse, gain_vec):
    scaled = grad_normed * gain_vec
    inner_mean = jnp.mean(scaled * unit_rows, axis=-1, keepdims=True)
    return inverse * (scaled - unit_rows * inner_mean)


def spread_rows(row_values):
    return lax.all_gather(row_values, "tp", axis=0, tiled=True)


def summed_rows(partial):
    total = lax.psum_scatter(partial.astype(BF16), "tp", scatter_dimension=0, tiled=True)
    return total.astype(F32)


def per_device(
    layer_input,
    lengths,
    attn_gain,
    w_query,
    w_key,
    w_value,
    w_forget,
    forget_bias,
    w_gate_out,
    w_out,
    mlp_gain,
    w_gate,
    w_up,
    w_down,
    cotangent,
):
    local_rows, seq_count, model_width = layer_input.shape
    head_count = forget_bias.shape[0]
    inner_width = w_query.shape[1]
    hidden = w_gate.shape[1]
    head_size = inner_width // head_count
    tp_size = lax.axis_size("tp")
    ctx_size = lax.axis_size("ctx")
    shard_count = lax.axis_size("fsdp") * ctx_size
    ctx_rows = local_rows * tp_size
    seq_len = ctx_rows * ctx_size
    all_rows = seq_count * ctx_rows
    ctx_index = lax.axis_index("ctx")
    tp_index = lax.axis_index("tp")
    shard_index = lax.axis_index("fsdp") * ctx_size + ctx_index

    pair = LANES // head_size
    groups = head_count // pair
    width = pair * head_size
    item_count = pl.cdiv(seq_count * groups, ctx_size)
    used = seq_count * groups

    def place(slot):
        slot = slot % used
        return (slot // groups + slot % groups) % seq_count, slot % groups

    places = tuple(place(slot) for slot in range(ctx_size * item_count))
    layout = (seq_count, groups, width, places)

    weights = ("fsdp", "ctx")
    packed_one = jnp.concatenate(
        [
            w_query,
            w_key,
            w_value,
            w_forget,
            attn_gain[:, None],
            mlp_gain[:, None],
            jnp.zeros((attn_gain.shape[0], LANES - head_count - 2), BF16),
        ],
        axis=1,
    )
    packed_two = jnp.concatenate([w_gate, w_up, w_down, w_out, w_gate_out], axis=1)
    full_one = lax.all_gather(packed_one, weights, axis=0, tiled=True)
    full_two = lax.all_gather(packed_two, weights, axis=0, tiled=True)
    edge = 3 * inner_width
    gains = full_one[:, edge + head_count : edge + head_count + 2].astype(F32).T
    gain_one, gain_two = gains[0:1], gains[1:2]
    down_w = full_two[:, 2 * hidden : 3 * hidden]
    out_column = 3 * hidden // inner_width
    gate_out_w = full_two[:, 3 * hidden + inner_width :]

    def by_sequence(rows):
        return rows.transpose(1, 0, 2).reshape(seq_count * local_rows, model_width)

    def by_position(rows):
        return rows.reshape(seq_count, local_rows, model_width).transpose(1, 0, 2)

    local_pos = (ctx_index * tp_size + tp_index) * local_rows + jnp.arange(
        local_rows, dtype=jnp.int32
    )
    valid_rows = (local_pos[None, :] < lengths[:, None]).astype(F32)
    valid_rows = valid_rows.reshape(seq_count * local_rows, 1)
    ctx_pos = ctx_index * ctx_rows + jnp.arange(ctx_rows, dtype=jnp.int32)
    ctx_pos = ctx_pos.reshape(tp_size, 1, local_rows)
    ctx_valid = (ctx_pos < lengths[None, :, None]).astype(F32)

    input_rows = by_sequence(layer_input)
    grad_out = (valid_rows * by_sequence(cotangent).astype(F32)).astype(BF16)
    input_all, grad_all = gather_two(input_rows, grad_out, 1)
    normed_one, forget_rows, *items = project(
        input_all, gain_one, full_one, layout, item_count, ctx_size
    )
    normed_flat = normed_one.reshape(all_rows, model_width)
    forget_logit = forget_rows.reshape(all_rows, LANES)[:, :head_count].T
    forget_logit = forget_logit + forget_bias.astype(F32)[:, None]
    forget_logit = forget_logit.reshape(head_count, tp_size, seq_count, local_rows)
    log_forget = (ctx_valid[None] * jax.nn.log_sigmoid(forget_logit)).astype(BF16)

    def forget_items(rows):
        cut = rows.reshape(groups, pair, tp_size, seq_count, local_rows)
        picked = jnp.stack([cut[g, :, :, s] for s, g in places])
        return picked.reshape(ctx_size, item_count, pair, ctx_rows)

    def exchange(items):
        return lax.all_to_all(items, "ctx", split_axis=0, concat_axis=0, tiled=True)

    decay_in = exchange(forget_items(log_forget)).transpose(1, 2, 0, 3)
    decay_sum = running_sum(decay_in.reshape(item_count, pair, seq_len).astype(F32))
    seq_ids = jnp.arange(seq_count, dtype=jnp.int32)
    saved, attended_items = [], []
    for m in range(item_count):
        qkv = exchange(items[m])
        slot = ctx_index * item_count + m
        own_seq, _ = place(slot)
        own_seq = jnp.where(slot < used, own_seq, seq_count)
        item_len = jnp.sum(jnp.where(seq_ids == own_seq, lengths, 0)).reshape(1)
        out, exact, lse = attend(item_len, qkv, decay_sum[m], head_size)
        saved.append((item_len, qkv, exact, lse))
        attended_items.append(exchange(out))
    gate_logit = dot(normed_flat, gate_out_w, NN)
    out_gate = jax.nn.sigmoid(gate_logit).reshape(tp_size, -1, inner_width)
    hidden_state, normed_two, attended, mixed = out_project(
        input_rows, out_gate, full_two, out_column, gain_two, attended_items, layout, 2
    )
    normed_two_all, inner_act, grad_pair = mlp(normed_two, grad_all, full_two, hidden, 3)
    normed_two_flat = normed_two_all.reshape(all_rows, model_width)
    inner_flat = inner_act.reshape(all_rows, hidden)
    grad_pair_flat = grad_pair.reshape(all_rows, 2 * hidden)
    grad_flat = grad_all.reshape(all_rows, model_width)
    grad_hidden, branch, mlp_gain_part = mlp_back(
        grad_pair, full_two, hidden_state, grad_out, gain_two, 4
    )
    feedforward = summed_rows(dot(inner_flat, down_w, NT))
    output = (valid_rows * (hidden_state + feedforward)).astype(BF16)

    def owned_sum(part):
        total = lax.psum_scatter(part, weights, scatter_dimension=0, tiled=True)
        return total.astype(F32)

    gate_up_sum = owned_sum(dot(normed_two_flat, grad_pair_flat, TN).astype(BF16))
    branch_all, grad_gate_logit, *grads = out_back(
        branch, full_two, out_column, out_gate, attended, layout, item_count, ctx_size, 5
    )
    branch_flat = branch_all.reshape(all_rows, model_width)
    logit_flat = grad_gate_logit.reshape(all_rows, inner_width)

    grad_items, decay_grads = [], []
    for m in range(item_count):
        item_len, qkv, exact, lse = saved[m]
        dqkv, row_sum, column_sum = attend_grad(
            item_len, qkv, exchange(grads[m]), exact, lse, decay_sum[m], head_size
        )
        grad_items.append(exchange(dqkv))
        decay_grads.append(row_sum - column_sum)
    down_out_part = jnp.concatenate(
        [
            dot(grad_flat, inner_flat, TN).astype(BF16),
            dot(branch_flat, mixed.reshape(all_rows, inner_width), TN).astype(BF16),
            dot(normed_flat, logit_flat, TN).astype(BF16),
        ],
        axis=1,
    )
    down_out_sum = owned_sum(down_out_part)

    decay_grad = jnp.stack(decay_grads)
    forget_grad = jnp.flip(running_sum(jnp.flip(decay_grad, -1)), -1).astype(BF16)
    forget_grad = forget_grad.reshape(item_count, pair, ctx_size, ctx_rows).transpose(2, 0, 1, 3)
    forget_back = exchange(forget_grad).reshape(
        ctx_size * item_count, pair, tp_size, local_rows
    )
    slots = {place(slot): slot for slot in range(used)}
    forget_back = jnp.stack(
        [
            jnp.stack([forget_back[slots[s, g]] for s in range(seq_count)], axis=2)
            for g in range(groups)
        ]
    ).reshape(head_count, tp_size, seq_count, local_rows)
    grad_forget_logit = forget_back.astype(F32) * ctx_valid[None] * jax.nn.sigmoid(-forget_logit)
    grad_forget_logit = grad_forget_logit.astype(BF16).reshape(head_count, all_rows)
    bias_part = jnp.sum(grad_forget_logit.astype(F32), axis=1)
    grad_forget_rows = jnp.pad(grad_forget_logit, ((0, LANES - head_count), (0, 0))).T
    grad_qkv = assemble(grad_items, layout, tp_size)
    grad_qkvf = jnp.concatenate([grad_qkv.reshape(all_rows, edge), grad_forget_rows], axis=1)
    qkv_sum = owned_sum(dot(normed_flat, grad_qkvf, TN).astype(BF16))
    input_grad, attn_gain_part = input_back(
        grad_qkv,
        grad_gate_logit,
        grad_forget_rows.reshape(tp_size, -1, LANES),
        full_one,
        full_two,
        out_column + 1,
        input_rows,
        grad_hidden,
        gain_one,
        6,
    )
    attn_gain_part = attn_gain_part[0]
    mlp_gain_part = mlp_gain_part[0]

    bias_full = lax.dynamic_update_slice(
        jnp.zeros((head_count * tp_size,), F32), bias_part, (tp_index * head_count,)
    )
    gain_one_sum, gain_two_sum, bias_sum = lax.psum(
        (attn_gain_part, mlp_gain_part, bias_full), ("fsdp", "ctx", "tp")
    )
    shard_rows = model_width // shard_count
    attn_gain_grad = lax.dynamic_slice_in_dim(gain_one_sum, shard_index * shard_rows, shard_rows, 0)
    mlp_gain_grad = lax.dynamic_slice_in_dim(gain_two_sum, shard_index * shard_rows, shard_rows, 0)
    forget_bias_grad = lax.dynamic_slice_in_dim(bias_sum, tp_index * head_count, head_count, 0)
    wide = inner_width
    return (
        by_position(output),
        by_position(input_grad),
        attn_gain_grad,
        qkv_sum[:, :wide],
        qkv_sum[:, wide : 2 * wide],
        qkv_sum[:, 2 * wide : 3 * wide],
        qkv_sum[:, 3 * wide : 3 * wide + head_count],
        forget_bias_grad,
        down_out_sum[:, hidden + wide :],
        down_out_sum[:, hidden : hidden + wide],
        mlp_gain_grad,
        gate_up_sum[:, :hidden],
        gate_up_sum[:, hidden:],
        down_out_sum[:, :hidden],
    )


def solution(mesh):
    rows = P(("ctx", "tp"), "fsdp", None)
    matrix = P(("fsdp", "ctx"), "tp")
    vector = P(("fsdp", "ctx"))
    return jax.shard_map(
        per_device,
        mesh=mesh,
        in_specs=(
            rows,
            P("fsdp"),
            vector,
            matrix,
            matrix,
            matrix,
            matrix,
            P("tp"),
            matrix,
            matrix,
            vector,
            matrix,
            matrix,
            matrix,
            rows,
        ),
        out_specs=(
            rows,
            rows,
            vector,
            matrix,
            matrix,
            matrix,
            matrix,
            P("tp"),
            matrix,
            matrix,
            vector,
            matrix,
            matrix,
            matrix,
        ),
        check_vma=False,
    )
```

time: 2700 us -> 1210 us (0.45)
  waiting for transfers between devices: 1550 us -> 199 us
  matrix products: 610 us -> 73.7 us
  Pallas kernels: 0 us -> 463 us
  blocking collectives: 95 us -> 319 us
  other arithmetic: 203 us -> 13.5 us
  local copies, waits for them, and re-layouts: 160 us -> 77.6 us
    reduce_scatter x12 -> x3, waiting for transfers between devices: 976 us -> 124 us  [the longest x2 117 us: owned_sum(): total = lax.psum_scatter(part, weights, scatter_dimension=0, tiled=True)]
    dot_general x55 -> x9, matrix products: 610 us -> 73.7 us  [the longest x7 73.2 us: dot(): return lax.dot_general(left, right, dims, preferred_element_type=F32)]
    pallas_call x0 -> x14, Pallas kernels: none -> 463 us  [the longest x1 99.7 us: gather_two(): pl.pallas_call(gather_two_kernel, out_shape=[jax.ShapeDtypeStruct((4, row...]
    all_gather x12 -> x2, waiting for transfers between devices: 449 us -> 0.01 us  [the longest x1 0.01 us: per_device(): full_one = lax.all_gather(packed_one, weights, axis=0, tiled=True)]
    all_to_all x0 -> x6, blocking collectives: none -> 282 us  [exchange(): return lax.all_to_all(items, 'ctx', split_axis=0, concat_axis=0, tiled=True)]
    reduce_sum x14 -> x6, other arithmetic: 156 us -> 1.25 us  [the longest x1 0.67 us: per_device(): item_len = jnp.sum(jnp.where(seq_ids == own_seq, lengths, 0)).reshape(1)]
    all_to_all x10 -> x8, waiting for transfers between devices: 125 us -> 74.5 us  [exchange(): return lax.all_to_all(items, 'ctx', split_axis=0, concat_axis=0, tiled=True)]
    all_to_all x13 -> x0, local copies, waits for them, and re-layouts: 45.7 us -> none  [the longest x2 7.61 us: per_device(): lax.all_to_all(grad_attended, 'ctx', split_axis=0, concat_axis=2, tiled=T...]
  transfers between devices with their start and end apart: 35 -> 14, of which waited for: 27 -> 7; matrix products, arithmetic and copies ran while one was open for 18% -> 10% of each run, Pallas kernels for 0% -> 22%
where the time goes in v1:
time: 1210 us; the launch traced here: 1190 us
  Pallas kernels  463 us (38%)
  blocking collectives  319 us (26%)
  waiting for transfers between devices  199 us (16%)
  local copies, waits for them, and re-layouts  77.6 us (6%)
  matrix products  73.7 us (6%)
  starting transfers between devices  33.1 us (3%)
  between operations  15.3 us (1%)
  other arithmetic  13.5 us (1%)
    all_to_all x6, blocking collectives, exchange(): return lax.all_to_all(items, 'ctx', split_axis=0, concat_axis=0, tiled=True)  282 us
    reduce_scatter x2, waiting for transfers between devices, owned_sum(): total = lax.psum_scatter(part, weights, scatter_dimension=0, tiled=True)  117 us
    pallas_call x1, Pallas kernels, gather_two(): pl.pallas_call(gather_two_kernel, out_shape=[jax.ShapeDtypeStruct((4, row...  99.7 us
    all_to_all x8, waiting for transfers between devices, exchange(): return lax.all_to_all(items, 'ctx', split_axis=0, concat_axis=0, tiled=True)  74.5 us
    dot_general x7, matrix products, dot(): return lax.dot_general(left, right, dims, preferred_element_type=F32)  73.2 us
    pallas_call x1, Pallas kernels, mlp_back(): pl.pallas_call(mlp_back_kernel, grid=(1,), out_shape=[jax.ShapeDtypeStruc...  57.4 us
    pallas_call x3, Pallas kernels, attend_grad(): pl.pallas_call(functools.partial(attend_backward, heads=heads, head_size=...  56.1 us
    pallas_call x1, Pallas kernels, input_back(): pl.pallas_call(input_kernel, grid=(1,), out_shape=[jax.ShapeDtypeStruct(x...  53.2 us
  transfers between devices with their start and end apart: 14, of which 7 were waited for; matrix products, arithmetic and copies ran while one was open for 10% of the time, Pallas kernels for 22%

profile of v1, /device:TPU:0, one launch (start us, length us, event | category | flops | bytes accessed | tf_op | source)
XLA Modules:
  0.0 1194.3 jit_solution(4286110254859299514)
XLA Ops:
  21.6 99.7 %gather_rows.1 = (bf16[4,512,1536]{2,1,0:T(8,128)(2,1)}, bf16[4,512,1536]{2,1,0:T(8,128)(2,1)}) custom-call(bf16[512,1536]{1,0:T(8,128)(2,1)} %bitcast.168, bf16[512,1536]{1,0:T(8,128)(2,1)} %fusion.4.second_ref.grad_ref), custom_call_target="tpu_custom_call" | custom-call | tf_op jit(solution)/shard_map/gather_rows/pallas_call | solution.py:447
  122.9 16.3 %project.1 = (bf16[4,512,1536]{2,1,0:T(8,128)(2,1)}, f32[4,512,128]{2,1,0:T(8,128)S(1)}, bf16[4,3,512,128]{3,2,1,0:T(8,128)(2,1)S(1)}, bf16[4,3,512,128]{3,2,1,0:T(8,128)(2,1)S(1)}, bf16[4,3,512,128]{3,2,1,0:T(8,128)(2,1)S(1)}) custom-call(bf16[4,512,1536]{2,1,0:T(8,128)(2,1)} %get-tuple-element.56.x_ref, f32[1,1536]{1,0:T(1,128)S(1)} %get-tuple-element.365.gain_ref, ...), custom_call_target="tpu_custom_call" | custom-call | flops 8053063680 | bytes 12582912 | tf_op jit(solution)/shard_map/project/pallas_call | solution.py:492
  144.5 10.5 all_to_all.70
  155.0 85.5 %all_to_all.71.qkv_ref = bf16[4,3,512,128]{3,2,1,0:T(8,128)(2,1)S(1)} all-to-all(bf16[4,3,512,128]{3,2,1,0:T(8,128)(2,1)} %copy-done.11), channel_id=1, replica_groups=mesh['fsdp'=2,'ctx'=4,'tp'=4] {'ctx'}, dimensions={0} | all-to-all | bytes 3145728 | tf_op jit(solution)/shard_map/all_to_all | solution.py:967
  240.5 68.9 %all_to_all.72.qkv_ref = bf16[4,3,512,128]{3,2,1,0:T(8,128)(2,1)} all-to-all(bf16[4,3,512,128]{3,2,1,0:T(8,128)(2,1)S(1)} %get-tuple-element.61), channel_id=1, replica_groups=mesh['fsdp'=2,'ctx'=4,'tp'=4] {'ctx'}, dimensions={0} | all-to-all | bytes 3145728 | tf_op jit(solution)/shard_map/all_to_all | solution.py:967
  314.4 5.3 attend_forward.3
  321.4 28.6 %all-to-all-done.5.qkv_ref = bf16[4,3,512,128]{3,2,1,0:T(8,128)(2,1)S(1)} async-done(((bf16[4,3,512,128]{3,2,1,0:T(8,128)(2,1)}), bf16[4,3,512,128]{3,2,1,0:T(8,128)(2,1)S(1)}, u32[]{:S(2)}, u32[]{:S(2)}) %all-to-all-start.5) | async-done | bytes 1572896 | tf_op jit(solution)/shard_map/all_to_all | solution.py:967
  356.1 15.8 %attend_forward.4 = (bf16[4,512,128]{2,1,0:T(8,128)(2,1)S(1)}, f32[4,512,128]{2,1,0:T(8,128)S(1)}, f32[2,2048]{1,0:T(2,128)S(1)}) custom-call(s32[1]{0:T(128)} %bitcast.14.len_ref, bf16[4,3,512,128]{3,2,1,0:T(8,128)(2,1)S(1)} %copy-done.6, f32[2,2048]{1,0:T(2,128)S(1)} %bitcast.166), custom_call_target="tpu_custom_call" | custom-call | flops 2863310848 | bytes 3145728 | tf_op jit(solution)/shard_map/attend_forward/pallas_call | solution.py:198
  379.4 15.4 %attend_forward.5 = (bf16[4,512,128]{2,1,0:T(8,128)(2,1)S(1)}, f32[4,512,128]{2,1,0:T(8,128)S(1)}, f32[2,2048]{1,0:T(2,128)S(1)}) custom-call(s32[1]{0:T(128)} %bitcast.15.len_ref, bf16[4,3,512,128]{3,2,1,0:T(8,128)(2,1)S(1)} %copy-done.4, f32[2,2048]{1,0:T(2,128)S(1)} %bitcast.164), custom_call_target="tpu_custom_call" | custom-call | flops 2863310848 | bytes 3145728 | tf_op jit(solution)/shard_map/attend_forward/pallas_call | solution.py:198
  401.6 8.5 add_divide_fusion
  415.2 45.1 %out_project.1 = (f32[512,1536]{1,0:T(8,128)}, bf16[512,1536]{1,0:T(8,128)(2,1)S(1)}, bf16[4,512,384]{2,1,0:T(8,128)(2,1)S(1)}, bf16[4,512,384]{2,1,0:T(8,128)(2,1)}) custom-call(bf16[512,1536]{1,0:T(8,128)(2,1)} %bitcast.169, f32[4,512,384]{2,1,0:T(8,128)} %bitcast.171, bf16[1536,3840]{1,0:T(8,128)(2,1)} %all-gather.5.cloned.1.call-done.w_ref.gate_w.up_w.down_w, ...), custom_call_target="tpu_custom_call" | custom-call | flops 2415919104 | bytes 104857600 | tf_op jit(solution)/shard_map/out_project/pallas_call | solution.py:556
  462.6 52.5 %mlp.1 = (bf16[4,512,1536]{2,1,0:T(8,128)(2,1)}, bf16[4,512,1024]{2,1,0:T(8,128)(2,1)}, bf16[4,512,2048]{2,1,0:T(8,128)(2,1)}) custom-call(bf16[512,1536]{1,0:T(8,128)(2,1)} %copy-done.23, bf16[4,512,1536]{2,1,0:T(8,128)(2,1)} %get-tuple-element.67.grad_ref, bf16[1536,3840]{1,0:T(8,128)(2,1)} %all-gather.5.cloned.1.call-done.w_ref.gate_w.up_w.down_w, ...), custom_call_target="tpu_custom_call" | custom-call | flops 19327352832 | bytes 104857600 | tf_op jit(solution)/shard_map/mlp/pallas_call | solution.py:612
  515.2 11.4 bitcast_convert_fusion.1
  526.5 57.4 %mlp_back.1 = (f32[512,1536]{1,0:T(8,128)}, bf16[512,1536]{1,0:T(8,128)(2,1)}, f32[1,1536]{1,0:T(1,128)}) custom-call(bf16[4,512,2048]{2,1,0:T(8,128)(2,1)} %get-tuple-element.69.pair_ref, bf16[1536,3840]{1,0:T(8,128)(2,1)} %all-gather.5.cloned.1.call-done.w_ref.gate_w.up_w.down_w, f32[512,1536]{1,0:T(8,128)} %get-tuple-element.65.hidden_ref, ...), custom_call_target="tpu_custom_call" | custom-call | flops 12884901888 | bytes 104857600 | tf_op jit(solution)/shard_map/mlp_back/pallas_call | solution.py:666
  585.3 43.8 %out_back.1 = (bf16[4,512,1536]{2,1,0:T(8,128)(2,1)}, bf16[4,512,384]{2,1,0:T(8,128)(2,1)S(1)}, bf16[4,512,128]{2,1,0:T(8,128)(2,1)S(1)}, bf16[4,512,128]{2,1,0:T(8,128)(2,1)S(1)}, bf16[4,512,128]{2,1,0:T(8,128)(2,1)}) custom-call(bf16[512,1536]{1,0:T(8,128)(2,1)S(1)} %copy-done.2, bf16[1536,3840]{1,0:T(8,128)(2,1)} %all-gather.5.cloned.1.call-done.w_ref.gate_w.up_w.down_w, ...), custom_call_target="tpu_custom_call" | custom-call | flops 2415919104 | bytes 104857600 | tf_op jit(solution)/shard_map/out_back/pallas_call | solution.py:731
  635.3 7.0 fusion.6
  655.2 6.0 pad_maximum_fusion
  661.1 8.3 copy.509
  673.1 23.0 %attend_backward.4 = (bf16[4,3,512,128]{3,2,1,0:T(8,128)(2,1)S(1)}, f32[2,2048]{1,0:T(2,128)S(1)}, f32[2,2048]{1,0:T(2,128)S(1)}) custom-call(s32[1]{0:T(128)} %bitcast.14.len_ref, bf16[4,3,512,128]{3,2,1,0:T(8,128)(2,1)S(1)} %copy-done.7, bf16[4,512,128]{2,1,0:T(8,128)(2,1)S(1)} %copy-done.15, f32[4,512,128]{2,1,0:T(8,128)S(1)} %copy-done.29, ...), custom_call_target="tpu_custom_call" | custom-call | flops 7158277120 | bytes 3145728 | tf_op jit(solution)/shard_map/attend_backward/pallas_call | solution.py:216
  702.7 24.1 %attend_backward.5 = (bf16[4,3,512,128]{3,2,1,0:T(8,128)(2,1)S(1)}, f32[2,2048]{1,0:T(2,128)S(1)}, f32[2,2048]{1,0:T(2,128)S(1)}) custom-call(s32[1]{0:T(128)} %bitcast.15.len_ref, bf16[4,3,512,128]{3,2,1,0:T(8,128)(2,1)S(1)} %copy-done.5, bf16[4,512,128]{2,1,0:T(8,128)(2,1)} %all-to-all-done.11.grad_ref, f32[4,512,128]{2,1,0:T(8,128)S(1)} %copy-done.27, ...), custom_call_target="tpu_custom_call" | custom-call | flops 7158277120 | bytes 3145728 | tf_op jit(solution)/shard_map/attend_backward/pallas_call | solution.py:216
  732.3 9.0 attend_backward.3
  744.9 22.5 %all_to_all.73 = bf16[4,3,2,512]{3,2,1,0:T(2,128)(2,1)S(1)} all-to-all(bf16[4,3,2,512]{3,2,1,0:T(2,128)(2,1)S(1)} %bitcast.181), channel_id=1, replica_groups=mesh['fsdp'=2,'ctx'=4,'tp'=4] {'ctx'}, dimensions={0} | all-to-all | bytes 49152 | tf_op jit(solution)/shard_map/all_to_all | solution.py:967
  767.4 54.1 %all_to_all.74.refs_0_ = bf16[4,3,512,128]{3,2,1,0:T(8,128)(2,1)S(1)} all-to-all(bf16[4,3,512,128]{3,2,1,0:T(8,128)(2,1)S(1)} %get-tuple-element.75), channel_id=1, replica_groups=mesh['fsdp'=2,'ctx'=4,'tp'=4] {'ctx'}, dimensions={0} | all-to-all | bytes 3145728 | tf_op jit(solution)/shard_map/all_to_all | solution.py:967
  821.5 40.2 %all_to_all.75.refs_1_ = bf16[4,3,512,128]{3,2,1,0:T(8,128)(2,1)S(1)} all-to-all(bf16[4,3,512,128]{3,2,1,0:T(8,128)(2,1)} %copy-done.10), channel_id=1, replica_groups=mesh['fsdp'=2,'ctx'=4,'tp'=4] {'ctx'}, dimensions={0} | all-to-all | bytes 3145728 | tf_op jit(solution)/shard_map/all_to_all | solution.py:967
  869.4 32.8 %all-to-all-done.12.refs_2_ = bf16[4,3,512,128]{3,2,1,0:T(8,128)(2,1)} async-done(((bf16[4,3,512,128]{3,2,1,0:T(8,128)(2,1)}), bf16[4,3,512,128]{3,2,1,0:T(8,128)(2,1)}, u32[]{:S(2)}, u32[]{:S(2)}) %all-to-all-start.12) | async-done | bytes 1572896 | tf_op jit(solution)/shard_map/all_to_all | solution.py:967
  907.2 12.0 %convolution_convert_fusion.1 = bf16[1536,1280]{1,0:T(8,128)(2,1)} fusion(bf16[2048,1536]{1,0:T(8,128)(2,1)} %bitcast.185, bf16[2048,128]{1,0:T(8,128)(2,1)S(1)} %copy-done.33, bf16[2048,1152]{1,0:T(8,128)(2,1)S(1)} %bitcast.160), kind=kOutput, calls=%fused_computation.2 | convolution fusion | flops 8065515520 | bytes 15466496 | tf_op jit(solution)/shard_map/dot_general | solution.py:21
  919.6 11.5 convolution_convert_fusion
  931.2 19.1 %bitcast_convert_fusion = bf16[1536,2048]{1,0:T(8,128)(2,1)} fusion(bf16[4,512,1536]{2,1,0:T(8,128)(2,1)} %get-tuple-element.97, bf16[4,512,2048]{2,1,0:T(8,128)(2,1)} %get-tuple-element.69.pair_ref), kind=kOutput, calls=%fused_computation | convolution fusion | flops 12888047616 | bytes 20971520 | tf_op jit(solution)/shard_map/dot_general | solution.py:21
  951.3 53.2 %input_back.1 = (bf16[512,1536]{1,0:T(8,128)(2,1)}, f32[1,1536]{1,0:T(1,128)}) custom-call(bf16[4,512,1152]{2,1,0:T(8,128)(2,1)} %copy-done, bf16[4,512,384]{2,1,0:T(8,128)(2,1)} %copy-done.22, bf16[4,512,128]{2,1,0:T(8,128)(2,1)} %bitcast.178, bf16[1536,1280]{1,0:T(8,128)(2,1)} %all-gather.3.cloned.1.call-done.w_ref.qkv_w.forget_w, ...), custom_call_target="tpu_custom_call" | custom-call | flops 10468982784 | bytes 104857600 | tf_op jit(solution)/shard_map/input_back/pallas_call | solution.py:811
  1008.3 37.6 %all-reduce.1 = (f32[1536]{0:T(1024)S(1)}, f32[24]{0:T(128)S(1)}, f32[1536]{0:T(1024)S(1)}) all-reduce(f32[1536]{0:T(1024)S(1)} %reduce, f32[24]{0:T(128)S(1)} %dynamic_update_slice.3, f32[1536]{0:T(1024)S(1)} %reduce.1), channel_id=1, replica_groups=mesh['fsdp'=2,'ctx'=4,'tp'=4] {'fsdp','ctx','tp'}, use_global_device_ids=true, to_apply=%region_8.9 | all-reduce | flops 3096 | bytes 24768 | tf_op jit(solution)/shard_map/psum | solution.py:1065
  1055.7 7.2 reduce-scatter.7.cloned.1.call-done
  1068.1 116.7 %reduce-scatter.11.cloned.1.call-done = bf16[192,2048]{1,0:T(8,128)(2,1)} async-done(((bf16[1536,2048]{1,0:T(8,128)(2,1)}), bf16[192,2048]{1,0:T(8,128)(2,1)}) %reduce-scatter.11.cloned.1.call-update) | async-done | bytes 786448 | tf_op jit(solution)/shard_map/reduce_scatter | solution.py:999
  (212 shorter events, 130.1 us)
Async XLA Ops:
  7.2 6.6 copy-start.34
  7.2 9.6 copy-start.42
  7.2 9.6 copy-start.31
  7.2 114.2 %all-gather.3.cloned.1.call-start = ((), (), s32[]{:S(2)}) async-start(), calls=%async_computation.18 | async-start | bytes 4423680 | tf_op jit(solution)/shard_map/all_gather | solution.py:925
  11.6 390.0 %all-gather.5.cloned.1.call-start = ((), (), s32[]{:S(2)}) async-start(), calls=%async_computation.19 | async-start | bytes 13271040 | tf_op jit(solution)/shard_map/all_gather | solution.py:926
  16.8 1.8 copy-start.32
  122.8 16.3 %copy-start.21 = (f32[1,1536]{1,0:T(1,128)}, f32[1,1536]{1,0:T(1,128)S(1)}, u32[]{:S(2)}) copy-start(f32[1,1536]{1,0:T(1,128)S(1)} %get-tuple-element.365.gain_ref) | copy-start | bytes 18436
  122.8 292.4 %copy-start.20 = (f32[1,1536]{1,0:T(1,128)}, f32[1,1536]{1,0:T(1,128)S(1)}, u32[]{:S(2)}) copy-start(f32[1,1536]{1,0:T(1,128)S(1)} %get-tuple-element.364.gain_ref) | copy-start | bytes 18436
  309.4 40.7 %all-to-all-start.5 = ((bf16[4,3,512,128]{3,2,1,0:T(8,128)(2,1)}), bf16[4,3,512,128]{3,2,1,0:T(8,128)(2,1)S(1)}, u32[]{:S(2)}, u32[]{:S(2)}) async-start(bf16[4,3,512,128]{3,2,1,0:T(8,128)(2,1)} %copy-done.8), calls=%async_computation.5 | async-start | bytes 3145728 | tf_op jit(solution)/shard_map/all_to_all | solution.py:967
  351.2 22.6 %all-to-all-start.2 = ((bf16[4,512,128]{2,1,0:T(8,128)(2,1)}), bf16[4,512,128]{2,1,0:T(8,128)(2,1)S(1)}, u32[]{:S(2)}, u32[]{:S(2)}) async-start(bf16[4,512,128]{2,1,0:T(8,128)(2,1)} %copy-done.17), calls=%async_computation.2 | async-start | bytes 1048576 | tf_op jit(solution)/shard_map/all_to_all | solution.py:967
  354.7 1.4 copy-start.6
  373.8 22.8 %all-to-all-start.4 = ((bf16[4,512,128]{2,1,0:T(8,128)(2,1)}), bf16[4,512,128]{2,1,0:T(8,128)(2,1)S(1)}, u32[]{:S(2)}, u32[]{:S(2)}) async-start(bf16[4,512,128]{2,1,0:T(8,128)(2,1)} %copy-done.16), calls=%async_computation.4 | async-start | bytes 1048576 | tf_op jit(solution)/shard_map/all_to_all | solution.py:967
  377.9 1.4 copy-start.4
  396.5 18.7 %all-to-all-start.6 = ((bf16[4,512,128]{2,1,0:T(8,128)(2,1)}), bf16[4,512,128]{2,1,0:T(8,128)(2,1)S(1)}, u32[]{:S(2)}, u32[]{:S(2)}) async-start(bf16[4,512,128]{2,1,0:T(8,128)(2,1)} %copy-done.18), calls=%async_computation.6 | async-start | bytes 1048576 | tf_op jit(solution)/shard_map/all_to_all | solution.py:967
  583.9 1.4 copy-start.2
  631.8 19.1 %all-to-all-start.9 = ((bf16[4,512,128]{2,1,0:T(8,128)(2,1)}), bf16[4,512,128]{2,1,0:T(8,128)(2,1)S(1)}, u32[]{:S(2)}, u32[]{:S(2)}) async-start(bf16[4,512,128]{2,1,0:T(8,128)(2,1)} %copy-done.19), calls=%async_computation.10 | async-start | bytes 1048576 | tf_op jit(solution)/shard_map/all_to_all | solution.py:967
  635.3 7.1 copy-start.40
  635.3 7.0 copy-start.41
  651.0 10.2 copy-start.14
  651.0 46.3 %all-to-all-start.11 = ((bf16[4,512,128]{2,1,0:T(8,128)(2,1)}), bf16[4,512,128]{2,1,0:T(8,128)(2,1)}, u32[]{:S(2)}, u32[]{:S(2)}) async-start(bf16[4,512,128]{2,1,0:T(8,128)(2,1)} %get-tuple-element.80), calls=%async_computation.12 | async-start | bytes 1048576 | tf_op jit(solution)/shard_map/all_to_all | solution.py:967
  655.1 392.6 %reduce-scatter.13.cloned.1.call-start = ((), (), s32[]{:S(2)}) async-start(), calls=%async_computation.23 | async-start | bytes 6193152
  669.4 1.4 copy-start.7
  673.1 28.3 %copy-start.5 = (bf16[4,3,512,128]{3,2,1,0:T(8,128)(2,1)S(1)}, bf16[4,3,512,128]{3,2,1,0:T(8,128)(2,1)}, u32[]{:S(2)}) copy-start(bf16[4,3,512,128]{3,2,1,0:T(8,128)(2,1)} %copy-done.3) | copy-start | bytes 4718596
  697.3 33.8 %all-to-all-start.7 = ((bf16[4,512,128]{2,1,0:T(8,128)(2,1)}), bf16[4,512,128]{2,1,0:T(8,128)(2,1)}, u32[]{:S(2)}, u32[]{:S(2)}) async-start(bf16[4,512,128]{2,1,0:T(8,128)(2,1)} %copy-done.13), calls=%async_computation.8 | async-start | bytes 1048576 | tf_op jit(solution)/shard_map/all_to_all | solution.py:967
  861.7 40.5 %all-to-all-start.12 = ((bf16[4,3,512,128]{3,2,1,0:T(8,128)(2,1)}), bf16[4,3,512,128]{3,2,1,0:T(8,128)(2,1)}, u32[]{:S(2)}, u32[]{:S(2)}) async-start(bf16[4,3,512,128]{3,2,1,0:T(8,128)(2,1)} %copy-done.9), calls=%async_computation.13 | async-start | bytes 3145728 | tf_op jit(solution)/shard_map/all_to_all | solution.py:967
  866.1 186.1 %reduce-scatter.9.cloned.1.call-start = ((), (), s32[]{:S(2)}) async-start(), calls=%async_computation.21 | async-start | bytes 4423680 | tf_op jit(solution)/shard_map/reduce_scatter | solution.py:999
  902.2 5.0 copy-start.33
  905.1 2.1 copy-start
  919.2 143.8 %reduce-scatter.7.cloned.1.call-start = ((), (), s32[]{:S(2)}) async-start(), calls=%async_computation.20 | async-start | bytes 7864320 | tf_op jit(solution)/shard_map/reduce_scatter | solution.py:862
  931.2 253.7 %reduce-scatter.11.cloned.1.call-start = ((), (), s32[]{:S(2)}) async-start(), calls=%async_computation.22 | async-start | bytes 7077888 | tf_op jit(solution)/shard_map/reduce_scatter | solution.py:999
  1004.5 3.8 copy-start.38
  1049.2 13.8 %copy-start.36 = (f32[512]{0:T(512)S(1)}, f32[512]{0:T(512)}, u32[]{:S(2)}) copy-start(f32[512]{0:T(512)} %copy-done.35) | copy-start | bytes 6148
  (25 other events, 26.2 us)
Sparse Core Ops, SparseCore 0:
  11.8 72.7 all-gather.2
  86.7 243.6 all-gather.4
  669.6 139.4 reduce-scatter.12
  919.3 82.4 reduce-scatter.8
  1004.2 58.7 reduce-scatter.6
  1066.8 117.9 reduce-scatter.10

commit v2 on v1

--- a/solution.py
+++ b/solution.py
@@ -10,6 +10,7 @@
 F32 = jnp.float32
 BF16 = jnp.bfloat16
 LANES = 128
+MESH = pl.DeviceIdType.MESH
 epsilon = 1e-06
 masked_score = -1e30
 NT = (((1,), (1,)), ((), ()))
@@ -33,19 +34,15 @@
     return ((head + 1) % 2) * head_size
 
 
-def attend_forward(len_ref, qkv_ref, decay_ref, out_ref, exact_ref, lse_ref, *, heads, head_size):
-    count, _, block, width = qkv_ref.shape
+def attend_item(qkv, decay, out, exact, lse, heads, head_size):
+    count, _, block, width = qkv.shape
     scale = head_size**-0.5
-    live = pl.cdiv(len_ref[0], block)
-    out_ref[...] = jnp.zeros_like(out_ref)
-    exact_ref[...] = jnp.zeros_like(exact_ref)
-    lse_ref[...] = jnp.zeros_like(lse_ref)
     row = lax.broadcasted_iota(jnp.int32, (block, block), 0)
     column = lax.broadcasted_iota(jnp.int32, (block, block), 1)
     causal = column <= row
 
     def query_block(i, _):
-        query = qkv_ref[i, 0]
+        query = qkv[i, 0]
         lanes = pl.ds(pl.multiple_of(i * block, block), block)
         result = jnp.zeros((block, width), F32)
         for head in range(heads):
@@ -54,15 +51,15 @@
             def step(j, carry, masked):
                 top, total, acc = carry
                 keys = pl.ds(pl.multiple_of(j * block, block), block)
-                score = dot(query_head, qkv_ref[j, 1], NT) * scale
-                score = score - decay_ref[head : head + 1, keys]
+                score = dot(query_head, qkv[j, 1], NT) * scale
+                score = score - decay[head : head + 1, keys]
                 if masked:
                     score = jnp.where(causal, score, masked_score)
                 new_top = jnp.maximum(top, jnp.max(score, axis=1, keepdims=True))
                 prob = jnp.exp(score - new_top)
                 shrink = jnp.exp(top - new_top)
                 total = total * shrink + jnp.sum(prob, axis=1, keepdims=True)
-                acc = acc * shrink + dot(prob.astype(BF16), qkv_ref[j, 2], NN)
+                acc = acc * shrink + dot(prob.astype(BF16), qkv[j, 2], NN)
                 return new_top, total, acc
 
             carry = (
@@ -75,42 +72,26 @@
             lane = lax.broadcasted_iota(jnp.int32, acc.shape, 1)
             result = jnp.where(lane // head_size == head, acc / total, result)
             stat = jnp.broadcast_to(top + jnp.log(total), (block, LANES)).T
-            lse_ref[head : head + 1, lanes] = stat[0:1]
-        exact_ref[i] = result
-        out_ref[i] = result.astype(BF16)
+            lse[head : head + 1, lanes] = stat[0:1]
+        exact[i] = result
+        out[i] = result.astype(BF16)
         return 0
 
-    lax.fori_loop(0, live, query_block, 0)
-
-
-def attend_backward(
-    len_ref,
-    qkv_ref,
-    grad_ref,
-    exact_ref,
-    lse_ref,
-    decay_ref,
-    dqkv_ref,
-    row_ref,
-    column_ref,
-    dq_acc,
-    delta,
-    *,
-    heads,
-    head_size,
-):
-    count, _, block, width = qkv_ref.shape
+    lax.fori_loop(0, count, query_block, 0)
+
+
+def attend_item_back(qkv, grads, exact, lse, decay, dqkv, change, dq_acc, delta, heads, head_size):
+    count, _, block, width = qkv.shape
     scale = head_size**-0.5
-    live = pl.cdiv(len_ref[0], block)
-    for ref in (dqkv_ref, row_ref, column_ref, dq_acc):
-        ref[...] = jnp.zeros_like(ref)
     row = lax.broadcasted_iota(jnp.int32, (block, block), 0)
     column = lax.broadcasted_iota(jnp.int32, (block, block), 1)
     causal = row <= column
+    dq_acc[...] = jnp.zeros_like(dq_acc)
+    change[...] = jnp.zeros_like(change)
 
     def prepare(i, _):
         lanes = pl.ds(pl.multiple_of(i * block, block), block)
-        product = grad_ref[i].astype(F32) * exact_ref[i]
+        product = grads[i].astype(F32) * exact[i]
         lane = lax.broadcasted_iota(jnp.int32, product.shape, 1)
         for head in range(heads):
             part = jnp.where(lane // head_size == head, product, 0.0)
@@ -118,26 +99,26 @@
             delta[head : head + 1, lanes] = jnp.broadcast_to(part, (block, LANES)).T[0:1]
         return 0
 
-    lax.fori_loop(0, live, prepare, 0)
+    lax.fori_loop(0, count, prepare, 0)
 
     def key_block(j, _):
         keys = pl.ds(pl.multiple_of(j * block, block), block)
-        key = qkv_ref[j, 1]
-        value = qkv_ref[j, 2]
+        key = qkv[j, 1]
+        value = qkv[j, 2]
         value_total = jnp.zeros((block, width), F32)
         key_total = jnp.zeros((block, width), F32)
         for head in range(heads):
             spare = spare_lane(head, head_size)
             key_ones = of_head(key, head, head_size, spare)
-            decay = jnp.broadcast_to(decay_ref[head : head + 1, keys], (LANES, block)).T[:, 0:1]
+            fall = jnp.broadcast_to(decay[head : head + 1, keys], (LANES, block)).T[:, 0:1]
 
             def step(i, carry, masked):
                 value_acc, key_acc = carry
                 lanes = pl.ds(pl.multiple_of(i * block, block), block)
-                query = qkv_ref[i, 0]
-                grad = of_head(grad_ref[i], head, head_size)
+                query = qkv[i, 0]
+                grad = of_head(grads[i], head, head_size)
                 score = dot(key, of_head(query, head, head_size), NT) * scale
-                score = score - decay - lse_ref[head : head + 1, lanes]
+                score = score - fall - lse[head : head + 1, lanes]
                 if masked:
                     score = jnp.where(causal, score, masked_score)
                 prob = jnp.exp(score)
@@ -152,17 +133,17 @@
 
             zero = jnp.zeros((block, width), F32)
             carry = step(j, (zero, zero), True)
-            carry = lax.fori_loop(j + 1, live, lambda i, c: step(i, c, False), carry)
+            carry = lax.fori_loop(j + 1, count, lambda i, c: step(i, c, False), carry)
             value_acc, key_acc = carry
             value_total = value_total + value_acc
             lane = lax.broadcasted_iota(jnp.int32, key_acc.shape, 1)
             key_total = jnp.where(lane // head_size == head, key_acc, key_total)
-            column_ref[head : head + 1, keys] = key_acc.T[spare : spare + 1]
-        dqkv_ref[j, 1] = (key_total * scale).astype(BF16)
-        dqkv_ref[j, 2] = value_total.astype(BF16)
+            change[head : head + 1, keys] -= key_acc.T[spare : spare + 1]
+        dqkv[j, 1] = (key_total * scale).astype(BF16)
+        dqkv[j, 2] = value_total.astype(BF16)
         return 0
 
-    lax.fori_loop(0, live, key_block, 0)
+    lax.fori_loop(0, count, key_block, 0)
 
     def finish(i, _):
         lanes = pl.ds(pl.multiple_of(i * block, block), block)
@@ -172,67 +153,274 @@
             part = dq_acc[head, i]
             lane = lax.broadcasted_iota(jnp.int32, part.shape, 1)
             total = jnp.where(lane // head_size == head, part, total)
-            row_ref[head : head + 1, lanes] = part.T[spare : spare + 1]
-        dqkv_ref[i, 0] = (total * scale).astype(BF16)
+            change[head : head + 1, lanes] += part.T[spare : spare + 1]
+        dqkv[i, 0] = (total * scale).astype(BF16)
         return 0
 
-    lax.fori_loop(0, live, finish, 0)
-
-
-def attend_specs(count):
-    smem = pl.BlockSpec(memory_space=pltpu.SMEM)
-    return [smem] + [pl.BlockSpec(memory_space=pltpu.VMEM)] * count
-
-
-def attend_cost(qkv, decay, products):
-    count, _, block, width = qkv.shape
-    heads = decay.shape[0]
-    pairs = heads * (count * block) ** 2 // 3
+    lax.fori_loop(0, count, finish, 0)
+
+
+def triangle(upward):
+    row = lax.broadcasted_iota(jnp.int32, (LANES, LANES), 0)
+    column = lax.broadcasted_iota(jnp.int32, (LANES, LANES), 1)
+    keep = (row <= column) if upward else (row >= column)
+    return jnp.where(keep, 1.0, 0.0).astype(BF16)
+
+
+def exact_product(values, matrix):
+    high = values.astype(BF16)
+    rest = values - high.astype(F32)
+    middle = rest.astype(BF16)
+    low = (rest - middle.astype(F32)).astype(BF16)
+    return dot(high, matrix, NN) + dot(middle, matrix, NN) + dot(low, matrix, NN)
+
+
+def ctx_sending(source, target, send_sem, recv_sem, peer):
+    return pltpu.make_async_remote_copy(
+        src_ref=source,
+        dst_ref=target,
+        send_sem=send_sem,
+        recv_sem=recv_sem,
+        device_id={"ctx": peer},
+        device_id_type=MESH,
+    )
+
+
+def ctx_greet(size):
+    me = lax.axis_index("ctx")
+    barrier = pltpu.get_barrier_semaphore()
+    for step in range(1, size):
+        peer = lax.rem(me + step, size)
+        pl.semaphore_signal(barrier, inc=1, device_id={"ctx": peer}, device_id_type=MESH)
+    pl.semaphore_wait(barrier, size - 1)
+    return me
+
+
+class Exchange:
+    def __init__(self, me, size, source, target, sems):
+        self.me, self.size, self.source, self.target = me, size, source, target
+        self.send_sem, self.recv_sem, self.own_sem = sems
+
+    def own(self, item):
+        return pltpu.make_async_copy(
+            self.source.at[item, self.me], self.target.at[item, self.me], self.own_sem.at[item]
+        )
+
+    def copy(self, item, step):
+        peer = lax.rem(self.me + step, self.size)
+        return ctx_sending(
+            self.source.at[item, peer],
+            self.target.at[item, self.me],
+            self.send_sem.at[item, step],
+            self.recv_sem.at[item, step],
+            peer,
+        )
+
+    def start(self, item):
+        self.own(item).start()
+        for step in range(1, self.size):
+            self.copy(item, step).start()
+
+    def arrive(self, item):
+        self.own(item).wait()
+        for step in range(1, self.size):
+            self.copy(item, step).wait_recv()
+
+    def drain(self, item):
+        for step in range(1, self.size):
+            self.copy(item, step).wait_send()
+
+
+def exchange_sems(items, size):
+    return [
+        pltpu.SemaphoreType.DMA((items, size)),
+        pltpu.SemaphoreType.DMA((items, size)),
+        pltpu.SemaphoreType.DMA((items,)),
+    ]
+
+
+def context_kernel(
+    heads, head_size, items_ref, forget_ref, back_ref, qkv_ref, exact_ref, lse_ref, decay_ref, *refs
+):
+    qkv, forget, out, save_sem = refs[:4]
+    sems = refs[4:]
+    count, size, _, block, width = items_ref.shape
+    me = ctx_greet(size)
+    forgets = Exchange(me, size, forget_ref, forget, sems[0:3])
+    inputs = Exchange(me, size, items_ref, qkv, sems[3:6])
+    results = Exchange(me, size, out, back_ref, sems[6:9])
+
+    @pl.loop(0, count)
+    def _(item):
+        forgets.start(item)
+
+    inputs.start(0)
+
+    @pl.loop(0, count)
+    def _(item):
+        forgets.arrive(item)
+
+    @pl.loop(0, count)
+    def _(item):
+        upper = triangle(True)
+        before = jnp.zeros((8, 1), F32)
+        for start in range(0, size * block, LANES):
+            part = forget[item, start // block, :, pl.ds(start % block, LANES)]
+            total = before + dot(part.astype(BF16), upper, NN)
+            decay_ref[item, :, pl.ds(start, LANES)] = total
+            before = total[:, LANES - 1 :]
+
+    lse_ref[...] = jnp.zeros_like(lse_ref)
+
+    @pl.loop(0, count)
+    def _(item):
+        @pl.when(item + 1 < count)
+        def _():
+            inputs.start(item + 1)
+
+        inputs.arrive(item)
+        saving = pltpu.make_async_copy(qkv.at[item], qkv_ref.at[item], save_sem)
+        saving.start()
+        attend_item(
+            qkv.at[item], decay_ref.at[item], out.at[item], exact_ref.at[item], lse_ref.at[item], heads, head_size
+        )
+        results.start(item)
+        saving.wait()
+
+    @pl.loop(0, count)
+    def _(item):
+        forgets.drain(item)
+        inputs.drain(item)
+        results.arrive(item)
+        results.drain(item)
+
+
+def full_block(shape):
+    return pl.BlockSpec(shape, lambda i: (0,) * len(shape), pipeline_mode=pl.Buffered(1))
+
+
+def attend_cost(items, heads, products):
+    count, size, _, block, width = items.shape
+    pairs = count * heads * (size * block) ** 2 // 2
     return pl.CostEstimate(
-        flops=2 * products * pairs * 256, bytes_accessed=2 * qkv.size * 2, transcendentals=pairs
-    )
-
-
-def attend(length, qkv, decay, head_size):
-    count, _, block, width = qkv.shape
+        flops=2 * products * pairs * 256, bytes_accessed=100 << 20, transcendentals=pairs
+    )
+
+
+def context(items, forget, head_size, ident):
+    count, size, _, block, width = items.shape
+    heads = width // head_size
+    place = pl.BlockSpec(memory_space=pl.ANY)
+    exact, stat = (count, size, block, width), (count, 8, size * block)
     return pl.pallas_call(
-        functools.partial(attend_forward, heads=decay.shape[0], head_size=head_size),
+        functools.partial(context_kernel, heads, head_size),
+        grid=(1,),
         out_shape=[
-            jax.ShapeDtypeStruct((count, block, width), BF16),
-            jax.ShapeDtypeStruct((count, block, width), F32),
-            jax.ShapeDtypeStruct(decay.shape, F32),
-        ],
-        in_specs=attend_specs(2),
-        out_specs=attend_specs(3)[1:],
-        compiler_params=pltpu.CompilerParams(vmem_limit_bytes=40 << 20),
-        cost_estimate=attend_cost(qkv, decay, 2),
-        name="attend_forward",
-    )(length, qkv, decay)
-
-
-def attend_grad(length, qkv, grad, exact, lse, decay, head_size):
-    count, _, block, width = qkv.shape
-    heads = decay.shape[0]
+            jax.ShapeDtypeStruct(exact, BF16),
+            jax.ShapeDtypeStruct(items.shape, BF16),
+            jax.ShapeDtypeStruct(exact, F32),
+            jax.ShapeDtypeStruct(stat, F32),
+            jax.ShapeDtypeStruct(stat, F32),
+        ],
+        in_specs=[place, place],
+        out_specs=[place, place, full_block(exact), full_block(stat), full_block(stat)],
+        scratch_shapes=[
+            pltpu.VMEM(items.shape, BF16),
+            pltpu.VMEM(forget.shape, F32),
+            pltpu.VMEM(exact, BF16),
+            pltpu.SemaphoreType.DMA,
+        ]
+        + exchange_sems(count, size) * 3,
+        compiler_params=remote_params(ident, 48),
+        cost_estimate=attend_cost(items, heads, 2),
+        name="context",
+    )(items, forget)
+
+
+def context_back_kernel(
+    heads, head_size, items_ref, qkv_ref, exact_ref, lse_ref, decay_ref, back_ref, forget_ref, *refs
+):
+    grads, dqkv, change, slope, dq_acc, delta = refs[:6]
+    sems = refs[6:]
+    count, size, block, width = items_ref.shape
+    me = ctx_greet(size)
+    inputs = Exchange(me, size, items_ref, grads, sems[0:3])
+    results = Exchange(me, size, dqkv, back_ref, sems[3:6])
+    forgets = Exchange(me, size, slope, forget_ref, sems[6:9])
+
+    @pl.loop(0, count)
+    def _(item):
+        inputs.start(item)
+
+    @pl.loop(0, count)
+    def _(item):
+        inputs.arrive(item)
+        attend_item_back(
+            qkv_ref.at[item],
+            grads.at[item],
+            exact_ref.at[item],
+            lse_ref.at[item],
+            decay_ref.at[item],
+            dqkv.at[item],
+            change,
+            dq_acc,
+            delta,
+            heads,
+            head_size,
+        )
+        results.start(item)
+        lower = triangle(False)
+        after = jnp.zeros((8, 1), F32)
+        for start in reversed(range(0, size * block, LANES)):
+            total = after + exact_product(change[:, pl.ds(start, LANES)], lower)
+            slope[item, start // block, :, pl.ds(start % block, LANES)] = total
+            after = total[:, 0:1]
+        forgets.start(item)
+
+    @pl.loop(0, count)
+    def _(item):
+        inputs.drain(item)
+        results.arrive(item)
+        results.drain(item)
+        forgets.arrive(item)
+        forgets.drain(item)
+
+
+def context_back(grads, qkv, exact, lse, decay, head_size, ident):
+    count, size, _, block, width = qkv.shape
+    heads = width // head_size
+    place = pl.BlockSpec(memory_space=pl.ANY)
+    forget = (count, size, 8, block)
     return pl.pallas_call(
-        functools.partial(attend_backward, heads=heads, head_size=head_size),
+        functools.partial(context_back_kernel, heads, head_size),
+        grid=(1,),
         out_shape=[
             jax.ShapeDtypeStruct(qkv.shape, BF16),
-            jax.ShapeDtypeStruct(decay.shape, F32),
-            jax.ShapeDtypeStruct(decay.shape, F32),
-        ],
-        in_specs=attend_specs(5),
-        out_specs=attend_specs(3)[1:],
+            jax.ShapeDtypeStruct(forget, F32),
+        ],
+        in_specs=[
+            place,
+            full_block(qkv.shape),
+            full_block(exact.shape),
+            full_block(lse.shape),
+            full_block(decay.shape),
+        ],
+        out_specs=[place, place],
         scratch_shapes=[
-            pltpu.VMEM((heads, count, block, width), F32),
-            pltpu.VMEM((8, count * block), F32),
-        ],
-        compiler_params=pltpu.CompilerParams(vmem_limit_bytes=40 << 20),
-        cost_estimate=attend_cost(qkv, decay, 5),
-        name="attend_backward",
-    )(length, qkv, grad, exact, lse, decay)
-
-
-MESH = pl.DeviceIdType.MESH
+            pltpu.VMEM(grads.shape, BF16),
+            pltpu.VMEM(qkv.shape, BF16),
+            pltpu.VMEM((8, size * block), F32),
+            pltpu.VMEM(forget, F32),
+            pltpu.VMEM((heads, size, block, width), F32),
+            pltpu.VMEM((8, size * block), F32),
+        ]
+        + exchange_sems(count, size) * 3,
+        compiler_params=remote_params(ident, 56),
+        cost_estimate=attend_cost(qkv, heads, 5),
+        name="context_back",
+    )(grads, qkv, exact, lse, decay)
+
+
 CHUNKS = 4
 
 
@@ -271,34 +459,40 @@
     return slot, chunk
 
 
-def gather_loop(table, sems, compute):
+def gather_loop(table, sems, compute, own=None, relative=False):
     near_send, near_recv, far_send, far_recv, pass_send, pass_recv = sems
-    me, sibling, across, diagonal = places = tp_places()
+    me, sibling, across, diagonal = tp_places()
+    places = (0, 1, 2, 3) if relative else (me, sibling, across, diagonal)
+    mine, near_by, far_off, corner = places
+    near_spot, far_spot, pass_spot = (1, 2, 3) if relative else (me, me, across)
     rows = table.shape[1] // CHUNKS
 
     def part(slot, chunk):
         return table.at[slot, pl.ds(pl.multiple_of(chunk * rows, rows), rows)]
 
     def far(chunk):
+        source = part(mine, chunk)
+        if own is not None:
+            source = own.at[pl.ds(pl.multiple_of(chunk * rows, rows), rows)]
+        return sending(source, part(far_spot, chunk), far_send.at[chunk], far_recv.at[chunk], across)
+
+    def far_arrival(chunk):
+        spot = part(far_off, chunk)
+        return sending(spot, spot, far_send.at[chunk], far_recv.at[chunk], across)
+
+    def passing(chunk):
         return sending(
-            part(me, chunk), part(me, chunk), far_send.at[chunk], far_recv.at[chunk], across
+            part(far_off, chunk), part(pass_spot, chunk), pass_send.at[chunk], pass_recv.at[chunk], sibling
         )
 
-    def far_arrival(chunk):
-        spot = part(across, chunk)
-        return sending(spot, spot, far_send.at[chunk], far_recv.at[chunk], across)
-
-    def passing(chunk):
-        spot = part(across, chunk)
-        return sending(spot, spot, pass_send.at[chunk], pass_recv.at[chunk], sibling)
-
     def pass_arrival(chunk):
-        spot = part(diagonal, chunk)
+        spot = part(corner, chunk)
         return sending(spot, spot, pass_send.at[chunk], pass_recv.at[chunk], sibling)
 
     for chunk in range(CHUNKS):
         far(chunk).start()
-    near = sending(table.at[me], table.at[me], near_send, near_recv, sibling)
+    own = table.at[mine] if own is None else own
+    near = sending(own, table.at[near_spot], near_send, near_recv, sibling)
     near.start()
 
     def body(step, _):
@@ -307,7 +501,7 @@
 
         @pl.when(step == CHUNKS)
         def _():
-            spot = table.at[sibling]
+            spot = table.at[near_by]
             sending(spot, spot, near_send, near_recv, sibling).wait_recv()
 
         @pl.when((late >= 0) & (lax.rem(late, 2) == 0))
@@ -332,10 +526,11 @@
 GATHER_SEMS = [pltpu.SemaphoreType.DMA] * 2 + [pltpu.SemaphoreType.DMA((CHUNKS,))] * 4
 
 
-def scatter_loop(buffers, sems, partial, finish):
+def scatter_loop(buffers, sems, partial, finish, relative=False):
     near_out, near_in, far_out, far_in = buffers
     near_send, near_recv, far_send, far_recv = sems
     me, sibling, across, diagonal = tp_places()
+    mine, near_by, far_off, corner = (0, 1, 2, 3) if relative else (me, sibling, across, diagonal)
     rows = far_out.shape[0] // CHUNKS
 
     def span(chunk):
@@ -362,7 +557,7 @@
     def body(step, _):
         phase, chunk = step // CHUNKS, lax.rem(step, CHUNKS)
         slot = jnp.where(
-            phase == 0, diagonal, jnp.where(phase == 1, across, jnp.where(phase == 2, sibling, me))
+            phase == 0, corner, jnp.where(phase == 1, far_off, jnp.where(phase == 2, near_by, mine))
         )
         value = partial(slot, chunk)
         spot = span(chunk)
@@ -406,53 +601,25 @@
     ]
 
 
-def gather_two_kernel(first_ref, second_ref, first_all, second_all, near_send, near_recv, far_send, far_recv, pass_send, pass_recv, own_sem):
+def gather_rows_kernel(rows_ref, all_ref, own_sem, *sems):
     me, sibling, across, diagonal = tp_places()
     greet((sibling, across))
-    pairs = ((first_ref, first_all), (second_ref, second_all))
-    rows = first_ref.shape[0] // CHUNKS
-    started = []
-    for n, (source, table) in enumerate(pairs):
-        own = pltpu.make_async_copy(source, table.at[me], own_sem.at[n])
-        own.start()
-        started.append(own)
-    fars, nears, passes = [], [], []
-    for n, (source, table) in enumerate(pairs):
-        for chunk in range(CHUNKS):
-            spot = pl.ds(chunk * rows, rows)
-            copy = sending(source.at[spot], table.at[me, spot], far_send.at[n, chunk], far_recv.at[n, chunk], across)
-            copy.start()
-            fars.append(copy)
-        near = sending(source, table.at[me], near_send.at[n], near_recv.at[n], sibling)
-        near.start()
-        nears.append(near)
-    for n, (source, table) in enumerate(pairs):
-        for chunk in range(CHUNKS):
-            spot = pl.ds(chunk * rows, rows)
-            fars[n * CHUNKS + chunk].wait_recv()
-            copy = sending(table.at[across, spot], table.at[across, spot], pass_send.at[n, chunk], pass_recv.at[n, chunk], sibling)
-            copy.start()
-            passes.append(copy)
-    for copy in passes + nears:
-        copy.wait()
-    for copy in fars:
-        copy.wait_send()
-    for copy in started:
-        copy.wait()
-
-
-def gather_two(first, second, ident):
-    rows, width = first.shape
-    many = pltpu.SemaphoreType.DMA((2, CHUNKS))
+    own = pltpu.make_async_copy(rows_ref, all_ref.at[me], own_sem)
+    own.start()
+    gather_loop(all_ref, sems, lambda slot, chunk: None, rows_ref)
+    own.wait()
+
+
+def gather_rows(rows, ident):
     return pl.pallas_call(
-        gather_two_kernel,
-        out_shape=[jax.ShapeDtypeStruct((4, rows, width), BF16)] * 2,
-        in_specs=[pl.BlockSpec(memory_space=pl.ANY)] * 2,
-        out_specs=[pl.BlockSpec(memory_space=pl.ANY)] * 2,
-        scratch_shapes=[pltpu.SemaphoreType.DMA((2,))] * 2 + [many] * 4 + [pltpu.SemaphoreType.DMA((2,))],
+        gather_rows_kernel,
+        out_shape=jax.ShapeDtypeStruct((4,) + rows.shape, BF16),
+        in_specs=[pl.BlockSpec(memory_space=pl.ANY)],
+        out_specs=pl.BlockSpec(memory_space=pl.ANY),
+        scratch_shapes=[pltpu.SemaphoreType.DMA] + GATHER_SEMS,
         compiler_params=pltpu.CompilerParams(collective_id=ident, has_side_effects=True),
         name="gather_rows",
-    )(first, second)
+    )(rows)
 
 
 def whole(shape, column=None):
@@ -466,19 +633,19 @@
     )
 
 
-def project_kernel(layout, x_ref, gain_ref, w_ref, normed_ref, forget_ref, *item_refs):
+def project_kernel(layout, x_ref, gain_ref, w_ref, normed_ref, forget_ref, items_ref):
     seq_count, groups, width, places = layout
     x = x_ref[0].astype(F32)
     normed = (x * lax.rsqrt(jnp.mean(x * x, axis=1, keepdims=True) + epsilon) * gain_ref[...]).astype(BF16)
     normed_ref[0] = normed
     inner = groups * width
     rows = x.shape[0] // seq_count
-    count = len(item_refs)
+    count = items_ref.shape[0]
     for kind in range(3):
         value = dot(normed, w_ref[:, kind * inner : (kind + 1) * inner], NN).astype(BF16)
         for slot, (s, g) in enumerate(places):
             piece = value[s * rows : (s + 1) * rows, g * width : (g + 1) * width]
-            item_refs[slot % count][slot // count, kind] = piece
+            items_ref[slot % count, slot // count, kind] = piece
     forget_ref[0] = dot(normed, w_ref[:, 3 * inner :], NN)
 
 
@@ -486,7 +653,7 @@
     seq_count, groups, width, places = layout
     tp_size, rows, model_width = x_all.shape
     local = rows // seq_count
-    item = jax.ShapeDtypeStruct((ctx_size, 3, tp_size * local, width), BF16)
+    item = jax.ShapeDtypeStruct((item_count, ctx_size, 3, tp_size * local, width), BF16)
     columns = full_one.shape[1]
     block = pl.BlockSpec((1, rows, model_width), lambda t: (t, 0, 0))
     return pl.pallas_call(
@@ -495,15 +662,18 @@
         out_shape=[
             jax.ShapeDtypeStruct(x_all.shape, BF16),
             jax.ShapeDtypeStruct((tp_size, rows, LANES), F32),
-        ]
-        + [item] * item_count,
+            item,
+        ],
         in_specs=[
             block,
             pl.BlockSpec((1, model_width), lambda t: (0, 0)),
             pl.BlockSpec((model_width, columns), lambda t: (0, 0), pipeline_mode=pl.Buffered(1)),
         ],
-        out_specs=[block, pl.BlockSpec((1, rows, LANES), lambda t: (t, 0, 0))]
-        + [pl.BlockSpec((ctx_size, 3, local, width), lambda t: (0, 0, t, 0))] * item_count,
+        out_specs=[
+            block,
+            pl.BlockSpec((1, rows, LANES), lambda t: (t, 0, 0)),
+            pl.BlockSpec((item_count, ctx_size, 3, local, width), lambda t: (0, 0, 0, t, 0)),
+        ],
         compiler_params=pltpu.CompilerParams(vmem_limit_bytes=48 << 20, dimension_semantics=("arbitrary",)),
         cost_estimate=pl.CostEstimate(
             flops=2 * x_all.size * columns, bytes_accessed=4 * x_all.size, transcendentals=0
@@ -512,10 +682,11 @@
     )(x_all, gain, full_one)
 
 
-def out_kernel(layout, count, x_ref, gate_ref, w_ref, gain_ref, *refs):
+def out_kernel(layout, x_ref, gate_ref, w_ref, gain_ref, items, *refs):
     seq_count, groups, width, places = layout
-    items, (hidden_ref, normed_ref, attended_ref, mixed_ref) = refs[:count], refs[count : count + 4]
-    buffers, sems = refs[count + 4 : count + 8], refs[count + 8 :]
+    hidden_ref, normed_ref, attended_ref, mixed_ref = refs[:4]
+    buffers, sems = refs[4:8], refs[8:]
+    count = items.shape[0]
     me, sibling, across, diagonal = tp_places()
     greet((sibling, across))
     tp_size, rows, _ = gate_ref.shape
@@ -525,7 +696,7 @@
         here = pl.ds(pl.multiple_of(t * local, local), local)
         for slot, (s, g) in enumerate(places[: seq_count * groups]):
             there = (t, pl.ds(s * local, local), pl.ds(g * width, width))
-            value = items[slot % count][slot // count, here]
+            value = items[slot % count, slot // count, here]
             attended_ref[there] = value
             mixed_ref[there] = (value.astype(F32) * gate_ref[there]).astype(BF16)
         return 0
@@ -554,7 +725,7 @@
     inner = groups * width
     tp_size = gate.shape[0]
     return pl.pallas_call(
-        functools.partial(out_kernel, layout, len(items)),
+        functools.partial(out_kernel, layout),
         grid=(1,),
         out_shape=[
             jax.ShapeDtypeStruct(x.shape, F32),
@@ -567,8 +738,8 @@
             whole(gate.shape),
             whole((model_width, inner), column),
             whole(gain.shape),
-        ]
-        + [whole(item.shape) for item in items],
+            whole(items.shape),
+        ],
         out_specs=[whole(x.shape), whole(x.shape), whole(gate.shape), whole(gate.shape)],
         scratch_shapes=scatter_buffers(rows, model_width) + SCATTER_SEMS,
         compiler_params=remote_params(ident, 48),
@@ -576,13 +747,13 @@
             flops=2 * gate.size * model_width, bytes_accessed=100 << 20, transcendentals=0
         ),
         name="out_project",
-    )(x, gate, full_two, gain, *items)
+    )(x, gate, full_two, gain, items)
 
 
 def mlp_kernel(normed_ref, grad_ref, gate_w, up_w, down_w, all_ref, inner_ref, pair_ref, table, own_sem, *sems):
     me, sibling, across, diagonal = tp_places()
     greet((sibling, across))
-    table[me] = normed_ref[...]
+    table[0] = normed_ref[...]
     rows, hidden = table.shape[1] // CHUNKS, gate_w.shape[1]
     tile = min(hidden, 512)
 
@@ -600,7 +771,7 @@
             pair_ref[slot, spot, columns] = (back * up * sig * (1.0 + gate * (1.0 - sig))).astype(BF16)
             pair_ref[slot, spot, pl.ds(hidden + start, tile)] = (back * silu).astype(BF16)
 
-    gather_loop(table, sems, compute)
+    gather_loop(table, sems, compute, relative=True)
     copy = pltpu.make_async_copy(table, all_ref, own_sem)
     copy.start()
     copy.wait()
@@ -657,7 +828,7 @@
         out_ref[span(chunk)] = grad
         branch_ref[span(chunk)] = grad.astype(BF16)
 
-    scatter_loop(buffers, sems, partial, finish)
+    scatter_loop(buffers, sems, partial, finish, relative=True)
 
 
 def mlp_back(pair, full_two, hidden_state, grad_out, gain, ident):
@@ -688,11 +859,11 @@
     )(pair, full_two, hidden_state, grad_out, gain)
 
 
-def out_back_kernel(layout, count, branch_ref, w_ref, gate_ref, attended_ref, *refs):
+def out_back_kernel(layout, branch_ref, w_ref, gate_ref, attended_ref, *refs):
     seq_count, groups, width, places = layout
-    all_ref, logit_ref, items = refs[0], refs[1], refs[2 : 2 + count]
-    table, grads, own_sem = refs[2 + count : 5 + count]
-    sems = refs[5 + count :]
+    all_ref, logit_ref, items, table, grads, own_sem = refs[:6]
+    sems = refs[6:]
+    count = items.shape[0]
     me, sibling, across, diagonal = tp_places()
     greet((sibling, across))
     table[me] = branch_ref[...]
@@ -715,7 +886,8 @@
     def deal(t, _):
         here = pl.ds(pl.multiple_of(t * local, local), local)
         for slot, (s, g) in enumerate(places):
-            items[slot % count][slot // count, here] = grads[t, pl.ds(s * local, local), pl.ds(g * width, width)]
+            piece = grads[t, pl.ds(s * local, local), pl.ds(g * width, width)]
+            items[slot % count, slot // count, here] = piece
         return 0
 
     lax.fori_loop(0, tp_size, deal, 0)
@@ -726,20 +898,23 @@
     seq_count, groups, width, places = layout
     rows, model_width = branch.shape
     tp_size, _, inner = gate.shape
-    item = (ctx_size, tp_size * rows // seq_count, width)
+    item = (item_count, ctx_size, tp_size * rows // seq_count, width)
     table = (tp_size, rows, model_width)
     return pl.pallas_call(
-        functools.partial(out_back_kernel, layout, item_count),
+        functools.partial(out_back_kernel, layout),
         grid=(1,),
-        out_shape=[jax.ShapeDtypeStruct(table, BF16), jax.ShapeDtypeStruct(gate.shape, BF16)]
-        + [jax.ShapeDtypeStruct(item, BF16)] * item_count,
+        out_shape=[
+            jax.ShapeDtypeStruct(table, BF16),
+            jax.ShapeDtypeStruct(gate.shape, BF16),
+            jax.ShapeDtypeStruct(item, BF16),
+        ],
         in_specs=[
             whole(branch.shape),
             whole((model_width, inner), column),
             whole(gate.shape),
             whole(attended.shape),
         ],
-        out_specs=[pl.BlockSpec(memory_space=pl.ANY), whole(gate.shape)] + [whole(item)] * item_count,
+        out_specs=[pl.BlockSpec(memory_space=pl.ANY), whole(gate.shape), whole(item)],
         scratch_shapes=[pltpu.VMEM(table, BF16), pltpu.VMEM(gate.shape, BF16), pltpu.SemaphoreType.DMA]
         + GATHER_SEMS,
         compiler_params=remote_params(ident, 48),
@@ -750,32 +925,31 @@
     )(branch, full_two, gate, attended)
 
 
-def assemble_kernel(layout, count, *refs):
+def assemble_kernel(layout, items, out_ref):
     seq_count, groups, width, places = layout
-    items, out_ref = refs[:count], refs[count]
-    local = items[0].shape[2]
+    count, local = items.shape[0], items.shape[3]
     inner = groups * width
     for slot, (s, g) in enumerate(places[: seq_count * groups]):
         for kind in range(3):
             columns = pl.ds(kind * inner + g * width, width)
-            out_ref[0, pl.ds(s * local, local), columns] = items[slot % count][slot // count, kind]
+            out_ref[0, pl.ds(s * local, local), columns] = items[slot % count, slot // count, kind]
 
 
 def assemble(items, layout, tp_size):
     seq_count, groups, width, places = layout
-    ctx_size, kinds, ctx_rows, _ = items[0].shape
+    count, ctx_size, kinds, ctx_rows, _ = items.shape
     local = ctx_rows // tp_size
     shape = (tp_size, seq_count * local, kinds * groups * width)
     return pl.pallas_call(
-        functools.partial(assemble_kernel, layout, len(items)),
+        functools.partial(assemble_kernel, layout),
         grid=(tp_size,),
         out_shape=jax.ShapeDtypeStruct(shape, BF16),
-        in_specs=[pl.BlockSpec((ctx_size, kinds, local, width), lambda t: (0, 0, t, 0))] * len(items),
+        in_specs=[pl.BlockSpec((count, ctx_size, kinds, local, width), lambda t: (0, 0, 0, t, 0))],
         out_specs=pl.BlockSpec((1,) + shape[1:], lambda t: (t, 0, 0)),
         compiler_params=pltpu.CompilerParams(vmem_limit_bytes=32 << 20, dimension_semantics=("arbitrary",)),
         cost_estimate=pl.CostEstimate(flops=0, bytes_accessed=16 << 20, transcendentals=0),
         name="assemble",
-    )(*items)
+    )(items)
 
 
 def input_kernel(qkv_ref, logit_ref, forget_ref, qkv_w, forget_w, gate_w, x_ref, grad_ref, gain_ref, out_ref, part_ref, *refs):
@@ -833,34 +1007,25 @@
     )(grad_qkv, grad_logit, grad_forget, full_one, full_one, full_two, x, grad_hidden, gain)
 
 
-def running_sum(values):
-    length = values.shape[-1]
-    cut = values.reshape(values.shape[:-1] + (length // LANES, LANES))
-    lower = jnp.tril(jnp.ones((LANES, LANES), F32))
-    inside = jnp.einsum("...bk,jk->...bj", cut, lower, precision=lax.Precision.HIGHEST)
-    ahead = jnp.tril(jnp.ones((length // LANES, length // LANES), F32), -1)
-    before = jnp.sum(jnp.sum(cut, axis=-1)[..., None, :] * ahead, axis=-1)
-    return (inside + before[..., None]).reshape(values.shape)
-
-
-def row_norm(values):
-    inverse = lax.rsqrt(jnp.mean(values * values, axis=-1, keepdims=True) + epsilon)
-    return (values * inverse, inverse)
-
-
-def norm_back(grad_normed, unit_rows, inverse, gain_vec):
-    scaled = grad_normed * gain_vec
-    inner_mean = jnp.mean(scaled * unit_rows, axis=-1, keepdims=True)
-    return inverse * (scaled - unit_rows * inner_mean)
-
-
-def spread_rows(row_values):
-    return lax.all_gather(row_values, "tp", axis=0, tiled=True)
+def to_sibling(values):
+    return lax.ppermute(values, "tp", [(i, i + 1 - 2 * (i % 2)) for i in range(4)])
+
+
+def to_across(values):
+    return lax.ppermute(values, "tp", [(i, (i + 2) % 4) for i in range(4)])
+
+
+def relative_rows(rows):
+    far = to_across(rows)
+    return jnp.stack([rows, to_sibling(rows), far, to_sibling(far)])
 
 
 def summed_rows(partial):
-    total = lax.psum_scatter(partial.astype(BF16), "tp", scatter_dimension=0, tiled=True)
-    return total.astype(F32)
+    own, near, far, corner = (partial[n] for n in range(4))
+    corner = to_sibling(corner.astype(BF16)).astype(F32)
+    near = to_sibling(near.astype(BF16)).astype(F32)
+    far = to_across((far + corner).astype(BF16)).astype(F32)
+    return own + near + far
 
 
 def per_device(
@@ -948,8 +1113,8 @@
 
     input_rows = by_sequence(layer_input)
     grad_out = (valid_rows * by_sequence(cotangent).astype(F32)).astype(BF16)
-    input_all, grad_all = gather_two(input_rows, grad_out, 1)
-    normed_one, forget_rows, *items = project(
+    input_all = gather_rows(input_rows, 1)
+    normed_one, forget_rows, items = project(
         input_all, gain_one, full_one, layout, item_count, ctx_size
     )
     normed_flat = normed_one.reshape(all_rows, model_width)
@@ -958,29 +1123,14 @@
     forget_logit = forget_logit.reshape(head_count, tp_size, seq_count, local_rows)
     log_forget = (ctx_valid[None] * jax.nn.log_sigmoid(forget_logit)).astype(BF16)
 
-    def forget_items(rows):
-        cut = rows.reshape(groups, pair, tp_size, seq_count, local_rows)
-        picked = jnp.stack([cut[g, :, :, s] for s, g in places])
-        return picked.reshape(ctx_size, item_count, pair, ctx_rows)
-
-    def exchange(items):
-        return lax.all_to_all(items, "ctx", split_axis=0, concat_axis=0, tiled=True)
-
-    decay_in = exchange(forget_items(log_forget)).transpose(1, 2, 0, 3)
-    decay_sum = running_sum(decay_in.reshape(item_count, pair, seq_len).astype(F32))
-    seq_ids = jnp.arange(seq_count, dtype=jnp.int32)
-    saved, attended_items = [], []
-    for m in range(item_count):
-        qkv = exchange(items[m])
-        slot = ctx_index * item_count + m
-        own_seq, _ = place(slot)
-        own_seq = jnp.where(slot < used, own_seq, seq_count)
-        item_len = jnp.sum(jnp.where(seq_ids == own_seq, lengths, 0)).reshape(1)
-        out, exact, lse = attend(item_len, qkv, decay_sum[m], head_size)
-        saved.append((item_len, qkv, exact, lse))
-        attended_items.append(exchange(out))
+    cut = log_forget.astype(F32).reshape(groups, pair, tp_size, seq_count, local_rows)
+    picked = jnp.stack([cut[g, :, :, s] for s, g in places])
+    picked = picked.reshape(ctx_size, item_count, pair, ctx_rows).transpose(1, 0, 2, 3)
+    picked = jnp.pad(picked, ((0, 0), (0, 0), (0, 8 - pair), (0, 0)))
+    attended_items, qkv, exact, lse, decay = context(items, picked, head_size, 7)
     gate_logit = dot(normed_flat, gate_out_w, NN)
     out_gate = jax.nn.sigmoid(gate_logit).reshape(tp_size, -1, inner_width)
+    grad_all = relative_rows(grad_out)
     hidden_state, normed_two, attended, mixed = out_project(
         input_rows, out_gate, full_two, out_column, gain_two, attended_items, layout, 2
     )
@@ -989,47 +1139,44 @@
     inner_flat = inner_act.reshape(all_rows, hidden)
     grad_pair_flat = grad_pair.reshape(all_rows, 2 * hidden)
     grad_flat = grad_all.reshape(all_rows, model_width)
-    grad_hidden, branch, mlp_gain_part = mlp_back(
-        grad_pair, full_two, hidden_state, grad_out, gain_two, 4
-    )
-    feedforward = summed_rows(dot(inner_flat, down_w, NT))
-    output = (valid_rows * (hidden_state + feedforward)).astype(BF16)
 
     def owned_sum(part):
         total = lax.psum_scatter(part, weights, scatter_dimension=0, tiled=True)
         return total.astype(F32)
 
-    gate_up_sum = owned_sum(dot(normed_two_flat, grad_pair_flat, TN).astype(BF16))
-    branch_all, grad_gate_logit, *grads = out_back(
+    mlp_part = jnp.concatenate(
+        [
+            dot(normed_two_flat, grad_pair_flat, TN).astype(BF16),
+            dot(grad_flat, inner_flat, TN).astype(BF16),
+        ],
+        axis=1,
+    )
+    mlp_part, grad_pair = lax.optimization_barrier((mlp_part, grad_pair))
+    mlp_sum = owned_sum(mlp_part)
+    grad_hidden, branch, mlp_gain_part = mlp_back(
+        grad_pair, full_two, hidden_state, grad_out, gain_two, 4
+    )
+    feedforward = summed_rows(dot(inner_flat, down_w, NT).reshape(tp_size, -1, model_width))
+    output = (valid_rows * (hidden_state + feedforward)).astype(BF16)
+
+    branch_all, grad_gate_logit, grads = out_back(
         branch, full_two, out_column, out_gate, attended, layout, item_count, ctx_size, 5
     )
     branch_flat = branch_all.reshape(all_rows, model_width)
     logit_flat = grad_gate_logit.reshape(all_rows, inner_width)
 
-    grad_items, decay_grads = [], []
-    for m in range(item_count):
-        item_len, qkv, exact, lse = saved[m]
-        dqkv, row_sum, column_sum = attend_grad(
-            item_len, qkv, exchange(grads[m]), exact, lse, decay_sum[m], head_size
-        )
-        grad_items.append(exchange(dqkv))
-        decay_grads.append(row_sum - column_sum)
-    down_out_part = jnp.concatenate(
+    grad_items, forget_items = context_back(grads, qkv, exact, lse, decay, head_size, 8)
+    out_part = jnp.concatenate(
         [
-            dot(grad_flat, inner_flat, TN).astype(BF16),
             dot(branch_flat, mixed.reshape(all_rows, inner_width), TN).astype(BF16),
             dot(normed_flat, logit_flat, TN).astype(BF16),
         ],
         axis=1,
     )
-    down_out_sum = owned_sum(down_out_part)
-
-    decay_grad = jnp.stack(decay_grads)
-    forget_grad = jnp.flip(running_sum(jnp.flip(decay_grad, -1)), -1).astype(BF16)
-    forget_grad = forget_grad.reshape(item_count, pair, ctx_size, ctx_rows).transpose(2, 0, 1, 3)
-    forget_back = exchange(forget_grad).reshape(
-        ctx_size * item_count, pair, tp_size, local_rows
-    )
+    out_sum = owned_sum(out_part)
+
+    forget_back = forget_items[:, :, :pair].astype(BF16).transpose(1, 0, 2, 3)
+    forget_back = forget_back.reshape(ctx_size * item_count, pair, tp_size, local_rows)
     slots = {place(slot): slot for slot in range(used)}
     forget_back = jnp.stack(
         [
@@ -1079,12 +1226,12 @@
         qkv_sum[:, 2 * wide : 3 * wide],
         qkv_sum[:, 3 * wide : 3 * wide + head_count],
         forget_bias_grad,
-        down_out_sum[:, hidden + wide :],
-        down_out_sum[:, hidden : hidden + wide],
+        out_sum[:, wide:],
+        out_sum[:, :wide],
         mlp_gain_grad,
-        gate_up_sum[:, :hidden],
-        gate_up_sum[:, hidden:],
-        down_out_sum[:, :hidden],
+        mlp_sum[:, :hidden],
+        mlp_sum[:, hidden : 2 * hidden],
+        mlp_sum[:, 2 * hidden :],
     )
 
 

time: 1210 us -> 1110 us (0.917)
  Pallas kernels: 463 us -> 761 us
  blocking collectives: 319 us -> 44.9 us
  waiting for transfers between devices: 199 us -> 138 us
  starting transfers between devices: 33.1 us -> 4.74 us
  local copies, waits for them, and re-layouts: 77.6 us -> 52.7 us
    all_to_all x6 -> x0, blocking collectives: 282 us -> none  [exchange(): return lax.all_to_all(items, 'ctx', split_axis=0, concat_axis=0, tiled=True)]
    pallas_call x10 -> x6, Pallas kernels: 284 us -> 564 us  [the longest x1 247 us: context(): pl.pallas_call(functools.partial(context_kernel, heads, head_size), grid=...]
    all_to_all x8 -> x0, waiting for transfers between devices: 74.5 us -> none  [exchange(): return lax.all_to_all(items, 'ctx', split_axis=0, concat_axis=0, tiled=True)]
    ppermute x0 -> x6, waiting for transfers between devices: none -> 38.7 us  [the longest x2 34.7 us: to_across(): return lax.ppermute(values, 'tp', [(i, (i + 2) % 4) for i in range(4)])]
    all_to_all x8 -> x0, starting transfers between devices: 32.4 us -> none  [exchange(): return lax.all_to_all(items, 'ctx', split_axis=0, concat_axis=0, tiled=True)]
    unnamed x114 -> x85, local copies, waits for them, and re-layouts: 50.9 us -> 27.4 us
    reduce_scatter x2, waiting for transfers between devices: 117 us -> 98.6 us  [owned_sum(): total = lax.psum_scatter(part, weights, scatter_dimension=0, tiled=True)]
    pallas_call x1, Pallas kernels: 53.2 us -> 71.2 us  [input_back(): pl.pallas_call(input_kernel, grid=(1,), out_shape=[jax.ShapeDtypeStruct(x...]
  transfers between devices with their start and end apart: 14 -> 11, of which waited for: 7 -> 3; matrix products, arithmetic and copies ran while one was open for 10% -> 6% of each run, Pallas kernels for 22% -> 51%
where the time goes in v2:
time: 1110 us; the launch traced here: 1100 us
  Pallas kernels  761 us (69%)
  waiting for transfers between devices  138 us (12%)
  matrix products  65.4 us (6%)
  local copies, waits for them, and re-layouts  52.7 us (5%)
  blocking collectives  44.9 us (4%)
  other arithmetic  20.3 us (2%)
  between operations  14.8 us (1%)
    pallas_call x1, Pallas kernels, context(): pl.pallas_call(functools.partial(context_kernel, heads, head_size), grid=...  247 us
    pallas_call x1, Pallas kernels, context_back(): pl.pallas_call(functools.partial(context_back_kernel, heads, head_size),...  177 us
    reduce_scatter x2, waiting for transfers between devices, owned_sum(): total = lax.psum_scatter(part, weights, scatter_dimension=0, tiled=True)  98.6 us
    pallas_call x1, Pallas kernels, input_back(): pl.pallas_call(input_kernel, grid=(1,), out_shape=[jax.ShapeDtypeStruct(x...  71.2 us
    dot_general x7, matrix products, dot(): return lax.dot_general(left, right, dims, preferred_element_type=F32)  65.4 us
    pallas_call x1, Pallas kernels, mlp_back(): pl.pallas_call(mlp_back_kernel, grid=(1,), out_shape=[jax.ShapeDtypeStruc...  57.2 us
    pallas_call x1, Pallas kernels, mlp(): pl.pallas_call(mlp_kernel, grid=(1,), out_shape=[jax.ShapeDtypeStruct(gra...  52.8 us
    pallas_call x1, Pallas kernels, gather_rows(): pl.pallas_call(gather_rows_kernel, out_shape=jax.ShapeDtypeStruct((4,) +...  50.7 us
  transfers between devices with their start and end apart: 11, of which 3 were waited for; matrix products, arithmetic and copies ran while one was open for 6% of the time, Pallas kernels for 51%

profile of v2, /device:TPU:0, one launch (start us, length us, event | category | flops | bytes accessed | tf_op | source)
XLA Modules:
  0.0 1101.9 jit_solution(4644258785943846391)
XLA Ops:
  19.9 3.0 collective-permute-start.1
  22.9 34.7 %collective-permute-done.1 = bf16[512,1536]{1,0:T(8,128)(2,1)} collective-permute-done((bf16[512,1536]{1,0:T(8,128)(2,1)}, bf16[512,1536]{1,0:T(8,128)(2,1)}, u32[]{:S(2)}, u32[]{:S(2)}) %collective-permute-start.1) | collective-permute-done | bytes 1572896 | tf_op jit(solution)/shard_map/ppermute | solution.py:1015
  57.6 2.8 copy.136
  60.4 50.7 %gather_rows.1.x_ref = bf16[4,512,1536]{2,1,0:T(8,128)(2,1)} custom-call(bf16[512,1536]{1,0:T(8,128)(2,1)} %bitcast.139), custom_call_target="tpu_custom_call" | custom-call | tf_op jit(solution)/shard_map/gather_rows/pallas_call | solution.py:614
  112.5 5.9 pad_maximum_fusion.1.grad_ref
  119.9 2.1 copy-done.5
  122.1 16.0 %project.1 = (bf16[4,512,1536]{2,1,0:T(8,128)(2,1)}, f32[4,512,128]{2,1,0:T(8,128)S(1)}, bf16[3,4,3,512,128]{4,3,2,1,0:T(8,128)(2,1)}) custom-call(bf16[4,512,1536]{2,1,0:T(8,128)(2,1)} %gather_rows.1.x_ref, f32[1,1536]{1,0:T(1,128)S(1)} %get-tuple-element.164.gain_ref, bf16[1536,1280]{1,0:T(8,128)(2,1)S(1)} %copy-done.5), custom_call_target="tpu_custom_call" | custom-call | flops 8053063680 | bytes 12582912 | tf_op jit(solution)/shard_map/project/pallas_call | solution.py:659
  138.9 247.1 %context.1 = (bf16[3,4,512,128]{3,2,1,0:T(8,128)(2,1)S(1)}, bf16[3,4,3,512,128]{4,3,2,1,0:T(8,128)(2,1)}, f32[3,4,512,128]{3,2,1,0:T(8,128)S(1)}, f32[3,8,2048]{2,1,0:T(8,128)S(1)}, f32[3,8,2048]{2,1,0:T(8,128)S(1)}) custom-call(bf16[3,4,3,512,128]{4,3,2,1,0:T(8,128)(2,1)} %get-tuple-element.42.items_ref, f32[3,4,8,512]{3,2,1,0:T(8,128)S(1)} %pad.8.forget_ref), custom_call_target="tpu_custom_call" | custom-call | flops 12884901888 | bytes 104857600 | tf_op jit(solution)/shard_map/context/pallas_call | solution.py:315
  390.3 8.5 add_divide_fusion
  398.7 45.4 %out_project.1 = (f32[512,1536]{1,0:T(8,128)}, bf16[512,1536]{1,0:T(8,128)(2,1)S(1)}, bf16[4,512,384]{2,1,0:T(8,128)(2,1)S(1)}, bf16[4,512,384]{2,1,0:T(8,128)(2,1)S(1)}) custom-call(bf16[512,1536]{1,0:T(8,128)(2,1)} %bitcast.140, f32[4,512,384]{2,1,0:T(8,128)} %bitcast.142, bf16[1536,3840]{1,0:T(8,128)(2,1)} %all-gather.5.cloned.1.call-done.w_ref.gate_w.up_w.down_w, ...), custom_call_target="tpu_custom_call" | custom-call | flops 2415919104 | bytes 104857600 | tf_op jit(solution)/shard_map/out_project/pallas_call | solution.py:727
  446.5 52.8 %mlp.1 = (bf16[4,512,1536]{2,1,0:T(8,128)(2,1)}, bf16[4,512,1024]{2,1,0:T(8,128)(2,1)}, bf16[4,512,2048]{2,1,0:T(8,128)(2,1)}) custom-call(bf16[512,1536]{1,0:T(8,128)(2,1)} %copy-done.10, bf16[4,512,1536]{2,1,0:T(8,128)(2,1)} %pad_maximum_fusion.1.grad_ref, bf16[1536,3840]{1,0:T(8,128)(2,1)} %all-gather.5.cloned.1.call-done.w_ref.gate_w.up_w.down_w, ...), custom_call_target="tpu_custom_call" | custom-call | flops 19327352832 | bytes 104857600 | tf_op jit(solution)/shard_map/mlp/pallas_call | solution.py:783
  499.3 10.3 bitcast_convert_fusion.1
  509.6 14.3 %bitcast_convert_fusion = bf16[1536,2048]{1,0:T(8,128)(2,1)S(1)} fusion(bf16[4,512,1536]{2,1,0:T(8,128)(2,1)S(1)} %copy-done.30, bf16[4,512,2048]{2,1,0:T(8,128)(2,1)S(1)} %copy-done.29), kind=kOutput, calls=%fused_computation | convolution fusion | flops 12888047616 | bytes 20971520 | tf_op jit(solution)/shard_map/dot_general | solution.py:22
  523.9 4.7 pad_maximum_fusion
  528.6 57.2 %mlp_back.1 = (f32[512,1536]{1,0:T(8,128)}, bf16[512,1536]{1,0:T(8,128)(2,1)}, f32[1,1536]{1,0:T(1,128)}) custom-call(bf16[4,512,2048]{2,1,0:T(8,128)(2,1)} %get-tuple-element.50.pair_ref, bf16[1536,3840]{1,0:T(8,128)(2,1)} %all-gather.5.cloned.1.call-done.w_ref.gate_w.up_w.down_w, f32[512,1536]{1,0:T(8,128)} %get-tuple-element.45.hidden_ref, ...), custom_call_target="tpu_custom_call" | custom-call | flops 12884901888 | bytes 104857600 | tf_op jit(solution)/shard_map/mlp_back/pallas_call | solution.py:837
  587.2 43.1 %out_back.1 = (bf16[4,512,1536]{2,1,0:T(8,128)(2,1)}, bf16[4,512,384]{2,1,0:T(8,128)(2,1)S(1)}, bf16[3,4,512,128]{3,2,1,0:T(8,128)(2,1)S(1)}) custom-call(bf16[512,1536]{1,0:T(8,128)(2,1)S(1)} %copy-done.3, bf16[1536,3840]{1,0:T(8,128)(2,1)} %all-gather.5.cloned.1.call-done.w_ref.gate_w.up_w.down_w, f32[4,512,384]{2,1,0:T(8,128)} %bitcast.143, ...), custom_call_target="tpu_custom_call" | custom-call | flops 2415919104 | bytes 104857600 | tf_op jit(solution)/shard_map/out_back/pallas_call | solution.py:903
  630.3 6.6 fusion.13
  637.0 2.7 fusion.12
  639.8 2.5 copy.179
  642.3 176.7 %context_back.1 = (bf16[3,4,3,512,128]{4,3,2,1,0:T(8,128)(2,1)}, f32[3,4,8,512]{3,2,1,0:T(8,128)}) custom-call(bf16[3,4,512,128]{3,2,1,0:T(8,128)(2,1)} %copy-done.9, bf16[3,4,3,512,128]{4,3,2,1,0:T(8,128)(2,1)} %get-tuple-element.54.qkv_ref, f32[3,4,512,128]{3,2,1,0:T(8,128)} %copy-done.11, f32[3,8,2048]{2,1,0:T(8,128)} %copy-done.12, f32[3,8,2048]{2,1,0:T(8,128)} %copy-done.13), custom_call_target="tpu_custom_call" | custom-call | flops 32212254720 | bytes 104857600 | tf_op jit(solution)/shard_map/context_back/pallas_call | solution.py:394
  819.0 2.3 copy-done.1
  822.6 2.1 copy-done
  826.4 13.4 %convolution_convert_fusion = bf16[1536,1280]{1,0:T(8,128)(2,1)} fusion(bf16[2048,1536]{1,0:T(8,128)(2,1)} %bitcast.166, bf16[2048,128]{1,0:T(8,128)(2,1)S(1)} %copy.164, bf16[2048,1152]{1,0:T(8,128)(2,1)} %bitcast.136), kind=kOutput, calls=%fused_computation.2 | convolution fusion | flops 8065515520 | bytes 15466496 | tf_op jit(solution)/shard_map/dot_general | solution.py:22
  840.4 9.7 fusion.29
  852.1 4.0 collective-permute-done.4
  859.0 71.2 %input_back.1 = (bf16[512,1536]{1,0:T(8,128)(2,1)}, f32[1,1536]{1,0:T(1,128)}) custom-call(bf16[4,512,1152]{2,1,0:T(8,128)(2,1)} %copy-done, bf16[4,512,384]{2,1,0:T(8,128)(2,1)} %copy-done.8, bf16[4,512,128]{2,1,0:T(8,128)(2,1)} %bitcast.149, bf16[1536,1280]{1,0:T(8,128)(2,1)} %all-gather.3.cloned.1.call-done.w_ref.qkv_w.forget_w, ...), custom_call_target="tpu_custom_call" | custom-call | flops 10468982784 | bytes 104857600 | tf_op jit(solution)/shard_map/input_back/pallas_call | solution.py:985
  930.2 3.9 copy.198
  934.4 44.9 %all-reduce.2 = (f32[1536]{0:T(1024)S(1)}, f32[24]{0:T(128)S(1)}, f32[1536]{0:T(1024)S(1)}) all-reduce(f32[1536]{0:T(1024)S(1)} %reduce, f32[24]{0:T(128)S(1)} %dynamic_update_slice.3, f32[1536]{0:T(1024)S(1)} %reduce.1), channel_id=1, replica_groups=mesh['fsdp'=2,'ctx'=4,'tp'=4] {'fsdp','ctx','tp'}, use_global_device_ids=true, to_apply=%region_0.1 | all-reduce | flops 3096 | bytes 24768 | tf_op jit(solution)/shard_map/psum | solution.py:1212
  981.2 3.9 fusion.7
  985.1 2.4 copy.199
  993.9 98.6 %reduce-scatter.8.cloned.1.call-done = bf16[192,3072]{1,0:T(8,128)(2,1)} async-done(((bf16[1536,3072]{1,0:T(8,128)(2,1)}), bf16[192,3072]{1,0:T(8,128)(2,1)}) %reduce-scatter.8.cloned.1.call-update) | async-done | bytes 1179664 | tf_op jit(solution)/shard_map/reduce_scatter | solution.py:1144
  1092.5 2.7 fusion.24
  (154 shorter events, 41.2 us)
Async XLA Ops:
  7.2 6.6 copy-start.21
  7.2 9.7 copy-start.19
  7.2 111.2 %all-gather.3.cloned.1.call-start = ((), (), s32[]{:S(2)}) async-start(), calls=%async_computation.3 | async-start | bytes 4423680 | tf_op jit(solution)/shard_map/all_gather | solution.py:1090
  11.6 378.7 %all-gather.5.cloned.1.call-start = ((), (), s32[]{:S(2)}) async-start(), calls=%async_computation.4 | async-start | bytes 13271040 | tf_op jit(solution)/shard_map/all_gather | solution.py:1091
  16.9 970.6 %reduce-scatter.10.cloned.1.call-start = ((), (), s32[]{:S(2)}) async-start(), calls=%async_computation.7 | async-start | bytes 2654208
  18.4 39.2 %copy-start.28 = (bf16[6]{0:T(256)(128)(2,1)S(1)}, bf16[6]{0:T(256)(128)(2,1)}, u32[]{:S(2)}) copy-start(bf16[6]{0:T(256)(128)(2,1)} %param.22) | copy-start | bytes 40
  18.5 92.7 %copy-start.22 = (f32[512]{0:T(512)}, f32[512]{0:T(512)S(1)}, u32[]{:S(2)}) copy-start(f32[512]{0:T(512)S(1)} %convert_bitcast_fusion.1) | copy-start | bytes 6148
  19.9 37.7 %collective-permute-start.1 = (bf16[512,1536]{1,0:T(8,128)(2,1)}, bf16[512,1536]{1,0:T(8,128)(2,1)}, u32[]{:S(2)}, u32[]{:S(2)}) collective-permute-start(bf16[512,1536]{1,0:T(8,128)(2,1)} %fusion.10.grad_ref), channel_id=1, source_target_pairs={{0,2},{1,3},{2,0},{3,1},{4,6},{5,7},{6,4},{7,5},{8,10},{9,11},{10,... | collective-permute-start | bytes 4718600 | tf_op jit(solution)/shard_map/ppermute | solution.py:1015
  22.9 88.5 %collective-permute-start = (bf16[512,1536]{1,0:T(8,128)(2,1)}, bf16[512,1536]{1,0:T(8,128)(2,1)}, u32[]{:S(2)}, u32[]{:S(2)}) collective-permute-start(bf16[512,1536]{1,0:T(8,128)(2,1)} %fusion.10.grad_ref), channel_id=1, source_target_pairs={{0,1},{1,0},{2,3},{3,2},{4,5},{5,4},{6,7},{7,6},{8,9},{9,8},{10,11... | collective-permute-start | bytes 4718600 | tf_op jit(solution)/shard_map/ppermute | solution.py:1011
  57.6 53.8 %collective-permute-start.2 = (bf16[512,1536]{1,0:T(8,128)(2,1)}, bf16[512,1536]{1,0:T(8,128)(2,1)}, u32[]{:S(2)}, u32[]{:S(2)}) collective-permute-start(bf16[512,1536]{1,0:T(8,128)(2,1)} %collective-permute-done.1), channel_id=1, source_target_pairs={{0,1},{1,0},{2,3},{3,2},{4,5},{5,4},{6,7},{7,6},{8,9},{9,8},{10,11... | collective-permute-start | bytes 4718600 | tf_op jit(solution)/shard_map/ppermute | solution.py:1011
  119.9 18.2 %copy-start.7 = (f32[1,1536]{1,0:T(1,128)}, f32[1,1536]{1,0:T(1,128)S(1)}, u32[]{:S(2)}) copy-start(f32[1,1536]{1,0:T(1,128)S(1)} %get-tuple-element.164.gain_ref) | copy-start | bytes 18436
  119.9 278.9 %copy-start.6 = (f32[1,1536]{1,0:T(1,128)}, f32[1,1536]{1,0:T(1,128)S(1)}, u32[]{:S(2)}) copy-start(f32[1,1536]{1,0:T(1,128)S(1)} %get-tuple-element.163.gain_ref) | copy-start | bytes 18436
  119.9 2.2 copy-start.5
  446.5 52.8 %copy-start.15 = (bf16[1,512,1536]{2,1,0:T(8,128)(2,1)S(1)}, bf16[1,512,1536]{2,1,0:T(8,128)(2,1)}, u32[]{:S(2)}) copy-start(bf16[1,512,1536]{2,1,0:T(8,128)(2,1)} %copy-done.14) | copy-start | bytes 4718596
  499.3 10.4 copy-start.29
  499.3 10.4 copy-start.30
  630.3 6.6 copy-start.8
  630.3 6.6 copy-start.9
  630.3 6.6 copy-start.27
  642.3 348.1 %reduce-scatter.6.cloned.1.call-start = ((), (), s32[]{:S(2)}) async-start(), calls=%async_computation.5 | async-start | bytes 4423680 | tf_op jit(solution)/shard_map/reduce_scatter | solution.py:1144
  819.0 2.3 copy-start.1
  822.6 2.1 copy-start
  826.4 13.4 %copy-start.20 = (bf16[2048,128]{1,0:T(8,128)(2,1)}, bf16[2048,128]{1,0:T(8,128)(2,1)S(1)}, u32[]{:S(2)}) copy-start(bf16[2048,128]{1,0:T(8,128)(2,1)S(1)} %copy.164) | copy-start | bytes 1572868
  839.8 252.7 %reduce-scatter.8.cloned.1.call-start = ((), (), s32[]{:S(2)}) async-start(), calls=%async_computation.6 | async-start | bytes 10616832 | tf_op jit(solution)/shard_map/reduce_scatter | solution.py:1144
  850.1 6.1 copy-start.16
  851.6 4.5 collective-permute-start.4
  851.7 129.4 %collective-permute-start.3 = (bf16[512,1536]{1,0:T(8,128)(2,1)}, bf16[512,1536]{1,0:T(8,128)(2,1)}, u32[]{:S(2)}, u32[]{:S(2)}) collective-permute-start(bf16[512,1536]{1,0:T(8,128)(2,1)} %get-tuple-element.129), channel_id=1, source_target_pairs={{0,1},{1,0},{2,3},{3,2},{4,5},{5,4},{6,7},{7,6},{8,9},{9,8},{10,11... | collective-permute-start | bytes 4718600 | tf_op jit(solution)/shard_map/ppermute | solution.py:1011
  857.9 123.3 %collective-permute-start.5 = (bf16[512,1536]{1,0:T(8,128)(2,1)}, bf16[512,1536]{1,0:T(8,128)(2,1)}, u32[]{:S(2)}, u32[]{:S(2)}) collective-permute-start(bf16[512,1536]{1,0:T(8,128)(2,1)} %fusion.3), channel_id=1, source_target_pairs={{0,2},{1,3},{2,0},{3,1},{4,6},{5,7},{6,4},{7,5},{8,10},{9,11},{10,... | collective-permute-start | bytes 4718600 | tf_op jit(solution)/shard_map/ppermute | solution.py:1015
  859.0 75.1 %copy-start.24 = (f32[1,1536]{1,0:T(1,128)S(1)}, f32[1,1536]{1,0:T(1,128)}, u32[]{:S(2)}) copy-start(f32[1,1536]{1,0:T(1,128)} %get-tuple-element.66) | copy-start | bytes 18436
  930.1 4.0 copy-start.25
  930.1 51.0 %copy-start.17 = (f32[512,1536]{1,0:T(8,128)S(1)}, f32[512,1536]{1,0:T(8,128)}, u32[]{:S(2)}) copy-start(f32[512,1536]{1,0:T(8,128)} %get-tuple-element.45.hidden_ref) | copy-start | bytes 9437188
  930.2 51.0 %copy-start.23 = (f32[512]{0:T(512)S(1)}, f32[512]{0:T(512)}, u32[]{:S(2)}) copy-start(f32[512]{0:T(512)} %copy-done.22) | copy-start | bytes 6148
  (10 other events, 11.3 us)
Sparse Core Ops, SparseCore 0:
  11.8 72.7 all-gather.2
  86.7 275.2 all-gather.4
  642.4 124.8 reduce-scatter.9
  839.9 84.6 reduce-scatter.5
  928.5 163.9 reduce-scatter.7

commit v3 on v2

--- a/solution.py
+++ b/solution.py
@@ -526,7 +526,7 @@
 GATHER_SEMS = [pltpu.SemaphoreType.DMA] * 2 + [pltpu.SemaphoreType.DMA((CHUNKS,))] * 4
 
 
-def scatter_loop(buffers, sems, partial, finish, relative=False):
+def scatter_loop(buffers, sems, partial, finish, relative=False, between=None):
     near_out, near_in, far_out, far_in = buffers
     near_send, near_recv, far_send, far_recv = sems
     me, sibling, across, diagonal = tp_places()
@@ -582,7 +582,13 @@
 
         return 0
 
-    lax.fori_loop(0, 4 * CHUNKS, body, 0)
+    if between is None:
+        lax.fori_loop(0, 4 * CHUNKS, body, 0)
+    else:
+        lax.fori_loop(0, 3 * CHUNKS, body, 0)
+        for chunk in range(CHUNKS):
+            between(chunk)
+            lax.fori_loop(3 * CHUNKS + chunk, 3 * CHUNKS + chunk + 1, body, 0)
     for chunk in range(CHUNKS):
         near(0, chunk).wait_send()
         near(1, chunk).wait_send()
@@ -601,25 +607,182 @@
     ]
 
 
-def gather_rows_kernel(rows_ref, all_ref, own_sem, *sems):
+def group_peers():
+    f_size, c_size = lax.axis_size("fsdp"), lax.axis_size("ctx")
+    f, c = lax.axis_index("fsdp"), lax.axis_index("ctx")
+    return [
+        {"fsdp": lax.rem(f + i, f_size), "ctx": lax.rem(c + j, c_size)}
+        for i in range(f_size)
+        for j in range(c_size)
+        if i or j
+    ]
+
+
+def greet_all(peers):
+    barrier = pltpu.get_barrier_semaphore()
+    for peer in peers:
+        pl.semaphore_signal(barrier, inc=1, device_id=peer, device_id_type=MESH)
+    pl.semaphore_wait(barrier, len(peers))
+
+
+def moving(source, target, send_sem, recv_sem, peer):
+    return pltpu.make_async_remote_copy(
+        src_ref=source,
+        dst_ref=target,
+        send_sem=send_sem,
+        recv_sem=recv_sem,
+        device_id=peer,
+        device_id_type=MESH,
+    )
+
+
+class WeightGather:
+    def __init__(self, shard, full, sems):
+        self.shard, self.full = shard, full
+        self.f_size, self.c_size = lax.axis_size("fsdp"), lax.axis_size("ctx")
+        self.f, self.c = lax.axis_index("fsdp"), lax.axis_index("ctx")
+        self.sems = sems
+
+    def spot(self, c, f=None):
+        rows = self.shard.shape[0]
+        block = (self.f if f is None else f) * self.c_size + c
+        return self.full.at[pl.ds(pl.multiple_of(block * rows, rows), rows)]
+
+    def along(self, c, hop, side, source=None):
+        source = self.spot(c) if source is None else source
+        peer = {"ctx": self.c + (1 if side else -1)}
+        return moving(
+            source, self.spot(c), self.sems[0].at[side, hop], self.sems[1].at[side, hop], peer
+        )
+
+    def over(self, c, step, source=None):
+        source = self.spot(c) if source is None else source
+        peer = {"fsdp": lax.rem(self.f + step, self.f_size)}
+        return moving(
+            source, self.spot(c), self.sems[2].at[step, c], self.sems[3].at[step, c], peer
+        )
+
+    def over_arrival(self, c, step):
+        spot = self.spot(c, lax.rem(self.f + self.f_size - step, self.f_size))
+        peer = {"fsdp": lax.rem(self.f + step, self.f_size)}
+        return moving(spot, spot, self.sems[2].at[step, c], self.sems[3].at[step, c], peer)
+
+    def can(self, side):
+        return self.c + 1 < self.c_size if side else self.c > 0
+
+    def holds(self, hop, side):
+        return self.c - hop >= 0 if side else self.c + hop < self.c_size
+
+    def begin(self):
+        pltpu.make_async_copy(self.shard, self.spot(self.c), self.sems[4]).start()
+        for side in (1, 0):
+
+            @pl.when(self.can(side))
+            def _(side=side):
+                self.along(self.c, 1, side, self.shard).start()
+
+        for step in range(1, self.f_size):
+            self.over(self.c, step, self.shard).start()
+
+    def advance(self, hop):
+        for side in (1, 0):
+
+            @pl.when(self.holds(hop, side))
+            def _(side=side):
+                c = self.c - hop if side else self.c + hop
+                self.along(c, hop, side).wait_recv()
+
+                @pl.when(self.can(side))
+                def _():
+                    self.along(c, hop + 1, side).start()
+
+                for step in range(1, self.f_size):
+                    self.over(c, step).start()
+
+    def end(self):
+        pltpu.make_async_copy(self.shard, self.spot(self.c), self.sems[4]).wait()
+        for step in range(1, self.f_size):
+            for c in range(self.c_size):
+                self.over_arrival(c, step).wait_recv()
+                self.over(c, step).wait_send()
+        for side in (1, 0):
+
+            @pl.when(self.can(side))
+            def _(side=side):
+                self.along(self.c, 1, side, self.shard).wait_send()
+
+            for hop in range(1, self.c_size):
+
+                @pl.when(self.holds(hop, side) & self.can(side))
+                def _(side=side, hop=hop):
+                    c = self.c - hop if side else self.c + hop
+                    self.along(c, hop + 1, side).wait_send()
+
+
+def weight_sems(f_size, c_size):
+    dma = pltpu.SemaphoreType.DMA
+    return [dma((2, c_size + 1))] * 2 + [dma((f_size, c_size))] * 2 + [dma]
+
+
+def startup_kernel(rows_ref, shard_ref, all_ref, full_ref, own_sem, *sems):
     me, sibling, across, diagonal = tp_places()
-    greet((sibling, across))
+    greet_all([{"tp": sibling}, {"tp": across}] + group_peers())
+    near_send, near_recv, far_send, far_recv, pass_send, pass_recv = sems[:6]
+    gather = WeightGather(shard_ref, full_ref, sems[6:])
+    size = rows_ref.shape[0] // CHUNKS
     own = pltpu.make_async_copy(rows_ref, all_ref.at[me], own_sem)
     own.start()
-    gather_loop(all_ref, sems, lambda slot, chunk: None, rows_ref)
+
+    def span(chunk):
+        return pl.ds(chunk * size, size)
+
+    def far(chunk):
+        return sending(
+            rows_ref.at[span(chunk)],
+            all_ref.at[me, span(chunk)],
+            far_send.at[chunk],
+            far_recv.at[chunk],
+            across,
+        )
+
+    def passing(chunk):
+        spot = all_ref.at[across, span(chunk)]
+        return sending(spot, spot, pass_send.at[chunk], pass_recv.at[chunk], sibling)
+
+    for chunk in range(CHUNKS):
+        far(chunk).start()
+    gather.begin()
+    near = sending(rows_ref, all_ref.at[me], near_send, near_recv, sibling)
+    near.start()
+    for turn in range(max(CHUNKS, gather.c_size - 1)):
+        if turn < CHUNKS:
+            far(turn).wait_recv()
+            passing(turn).start()
+        if turn + 1 < gather.c_size:
+            gather.advance(turn + 1)
+    near.wait()
+    for chunk in range(CHUNKS):
+        far(chunk).wait_send()
+        passing(chunk).wait()
     own.wait()
-
-
-def gather_rows(rows, ident):
+    gather.end()
+
+
+def startup(rows, shard, f_size, c_size, ident):
+    place = pl.BlockSpec(memory_space=pl.ANY)
+    full = (shard.shape[0] * f_size * c_size, shard.shape[1])
     return pl.pallas_call(
-        gather_rows_kernel,
-        out_shape=jax.ShapeDtypeStruct((4,) + rows.shape, BF16),
-        in_specs=[pl.BlockSpec(memory_space=pl.ANY)],
-        out_specs=pl.BlockSpec(memory_space=pl.ANY),
-        scratch_shapes=[pltpu.SemaphoreType.DMA] + GATHER_SEMS,
+        startup_kernel,
+        out_shape=[
+            jax.ShapeDtypeStruct((4,) + rows.shape, BF16),
+            jax.ShapeDtypeStruct(full, BF16),
+        ],
+        in_specs=[place, place],
+        out_specs=[place, place],
+        scratch_shapes=[pltpu.SemaphoreType.DMA] + GATHER_SEMS + weight_sems(f_size, c_size),
         compiler_params=pltpu.CompilerParams(collective_id=ident, has_side_effects=True),
-        name="gather_rows",
-    )(rows)
+        name="startup",
+    )(rows, shard)
 
 
 def whole(shape, column=None):
@@ -952,11 +1115,115 @@
     )(items)
 
 
-def input_kernel(qkv_ref, logit_ref, forget_ref, qkv_w, forget_w, gate_w, x_ref, grad_ref, gain_ref, out_ref, part_ref, *refs):
-    buffers, sems = refs[:4], refs[4:]
+class WeightSum:
+    def __init__(self, part, out, buffers, sems):
+        self.part, self.out = part, out
+        self.over_in, self.total, self.along_out, self.along_in = buffers
+        self.over_send, self.over_recv, self.along_send, self.along_recv = sems
+        self.f_size, self.c_size = lax.axis_size("fsdp"), lax.axis_size("ctx")
+        self.f, self.c = lax.axis_index("fsdp"), lax.axis_index("ctx")
+        self.rows = out.shape[0]
+        ends = [(self.c_size - 1 - i // 2) if i % 2 == 0 else i // 2 for i in range(self.c_size)]
+        self.order = ends
+
+    def block(self, f, c):
+        index = f * self.c_size + c
+        return pl.ds(pl.multiple_of(index * self.rows, self.rows), self.rows)
+
+    def over(self, c, step):
+        f = lax.rem(self.f + step, self.f_size)
+        return moving(
+            self.part.at[self.block(f, c)],
+            self.over_in.at[step, c],
+            self.over_send.at[step, c],
+            self.over_recv.at[step, c],
+            {"fsdp": f},
+        )
+
+    def along(self, c, side):
+        peer = {"ctx": self.c + (1 if side else -1)}
+        return moving(
+            self.along_out.at[side, c],
+            self.along_in.at[side, c],
+            self.along_send.at[side, c],
+            self.along_recv.at[side, c],
+            peer,
+        )
+
+    def begin(self):
+        for c in self.order:
+            for step in range(1, self.f_size):
+                self.over(c, step).start()
+
+    def receive(self, c):
+        value = self.part[self.block(self.f, c)].astype(F32)
+        for step in range(1, self.f_size):
+            self.over(c, step).wait_recv()
+            value = value + self.over_in[step, c].astype(F32)
+        self.total[c] = value
+        for side, end in ((1, 0), (0, self.c_size - 1)):
+
+            @pl.when((self.c == end) & (self.c != c))
+            def _(side=side):
+                self.along_out[side, c] = value.astype(BF16)
+                self.along(c, side).start()
+
+    def advance(self, c):
+        for side in (1, 0):
+            comes = (self.c > 0) & (self.c <= c) if side else (self.c >= c) & (self.c < self.c_size - 1)
+
+            @pl.when(comes)
+            def _(side=side):
+                self.along(c, side).wait_recv()
+                value = self.total[c] + self.along_in[side, c].astype(F32)
+
+                @pl.when(self.c == c)
+                def _():
+                    self.total[c] = value
+
+                @pl.when(self.c != c)
+                def _():
+                    self.along_out[side, c] = value.astype(BF16)
+                    self.along(c, side).start()
+
+    def end(self):
+        self.out[...] = self.total[self.c]
+        for c in range(self.c_size):
+            for step in range(1, self.f_size):
+                self.over(c, step).wait_send()
+            for side in (1, 0):
+
+                @pl.when(self.c < c if side else self.c > c)
+                def _(side=side):
+                    self.along(c, side).wait_send()
+
+
+def last_kernel(
+    qkv_ref,
+    logit_ref,
+    forget_ref,
+    qkv_w,
+    forget_w,
+    gate_w,
+    x_ref,
+    grad_ref,
+    gain_ref,
+    part_ref,
+    extra_ref,
+    out_ref,
+    sum_ref,
+    vector_ref,
+    *refs,
+):
+    buffers, weight_buffers = refs[:4], refs[4:8]
+    mine, near_in, group_in = refs[8:11]
+    sems, weight_sum_sems, vector_sems = refs[11:15], refs[15:19], refs[19:]
     me, sibling, across, diagonal = tp_places()
-    greet((sibling, across))
-    part_ref[...] = jnp.zeros_like(part_ref)
+    others = group_peers()
+    greet_all([{"tp": sibling}, {"tp": across}, {"tp": diagonal}] + others)
+    weights = WeightSum(part_ref, sum_ref, weight_buffers, weight_sum_sems)
+    weights.begin()
+    mine[...] = extra_ref[...]
     size = x_ref.shape[0] // CHUNKS
 
     def span(chunk):
@@ -971,21 +1238,57 @@
         x = x_ref[span(chunk)].astype(F32)
         inverse = lax.rsqrt(jnp.mean(x * x, axis=1, keepdims=True) + epsilon)
         unit = x * inverse
-        part_ref[...] += jnp.sum(total * unit, axis=0, keepdims=True)
+        mine[0:1] += jnp.sum(total * unit, axis=0, keepdims=True)
         scaled = total * gain_ref[...]
         middle = jnp.mean(scaled * unit, axis=1, keepdims=True)
         out_ref[span(chunk)] = (grad_ref[span(chunk)] + inverse * (scaled - unit * middle)).astype(BF16)
 
-    scatter_loop(buffers, sems, partial, finish)
-
-
-def input_back(grad_qkv, grad_logit, grad_forget, full_one, full_two, column, x, grad_hidden, gain, ident):
+    order = weights.order
+    tasks = []
+    for turn, c in enumerate(order):
+        tasks.append((weights.receive, c))
+        if turn:
+            tasks.append((weights.advance, order[turn - 1]))
+    tasks.append((weights.advance, order[-1]))
+    share = -(-len(tasks) // CHUNKS)
+
+    def between(chunk):
+        for task, c in tasks[chunk * share : (chunk + 1) * share]:
+            task(c)
+
+    scatter_loop(buffers, sems, partial, finish, between=between)
+    near_send, near_recv, group_send, group_recv = vector_sems
+    copies = []
+    for n, peer in enumerate((sibling, across, diagonal)):
+        copies.append(sending(mine, near_in.at[n], near_send.at[n], near_recv.at[n], peer))
+        copies[-1].start()
+    for copy in copies:
+        copy.wait()
+    vector_ref[...] = mine[...] + near_in[0] + near_in[1] + near_in[2]
+    mine[...] = vector_ref[...]
+    copies = []
+    for n, peer in enumerate(others):
+        copies.append(moving(mine, group_in.at[n], group_send.at[n], group_recv.at[n], peer))
+        copies[-1].start()
+    for n, copy in enumerate(copies):
+        copy.wait()
+        vector_ref[...] += group_in[n]
+    weights.end()
+
+
+def last(grad_qkv, grad_logit, grad_forget, full_one, full_two, column, x, grad_hidden, gain, part, extra, f_size, c_size, ident):
     rows, model_width = x.shape
     wide, inner = grad_qkv.shape[2], grad_logit.shape[2]
+    shard, columns = part.shape[0] // (f_size * c_size), part.shape[1]
+    dma = pltpu.SemaphoreType.DMA
     return pl.pallas_call(
-        input_kernel,
+        last_kernel,
         grid=(1,),
-        out_shape=[jax.ShapeDtypeStruct(x.shape, BF16), jax.ShapeDtypeStruct(gain.shape, F32)],
+        out_shape=[
+            jax.ShapeDtypeStruct(x.shape, BF16),
+            jax.ShapeDtypeStruct((shard, columns), F32),
+            jax.ShapeDtypeStruct(extra.shape, F32),
+        ],
         in_specs=[
             whole(grad_qkv.shape),
             whole(grad_logit.shape),
@@ -996,15 +1299,31 @@
             whole(x.shape),
             whole(x.shape),
             whole(gain.shape),
-        ],
-        out_specs=[whole(x.shape), whole(gain.shape)],
-        scratch_shapes=scatter_buffers(rows, model_width) + SCATTER_SEMS,
-        compiler_params=remote_params(ident, 56),
+            whole(part.shape),
+            whole(extra.shape),
+        ],
+        out_specs=[whole(x.shape), whole((shard, columns)), whole(extra.shape)],
+        scratch_shapes=scatter_buffers(rows, model_width)
+        + [
+            pltpu.VMEM((f_size, c_size, shard, columns), BF16),
+            pltpu.VMEM((c_size, shard, columns), F32),
+            pltpu.VMEM((2, c_size, shard, columns), BF16),
+            pltpu.VMEM((2, c_size, shard, columns), BF16),
+            pltpu.VMEM(extra.shape, F32),
+            pltpu.VMEM((3,) + extra.shape, F32),
+            pltpu.VMEM((f_size * c_size - 1,) + extra.shape, F32),
+        ]
+        + SCATTER_SEMS
+        + [dma((f_size, c_size))] * 2
+        + [dma((2, c_size))] * 2
+        + [dma((3,))] * 2
+        + [dma((f_size * c_size - 1,))] * 2,
+        compiler_params=remote_params(ident, 60),
         cost_estimate=pl.CostEstimate(
             flops=8 * rows * model_width * (wide + inner + LANES), bytes_accessed=100 << 20, transcendentals=0
         ),
-        name="input_back",
-    )(grad_qkv, grad_logit, grad_forget, full_one, full_one, full_two, x, grad_hidden, gain)
+        name="last",
+    )(grad_qkv, grad_logit, grad_forget, full_one, full_one, full_two, x, grad_hidden, gain, part, extra)
 
 
 def to_sibling(values):
@@ -1087,9 +1406,10 @@
         axis=1,
     )
     packed_two = jnp.concatenate([w_gate, w_up, w_down, w_out, w_gate_out], axis=1)
-    full_one = lax.all_gather(packed_one, weights, axis=0, tiled=True)
     full_two = lax.all_gather(packed_two, weights, axis=0, tiled=True)
     edge = 3 * inner_width
+    input_rows = layer_input.transpose(1, 0, 2).reshape(seq_count * local_rows, model_width)
+    input_all, full_one = startup(input_rows, packed_one, lax.axis_size("fsdp"), ctx_size, 1)
     gains = full_one[:, edge + head_count : edge + head_count + 2].astype(F32).T
     gain_one, gain_two = gains[0:1], gains[1:2]
     down_w = full_two[:, 2 * hidden : 3 * hidden]
@@ -1111,9 +1431,7 @@
     ctx_pos = ctx_pos.reshape(tp_size, 1, local_rows)
     ctx_valid = (ctx_pos < lengths[None, :, None]).astype(F32)
 
-    input_rows = by_sequence(layer_input)
     grad_out = (valid_rows * by_sequence(cotangent).astype(F32)).astype(BF16)
-    input_all = gather_rows(input_rows, 1)
     normed_one, forget_rows, items = project(
         input_all, gain_one, full_one, layout, item_count, ctx_size
     )
@@ -1190,8 +1508,13 @@
     grad_forget_rows = jnp.pad(grad_forget_logit, ((0, LANES - head_count), (0, 0))).T
     grad_qkv = assemble(grad_items, layout, tp_size)
     grad_qkvf = jnp.concatenate([grad_qkv.reshape(all_rows, edge), grad_forget_rows], axis=1)
-    qkv_sum = owned_sum(dot(normed_flat, grad_qkvf, TN).astype(BF16))
-    input_grad, attn_gain_part = input_back(
+    bias_full = lax.dynamic_update_slice(
+        jnp.zeros((1, model_width), F32), bias_part[None], (0, tp_index * head_count)
+    )
+    extra = jnp.concatenate(
+        [jnp.zeros_like(bias_full), mlp_gain_part, bias_full, jnp.zeros((5, model_width), F32)]
+    )
+    input_grad, qkv_sum, vectors = last(
         grad_qkv,
         grad_gate_logit,
         grad_forget_rows.reshape(tp_size, -1, LANES),
@@ -1201,17 +1524,13 @@
         input_rows,
         grad_hidden,
         gain_one,
+        dot(normed_flat, grad_qkvf, TN).astype(BF16),
+        extra,
+        lax.axis_size("fsdp"),
+        ctx_size,
         6,
     )
-    attn_gain_part = attn_gain_part[0]
-    mlp_gain_part = mlp_gain_part[0]
-
-    bias_full = lax.dynamic_update_slice(
-        jnp.zeros((head_count * tp_size,), F32), bias_part, (tp_index * head_count,)
-    )
-    gain_one_sum, gain_two_sum, bias_sum = lax.psum(
-        (attn_gain_part, mlp_gain_part, bias_full), ("fsdp", "ctx", "tp")
-    )
+    gain_one_sum, gain_two_sum, bias_sum = vectors[0], vectors[1], vectors[2]
     shard_rows = model_width // shard_count
     attn_gain_grad = lax.dynamic_slice_in_dim(gain_one_sum, shard_index * shard_rows, shard_rows, 0)
     mlp_gain_grad = lax.dynamic_slice_in_dim(gain_two_sum, shard_index * shard_rows, shard_rows, 0)

time: 1110 us -> 1060 us (0.955)
  waiting for transfers between devices: 138 us -> 0.73 us
  Pallas kernels: 761 us -> 890 us
  blocking collectives: 44.9 us -> 0 us
    pallas_call x2, Pallas kernels: 122 us -> 245 us  [the longest x1 124 us: last(): pl.pallas_call(last_kernel, grid=(1,), out_shape=[jax.ShapeDtypeStruct(x....]
    reduce_scatter x2 -> x1, waiting for transfers between devices: 98.6 us -> 0.01 us  [owned_sum(): total = lax.psum_scatter(part, weights, scatter_dimension=0, tiled=True)]
    pallas_call x1, Pallas kernels: 177 us -> 252 us  [context_back(): pl.pallas_call(functools.partial(context_back_kernel, heads, head_size),...]
    pallas_call x1, Pallas kernels: 247 us -> 178 us  [context(): pl.pallas_call(functools.partial(context_kernel, heads, head_size), grid=...]
    psum x1 -> x0, blocking collectives: 44.9 us -> none  [per_device(): lax.psum((attn_gain_part, mlp_gain_part, bias_full), ('fsdp', 'ctx', 'tp'))]
    ppermute x2, waiting for transfers between devices: 34.7 us -> 0.01 us  [to_across(): return lax.ppermute(values, 'tp', [(i, (i + 2) % 4) for i in range(4)])]
    unnamed x85 -> x104, local copies, waits for them, and re-layouts: 27.4 us -> 27.4 us
  transfers between devices with their start and end apart: 11 -> 9, of which waited for: 3 -> 0; matrix products, arithmetic and copies ran while one was open for 6% -> 7% of each run, Pallas kernels for 51% -> 65%
where the time goes in v3:
time: 1060 us
  Pallas kernels  890 us (84%)
  matrix products  67 us (6%)
  local copies, waits for them, and re-layouts  57.8 us (5%)
  other arithmetic  23.7 us (2%)
  between operations  15 us (1%)
    pallas_call x1, Pallas kernels, context_back(): pl.pallas_call(functools.partial(context_back_kernel, heads, head_size),...  252 us
    pallas_call x1, Pallas kernels, context(): pl.pallas_call(functools.partial(context_kernel, heads, head_size), grid=...  178 us
    pallas_call x1, Pallas kernels, last(): pl.pallas_call(last_kernel, grid=(1,), out_shape=[jax.ShapeDtypeStruct(x....  124 us
    pallas_call x1, Pallas kernels, startup(): pl.pallas_call(startup_kernel, out_shape=[jax.ShapeDtypeStruct((4,) + row...  120 us
    dot_general x7, matrix products, dot(): return lax.dot_general(left, right, dims, preferred_element_type=F32)  67 us
    pallas_call x1, Pallas kernels, mlp_back(): pl.pallas_call(mlp_back_kernel, grid=(1,), out_shape=[jax.ShapeDtypeStruc...  57.2 us
    pallas_call x1, Pallas kernels, mlp(): pl.pallas_call(mlp_kernel, grid=(1,), out_shape=[jax.ShapeDtypeStruct(gra...  52.8 us
    pallas_call x1, Pallas kernels, out_project(): pl.pallas_call(functools.partial(out_kernel, layout), grid=(1,), out_shap...  45.3 us
  transfers between devices with their start and end apart: 9, of which 0 were waited for; matrix products, arithmetic and copies ran while one was open for 7% of the time, Pallas kernels for 65%

profile of v3, /device:TPU:0, one launch (start us, length us, event | category | flops | bytes accessed | tf_op | source)
XLA Modules:
  0.0 1058.8 jit_solution(14827838922081389734)
XLA Ops:
  16.6 3.0 collective-permute-start.1
  21.4 2.0 concatenate.18.shard_ref
  23.4 120.4 %startup.1 = (bf16[4,512,1536]{2,1,0:T(8,128)(2,1)}, bf16[1536,1280]{1,0:T(8,128)(2,1)}) custom-call(bf16[512,1536]{1,0:T(8,128)(2,1)} %bitcast.145, bf16[192,1280]{1,0:T(8,128)(2,1)} %concatenate.18.shard_ref), custom_call_target="tpu_custom_call" | custom-call | tf_op jit(solution)/shard_map/startup/pallas_call | solution.py:774
  143.8 6.3 copy.100
  150.9 2.2 copy-done.2
  153.1 16.0 %project.1 = (bf16[4,512,1536]{2,1,0:T(8,128)(2,1)}, f32[4,512,128]{2,1,0:T(8,128)S(1)}, bf16[3,4,3,512,128]{4,3,2,1,0:T(8,128)(2,1)}) custom-call(bf16[4,512,1536]{2,1,0:T(8,128)(2,1)} %get-tuple-element.44.x_ref, f32[1,1536]{1,0:T(1,128)S(1)} %get-tuple-element.156.gain_ref, bf16[1536,1280]{1,0:T(8,128)(2,1)S(1)} %copy-done.2), custom_call_target="tpu_custom_call" | custom-call | flops 8053063680 | bytes 12582912 | tf_op jit(solution)/shard_map/project/pallas_call | solution.py:822
  171.0 2.1 fusion.11
  173.1 177.7 %context.1 = (bf16[3,4,512,128]{3,2,1,0:T(8,128)(2,1)S(1)}, bf16[3,4,3,512,128]{4,3,2,1,0:T(8,128)(2,1)}, f32[3,4,512,128]{3,2,1,0:T(8,128)S(1)}, f32[3,8,2048]{2,1,0:T(8,128)S(1)}, f32[3,8,2048]{2,1,0:T(8,128)S(1)}) custom-call(bf16[3,4,3,512,128]{4,3,2,1,0:T(8,128)(2,1)} %get-tuple-element.47.items_ref, f32[3,4,8,512]{3,2,1,0:T(8,128)S(1)} %pad.8.forget_ref), custom_call_target="tpu_custom_call" | custom-call | flops 12884901888 | bytes 104857600 | tf_op jit(solution)/shard_map/context/pallas_call | solution.py:315
  355.0 5.6 pad_maximum_fusion.1.grad_ref
  360.6 8.5 add_divide_fusion
  369.1 45.3 %out_project.1 = (f32[512,1536]{1,0:T(8,128)}, bf16[512,1536]{1,0:T(8,128)(2,1)S(1)}, bf16[4,512,384]{2,1,0:T(8,128)(2,1)S(1)}, bf16[4,512,384]{2,1,0:T(8,128)(2,1)S(1)}) custom-call(bf16[512,1536]{1,0:T(8,128)(2,1)} %bitcast.146, f32[4,512,384]{2,1,0:T(8,128)} %bitcast.148, bf16[1536,3840]{1,0:T(8,128)(2,1)} %all-gather.2.cloned.1.call-done.w_ref.gate_w.up_w.down_w, ...), custom_call_target="tpu_custom_call" | custom-call | flops 2415919104 | bytes 104857600 | tf_op jit(solution)/shard_map/out_project/pallas_call | solution.py:890
  416.8 52.8 %mlp.1 = (bf16[4,512,1536]{2,1,0:T(8,128)(2,1)}, bf16[4,512,1024]{2,1,0:T(8,128)(2,1)}, bf16[4,512,2048]{2,1,0:T(8,128)(2,1)}) custom-call(bf16[512,1536]{1,0:T(8,128)(2,1)} %copy-done.10, bf16[4,512,1536]{2,1,0:T(8,128)(2,1)} %pad_maximum_fusion.1.grad_ref, bf16[1536,3840]{1,0:T(8,128)(2,1)} %all-gather.2.cloned.1.call-done.w_ref.gate_w.up_w.down_w, ...), custom_call_target="tpu_custom_call" | custom-call | flops 19327352832 | bytes 104857600 | tf_op jit(solution)/shard_map/mlp/pallas_call | solution.py:946
  469.6 9.9 bitcast_convert_fusion.1
  479.5 14.3 %bitcast_convert_fusion = bf16[1536,2048]{1,0:T(8,128)(2,1)S(1)} fusion(bf16[4,512,1536]{2,1,0:T(8,128)(2,1)S(1)} %copy-done.40, bf16[4,512,2048]{2,1,0:T(8,128)(2,1)S(1)} %copy-done.39), kind=kOutput, calls=%fused_computation | convolution fusion | flops 12888047616 | bytes 20971520 | tf_op jit(solution)/shard_map/dot_general | solution.py:22
  493.8 4.6 pad_maximum_fusion
  498.5 57.2 %mlp_back.1 = (f32[512,1536]{1,0:T(8,128)}, bf16[512,1536]{1,0:T(8,128)(2,1)}, f32[1,1536]{1,0:T(1,128)}) custom-call(bf16[4,512,2048]{2,1,0:T(8,128)(2,1)} %get-tuple-element.55.pair_ref, bf16[1536,3840]{1,0:T(8,128)(2,1)} %all-gather.2.cloned.1.call-done.w_ref.gate_w.up_w.down_w, f32[512,1536]{1,0:T(8,128)} %get-tuple-element.50.hidden_ref, ...), custom_call_target="tpu_custom_call" | custom-call | flops 12884901888 | bytes 104857600 | tf_op jit(solution)/shard_map/mlp_back/pallas_call | solution.py:1000
  557.1 43.0 %out_back.1 = (bf16[4,512,1536]{2,1,0:T(8,128)(2,1)}, bf16[4,512,384]{2,1,0:T(8,128)(2,1)S(1)}, bf16[3,4,512,128]{3,2,1,0:T(8,128)(2,1)S(1)}) custom-call(bf16[512,1536]{1,0:T(8,128)(2,1)S(1)} %copy-done.4, bf16[1536,3840]{1,0:T(8,128)(2,1)} %all-gather.2.cloned.1.call-done.w_ref.gate_w.up_w.down_w, f32[4,512,384]{2,1,0:T(8,128)} %bitcast.149, ...), custom_call_target="tpu_custom_call" | custom-call | flops 2415919104 | bytes 104857600 | tf_op jit(solution)/shard_map/out_back/pallas_call | solution.py:1066
  600.2 6.6 fusion.13
  606.8 2.7 fusion.12
  609.6 2.4 copy.139
  612.9 252.2 %context_back.1 = (bf16[3,4,3,512,128]{4,3,2,1,0:T(8,128)(2,1)}, f32[3,4,8,512]{3,2,1,0:T(8,128)}) custom-call(bf16[3,4,512,128]{3,2,1,0:T(8,128)(2,1)} %copy-done.9, bf16[3,4,3,512,128]{4,3,2,1,0:T(8,128)(2,1)} %get-tuple-element.59.qkv_ref, f32[3,4,512,128]{3,2,1,0:T(8,128)} %copy-done.11, f32[3,8,2048]{2,1,0:T(8,128)} %copy-done.12, f32[3,8,2048]{2,1,0:T(8,128)} %copy-done.13), custom_call_target="tpu_custom_call" | custom-call | flops 32212254720 | bytes 104857600 | tf_op jit(solution)/shard_map/context_back/pallas_call | solution.py:394
  867.6 2.5 copy-done
  871.3 2.1 copy-done.1
  873.4 11.5 %fusion.31 = (bf16[2048,1536]{1,0:T(8,128)(2,1)S(1)}, f32[2048,1536]{1,0:T(8,128)}) fusion(bf16[2048,1024]{1,0:T(8,128)(2,1)S(1)} %bitcast.177, bf16[1536,3840]{1,0:T(8,128)(2,1)} %all-gather.2.cloned.1.call-done.w_ref.gate_w.up_w.down_w), kind=kOutput, calls=%fused_computation.95 | convolution fusion | flops 6445596672 | bytes 26214400 | tf_op jit(solution)/shard_map/dot_general | solution.py:22
  887.6 13.6 %convolution_convert_fusion.part_ref = bf16[1536,1280]{1,0:T(8,128)(2,1)} fusion(bf16[2048,1536]{1,0:T(8,128)(2,1)} %bitcast.176, bf16[2048,128]{1,0:T(8,128)(2,1)} %copy.124, bf16[2048,1152]{1,0:T(8,128)(2,1)} %bitcast.142), kind=kOutput, calls=%fused_computation.2 | convolution fusion | flops 8065515520 | bytes 15466496 | tf_op jit(solution)/shard_map/dot_general | solution.py:22
  901.1 3.5 fusion.3
  905.2 124.4 %last.1 = (bf16[512,1536]{1,0:T(8,128)(2,1)}, f32[192,1280]{1,0:T(8,128)}, f32[8,1536]{1,0:T(8,128)}) custom-call(bf16[4,512,1152]{2,1,0:T(8,128)(2,1)} %copy-done.1, bf16[4,512,384]{2,1,0:T(8,128)(2,1)} %copy-done.8, bf16[4,512,128]{2,1,0:T(8,128)(2,1)} %bitcast.157, bf16[1536,1280]{1,0:T(8,128)(2,1)} %get-tuple-element.45.w_ref.qkv_w.forget_w, ...), custom_call_target="tpu_custom_call" | custom-call | flops 10468982784 | bytes 104857600 | tf_op jit(solution)/shard_map/last/pallas_call | solution.py:1284
  1029.6 3.9 copy.156
  1037.9 2.1 fusion.26
  1040.0 3.9 fusion.7
  1043.9 2.4 copy.157
  1049.2 2.7 fusion.25
  (170 shorter events, 36.5 us)
Async XLA Ops:
  7.2 6.4 copy-start.20
  7.2 353.4 %all-gather.2.cloned.1.call-start = ((), (), s32[]{:S(2)}) async-start(), calls=%async_computation.2 | async-start | bytes 13271040 | tf_op jit(solution)/shard_map/all_gather | solution.py:1409
  13.5 1032.7 %reduce-scatter.7.cloned.1.call-start = ((), (), s32[]{:S(2)}) async-start(), calls=%async_computation.4 | async-start | bytes 2654208
  15.0 6.0 copy-start.14
  15.1 155.8 %copy-start.27 = (f32[512]{0:T(512)}, f32[512]{0:T(512)S(1)}, u32[]{:S(2)}) copy-start(f32[512]{0:T(512)S(1)} %convert_bitcast_fusion.2) | copy-start | bytes 6148
  15.1 5.8 copy-start.34
  15.1 5.9 copy-start.35
  15.1 6.0 copy-start.30
  15.2 6.2 copy-start.23
  15.2 6.2 copy-start.24
  16.6 154.3 %collective-permute-start.1 = (bf16[512,1536]{1,0:T(8,128)(2,1)}, bf16[512,1536]{1,0:T(8,128)(2,1)}, u32[]{:S(2)}, u32[]{:S(2)}) collective-permute-start(bf16[512,1536]{1,0:T(8,128)(2,1)} %fusion.10.grad_ref), channel_id=1, source_target_pairs={{0,2},{1,3},{2,0},{3,1},{4,6},{5,7},{6,4},{7,5},{8,10},{9,11},{10,... | collective-permute-start | bytes 4718600 | tf_op jit(solution)/shard_map/ppermute | solution.py:1334
  19.6 335.4 %collective-permute-start = (bf16[512,1536]{1,0:T(8,128)(2,1)}, bf16[512,1536]{1,0:T(8,128)(2,1)}, u32[]{:S(2)}, u32[]{:S(2)}) collective-permute-start(bf16[512,1536]{1,0:T(8,128)(2,1)} %fusion.10.grad_ref), channel_id=1, source_target_pairs={{0,1},{1,0},{2,3},{3,2},{4,5},{5,4},{6,7},{7,6},{8,9},{9,8},{10,11... | collective-permute-start | bytes 4718600 | tf_op jit(solution)/shard_map/ppermute | solution.py:1330
  150.9 18.2 %copy-start.7 = (f32[1,1536]{1,0:T(1,128)}, f32[1,1536]{1,0:T(1,128)S(1)}, u32[]{:S(2)}) copy-start(f32[1,1536]{1,0:T(1,128)S(1)} %get-tuple-element.156.gain_ref) | copy-start | bytes 18436
  150.9 218.3 %copy-start.6 = (f32[1,1536]{1,0:T(1,128)}, f32[1,1536]{1,0:T(1,128)S(1)}, u32[]{:S(2)}) copy-start(f32[1,1536]{1,0:T(1,128)S(1)} %get-tuple-element.155.gain_ref) | copy-start | bytes 18436
  153.1 16.4 %copy-start.37 = (bf16[6]{0:T(256)(128)(2,1)S(1)}, bf16[6]{0:T(256)(128)(2,1)}, u32[]{:S(2)}) copy-start(bf16[6]{0:T(256)(128)(2,1)} %param.22) | copy-start | bytes 40
  170.9 184.1 %collective-permute-start.2 = (bf16[512,1536]{1,0:T(8,128)(2,1)}, bf16[512,1536]{1,0:T(8,128)(2,1)S(1)}, u32[]{:S(2)}, u32[]{:S(2)}) collective-permute-start(bf16[512,1536]{1,0:T(8,128)(2,1)} %collective-permute-done.1), channel_id=1, source_target_pairs={{0,1},{1,0},{2,3},{3,2},{4,5},{5,4},{6,7},{7,6},{8,9},{9,8},{10,11... | collective-permute-start | bytes 4718600 | tf_op jit(solution)/shard_map/ppermute | solution.py:1330
  355.0 5.7 copy-start.17
  416.8 52.8 %copy-start.18 = (bf16[512,1536]{1,0:T(8,128)(2,1)S(1)}, bf16[512,1536]{1,0:T(8,128)(2,1)}, u32[]{:S(2)}) copy-start(bf16[512,1536]{1,0:T(8,128)(2,1)} %copy-done.17) | copy-start | bytes 4718596
  469.6 9.9 copy-start.39
  469.6 9.9 copy-start.40
  600.2 6.6 copy-start.8
  600.2 6.6 copy-start.9
  600.2 6.6 copy-start.36
  612.1 437.1 %reduce-scatter.5.cloned.1.call-start = ((), (), s32[]{:S(2)}) async-start(), calls=%async_computation.3 | async-start | bytes 10616832 | tf_op jit(solution)/shard_map/reduce_scatter | solution.py:1462
  612.9 253.4 %copy-start.22 = (f32[2048,6]{0,1:T(8,128)S(1)}, f32[2048,6]{0,1:T(8,128)}, u32[]{:S(2)}) copy-start(f32[2048,6]{0,1:T(8,128)} %copy-done.21) | copy-start | bytes 147460
  612.9 253.4 %copy-start.26 = (f32[4,4,128]{2,1,0:T(4,128)S(1)}, f32[4,4,128]{2,1,0:T(4,128)}, u32[]{:S(2)}) copy-start(f32[4,4,128]{2,1,0:T(4,128)} %copy-done.25) | copy-start | bytes 24580
  612.9 253.4 %copy-start.32 = (f32[6]{0:T(128)S(1)}, f32[6]{0:T(128)}, u32[]{:S(2)}) copy-start(f32[6]{0:T(128)} %copy-done.31) | copy-start | bytes 76
  886.2 14.9 %collective-permute-start.4 = (bf16[512,1536]{1,0:T(8,128)(2,1)S(1)}, bf16[512,1536]{1,0:T(8,128)(2,1)S(1)}, u32[]{:S(2)}, u32[]{:S(2)}) collective-permute-start(bf16[512,1536]{1,0:T(8,128)(2,1)S(1)} %get-tuple-element.119), channel_id=1, source_target_pairs={{0,1},{1,0},{2,3},{3,2},{4,5},{5,4},{6,7},{7,6},{8,9},{9,8},{10,11... | collective-permute-start | bytes 4718600 | tf_op jit(solution)/shard_map/ppermute | solution.py:1330
  886.6 153.3 %collective-permute-start.3 = (bf16[512,1536]{1,0:T(8,128)(2,1)}, bf16[512,1536]{1,0:T(8,128)(2,1)}, u32[]{:S(2)}, u32[]{:S(2)}) collective-permute-start(bf16[512,1536]{1,0:T(8,128)(2,1)} %get-tuple-element.118), channel_id=1, source_target_pairs={{0,1},{1,0},{2,3},{3,2},{4,5},{5,4},{6,7},{7,6},{8,9},{9,8},{10,11... | collective-permute-start | bytes 4718600 | tf_op jit(solution)/shard_map/ppermute | solution.py:1330
  904.6 135.4 %collective-permute-start.5 = (bf16[512,1536]{1,0:T(8,128)(2,1)}, bf16[512,1536]{1,0:T(8,128)(2,1)}, u32[]{:S(2)}, u32[]{:S(2)}) collective-permute-start(bf16[512,1536]{1,0:T(8,128)(2,1)} %fusion.3), channel_id=1, source_target_pairs={{0,2},{1,3},{2,0},{3,1},{4,6},{5,7},{6,4},{7,5},{8,10},{9,11},{10,... | collective-permute-start | bytes 4718600 | tf_op jit(solution)/shard_map/ppermute | solution.py:1334
  1029.6 10.4 copy-start.15
  1029.6 10.4 copy-start.28
  (18 other events, 29.3 us)
Sparse Core Ops, SparseCore 0:
  13.6 241.9 all-gather.1
  612.2 126.2 reduce-scatter.6
  742.1 207.2 reduce-scatter.4

commit v4 on v3

--- a/solution.py
+++ b/solution.py
@@ -240,12 +240,25 @@
 
 
 def context_kernel(
-    heads, head_size, items_ref, forget_ref, back_ref, qkv_ref, exact_ref, lse_ref, decay_ref, *refs
+    heads,
+    head_size,
+    items_ref,
+    forget_ref,
+    shard_ref,
+    back_ref,
+    qkv_ref,
+    full_ref,
+    exact_ref,
+    lse_ref,
+    decay_ref,
+    *refs,
 ):
     qkv, forget, out, save_sem = refs[:4]
     sems = refs[4:]
     count, size, _, block, width = items_ref.shape
-    me = ctx_greet(size)
+    greet_all(group_peers())
+    me = lax.axis_index("ctx")
+    gather = WeightGather(shard_ref, full_ref, sems[9:])
     forgets = Exchange(me, size, forget_ref, forget, sems[0:3])
     inputs = Exchange(me, size, items_ref, qkv, sems[3:6])
     results = Exchange(me, size, out, back_ref, sems[6:9])
@@ -255,6 +268,7 @@
         forgets.start(item)
 
     inputs.start(0)
+    gather.begin()
 
     @pl.loop(0, count)
     def _(item):
@@ -286,6 +300,14 @@
         )
         results.start(item)
         saving.wait()
+        for hop in range(1, min(size, count + 1)):
+
+            @pl.when(item == hop - 1)
+            def _(hop=hop):
+                gather.advance(hop)
+
+    for hop in range(count + 1, size):
+        gather.advance(hop)
 
     @pl.loop(0, count)
     def _(item):
@@ -294,6 +316,8 @@
         results.arrive(item)
         results.drain(item)
 
+    gather.end()
+
 
 def full_block(shape):
     return pl.BlockSpec(shape, lambda i: (0,) * len(shape), pipeline_mode=pl.Buffered(1))
@@ -307,7 +331,7 @@
     )
 
 
-def context(items, forget, head_size, ident):
+def context(items, forget, shard, f_size, head_size, ident):
     count, size, _, block, width = items.shape
     heads = width // head_size
     place = pl.BlockSpec(memory_space=pl.ANY)
@@ -318,32 +342,47 @@
         out_shape=[
             jax.ShapeDtypeStruct(exact, BF16),
             jax.ShapeDtypeStruct(items.shape, BF16),
+            jax.ShapeDtypeStruct((shard.shape[0] * f_size * size, shard.shape[1]), BF16),
             jax.ShapeDtypeStruct(exact, F32),
             jax.ShapeDtypeStruct(stat, F32),
             jax.ShapeDtypeStruct(stat, F32),
         ],
-        in_specs=[place, place],
-        out_specs=[place, place, full_block(exact), full_block(stat), full_block(stat)],
+        in_specs=[place, place, place],
+        out_specs=[place, place, place, full_block(exact), full_block(stat), full_block(stat)],
         scratch_shapes=[
             pltpu.VMEM(items.shape, BF16),
             pltpu.VMEM(forget.shape, F32),
             pltpu.VMEM(exact, BF16),
             pltpu.SemaphoreType.DMA,
         ]
-        + exchange_sems(count, size) * 3,
+        + exchange_sems(count, size) * 3
+        + weight_sems(f_size, size),
         compiler_params=remote_params(ident, 48),
         cost_estimate=attend_cost(items, heads, 2),
         name="context",
-    )(items, forget)
+    )(items, forget, shard)
 
 
 def context_back_kernel(
-    heads, head_size, items_ref, qkv_ref, exact_ref, lse_ref, decay_ref, back_ref, forget_ref, *refs
+    heads,
+    head_size,
+    items_ref,
+    qkv_ref,
+    exact_ref,
+    lse_ref,
+    decay_ref,
+    part_ref,
+    back_ref,
+    forget_ref,
+    sum_ref,
+    *refs,
 ):
     grads, dqkv, change, slope, dq_acc, delta = refs[:6]
-    sems = refs[6:]
+    sems = refs[6:15]
     count, size, block, width = items_ref.shape
-    me = ctx_greet(size)
+    greet_all(group_peers())
+    me = lax.axis_index("ctx")
+    weights = WeightSum(part_ref, 0, sum_ref, refs[15:])
     inputs = Exchange(me, size, items_ref, grads, sems[0:3])
     results = Exchange(me, size, dqkv, back_ref, sems[3:6])
     forgets = Exchange(me, size, slope, forget_ref, sems[6:9])
@@ -351,6 +390,8 @@
     @pl.loop(0, count)
     def _(item):
         inputs.start(item)
+
+    weights.begin()
 
     @pl.loop(0, count)
     def _(item):
@@ -377,6 +418,14 @@
             after = total[:, 0:1]
         forgets.start(item)
 
+        @pl.when(item == count - 2)
+        def _():
+            for c in weights.order:
+                weights.receive(c)
+
+    for c in weights.order:
+        weights.advance(c)
+
     @pl.loop(0, count)
     def _(item):
         inputs.drain(item)
@@ -385,18 +434,22 @@
         forgets.arrive(item)
         forgets.drain(item)
 
-
-def context_back(grads, qkv, exact, lse, decay, head_size, ident):
+    weights.end()
+
+
+def context_back(grads, qkv, exact, lse, decay, part, f_size, head_size, ident):
     count, size, _, block, width = qkv.shape
     heads = width // head_size
     place = pl.BlockSpec(memory_space=pl.ANY)
     forget = (count, size, 8, block)
+    total = (part.shape[0] // (f_size * size), part.shape[1])
     return pl.pallas_call(
         functools.partial(context_back_kernel, heads, head_size),
         grid=(1,),
         out_shape=[
             jax.ShapeDtypeStruct(qkv.shape, BF16),
             jax.ShapeDtypeStruct(forget, F32),
+            jax.ShapeDtypeStruct(total, F32),
         ],
         in_specs=[
             place,
@@ -404,8 +457,9 @@
             full_block(exact.shape),
             full_block(lse.shape),
             full_block(decay.shape),
-        ],
-        out_specs=[place, place],
+            place,
+        ],
+        out_specs=[place, place, full_block(total)],
         scratch_shapes=[
             pltpu.VMEM(grads.shape, BF16),
             pltpu.VMEM(qkv.shape, BF16),
@@ -414,11 +468,12 @@
             pltpu.VMEM((heads, size, block, width), F32),
             pltpu.VMEM((8, size * block), F32),
         ]
-        + exchange_sems(count, size) * 3,
+        + exchange_sems(count, size) * 3
+        + sum_scratch(f_size, size, *total),
         compiler_params=remote_params(ident, 56),
         cost_estimate=attend_cost(qkv, heads, 5),
         name="context_back",
-    )(grads, qkv, exact, lse, decay)
+    )(grads, qkv, exact, lse, decay, part)
 
 
 CHUNKS = 4
@@ -459,7 +514,7 @@
     return slot, chunk
 
 
-def gather_loop(table, sems, compute, own=None, relative=False):
+def gather_loop(table, sems, compute, own=None, relative=False, between=None):
     near_send, near_recv, far_send, far_recv, pass_send, pass_recv = sems
     me, sibling, across, diagonal = tp_places()
     places = (0, 1, 2, 3) if relative else (me, sibling, across, diagonal)
@@ -516,7 +571,14 @@
         compute(slot, chunk)
         return 0
 
-    lax.fori_loop(0, 4 * CHUNKS, body, 0)
+    if between is None:
+        lax.fori_loop(0, 4 * CHUNKS, body, 0)
+    else:
+        lax.fori_loop(0, 2 * CHUNKS, body, 0)
+        for turn in range(CHUNKS):
+            between(turn)
+            first = 2 * (CHUNKS + turn)
+            lax.fori_loop(first, first + 2, body, 0)
     near.wait_send()
     for chunk in range(CHUNKS):
         far(chunk).wait_send()
@@ -722,6 +784,127 @@
 def weight_sems(f_size, c_size):
     dma = pltpu.SemaphoreType.DMA
     return [dma((2, c_size + 1))] * 2 + [dma((f_size, c_size))] * 2 + [dma]
+
+
+class WeightSum:
+    def __init__(self, part, first_column, out, refs):
+        self.part, self.out = part, out
+        self.stage, self.total, self.along_in = refs[:3]
+        self.own_sem, self.over_send, self.over_recv, self.along_send, self.along_recv = refs[3:]
+        self.f_size, self.c_size = lax.axis_size("fsdp"), lax.axis_size("ctx")
+        self.f, self.c = lax.axis_index("fsdp"), lax.axis_index("ctx")
+        self.rows, columns = out.shape
+        self.columns = pl.ds(first_column, columns)
+        self.order = [
+            (self.c_size - 1 - i // 2) if i % 2 == 0 else i // 2 for i in range(self.c_size)
+        ]
+
+    def piece(self, f, c):
+        row = (f * self.c_size + c) * self.rows
+        return self.part.at[pl.ds(pl.multiple_of(row, self.rows), self.rows), self.columns]
+
+    def own(self, c):
+        return pltpu.make_async_copy(self.piece(self.f, c), self.stage.at[c], self.own_sem.at[c])
+
+    def over(self, c, step):
+        f = lax.rem(self.f + step, self.f_size)
+        return moving(
+            self.piece(f, c),
+            self.total.at[step - 1, c],
+            self.over_send.at[step - 1, c],
+            self.over_recv.at[step - 1, c],
+            {"fsdp": f},
+        )
+
+    def along(self, c, side, source=None):
+        peer = {"ctx": self.c + (1 if side else -1)}
+        target = self.along_in.at[side, c]
+        return moving(
+            target if source is None else source,
+            target,
+            self.along_send.at[side, c],
+            self.along_recv.at[side, c],
+            peer,
+        )
+
+    def begin(self):
+        for c in self.order:
+            self.own(c).start()
+            for step in range(1, self.f_size):
+                self.over(c, step).start()
+
+    def receive(self, c):
+        self.own(c).wait()
+        value = self.stage[c].astype(F32)
+        for step in range(1, self.f_size):
+            self.over(c, step).wait_recv()
+            value = value + self.total[step - 1, c].astype(F32)
+        self.total[0, c] = value.astype(BF16)
+        for side, end in ((1, 0), (0, self.c_size - 1)):
+
+            @pl.when((self.c == end) & (self.c != c))
+            def _(side=side):
+                self.along(c, side, self.total.at[0, c]).start()
+
+    def advance(self, c):
+        for side in (1, 0):
+            comes = (self.c > 0) & (self.c <= c) if side else (self.c >= c) & (self.c < self.c_size - 1)
+
+            @pl.when(comes)
+            def _(side=side):
+                self.along(c, side).wait_recv()
+                value = self.total[0, c].astype(F32) + self.along_in[side, c].astype(F32)
+
+                @pl.when(self.c == c)
+                def _():
+                    self.total[0, c] = value.astype(BF16)
+
+                @pl.when(self.c != c)
+                def _():
+                    self.along_in[side, c] = value.astype(BF16)
+                    self.along(c, side).start()
+
+    def tasks(self):
+        found = []
+        for turn, c in enumerate(self.order):
+            found.append(functools.partial(self.receive, c))
+            if turn:
+                found.append(functools.partial(self.advance, self.order[turn - 1]))
+        return found + [functools.partial(self.advance, self.order[-1])]
+
+    def end(self):
+        self.out[...] = self.total[0, self.c].astype(F32)
+        for c in range(self.c_size):
+            for step in range(1, self.f_size):
+                self.over(c, step).wait_send()
+            for side in (1, 0):
+
+                @pl.when(self.c < c if side else self.c > c)
+                def _(side=side):
+                    self.along(c, side).wait_send()
+
+
+SUM_REFS = 8
+
+
+def sum_scratch(f_size, c_size, rows, columns):
+    dma = pltpu.SemaphoreType.DMA
+    return (
+        [
+            pltpu.VMEM((c_size, rows, columns), BF16),
+            pltpu.VMEM((f_size - 1, c_size, rows, columns), BF16),
+            pltpu.VMEM((2, c_size, rows, columns), BF16),
+        ]
+        + [dma((c_size,))]
+        + [dma((f_size - 1, c_size))] * 2
+        + [dma((2, c_size))] * 2
+    )
+
+
+def shared(tasks, turn, turns):
+    share = -(-len(tasks) // turns)
+    for task in tasks[turn * share : (turn + 1) * share]:
+        task()
 
 
 def startup_kernel(rows_ref, shard_ref, all_ref, full_ref, own_sem, *sems):
@@ -967,10 +1150,15 @@
     )(normed, grad_all, full_two, full_two, full_two)
 
 
-def mlp_back_kernel(pair_ref, w_ref, hidden_ref, grad_ref, gain_ref, out_ref, branch_ref, part_ref, *refs):
-    buffers, sems = refs[:4], refs[4:]
+def mlp_back_kernel(
+    pair_ref, w_ref, hidden_ref, grad_ref, gain_ref, sums_ref, out_ref, branch_ref, part_ref, sum_ref, *refs
+):
+    buffers, sems = refs[:4], refs[4:8]
     me, sibling, across, diagonal = tp_places()
-    greet((sibling, across))
+    greet_all([{"tp": sibling}, {"tp": across}] + group_peers())
+    weights = WeightSum(sums_ref, 0, sum_ref, refs[8:])
+    weights.begin()
+    tasks = weights.tasks()
     part_ref[...] = jnp.zeros_like(part_ref)
     size = hidden_ref.shape[0] // CHUNKS
 
@@ -991,12 +1179,16 @@
         out_ref[span(chunk)] = grad
         branch_ref[span(chunk)] = grad.astype(BF16)
 
-    scatter_loop(buffers, sems, partial, finish, relative=True)
-
-
-def mlp_back(pair, full_two, hidden_state, grad_out, gain, ident):
+    scatter_loop(
+        buffers, sems, partial, finish, relative=True, between=lambda chunk: shared(tasks, chunk, CHUNKS)
+    )
+    weights.end()
+
+
+def mlp_back(pair, full_two, hidden_state, grad_out, gain, part, f_size, c_size, ident):
     tp_size, rows, wide = pair.shape
     model_width = hidden_state.shape[1]
+    total = (part.shape[0] // (f_size * c_size), part.shape[1] // 2)
     return pl.pallas_call(
         mlp_back_kernel,
         grid=(1,),
@@ -1004,6 +1196,7 @@
             jax.ShapeDtypeStruct(hidden_state.shape, F32),
             jax.ShapeDtypeStruct(hidden_state.shape, BF16),
             jax.ShapeDtypeStruct(gain.shape, F32),
+            jax.ShapeDtypeStruct(total, F32),
         ],
         in_specs=[
             whole(pair.shape),
@@ -1011,24 +1204,35 @@
             whole(hidden_state.shape),
             whole(grad_out.shape),
             whole(gain.shape),
-        ],
-        out_specs=[whole(hidden_state.shape), whole(hidden_state.shape), whole(gain.shape)],
-        scratch_shapes=scatter_buffers(rows, model_width) + SCATTER_SEMS,
+            pl.BlockSpec(memory_space=pl.ANY),
+        ],
+        out_specs=[
+            whole(hidden_state.shape),
+            whole(hidden_state.shape),
+            whole(gain.shape),
+            whole(total),
+        ],
+        scratch_shapes=scatter_buffers(rows, model_width)
+        + SCATTER_SEMS
+        + sum_scratch(f_size, c_size, *total),
         compiler_params=remote_params(ident, 56),
         cost_estimate=pl.CostEstimate(
             flops=2 * pair.size * model_width, bytes_accessed=100 << 20, transcendentals=0
         ),
         name="mlp_back",
-    )(pair, full_two, hidden_state, grad_out, gain)
-
-
-def out_back_kernel(layout, branch_ref, w_ref, gate_ref, attended_ref, *refs):
+    )(pair, full_two, hidden_state, grad_out, gain, part)
+
+
+def out_back_kernel(layout, branch_ref, w_ref, gate_ref, attended_ref, sums_ref, *refs):
     seq_count, groups, width, places = layout
-    all_ref, logit_ref, items, table, grads, own_sem = refs[:6]
-    sems = refs[6:]
+    all_ref, logit_ref, items, sum_ref, table, grads, own_sem = refs[:7]
+    sems = refs[7:13]
     count = items.shape[0]
     me, sibling, across, diagonal = tp_places()
-    greet((sibling, across))
+    greet_all([{"tp": sibling}, {"tp": across}] + group_peers())
+    weights = WeightSum(sums_ref, sum_ref.shape[1], sum_ref, refs[13:])
+    weights.begin()
+    tasks = weights.tasks()
     table[me] = branch_ref[...]
     tp_size, rows, _ = gate_ref.shape
     local, size = rows // seq_count, rows // CHUNKS
@@ -1042,7 +1246,7 @@
         attended = attended_ref[slot, spot].astype(F32)
         logit_ref[slot, spot] = (scaled * attended * (1.0 - gate)).astype(BF16)
 
-    gather_loop(table, sems, compute)
+    gather_loop(table, sems, compute, between=lambda turn: shared(tasks, turn, CHUNKS))
     copy = pltpu.make_async_copy(table, all_ref, own_sem)
     copy.start()
 
@@ -1055,14 +1259,16 @@
 
     lax.fori_loop(0, tp_size, deal, 0)
     copy.wait()
-
-
-def out_back(branch, full_two, column, gate, attended, layout, item_count, ctx_size, ident):
+    weights.end()
+
+
+def out_back(branch, full_two, column, gate, attended, part, layout, item_count, f_size, ctx_size, ident):
     seq_count, groups, width, places = layout
     rows, model_width = branch.shape
     tp_size, _, inner = gate.shape
     item = (item_count, ctx_size, tp_size * rows // seq_count, width)
     table = (tp_size, rows, model_width)
+    total = (part.shape[0] // (f_size * ctx_size), part.shape[1] // 2)
     return pl.pallas_call(
         functools.partial(out_back_kernel, layout),
         grid=(1,),
@@ -1070,22 +1276,25 @@
             jax.ShapeDtypeStruct(table, BF16),
             jax.ShapeDtypeStruct(gate.shape, BF16),
             jax.ShapeDtypeStruct(item, BF16),
+            jax.ShapeDtypeStruct(total, F32),
         ],
         in_specs=[
             whole(branch.shape),
             whole((model_width, inner), column),
             whole(gate.shape),
             whole(attended.shape),
-        ],
-        out_specs=[pl.BlockSpec(memory_space=pl.ANY), whole(gate.shape), whole(item)],
+            pl.BlockSpec(memory_space=pl.ANY),
+        ],
+        out_specs=[pl.BlockSpec(memory_space=pl.ANY), whole(gate.shape), whole(item), whole(total)],
         scratch_shapes=[pltpu.VMEM(table, BF16), pltpu.VMEM(gate.shape, BF16), pltpu.SemaphoreType.DMA]
-        + GATHER_SEMS,
+        + GATHER_SEMS
+        + sum_scratch(f_size, ctx_size, *total),
         compiler_params=remote_params(ident, 48),
         cost_estimate=pl.CostEstimate(
             flops=2 * gate.size * model_width, bytes_accessed=100 << 20, transcendentals=0
         ),
         name="out_back",
-    )(branch, full_two, gate, attended)
+    )(branch, full_two, gate, attended, part)
 
 
 def assemble_kernel(layout, items, out_ref):
@@ -1113,89 +1322,6 @@
         cost_estimate=pl.CostEstimate(flops=0, bytes_accessed=16 << 20, transcendentals=0),
         name="assemble",
     )(items)
-
-
-class WeightSum:
-    def __init__(self, part, out, buffers, sems):
-        self.part, self.out = part, out
-        self.over_in, self.total, self.along_out, self.along_in = buffers
-        self.over_send, self.over_recv, self.along_send, self.along_recv = sems
-        self.f_size, self.c_size = lax.axis_size("fsdp"), lax.axis_size("ctx")
-        self.f, self.c = lax.axis_index("fsdp"), lax.axis_index("ctx")
-        self.rows = out.shape[0]
-        ends = [(self.c_size - 1 - i // 2) if i % 2 == 0 else i // 2 for i in range(self.c_size)]
-        self.order = ends
-
-    def block(self, f, c):
-        index = f * self.c_size + c
-        return pl.ds(pl.multiple_of(index * self.rows, self.rows), self.rows)
-
-    def over(self, c, step):
-        f = lax.rem(self.f + step, self.f_size)
-        return moving(
-            self.part.at[self.block(f, c)],
-            self.over_in.at[step, c],
-            self.over_send.at[step, c],
-            self.over_recv.at[step, c],
-            {"fsdp": f},
-        )
-
-    def along(self, c, side):
-        peer = {"ctx": self.c + (1 if side else -1)}
-        return moving(
-            self.along_out.at[side, c],
-            self.along_in.at[side, c],
-            self.along_send.at[side, c],
-            self.along_recv.at[side, c],
-            peer,
-        )
-
-    def begin(self):
-        for c in self.order:
-            for step in range(1, self.f_size):
-                self.over(c, step).start()
-
-    def receive(self, c):
-        value = self.part[self.block(self.f, c)].astype(F32)
-        for step in range(1, self.f_size):
-            self.over(c, step).wait_recv()
-            value = value + self.over_in[step, c].astype(F32)
-        self.total[c] = value
-        for side, end in ((1, 0), (0, self.c_size - 1)):
-
-            @pl.when((self.c == end) & (self.c != c))
-            def _(side=side):
-                self.along_out[side, c] = value.astype(BF16)
-                self.along(c, side).start()
-
-    def advance(self, c):
-        for side in (1, 0):
-            comes = (self.c > 0) & (self.c <= c) if side else (self.c >= c) & (self.c < self.c_size - 1)
-
-            @pl.when(comes)
-            def _(side=side):
-                self.along(c, side).wait_recv()
-                value = self.total[c] + self.along_in[side, c].astype(F32)
-
-                @pl.when(self.c == c)
-                def _():
-                    self.total[c] = value
-
-                @pl.when(self.c != c)
-                def _():
-                    self.along_out[side, c] = value.astype(BF16)
-                    self.along(c, side).start()
-
-    def end(self):
-        self.out[...] = self.total[self.c]
-        for c in range(self.c_size):
-            for step in range(1, self.f_size):
-                self.over(c, step).wait_send()
-            for side in (1, 0):
-
-                @pl.when(self.c < c if side else self.c > c)
-                def _(side=side):
-                    self.along(c, side).wait_send()
 
 
 def last_kernel(
@@ -1215,13 +1341,12 @@
     vector_ref,
     *refs,
 ):
-    buffers, weight_buffers = refs[:4], refs[4:8]
-    mine, near_in, group_in = refs[8:11]
-    sems, weight_sum_sems, vector_sems = refs[11:15], refs[15:19], refs[19:]
+    buffers, sems, (mine, near_in, group_in) = refs[:4], refs[4:8], refs[8:11]
+    vector_sems, sum_refs = refs[11:15], refs[15:]
     me, sibling, across, diagonal = tp_places()
     others = group_peers()
     greet_all([{"tp": sibling}, {"tp": across}, {"tp": diagonal}] + others)
-    weights = WeightSum(part_ref, sum_ref, weight_buffers, weight_sum_sems)
+    weights = WeightSum(part_ref, 0, sum_ref, sum_refs)
     weights.begin()
     mine[...] = extra_ref[...]
     size = x_ref.shape[0] // CHUNKS
@@ -1243,18 +1368,10 @@
         middle = jnp.mean(scaled * unit, axis=1, keepdims=True)
         out_ref[span(chunk)] = (grad_ref[span(chunk)] + inverse * (scaled - unit * middle)).astype(BF16)
 
-    order = weights.order
-    tasks = []
-    for turn, c in enumerate(order):
-        tasks.append((weights.receive, c))
-        if turn:
-            tasks.append((weights.advance, order[turn - 1]))
-    tasks.append((weights.advance, order[-1]))
-    share = -(-len(tasks) // CHUNKS)
+    tasks = weights.tasks()
 
     def between(chunk):
-        for task, c in tasks[chunk * share : (chunk + 1) * share]:
-            task(c)
+        shared(tasks, chunk, CHUNKS)
 
     scatter_loop(buffers, sems, partial, finish, between=between)
     near_send, near_recv, group_send, group_recv = vector_sems
@@ -1299,25 +1416,20 @@
             whole(x.shape),
             whole(x.shape),
             whole(gain.shape),
-            whole(part.shape),
+            pl.BlockSpec(memory_space=pl.ANY),
             whole(extra.shape),
         ],
         out_specs=[whole(x.shape), whole((shard, columns)), whole(extra.shape)],
         scratch_shapes=scatter_buffers(rows, model_width)
+        + SCATTER_SEMS
         + [
-            pltpu.VMEM((f_size, c_size, shard, columns), BF16),
-            pltpu.VMEM((c_size, shard, columns), F32),
-            pltpu.VMEM((2, c_size, shard, columns), BF16),
-            pltpu.VMEM((2, c_size, shard, columns), BF16),
             pltpu.VMEM(extra.shape, F32),
             pltpu.VMEM((3,) + extra.shape, F32),
             pltpu.VMEM((f_size * c_size - 1,) + extra.shape, F32),
         ]
-        + SCATTER_SEMS
-        + [dma((f_size, c_size))] * 2
-        + [dma((2, c_size))] * 2
         + [dma((3,))] * 2
-        + [dma((f_size * c_size - 1,))] * 2,
+        + [dma((f_size * c_size - 1,))] * 2
+        + sum_scratch(f_size, c_size, shard, columns),
         compiler_params=remote_params(ident, 60),
         cost_estimate=pl.CostEstimate(
             flops=8 * rows * model_width * (wide + inner + LANES), bytes_accessed=100 << 20, transcendentals=0
@@ -1392,7 +1504,7 @@
     places = tuple(place(slot) for slot in range(ctx_size * item_count))
     layout = (seq_count, groups, width, places)
 
-    weights = ("fsdp", "ctx")
+    fsdp_size = lax.axis_size("fsdp")
     packed_one = jnp.concatenate(
         [
             w_query,
@@ -1406,15 +1518,12 @@
         axis=1,
     )
     packed_two = jnp.concatenate([w_gate, w_up, w_down, w_out, w_gate_out], axis=1)
-    full_two = lax.all_gather(packed_two, weights, axis=0, tiled=True)
     edge = 3 * inner_width
     input_rows = layer_input.transpose(1, 0, 2).reshape(seq_count * local_rows, model_width)
-    input_all, full_one = startup(input_rows, packed_one, lax.axis_size("fsdp"), ctx_size, 1)
+    input_all, full_one = startup(input_rows, packed_one, fsdp_size, ctx_size, 1)
     gains = full_one[:, edge + head_count : edge + head_count + 2].astype(F32).T
     gain_one, gain_two = gains[0:1], gains[1:2]
-    down_w = full_two[:, 2 * hidden : 3 * hidden]
     out_column = 3 * hidden // inner_width
-    gate_out_w = full_two[:, 3 * hidden + inner_width :]
 
     def by_sequence(rows):
         return rows.transpose(1, 0, 2).reshape(seq_count * local_rows, model_width)
@@ -1432,6 +1541,7 @@
     ctx_valid = (ctx_pos < lengths[None, :, None]).astype(F32)
 
     grad_out = (valid_rows * by_sequence(cotangent).astype(F32)).astype(BF16)
+    grad_all = relative_rows(lax.optimization_barrier((grad_out, input_all[0, :8]))[0])
     normed_one, forget_rows, items = project(
         input_all, gain_one, full_one, layout, item_count, ctx_size
     )
@@ -1445,10 +1555,13 @@
     picked = jnp.stack([cut[g, :, :, s] for s, g in places])
     picked = picked.reshape(ctx_size, item_count, pair, ctx_rows).transpose(1, 0, 2, 3)
     picked = jnp.pad(picked, ((0, 0), (0, 0), (0, 8 - pair), (0, 0)))
-    attended_items, qkv, exact, lse, decay = context(items, picked, head_size, 7)
+    attended_items, qkv, full_two, exact, lse, decay = context(
+        items, picked, packed_two, fsdp_size, head_size, 7
+    )
+    down_w = full_two[:, 2 * hidden : 3 * hidden]
+    gate_out_w = full_two[:, 3 * hidden + inner_width :]
     gate_logit = dot(normed_flat, gate_out_w, NN)
     out_gate = jax.nn.sigmoid(gate_logit).reshape(tp_size, -1, inner_width)
-    grad_all = relative_rows(grad_out)
     hidden_state, normed_two, attended, mixed = out_project(
         input_rows, out_gate, full_two, out_column, gain_two, attended_items, layout, 2
     )
@@ -1458,41 +1571,40 @@
     grad_pair_flat = grad_pair.reshape(all_rows, 2 * hidden)
     grad_flat = grad_all.reshape(all_rows, model_width)
 
-    def owned_sum(part):
-        total = lax.psum_scatter(part, weights, scatter_dimension=0, tiled=True)
-        return total.astype(F32)
-
-    mlp_part = jnp.concatenate(
-        [
-            dot(normed_two_flat, grad_pair_flat, TN).astype(BF16),
-            dot(grad_flat, inner_flat, TN).astype(BF16),
-        ],
-        axis=1,
-    )
-    mlp_part, grad_pair = lax.optimization_barrier((mlp_part, grad_pair))
-    mlp_sum = owned_sum(mlp_part)
-    grad_hidden, branch, mlp_gain_part = mlp_back(
-        grad_pair, full_two, hidden_state, grad_out, gain_two, 4
+    gate_up_part = dot(normed_two_flat, grad_pair_flat, TN).astype(BF16)
+    grad_hidden, branch, mlp_gain_part, gate_sum = mlp_back(
+        grad_pair, full_two, hidden_state, grad_out, gain_two, gate_up_part, fsdp_size, ctx_size, 4
     )
     feedforward = summed_rows(dot(inner_flat, down_w, NT).reshape(tp_size, -1, model_width))
     output = (valid_rows * (hidden_state + feedforward)).astype(BF16)
 
-    branch_all, grad_gate_logit, grads = out_back(
-        branch, full_two, out_column, out_gate, attended, layout, item_count, ctx_size, 5
+    branch_all, grad_gate_logit, grads, up_sum = out_back(
+        branch,
+        full_two,
+        out_column,
+        out_gate,
+        attended,
+        gate_up_part,
+        layout,
+        item_count,
+        fsdp_size,
+        ctx_size,
+        5,
     )
     branch_flat = branch_all.reshape(all_rows, model_width)
     logit_flat = grad_gate_logit.reshape(all_rows, inner_width)
 
-    grad_items, forget_items = context_back(grads, qkv, exact, lse, decay, head_size, 8)
     out_part = jnp.concatenate(
         [
+            dot(grad_flat, inner_flat, TN).astype(BF16),
             dot(branch_flat, mixed.reshape(all_rows, inner_width), TN).astype(BF16),
             dot(normed_flat, logit_flat, TN).astype(BF16),
         ],
         axis=1,
     )
-    out_sum = owned_sum(out_part)
-
+    grad_items, forget_items, out_sum = context_back(
+        grads, qkv, exact, lse, decay, out_part, fsdp_size, head_size, 8
+    )
     forget_back = forget_items[:, :, :pair].astype(BF16).transpose(1, 0, 2, 3)
     forget_back = forget_back.reshape(ctx_size * item_count, pair, tp_size, local_rows)
     slots = {place(slot): slot for slot in range(used)}
@@ -1526,7 +1638,7 @@
         gain_one,
         dot(normed_flat, grad_qkvf, TN).astype(BF16),
         extra,
-        lax.axis_size("fsdp"),
+        fsdp_size,
         ctx_size,
         6,
     )
@@ -1545,12 +1657,12 @@
         qkv_sum[:, 2 * wide : 3 * wide],
         qkv_sum[:, 3 * wide : 3 * wide + head_count],
         forget_bias_grad,
-        out_sum[:, wide:],
-        out_sum[:, :wide],
+        out_sum[:, hidden + wide :],
+        out_sum[:, hidden : hidden + wide],
         mlp_gain_grad,
-        mlp_sum[:, :hidden],
-        mlp_sum[:, hidden : 2 * hidden],
-        mlp_sum[:, 2 * hidden :],
+        gate_sum,
+        up_sum,
+        out_sum[:, :hidden],
     )
 
 

time: 1060 us -> 1100 us (1.038)
  Pallas kernels: 890 us -> 957 us
  local copies, waits for them, and re-layouts: 57.8 us -> 43.5 us
  between operations: 15 us -> 1.98 us
    pallas_call x1, Pallas kernels: 178 us -> 259 us  [context(): pl.pallas_call(functools.partial(context_kernel, heads, head_size), grid=...]
    pallas_call x1, Pallas kernels: 120 us -> 73.5 us  [startup(): pl.pallas_call(startup_kernel, out_shape=[jax.ShapeDtypeStruct((4,) + row...]
    pallas_call x1, Pallas kernels: 252 us -> 219 us  [context_back(): pl.pallas_call(functools.partial(context_back_kernel, heads, head_size),...]
    pallas_call x1, Pallas kernels: 43 us -> 75.2 us  [out_back(): pl.pallas_call(functools.partial(out_back_kernel, layout), grid=(1,), out...]
    pallas_call x1, Pallas kernels: 57.2 us -> 84.6 us  [mlp_back(): pl.pallas_call(mlp_back_kernel, grid=(1,), out_shape=[jax.ShapeDtypeStruc...]
    unnamed x104 -> x96, local copies, waits for them, and re-layouts: 27.4 us -> 15.9 us
  transfers between devices with their start and end apart: 9 -> 6, of which waited for: 0 -> 0; matrix products, arithmetic and copies ran while one was open for 7% -> 5% of each run, Pallas kernels for 65% -> 48%
where the time goes in v4:
time: 1100 us
  Pallas kernels  957 us (87%)
  matrix products  71.9 us (7%)
  local copies, waits for them, and re-layouts  43.5 us (4%)
  other arithmetic  21 us (2%)
    pallas_call x1, Pallas kernels, context(): pl.pallas_call(functools.partial(context_kernel, heads, head_size), grid=...  259 us
    pallas_call x1, Pallas kernels, context_back(): pl.pallas_call(functools.partial(context_back_kernel, heads, head_size),...  219 us
    pallas_call x1, Pallas kernels, last(): pl.pallas_call(last_kernel, grid=(1,), out_shape=[jax.ShapeDtypeStruct(x....  130 us
    pallas_call x1, Pallas kernels, mlp_back(): pl.pallas_call(mlp_back_kernel, grid=(1,), out_shape=[jax.ShapeDtypeStruc...  84.6 us
    pallas_call x1, Pallas kernels, out_back(): pl.pallas_call(functools.partial(out_back_kernel, layout), grid=(1,), out...  75.2 us
    pallas_call x1, Pallas kernels, startup(): pl.pallas_call(startup_kernel, out_shape=[jax.ShapeDtypeStruct((4,) + row...  73.5 us
    dot_general x7, matrix products, dot(): return lax.dot_general(left, right, dims, preferred_element_type=F32)  71.9 us
    pallas_call x1, Pallas kernels, mlp(): pl.pallas_call(mlp_kernel, grid=(1,), out_shape=[jax.ShapeDtypeStruct(gra...  53 us
  transfers between devices with their start and end apart: 6, of which 0 were waited for; matrix products, arithmetic and copies ran while one was open for 5% of the time, Pallas kernels for 48%

profile of v4, /device:TPU:0, one launch (start us, length us, event | category | flops | bytes accessed | tf_op | source)
XLA Modules:
  0.0 1099.7 jit_solution(13493335974302328095)
XLA Ops:
  0.7 1.8 convert_bitcast_fusion
  3.9 3.0 collective-permute-start.1
  7.0 1.4 copy.59
  8.8 1.5 concatenate.15.shard_ref
  10.3 73.5 %startup.1 = (bf16[4,512,1536]{2,1,0:T(8,128)(2,1)}, bf16[1536,1280]{1,0:T(8,128)(2,1)}) custom-call(bf16[512,1536]{1,0:T(8,128)(2,1)} %bitcast.139, bf16[192,1280]{1,0:T(8,128)(2,1)} %concatenate.15.shard_ref), custom_call_target="tpu_custom_call" | custom-call | tf_op jit(solution)/shard_map/startup/pallas_call | solution.py:957
  83.8 6.3 copy.63
  90.9 2.1 copy-done.2
  93.0 16.1 %project.1 = (bf16[4,512,1536]{2,1,0:T(8,128)(2,1)}, f32[4,512,128]{2,1,0:T(8,128)S(1)}, bf16[3,4,3,512,128]{4,3,2,1,0:T(8,128)(2,1)}) custom-call(bf16[4,512,1536]{2,1,0:T(8,128)(2,1)} %get-tuple-element.46.x_ref, f32[1,1536]{1,0:T(1,128)S(1)} %get-tuple-element.143.gain_ref, bf16[1536,1280]{1,0:T(8,128)(2,1)S(1)} %copy-done.2), custom_call_target="tpu_custom_call" | custom-call | flops 8053063680 | bytes 12582912 | tf_op jit(solution)/shard_map/project/pallas_call | solution.py:1005
  112.3 259.4 %context.1 = (bf16[3,4,512,128]{3,2,1,0:T(8,128)(2,1)S(1)}, bf16[3,4,3,512,128]{4,3,2,1,0:T(8,128)(2,1)}, bf16[1536,3840]{1,0:T(8,128)(2,1)}, f32[3,4,512,128]{3...) custom-call(bf16[3,4,3,512,128]{4,3,2,1,0:T(8,128)(2,1)} %get-tuple-element.49.items_ref, ...), custom_call_target="tpu_custom_call" | custom-call | flops 12884901888 | bytes 104857600 | tf_op jit(solution)/shard_map/context/pallas_call | solution.py:339
  374.3 8.4 add_divide_fusion
  382.7 45.3 %out_project.1 = (f32[512,1536]{1,0:T(8,128)}, bf16[512,1536]{1,0:T(8,128)(2,1)S(1)}, bf16[4,512,384]{2,1,0:T(8,128)(2,1)S(1)}, bf16[4,512,384]{2,1,0:T(8,128)(2,1)S(1)}) custom-call(bf16[512,1536]{1,0:T(8,128)(2,1)} %bitcast.140, f32[4,512,384]{2,1,0:T(8,128)} %bitcast.142, bf16[1536,3840]{1,0:T(8,128)(2,1)} %get-tuple-element.51.w_ref.gate_w.up_w.down_w, ...), custom_call_target="tpu_custom_call" | custom-call | flops 2415919104 | bytes 104857600 | tf_op jit(solution)/shard_map/out_project/pallas_call | solution.py:1073
  428.1 6.1 pad_maximum_fusion.grad_ref
  434.3 53.0 %mlp.1 = (bf16[4,512,1536]{2,1,0:T(8,128)(2,1)}, bf16[4,512,1024]{2,1,0:T(8,128)(2,1)}, bf16[4,512,2048]{2,1,0:T(8,128)(2,1)}) custom-call(bf16[512,1536]{1,0:T(8,128)(2,1)} %copy-done.10, bf16[4,512,1536]{2,1,0:T(8,128)(2,1)} %pad_maximum_fusion.grad_ref, bf16[1536,3840]{1,0:T(8,128)(2,1)} %get-tuple-element.51.w_ref.gate_w.up_w.down_w, ...), custom_call_target="tpu_custom_call" | custom-call | flops 19327352832 | bytes 104857600 | tf_op jit(solution)/shard_map/mlp/pallas_call | solution.py:1129
  487.3 19.2 %bitcast_convert_fusion.sums_ref = bf16[1536,2048]{1,0:T(8,128)(2,1)} fusion(bf16[4,512,1536]{2,1,0:T(8,128)(2,1)} %get-tuple-element.57, bf16[4,512,2048]{2,1,0:T(8,128)(2,1)} %get-tuple-element.56.pair_ref), kind=kOutput, calls=%fused_computation | convolution fusion | flops 12888047616 | bytes 20971520 | tf_op jit(solution)/shard_map/dot_general | solution.py:22
  506.4 84.6 %mlp_back.1 = (f32[512,1536]{1,0:T(8,128)}, bf16[512,1536]{1,0:T(8,128)(2,1)}, f32[1,1536]{1,0:T(1,128)}, f32[192,1024]{1,0:T(8,128)}) custom-call(bf16[4,512,2048]{2,1,0:T(8,128)(2,1)} %get-tuple-element.56.pair_ref, bf16[1536,3840]{1,0:T(8,128)(2,1)} %get-tuple-element.51.w_ref.gate_w.up_w.down_w, f32[512,1536]{1,0:T(8,128)} %get-tuple-element.53.hidden_ref, ...), custom_call_target="tpu_custom_call" | custom-call | flops 12884901888 | bytes 104857600 | tf_op jit(solution)/shard_map/mlp_back/pallas_call | solution.py:1192
  592.4 75.2 %out_back.1 = (bf16[4,512,1536]{2,1,0:T(8,128)(2,1)}, bf16[4,512,384]{2,1,0:T(8,128)(2,1)S(1)}, bf16[3,4,512,128]{3,2,1,0:T(8,128)(2,1)S(1)}, f32[192,1024]{1,0:T(8,128)S(1)}) custom-call(bf16[512,1536]{1,0:T(8,128)(2,1)S(1)} %copy-done.4, bf16[1536,3840]{1,0:T(8,128)(2,1)} %get-tuple-element.51.w_ref.gate_w.up_w.down_w, f32[4,512,384]{2,1,0:T(8,128)} %bitcast.143, ...), custom_call_target="tpu_custom_call" | custom-call | flops 2415919104 | bytes 104857600 | tf_op jit(solution)/shard_map/out_back/pallas_call | solution.py:1272
  667.7 7.4 fusion.12
  675.2 8.7 bitcast_convert_fusion.1
  683.9 3.5 fusion.11
  687.5 2.8 pad_maximum_fusion.1.part_ref
  690.3 218.8 %context_back.1 = (bf16[3,4,3,512,128]{4,3,2,1,0:T(8,128)(2,1)}, f32[3,4,8,512]{3,2,1,0:T(8,128)}, f32[192,1792]{1,0:T(8,128)}) custom-call(bf16[3,4,512,128]{3,2,1,0:T(8,128)(2,1)} %copy-done.9, bf16[3,4,3,512,128]{4,3,2,1,0:T(8,128)(2,1)} %get-tuple-element.61.qkv_ref, f32[3,4,512,128]{3,2,1,0:T(8,128)} %get-tuple-element.62.exact_ref, ...), custom_call_target="tpu_custom_call" | custom-call | flops 32212254720 | bytes 104857600 | tf_op jit(solution)/shard_map/context_back/pallas_call | solution.py:446
  910.8 2.5 copy-done
  914.5 2.1 copy-done.1
  916.7 11.5 %fusion.29 = (bf16[2048,1536]{1,0:T(8,128)(2,1)S(1)}, f32[2048,1536]{1,0:T(8,128)}) fusion(bf16[2048,1024]{1,0:T(8,128)(2,1)S(1)} %bitcast.175, bf16[1536,3840]{1,0:T(8,128)(2,1)} %get-tuple-element.51.w_ref.gate_w.up_w.down_w), kind=kOutput, calls=%fused_computation.91 | convolution fusion | flops 6445596672 | bytes 26214400 | tf_op jit(solution)/shard_map/dot_general | solution.py:22
  930.9 13.2 %convolution_convert_fusion.part_ref = bf16[1536,1280]{1,0:T(8,128)(2,1)} fusion(bf16[2048,1536]{1,0:T(8,128)(2,1)} %bitcast.174, bf16[2048,128]{1,0:T(8,128)(2,1)S(1)} %copy.90, bf16[2048,1152]{1,0:T(8,128)(2,1)} %bitcast.137), kind=kOutput, calls=%fused_computation.1 | convolution fusion | flops 8065515520 | bytes 15466496 | tf_op jit(solution)/shard_map/dot_general | solution.py:22
  944.1 4.0 fusion.3
  949.0 129.6 %last.1 = (bf16[512,1536]{1,0:T(8,128)(2,1)}, f32[192,1280]{1,0:T(8,128)}, f32[8,1536]{1,0:T(8,128)}) custom-call(bf16[4,512,1152]{2,1,0:T(8,128)(2,1)} %copy-done.1, bf16[4,512,384]{2,1,0:T(8,128)(2,1)} %copy-done.8, bf16[4,512,128]{2,1,0:T(8,128)(2,1)} %bitcast.153, bf16[1536,1280]{1,0:T(8,128)(2,1)} %get-tuple-element.47.w_ref.qkv_w.forget_w, ...), custom_call_target="tpu_custom_call" | custom-call | flops 10468982784 | bytes 104857600 | tf_op jit(solution)/shard_map/last/pallas_call | solution.py:1401
  1078.6 3.8 copy.120
  1083.2 2.2 slice.187
  1088.2 1.9 fusion.24
  1091.1 4.0 fusion.7
  1095.1 2.4 copy.121
  (152 shorter events, 22.2 us)
Async XLA Ops:
  3.6 3.4 copy-start.16
  3.6 3.3 copy-start.26
  3.6 4.7 copy-start.31
  3.6 4.8 copy-start.32
  3.6 4.9 copy-start.29
  3.7 5.1 copy-start.21
  3.7 5.1 copy-start.22
  3.7 5.1 copy-start.23
  3.9 424.2 %copy-start.13 = (bf16[512,1536]{1,0:T(8,128)(2,1)}, bf16[512,1536]{1,0:T(8,128)(2,1)S(1)}, u32[]{:S(2)}) copy-start(bf16[512,1536]{1,0:T(8,128)(2,1)S(1)} %fusion.8.grad_ref) | copy-start | bytes 4718596
  3.9 108.3 %collective-permute-start.1 = (bf16[512,1536]{1,0:T(8,128)(2,1)S(1)}, bf16[512,1536]{1,0:T(8,128)(2,1)}, u32[]{:S(2)}, u32[]{:S(2)}) collective-permute-start(bf16[512,1536]{1,0:T(8,128)(2,1)S(1)} %fusion.8.grad_ref), channel_id=1, source_target_pairs={{0,2},{1,3},{2,0},{3,1},{4,6},{5,7},{6,4},{7,5},{8,10},{9,11},{10,... | collective-permute-start | bytes 4718600 | tf_op jit(solution)/shard_map/ppermute | solution.py:1446
  7.0 421.1 %collective-permute-start = (bf16[512,1536]{1,0:T(8,128)(2,1)S(1)}, bf16[512,1536]{1,0:T(8,128)(2,1)}, u32[]{:S(2)}, u32[]{:S(2)}) collective-permute-start(bf16[512,1536]{1,0:T(8,128)(2,1)S(1)} %fusion.8.grad_ref), channel_id=1, source_target_pairs={{0,1},{1,0},{2,3},{3,2},{4,5},{5,4},{6,7},{7,6},{8,9},{9,8},{10,11... | collective-permute-start | bytes 4718600 | tf_op jit(solution)/shard_map/ppermute | solution.py:1442
  90.9 18.2 %copy-start.7 = (f32[1,1536]{1,0:T(1,128)}, f32[1,1536]{1,0:T(1,128)S(1)}, u32[]{:S(2)}) copy-start(f32[1,1536]{1,0:T(1,128)S(1)} %get-tuple-element.143.gain_ref) | copy-start | bytes 18436
  90.9 291.8 %copy-start.6 = (f32[1,1536]{1,0:T(1,128)}, f32[1,1536]{1,0:T(1,128)S(1)}, u32[]{:S(2)}) copy-start(f32[1,1536]{1,0:T(1,128)S(1)} %get-tuple-element.142.gain_ref) | copy-start | bytes 18436
  93.0 16.4 %copy-start.33 = (bf16[6]{0:T(256)(128)(2,1)S(1)}, bf16[6]{0:T(256)(128)(2,1)}, u32[]{:S(2)}) copy-start(bf16[6]{0:T(256)(128)(2,1)} %param.22) | copy-start | bytes 40
  93.0 17.0 %copy-start.20 = (bf16[192,1024]{1,0:T(8,128)(2,1)S(1)}, bf16[192,1024]{1,0:T(8,128)(2,1)}, u32[]{:S(2)}) copy-start(bf16[192,1024]{1,0:T(8,128)(2,1)} %param.26) | copy-start | bytes 1179652
  112.2 315.9 %collective-permute-start.2 = (bf16[512,1536]{1,0:T(8,128)(2,1)}, bf16[512,1536]{1,0:T(8,128)(2,1)S(1)}, u32[]{:S(2)}, u32[]{:S(2)}) collective-permute-start(bf16[512,1536]{1,0:T(8,128)(2,1)} %collective-permute-done.1), channel_id=1, source_target_pairs={{0,1},{1,0},{2,3},{3,2},{4,5},{5,4},{6,7},{7,6},{8,9},{9,8},{10,11... | collective-permute-start | bytes 4718600 | tf_op jit(solution)/shard_map/ppermute | solution.py:1442
  428.0 6.2 copy-start.3
  428.1 6.2 copy-start.10
  667.7 7.5 copy-start.8
  667.7 7.5 copy-start.9
  667.7 7.5 copy-start.14
  667.7 7.5 copy-start.34
  667.7 16.2 %slice-start = ((s8[6291456]{0:T(1024)(128)(4,1)}), s8[4194304]{0:T(1024)(128)(4,1)S(1)}, s32[]{:S(2)}) async-start(s8[6291456]{0:T(1024)(128)(4,1)} %bitcast.171), calls=%async_computation | async-start | bytes 8388608
  675.2 8.7 slice-start.1
  910.8 20.1 %copy-start.19 = (bf16[2048,128]{1,0:T(8,128)(2,1)}, bf16[2048,128]{1,0:T(8,128)(2,1)S(1)}, u32[]{:S(2)}) copy-start(bf16[2048,128]{1,0:T(8,128)(2,1)S(1)} %copy.90) | copy-start | bytes 1572868
  913.3 3.4 copy-start.35
  929.5 14.5 %collective-permute-start.4 = (bf16[512,1536]{1,0:T(8,128)(2,1)}, bf16[512,1536]{1,0:T(8,128)(2,1)}, u32[]{:S(2)}, u32[]{:S(2)}) collective-permute-start(bf16[512,1536]{1,0:T(8,128)(2,1)} %get-tuple-element.109), channel_id=1, source_target_pairs={{0,1},{1,0},{2,3},{3,2},{4,5},{5,4},{6,7},{7,6},{8,9},{9,8},{10,11... | collective-permute-start | bytes 4718600 | tf_op jit(solution)/shard_map/ppermute | solution.py:1442
  929.5 161.5 %collective-permute-start.3 = (bf16[512,1536]{1,0:T(8,128)(2,1)S(1)}, bf16[512,1536]{1,0:T(8,128)(2,1)}, u32[]{:S(2)}, u32[]{:S(2)}) collective-permute-start(bf16[512,1536]{1,0:T(8,128)(2,1)S(1)} %get-tuple-element.108), channel_id=1, source_target_pairs={{0,1},{1,0},{2,3},{3,2},{4,5},{5,4},{6,7},{7,6},{8,9},{9,8},{10,11... | collective-permute-start | bytes 4718600 | tf_op jit(solution)/shard_map/ppermute | solution.py:1442
  948.0 143.0 %collective-permute-start.5 = (bf16[512,1536]{1,0:T(8,128)(2,1)}, bf16[512,1536]{1,0:T(8,128)(2,1)}, u32[]{:S(2)}, u32[]{:S(2)}) collective-permute-start(bf16[512,1536]{1,0:T(8,128)(2,1)} %fusion.3), channel_id=1, source_target_pairs={{0,2},{1,3},{2,0},{3,1},{4,6},{5,7},{6,4},{7,5},{8,10},{9,11},{10,... | collective-permute-start | bytes 4718600 | tf_op jit(solution)/shard_map/ppermute | solution.py:1446
  1078.6 3.9 copy-start.17
  1082.5 8.6 copy-start.27
  1083.2 7.9 copy-start.15
  (12 other events, 22.2 us)

commit v5 on v4

--- a/solution.py
+++ b/solution.py
@@ -245,9 +245,11 @@
     items_ref,
     forget_ref,
     shard_ref,
+    rows_ref,
     back_ref,
     qkv_ref,
     full_ref,
+    table_ref,
     exact_ref,
     lse_ref,
     decay_ref,
@@ -256,9 +258,11 @@
     qkv, forget, out, save_sem = refs[:4]
     sems = refs[4:]
     count, size, _, block, width = items_ref.shape
-    greet_all(group_peers())
+    tp, sibling, across, diagonal = tp_places()
+    greet_all([{"tp": sibling}, {"tp": across}] + group_peers())
     me = lax.axis_index("ctx")
-    gather = WeightGather(shard_ref, full_ref, sems[9:])
+    gather = WeightGather(shard_ref, full_ref, sems[9:14])
+    rows = RowGather(rows_ref, table_ref, sems[14:])
     forgets = Exchange(me, size, forget_ref, forget, sems[0:3])
     inputs = Exchange(me, size, items_ref, qkv, sems[3:6])
     results = Exchange(me, size, out, back_ref, sems[6:9])
@@ -267,8 +271,9 @@
     def _(item):
         forgets.start(item)
 
+    gather.begin()
     inputs.start(0)
-    gather.begin()
+    rows.begin()
 
     @pl.loop(0, count)
     def _(item):
@@ -288,11 +293,18 @@
 
     @pl.loop(0, count)
     def _(item):
+        inputs.arrive(item)
+
         @pl.when(item + 1 < count)
         def _():
             inputs.start(item + 1)
 
-        inputs.arrive(item)
+        for hop in range(1, min(size, count + 1)):
+
+            @pl.when(item == hop - 1)
+            def _(hop=hop):
+                gather.advance(hop)
+
         saving = pltpu.make_async_copy(qkv.at[item], qkv_ref.at[item], save_sem)
         saving.start()
         attend_item(
@@ -300,12 +312,8 @@
         )
         results.start(item)
         saving.wait()
-        for hop in range(1, min(size, count + 1)):
-
-            @pl.when(item == hop - 1)
-            def _(hop=hop):
-                gather.advance(hop)
-
+
+    rows.advance()
     for hop in range(count + 1, size):
         gather.advance(hop)
 
@@ -317,6 +325,7 @@
         results.drain(item)
 
     gather.end()
+    rows.end()
 
 
 def full_block(shape):
@@ -331,7 +340,7 @@
     )
 
 
-def context(items, forget, shard, f_size, head_size, ident):
+def context(items, forget, shard, rows, f_size, head_size, ident):
     count, size, _, block, width = items.shape
     heads = width // head_size
     place = pl.BlockSpec(memory_space=pl.ANY)
@@ -343,12 +352,13 @@
             jax.ShapeDtypeStruct(exact, BF16),
             jax.ShapeDtypeStruct(items.shape, BF16),
             jax.ShapeDtypeStruct((shard.shape[0] * f_size * size, shard.shape[1]), BF16),
+            jax.ShapeDtypeStruct((4,) + rows.shape, BF16),
             jax.ShapeDtypeStruct(exact, F32),
             jax.ShapeDtypeStruct(stat, F32),
             jax.ShapeDtypeStruct(stat, F32),
         ],
-        in_specs=[place, place, place],
-        out_specs=[place, place, place, full_block(exact), full_block(stat), full_block(stat)],
+        in_specs=[place] * 4,
+        out_specs=[place, place, place, place, full_block(exact), full_block(stat), full_block(stat)],
         scratch_shapes=[
             pltpu.VMEM(items.shape, BF16),
             pltpu.VMEM(forget.shape, F32),
@@ -356,11 +366,13 @@
             pltpu.SemaphoreType.DMA,
         ]
         + exchange_sems(count, size) * 3
-        + weight_sems(f_size, size),
+        + weight_sems(f_size, size)
+        + [pltpu.SemaphoreType.DMA((3,))] * 2
+        + [pltpu.SemaphoreType.DMA],
         compiler_params=remote_params(ident, 48),
         cost_estimate=attend_cost(items, heads, 2),
         name="context",
-    )(items, forget, shard)
+    )(items, forget, shard, rows)
 
 
 def context_back_kernel(
@@ -372,17 +384,21 @@
     lse_ref,
     decay_ref,
     part_ref,
+    table_ref,
     back_ref,
     forget_ref,
     sum_ref,
+    rows_ref,
     *refs,
 ):
     grads, dqkv, change, slope, dq_acc, delta = refs[:6]
     sems = refs[6:15]
     count, size, block, width = items_ref.shape
-    greet_all(group_peers())
+    tp, sibling, across, diagonal = tp_places()
+    greet_all([{"tp": sibling}, {"tp": across}] + group_peers())
     me = lax.axis_index("ctx")
-    weights = WeightSum(part_ref, 0, sum_ref, refs[15:])
+    weights = WeightSum(part_ref, 0, sum_ref, refs[15:23])
+    rows = RowSum(table_ref, rows_ref, refs[23:])
     inputs = Exchange(me, size, items_ref, grads, sems[0:3])
     results = Exchange(me, size, dqkv, back_ref, sems[3:6])
     forgets = Exchange(me, size, slope, forget_ref, sems[6:9])
@@ -392,6 +408,7 @@
         inputs.start(item)
 
     weights.begin()
+    rows.begin()
 
     @pl.loop(0, count)
     def _(item):
@@ -418,13 +435,15 @@
             after = total[:, 0:1]
         forgets.start(item)
 
-        @pl.when(item == count - 2)
-        def _():
-            for c in weights.order:
-                weights.receive(c)
-
-    for c in weights.order:
-        weights.advance(c)
+        for turn in range(count):
+
+            @pl.when(item == turn)
+            def _(turn=turn):
+                weights.run_share(turn, count + 1)
+                if turn == 0:
+                    rows.advance()
+
+    weights.run_share(count, count + 1)
 
     @pl.loop(0, count)
     def _(item):
@@ -435,9 +454,10 @@
         forgets.drain(item)
 
     weights.end()
-
-
-def context_back(grads, qkv, exact, lse, decay, part, f_size, head_size, ident):
+    rows.end()
+
+
+def context_back(grads, qkv, exact, lse, decay, part, table, f_size, head_size, ident):
     count, size, _, block, width = qkv.shape
     heads = width // head_size
     place = pl.BlockSpec(memory_space=pl.ANY)
@@ -450,6 +470,7 @@
             jax.ShapeDtypeStruct(qkv.shape, BF16),
             jax.ShapeDtypeStruct(forget, F32),
             jax.ShapeDtypeStruct(total, F32),
+            jax.ShapeDtypeStruct(table.shape[1:], BF16),
         ],
         in_specs=[
             place,
@@ -458,8 +479,9 @@
             full_block(lse.shape),
             full_block(decay.shape),
             place,
-        ],
-        out_specs=[place, place, full_block(total)],
+            place,
+        ],
+        out_specs=[place, place, full_block(total), full_block(table.shape[1:])],
         scratch_shapes=[
             pltpu.VMEM(grads.shape, BF16),
             pltpu.VMEM(qkv.shape, BF16),
@@ -469,14 +491,16 @@
             pltpu.VMEM((8, size * block), F32),
         ]
         + exchange_sems(count, size) * 3
-        + sum_scratch(f_size, size, *total),
-        compiler_params=remote_params(ident, 56),
+        + sum_scratch(f_size, size, *total)
+        + row_sum_scratch(*table.shape[1:]),
+        compiler_params=remote_params(ident, 60),
         cost_estimate=attend_cost(qkv, heads, 5),
         name="context_back",
-    )(grads, qkv, exact, lse, decay, part)
+    )(grads, qkv, exact, lse, decay, part, table)
 
 
 CHUNKS = 4
+HALVES = 2
 
 
 def tp_places():
@@ -705,29 +729,37 @@
         self.f, self.c = lax.axis_index("fsdp"), lax.axis_index("ctx")
         self.sems = sems
 
-    def spot(self, c, f=None):
+    def half(self, h):
+        wide = self.shard.shape[1] // HALVES
+        return pl.ds(h * wide, wide)
+
+    def spot(self, c, h, f=None):
         rows = self.shard.shape[0]
         block = (self.f if f is None else f) * self.c_size + c
-        return self.full.at[pl.ds(pl.multiple_of(block * rows, rows), rows)]
-
-    def along(self, c, hop, side, source=None):
-        source = self.spot(c) if source is None else source
+        return self.full.at[pl.ds(pl.multiple_of(block * rows, rows), rows), self.half(h)]
+
+    def own(self):
+        rows = self.shard.shape[0]
+        block = self.f * self.c_size + self.c
+        target = self.full.at[pl.ds(pl.multiple_of(block * rows, rows), rows)]
+        return pltpu.make_async_copy(self.shard, target, self.sems[4])
+
+    def along(self, c, h, hop, side, first=False):
+        source = self.shard.at[:, self.half(h)] if first else self.spot(c, h)
         peer = {"ctx": self.c + (1 if side else -1)}
-        return moving(
-            source, self.spot(c), self.sems[0].at[side, hop], self.sems[1].at[side, hop], peer
-        )
-
-    def over(self, c, step, source=None):
-        source = self.spot(c) if source is None else source
+        send, recv = self.sems[0].at[side, hop, h], self.sems[1].at[side, hop, h]
+        return moving(source, self.spot(c, h), send, recv, peer)
+
+    def over(self, c, h, step, first=False):
+        source = self.shard.at[:, self.half(h)] if first else self.spot(c, h)
         peer = {"fsdp": lax.rem(self.f + step, self.f_size)}
-        return moving(
-            source, self.spot(c), self.sems[2].at[step, c], self.sems[3].at[step, c], peer
-        )
-
-    def over_arrival(self, c, step):
-        spot = self.spot(c, lax.rem(self.f + self.f_size - step, self.f_size))
+        send, recv = self.sems[2].at[step, c, h], self.sems[3].at[step, c, h]
+        return moving(source, self.spot(c, h), send, recv, peer)
+
+    def over_arrival(self, c, h, step):
+        spot = self.spot(c, h, lax.rem(self.f + self.f_size - step, self.f_size))
         peer = {"fsdp": lax.rem(self.f + step, self.f_size)}
-        return moving(spot, spot, self.sems[2].at[step, c], self.sems[3].at[step, c], peer)
+        return moving(spot, spot, self.sems[2].at[step, c, h], self.sems[3].at[step, c, h], peer)
 
     def can(self, side):
         return self.c + 1 < self.c_size if side else self.c > 0
@@ -736,182 +768,276 @@
         return self.c - hop >= 0 if side else self.c + hop < self.c_size
 
     def begin(self):
-        pltpu.make_async_copy(self.shard, self.spot(self.c), self.sems[4]).start()
-        for side in (1, 0):
-
-            @pl.when(self.can(side))
-            def _(side=side):
-                self.along(self.c, 1, side, self.shard).start()
-
-        for step in range(1, self.f_size):
-            self.over(self.c, step, self.shard).start()
+        self.own().start()
+        for h in range(HALVES):
+            for side in (1, 0):
+
+                @pl.when(self.can(side))
+                def _(side=side):
+                    self.along(self.c, h, 1, side, True).start()
+
+            for step in range(1, self.f_size):
+                self.over(self.c, h, step, True).start()
 
     def advance(self, hop):
-        for side in (1, 0):
-
-            @pl.when(self.holds(hop, side))
-            def _(side=side):
-                c = self.c - hop if side else self.c + hop
-                self.along(c, hop, side).wait_recv()
+        for h in range(HALVES):
+            for side in (1, 0):
+
+                @pl.when(self.holds(hop, side))
+                def _(side=side):
+                    c = self.c - hop if side else self.c + hop
+                    self.along(c, h, hop, side).wait_recv()
+
+                    @pl.when(self.can(side))
+                    def _():
+                        self.along(c, h, hop + 1, side).start()
+
+                    for step in range(1, self.f_size):
+                        self.over(c, h, step).start()
+
+    def end(self):
+        self.own().wait()
+        for h in range(HALVES):
+            for step in range(1, self.f_size):
+                for c in range(self.c_size):
+                    self.over_arrival(c, h, step).wait_recv()
+                    self.over(c, h, step).wait_send()
+            for side in (1, 0):
 
                 @pl.when(self.can(side))
-                def _():
-                    self.along(c, hop + 1, side).start()
-
-                for step in range(1, self.f_size):
-                    self.over(c, step).start()
-
-    def end(self):
-        pltpu.make_async_copy(self.shard, self.spot(self.c), self.sems[4]).wait()
-        for step in range(1, self.f_size):
-            for c in range(self.c_size):
-                self.over_arrival(c, step).wait_recv()
-                self.over(c, step).wait_send()
-        for side in (1, 0):
-
-            @pl.when(self.can(side))
-            def _(side=side):
-                self.along(self.c, 1, side, self.shard).wait_send()
-
-            for hop in range(1, self.c_size):
-
-                @pl.when(self.holds(hop, side) & self.can(side))
-                def _(side=side, hop=hop):
-                    c = self.c - hop if side else self.c + hop
-                    self.along(c, hop + 1, side).wait_send()
+                def _(side=side):
+                    self.along(self.c, h, 1, side, True).wait_send()
+
+                for hop in range(1, self.c_size):
+
+                    @pl.when(self.holds(hop, side) & self.can(side))
+                    def _(side=side, hop=hop):
+                        c = self.c - hop if side else self.c + hop
+                        self.along(c, h, hop + 1, side).wait_send()
 
 
 def weight_sems(f_size, c_size):
     dma = pltpu.SemaphoreType.DMA
-    return [dma((2, c_size + 1))] * 2 + [dma((f_size, c_size))] * 2 + [dma]
+    return [dma((2, c_size + 1, HALVES))] * 2 + [dma((f_size, c_size, HALVES))] * 2 + [dma]
 
 
 class WeightSum:
     def __init__(self, part, first_column, out, refs):
-        self.part, self.out = part, out
+        self.part, self.out, self.first = part, out, first_column
         self.stage, self.total, self.along_in = refs[:3]
         self.own_sem, self.over_send, self.over_recv, self.along_send, self.along_recv = refs[3:]
         self.f_size, self.c_size = lax.axis_size("fsdp"), lax.axis_size("ctx")
         self.f, self.c = lax.axis_index("fsdp"), lax.axis_index("ctx")
-        self.rows, columns = out.shape
-        self.columns = pl.ds(first_column, columns)
-        self.order = [
-            (self.c_size - 1 - i // 2) if i % 2 == 0 else i // 2 for i in range(self.c_size)
-        ]
-
-    def piece(self, f, c):
+        self.rows, self.wide = out.shape[0], out.shape[1] // HALVES
+        ends = [(self.c_size - 1 - i // 2) if i % 2 == 0 else i // 2 for i in range(self.c_size)]
+        self.order = [(c, h) for c in ends for h in range(HALVES)]
+        self.stages = len(self.order) + self.c_size - 1
+
+    def piece(self, f, c, h):
         row = (f * self.c_size + c) * self.rows
-        return self.part.at[pl.ds(pl.multiple_of(row, self.rows), self.rows), self.columns]
-
-    def own(self, c):
-        return pltpu.make_async_copy(self.piece(self.f, c), self.stage.at[c], self.own_sem.at[c])
-
-    def over(self, c, step):
-        f = lax.rem(self.f + step, self.f_size)
+        columns = pl.ds(self.first + h * self.wide, self.wide)
+        return self.part.at[pl.ds(pl.multiple_of(row, self.rows), self.rows), columns]
+
+    def own(self, c, h):
+        n = c * HALVES + h
+        return pltpu.make_async_copy(self.piece(self.f, c, h), self.stage.at[n], self.own_sem.at[n])
+
+    def over(self, c, h, step):
+        f, n = lax.rem(self.f + step, self.f_size), c * HALVES + h
         return moving(
-            self.piece(f, c),
-            self.total.at[step - 1, c],
-            self.over_send.at[step - 1, c],
-            self.over_recv.at[step - 1, c],
+            self.piece(f, c, h),
+            self.total.at[step - 1, n],
+            self.over_send.at[step - 1, n],
+            self.over_recv.at[step - 1, n],
             {"fsdp": f},
         )
 
-    def along(self, c, side, source=None):
-        peer = {"ctx": self.c + (1 if side else -1)}
-        target = self.along_in.at[side, c]
+    def along(self, c, h, side, source=None):
+        peer, n = {"ctx": self.c + (1 if side else -1)}, c * HALVES + h
+        target = self.along_in.at[side, n]
         return moving(
             target if source is None else source,
             target,
-            self.along_send.at[side, c],
-            self.along_recv.at[side, c],
+            self.along_send.at[side, n],
+            self.along_recv.at[side, n],
             peer,
         )
 
+    def launch(self, i):
+        if i < len(self.order):
+            for step in range(1, self.f_size):
+                self.over(*self.order[i], step).start()
+
     def begin(self):
-        for c in self.order:
-            self.own(c).start()
+        for c, h in self.order:
+            self.own(c, h).start()
+        self.launch(0)
+        self.launch(1)
+
+    def receive(self, i):
+        c, h = self.order[i]
+        n = c * HALVES + h
+        self.own(c, h).wait()
+        value = self.stage[n].astype(F32)
+        for step in range(1, self.f_size):
+            self.over(c, h, step).wait_recv()
+        self.launch(i + 2)
+        for step in range(1, self.f_size):
+            value = value + self.total[step - 1, n].astype(F32)
+        self.total[0, n] = value.astype(BF16)
+        for side, end in ((1, 0), (0, self.c_size - 1)):
+            if c != end:
+
+                @pl.when(self.c == end)
+                def _(side=side):
+                    self.along(c, h, side, self.total.at[0, n]).start()
+
+    def hop(self, c, h, side, device):
+        n = c * HALVES + h
+
+        @pl.when(self.c == device)
+        def _():
+            self.along(c, h, side).wait_recv()
+            value = self.total[0, n].astype(F32) + self.along_in[side, n].astype(F32)
+            if device == c:
+                self.total[0, n] = value.astype(BF16)
+            else:
+                self.along_in[side, n] = value.astype(BF16)
+                self.along(c, h, side).start()
+
+    def run(self, n):
+        if n < len(self.order):
+            self.receive(n)
+        for i, (c, h) in enumerate(self.order):
+            if 1 <= n - i <= c:
+                self.hop(c, h, 1, n - i)
+            if 1 <= n - i <= self.c_size - 1 - c:
+                self.hop(c, h, 0, self.c_size - 1 - (n - i))
+
+    def run_share(self, turn, turns):
+        share = -(-self.stages // turns)
+        for n in range(turn * share, min(self.stages, (turn + 1) * share)):
+            self.run(n)
+
+    def end(self):
+        for c in range(self.c_size):
+
+            @pl.when(self.c == c)
+            def _(c=c):
+                for h in range(HALVES):
+                    columns = pl.ds(h * self.wide, self.wide)
+                    self.out[:, columns] = self.total[0, c * HALVES + h].astype(F32)
+
+        for c, h in self.order:
             for step in range(1, self.f_size):
-                self.over(c, step).start()
-
-    def receive(self, c):
-        self.own(c).wait()
-        value = self.stage[c].astype(F32)
-        for step in range(1, self.f_size):
-            self.over(c, step).wait_recv()
-            value = value + self.total[step - 1, c].astype(F32)
-        self.total[0, c] = value.astype(BF16)
-        for side, end in ((1, 0), (0, self.c_size - 1)):
-
-            @pl.when((self.c == end) & (self.c != c))
-            def _(side=side):
-                self.along(c, side, self.total.at[0, c]).start()
-
-    def advance(self, c):
-        for side in (1, 0):
-            comes = (self.c > 0) & (self.c <= c) if side else (self.c >= c) & (self.c < self.c_size - 1)
-
-            @pl.when(comes)
-            def _(side=side):
-                self.along(c, side).wait_recv()
-                value = self.total[0, c].astype(F32) + self.along_in[side, c].astype(F32)
-
-                @pl.when(self.c == c)
-                def _():
-                    self.total[0, c] = value.astype(BF16)
-
-                @pl.when(self.c != c)
-                def _():
-                    self.along_in[side, c] = value.astype(BF16)
-                    self.along(c, side).start()
-
-    def tasks(self):
-        found = []
-        for turn, c in enumerate(self.order):
-            found.append(functools.partial(self.receive, c))
-            if turn:
-                found.append(functools.partial(self.advance, self.order[turn - 1]))
-        return found + [functools.partial(self.advance, self.order[-1])]
-
-    def end(self):
-        self.out[...] = self.total[0, self.c].astype(F32)
-        for c in range(self.c_size):
-            for step in range(1, self.f_size):
-                self.over(c, step).wait_send()
+                self.over(c, h, step).wait_send()
             for side in (1, 0):
 
                 @pl.when(self.c < c if side else self.c > c)
                 def _(side=side):
-                    self.along(c, side).wait_send()
-
-
-SUM_REFS = 8
+                    self.along(c, h, side).wait_send()
 
 
 def sum_scratch(f_size, c_size, rows, columns):
-    dma = pltpu.SemaphoreType.DMA
+    dma, count, wide = pltpu.SemaphoreType.DMA, c_size * HALVES, columns // HALVES
     return (
         [
-            pltpu.VMEM((c_size, rows, columns), BF16),
-            pltpu.VMEM((f_size - 1, c_size, rows, columns), BF16),
-            pltpu.VMEM((2, c_size, rows, columns), BF16),
+            pltpu.VMEM((count, rows, wide), BF16),
+            pltpu.VMEM((f_size - 1, count, rows, wide), BF16),
+            pltpu.VMEM((2, count, rows, wide), BF16),
         ]
-        + [dma((c_size,))]
-        + [dma((f_size - 1, c_size))] * 2
-        + [dma((2, c_size))] * 2
-    )
-
-
-def shared(tasks, turn, turns):
-    share = -(-len(tasks) // turns)
-    for task in tasks[turn * share : (turn + 1) * share]:
-        task()
-
-
-def startup_kernel(rows_ref, shard_ref, all_ref, full_ref, own_sem, *sems):
+        + [dma((count,))]
+        + [dma((f_size - 1, count))] * 2
+        + [dma((2, count))] * 2
+    )
+
+
+class RowGather:
+    def __init__(self, rows, table, sems):
+        self.rows, self.table, self.sems = rows, table, sems
+        _, self.sibling, self.across, _ = tp_places()
+
+    def own(self):
+        return pltpu.make_async_copy(self.rows, self.table.at[0], self.sems[2])
+
+    def copy(self, n):
+        source = self.table.at[2] if n == 2 else self.rows
+        peer = {"tp": self.across if n == 1 else self.sibling}
+        return moving(source, self.table.at[n + 1], self.sems[0].at[n], self.sems[1].at[n], peer)
+
+    def begin(self):
+        self.own().start()
+        self.copy(0).start()
+        self.copy(1).start()
+
+    def advance(self):
+        self.copy(1).wait_recv()
+        self.copy(2).start()
+
+    def end(self):
+        self.own().wait()
+        self.copy(0).wait()
+        self.copy(1).wait_send()
+        self.copy(2).wait()
+
+
+class RowSum:
+    def __init__(self, table, out, refs):
+        self.table, self.out = table, out
+        self.mine, self.near, self.far_out, self.far_in, self.send, self.recv, self.own_sem = refs
+        _, self.sibling, self.across, _ = tp_places()
+
+    def own(self, n):
+        return pltpu.make_async_copy(self.table.at[0 if n else 2], self.mine.at[n], self.own_sem.at[n])
+
+    def copy(self, n):
+        if n == 2:
+            source, target, peer = self.far_out, self.far_in, self.across
+        else:
+            source, target, peer = self.table.at[1 if n else 3], self.near.at[n], self.sibling
+        return moving(source, target, self.send.at[n], self.recv.at[n], {"tp": peer})
+
+    def begin(self):
+        for n in range(2):
+            self.own(n).start()
+            self.copy(n).start()
+
+    def advance(self):
+        self.own(0).wait()
+        self.copy(0).wait_recv()
+        self.far_out[...] = (self.mine[0].astype(F32) + self.near[0].astype(F32)).astype(BF16)
+        self.copy(2).start()
+
+    def end(self):
+        self.own(1).wait()
+        self.copy(1).wait_recv()
+        self.copy(2).wait_recv()
+        total = self.mine[1].astype(F32) + self.near[1].astype(F32)
+        self.out[...] = (total + self.far_in[...].astype(F32)).astype(BF16)
+        for n in range(3):
+            self.copy(n).wait_send()
+
+
+def row_sum_scratch(rows, width):
+    dma, pair, one = pltpu.SemaphoreType.DMA, (2, rows, width), (rows, width)
+    return [pltpu.VMEM(pair, BF16)] * 2 + [pltpu.VMEM(one, BF16)] * 2 + [dma((3,))] * 2 + [dma((2,))]
+
+
+def startup_kernel(rows_ref, shard_ref, gain_ref, all_ref, full_ref, gains_ref, own_sem, *sems):
     me, sibling, across, diagonal = tp_places()
-    greet_all([{"tp": sibling}, {"tp": across}] + group_peers())
+    others = group_peers()
+    greet_all([{"tp": sibling}, {"tp": across}] + others)
     near_send, near_recv, far_send, far_recv, pass_send, pass_recv = sems[:6]
-    gather = WeightGather(shard_ref, full_ref, sems[6:])
+    gather = WeightGather(shard_ref, full_ref, sems[6:11])
+    gain_send, gain_recv, gain_own = sems[11:]
+    spot = gains_ref.at[gather.f * gather.c_size + gather.c]
+    gain_copies = [
+        moving(gain_ref, spot, gain_send.at[n], gain_recv.at[n], peer) for n, peer in enumerate(others)
+    ]
+    for copy in gain_copies:
+        copy.start()
+    own_gain = pltpu.make_async_copy(gain_ref, spot, gain_own)
+    own_gain.start()
     size = rows_ref.shape[0] // CHUNKS
     own = pltpu.make_async_copy(rows_ref, all_ref.at[me], own_sem)
     own.start()
@@ -949,9 +1075,12 @@
         passing(chunk).wait()
     own.wait()
     gather.end()
-
-
-def startup(rows, shard, f_size, c_size, ident):
+    for copy in gain_copies:
+        copy.wait()
+    own_gain.wait()
+
+
+def startup(rows, shard, gains, f_size, c_size, ident):
     place = pl.BlockSpec(memory_space=pl.ANY)
     full = (shard.shape[0] * f_size * c_size, shard.shape[1])
     return pl.pallas_call(
@@ -959,13 +1088,18 @@
         out_shape=[
             jax.ShapeDtypeStruct((4,) + rows.shape, BF16),
             jax.ShapeDtypeStruct(full, BF16),
-        ],
-        in_specs=[place, place],
-        out_specs=[place, place],
-        scratch_shapes=[pltpu.SemaphoreType.DMA] + GATHER_SEMS + weight_sems(f_size, c_size),
+            jax.ShapeDtypeStruct((f_size * c_size,) + gains.shape, F32),
+        ],
+        in_specs=[place] * 3,
+        out_specs=[place] * 3,
+        scratch_shapes=[pltpu.SemaphoreType.DMA]
+        + GATHER_SEMS
+        + weight_sems(f_size, c_size)
+        + [pltpu.SemaphoreType.DMA((f_size * c_size - 1,))] * 2
+        + [pltpu.SemaphoreType.DMA],
         compiler_params=pltpu.CompilerParams(collective_id=ident, has_side_effects=True),
         name="startup",
-    )(rows, shard)
+    )(rows, shard, gains)
 
 
 def whole(shape, column=None):
@@ -1158,7 +1292,6 @@
     greet_all([{"tp": sibling}, {"tp": across}] + group_peers())
     weights = WeightSum(sums_ref, 0, sum_ref, refs[8:])
     weights.begin()
-    tasks = weights.tasks()
     part_ref[...] = jnp.zeros_like(part_ref)
     size = hidden_ref.shape[0] // CHUNKS
 
@@ -1180,7 +1313,7 @@
         branch_ref[span(chunk)] = grad.astype(BF16)
 
     scatter_loop(
-        buffers, sems, partial, finish, relative=True, between=lambda chunk: shared(tasks, chunk, CHUNKS)
+        buffers, sems, partial, finish, relative=True, between=lambda turn: weights.run_share(turn, CHUNKS)
     )
     weights.end()
 
@@ -1232,7 +1365,6 @@
     greet_all([{"tp": sibling}, {"tp": across}] + group_peers())
     weights = WeightSum(sums_ref, sum_ref.shape[1], sum_ref, refs[13:])
     weights.begin()
-    tasks = weights.tasks()
     table[me] = branch_ref[...]
     tp_size, rows, _ = gate_ref.shape
     local, size = rows // seq_count, rows // CHUNKS
@@ -1246,7 +1378,7 @@
         attended = attended_ref[slot, spot].astype(F32)
         logit_ref[slot, spot] = (scaled * attended * (1.0 - gate)).astype(BF16)
 
-    gather_loop(table, sems, compute, between=lambda turn: shared(tasks, turn, CHUNKS))
+    gather_loop(table, sems, compute, between=lambda turn: weights.run_share(turn, CHUNKS))
     copy = pltpu.make_async_copy(table, all_ref, own_sem)
     copy.start()
 
@@ -1368,12 +1500,9 @@
         middle = jnp.mean(scaled * unit, axis=1, keepdims=True)
         out_ref[span(chunk)] = (grad_ref[span(chunk)] + inverse * (scaled - unit * middle)).astype(BF16)
 
-    tasks = weights.tasks()
-
-    def between(chunk):
-        shared(tasks, chunk, CHUNKS)
-
-    scatter_loop(buffers, sems, partial, finish, between=between)
+    scatter_loop(
+        buffers, sems, partial, finish, between=lambda turn: weights.run_share(turn, CHUNKS)
+    )
     near_send, near_recv, group_send, group_recv = vector_sems
     copies = []
     for n, peer in enumerate((sibling, across, diagonal)):
@@ -1436,27 +1565,6 @@
         ),
         name="last",
     )(grad_qkv, grad_logit, grad_forget, full_one, full_one, full_two, x, grad_hidden, gain, part, extra)
-
-
-def to_sibling(values):
-    return lax.ppermute(values, "tp", [(i, i + 1 - 2 * (i % 2)) for i in range(4)])
-
-
-def to_across(values):
-    return lax.ppermute(values, "tp", [(i, (i + 2) % 4) for i in range(4)])
-
-
-def relative_rows(rows):
-    far = to_across(rows)
-    return jnp.stack([rows, to_sibling(rows), far, to_sibling(far)])
-
-
-def summed_rows(partial):
-    own, near, far, corner = (partial[n] for n in range(4))
-    corner = to_sibling(corner.astype(BF16)).astype(F32)
-    near = to_sibling(near.astype(BF16)).astype(F32)
-    far = to_across((far + corner).astype(BF16)).astype(F32)
-    return own + near + far
 
 
 def per_device(
@@ -1511,18 +1619,21 @@
             w_key,
             w_value,
             w_forget,
-            attn_gain[:, None],
-            mlp_gain[:, None],
-            jnp.zeros((attn_gain.shape[0], LANES - head_count - 2), BF16),
+            jnp.zeros((attn_gain.shape[0], LANES - head_count), BF16),
         ],
         axis=1,
     )
     packed_two = jnp.concatenate([w_gate, w_up, w_down, w_out, w_gate_out], axis=1)
     edge = 3 * inner_width
     input_rows = layer_input.transpose(1, 0, 2).reshape(seq_count * local_rows, model_width)
-    input_all, full_one = startup(input_rows, packed_one, fsdp_size, ctx_size, 1)
-    gains = full_one[:, edge + head_count : edge + head_count + 2].astype(F32).T
-    gain_one, gain_two = gains[0:1], gains[1:2]
+    shard_rows = model_width // shard_count
+    own_gains = jnp.stack([attn_gain, mlp_gain]).astype(F32)
+    own_gains = jnp.pad(own_gains, ((0, 6), (0, -shard_rows % LANES)))
+    input_all, full_one, gains = startup(
+        input_rows, packed_one, own_gains, fsdp_size, ctx_size, 1
+    )
+    gain_one = gains[:, 0, :shard_rows].reshape(1, model_width)
+    gain_two = gains[:, 1, :shard_rows].reshape(1, model_width)
     out_column = 3 * hidden // inner_width
 
     def by_sequence(rows):
@@ -1541,7 +1652,6 @@
     ctx_valid = (ctx_pos < lengths[None, :, None]).astype(F32)
 
     grad_out = (valid_rows * by_sequence(cotangent).astype(F32)).astype(BF16)
-    grad_all = relative_rows(lax.optimization_barrier((grad_out, input_all[0, :8]))[0])
     normed_one, forget_rows, items = project(
         input_all, gain_one, full_one, layout, item_count, ctx_size
     )
@@ -1555,8 +1665,8 @@
     picked = jnp.stack([cut[g, :, :, s] for s, g in places])
     picked = picked.reshape(ctx_size, item_count, pair, ctx_rows).transpose(1, 0, 2, 3)
     picked = jnp.pad(picked, ((0, 0), (0, 0), (0, 8 - pair), (0, 0)))
-    attended_items, qkv, full_two, exact, lse, decay = context(
-        items, picked, packed_two, fsdp_size, head_size, 7
+    attended_items, qkv, full_two, grad_all, exact, lse, decay = context(
+        items, picked, packed_two, grad_out, fsdp_size, head_size, 7
     )
     down_w = full_two[:, 2 * hidden : 3 * hidden]
     gate_out_w = full_two[:, 3 * hidden + inner_width :]
@@ -1575,9 +1685,7 @@
     grad_hidden, branch, mlp_gain_part, gate_sum = mlp_back(
         grad_pair, full_two, hidden_state, grad_out, gain_two, gate_up_part, fsdp_size, ctx_size, 4
     )
-    feedforward = summed_rows(dot(inner_flat, down_w, NT).reshape(tp_size, -1, model_width))
-    output = (valid_rows * (hidden_state + feedforward)).astype(BF16)
-
+    feedforward_part = dot(inner_flat, down_w, NT).astype(BF16)
     branch_all, grad_gate_logit, grads, up_sum = out_back(
         branch,
         full_two,
@@ -1602,9 +1710,19 @@
         ],
         axis=1,
     )
-    grad_items, forget_items, out_sum = context_back(
-        grads, qkv, exact, lse, decay, out_part, fsdp_size, head_size, 8
-    )
+    grad_items, forget_items, out_sum, feedforward = context_back(
+        grads,
+        qkv,
+        exact,
+        lse,
+        decay,
+        out_part,
+        feedforward_part.reshape(tp_size, -1, model_width),
+        fsdp_size,
+        head_size,
+        8,
+    )
+    output = (valid_rows * (hidden_state + feedforward.astype(F32))).astype(BF16)
     forget_back = forget_items[:, :, :pair].astype(BF16).transpose(1, 0, 2, 3)
     forget_back = forget_back.reshape(ctx_size * item_count, pair, tp_size, local_rows)
     slots = {place(slot): slot for slot in range(used)}
@@ -1643,7 +1761,6 @@
         6,
     )
     gain_one_sum, gain_two_sum, bias_sum = vectors[0], vectors[1], vectors[2]
-    shard_rows = model_width // shard_count
     attn_gain_grad = lax.dynamic_slice_in_dim(gain_one_sum, shard_index * shard_rows, shard_rows, 0)
     mlp_gain_grad = lax.dynamic_slice_in_dim(gain_two_sum, shard_index * shard_rows, shard_rows, 0)
     forget_bias_grad = lax.dynamic_slice_in_dim(bias_sum, tp_index * head_count, head_count, 0)

time: 1100 us -> 1010 us (0.918)
  Pallas kernels: 957 us -> 880 us
    pallas_call x1, Pallas kernels: 259 us -> 230 us  [context(): pl.pallas_call(functools.partial(context_kernel, heads, head_size), grid=...]
    pallas_call x1, Pallas kernels: 130 us -> 110 us  [last(): pl.pallas_call(last_kernel, grid=(1,), out_shape=[jax.ShapeDtypeStruct(x....]
    pallas_call x1, Pallas kernels: 75.2 us -> 57.6 us  [out_back(): pl.pallas_call(functools.partial(out_back_kernel, layout), grid=(1,), out...]
  transfers between devices with their start and end apart: 6 -> 0, of which waited for: 0 -> 0; matrix products, arithmetic and copies ran while one was open for 5% -> 0% of each run, Pallas kernels for 48% -> 0%
where the time goes in v5:
time: 1010 us; the launch traced here: 1000 us
  Pallas kernels  880 us (87%)
  matrix products  69.2 us (7%)
  local copies, waits for them, and re-layouts  41.7 us (4%)
  other arithmetic  10.6 us (1%)
    pallas_call x1, Pallas kernels, context(): pl.pallas_call(functools.partial(context_kernel, heads, head_size), grid=...  230 us
    pallas_call x1, Pallas kernels, context_back(): pl.pallas_call(functools.partial(context_back_kernel, heads, head_size),...  216 us
    pallas_call x1, Pallas kernels, last(): pl.pallas_call(last_kernel, grid=(1,), out_shape=[jax.ShapeDtypeStruct(x....  110 us
    pallas_call x1, Pallas kernels, mlp_back(): pl.pallas_call(mlp_back_kernel, grid=(1,), out_shape=[jax.ShapeDtypeStruc...  79.9 us
    pallas_call x1, Pallas kernels, startup(): pl.pallas_call(startup_kernel, out_shape=[jax.ShapeDtypeStruct((4,) + row...  71.2 us
    dot_general x7, matrix products, dot(): return lax.dot_general(left, right, dims, preferred_element_type=F32)  69.2 us
    pallas_call x1, Pallas kernels, out_back(): pl.pallas_call(functools.partial(out_back_kernel, layout), grid=(1,), out...  57.6 us
    pallas_call x1, Pallas kernels, mlp(): pl.pallas_call(mlp_kernel, grid=(1,), out_shape=[jax.ShapeDtypeStruct(gra...  52.8 us

profile of v5, /device:TPU:0, one launch (start us, length us, event | category | flops | bytes accessed | tf_op | source)
XLA Modules:
  0.0 1003.2 jit_solution(3249333293383651017)
XLA Ops:
  6.3 1.9 concatenate.15.shard_ref
  8.2 1.1 constant_dynamic-update-slice_fusion.16
  11.5 1.1 copy-done.6
  12.7 1.4 copy.58
  15.8 71.2 %startup.1 = (bf16[4,512,1536]{2,1,0:T(8,128)(2,1)}, bf16[1536,1280]{1,0:T(8,128)(2,1)}, f32[8,8,256]{2,1,0:T(8,128)}) custom-call(bf16[512,1536]{1,0:T(8,128)(2,1)} %bitcast.135, bf16[192,1280]{1,0:T(8,128)(2,1)} %concatenate.15.shard_ref, f32[8,256]{1,0:T(8,128)} %fusion.20.gain_ref), custom_call_target="tpu_custom_call" | custom-call | tf_op jit(solution)/shard_map/startup/pallas_call | solution.py:1086
  88.1 2.1 copy-done.10
  90.3 15.8 %project.1 = (bf16[4,512,1536]{2,1,0:T(8,128)(2,1)}, f32[4,512,128]{2,1,0:T(8,128)S(1)}, bf16[3,4,3,512,128]{4,3,2,1,0:T(8,128)(2,1)}) custom-call(bf16[4,512,1536]{2,1,0:T(8,128)(2,1)} %get-tuple-element.49.x_ref, f32[1,1536]{1,0:T(1,128)S(1)} %reshape_squeeze.6.gain_ref, bf16[1536,1280]{1,0:T(8,128)(2,1)S(1)} %copy-done.10), custom_call_target="tpu_custom_call" | custom-call | flops 8053063680 | bytes 12582912 | tf_op jit(solution)/shard_map/project/pallas_call | solution.py:1139
  106.9 1.4 copy-done.7
  108.3 229.5 %context.1 = (bf16[3,4,512,128]{3,2,1,0:T(8,128)(2,1)S(1)}, bf16[3,4,3,512,128]{4,3,2,1,0:T(8,128)(2,1)}, bf16[1536,3840]{1,0:T(8,128)(2,1)}, bf16[4,512,1536]{2...) custom-call(bf16[3,4,3,512,128]{4,3,2,1,0:T(8,128)(2,1)} %get-tuple-element.53., ...), custom_call_target="tpu_custom_call" | custom-call | flops 12884901888 | bytes 104857600 | tf_op jit(solution)/shard_map/context/pallas_call | solution.py:348
  337.9 7.4 add_divide_fusion
  345.3 45.4 %out_project.1 = (f32[512,1536]{1,0:T(8,128)}, bf16[512,1536]{1,0:T(8,128)(2,1)S(1)}, bf16[4,512,384]{2,1,0:T(8,128)(2,1)S(1)}, bf16[4,512,384]{2,1,0:T(8,128)(2,1)S(1)}) custom-call(bf16[512,1536]{1,0:T(8,128)(2,1)} %bitcast.136, f32[4,512,384]{2,1,0:T(8,128)} %bitcast.138, bf16[1536,3840]{1,0:T(8,128)(2,1)} %get-tuple-element.55.w_ref.gate_w.up_w.down_w, ...), custom_call_target="tpu_custom_call" | custom-call | flops 2415919104 | bytes 104857600 | tf_op jit(solution)/shard_map/out_project/pallas_call | solution.py:1207
  390.8 1.2 copy-done.2
  391.9 1.1 copy-done.13
  393.1 52.8 %mlp.1 = (bf16[4,512,1536]{2,1,0:T(8,128)(2,1)}, bf16[4,512,1024]{2,1,0:T(8,128)(2,1)}, bf16[4,512,2048]{2,1,0:T(8,128)(2,1)}) custom-call(bf16[512,1536]{1,0:T(8,128)(2,1)} %copy-done.13, bf16[4,512,1536]{2,1,0:T(8,128)(2,1)} %get-tuple-element.59.grad_ref, bf16[1536,3840]{1,0:T(8,128)(2,1)} %get-tuple-element.55.w_ref.gate_w.up_w.down_w, ...), custom_call_target="tpu_custom_call" | custom-call | flops 19327352832 | bytes 104857600 | tf_op jit(solution)/shard_map/mlp/pallas_call | solution.py:1263
  446.0 10.0 bitcast_convert_fusion.1
  455.9 15.6 %bitcast_convert_fusion.sums_ref = bf16[1536,2048]{1,0:T(8,128)(2,1)} fusion(bf16[4,512,1536]{2,1,0:T(8,128)(2,1)S(1)} %copy-done.38, bf16[4,512,2048]{2,1,0:T(8,128)(2,1)S(1)} %copy-done.37), kind=kOutput, calls=%fused_computation | convolution fusion | flops 12888047616 | bytes 20971520 | tf_op jit(solution)/shard_map/dot_general | solution.py:22
  471.5 79.9 %mlp_back.1 = (f32[512,1536]{1,0:T(8,128)}, bf16[512,1536]{1,0:T(8,128)(2,1)}, f32[1,1536]{1,0:T(1,128)}, f32[192,1024]{1,0:T(8,128)}) custom-call(bf16[4,512,2048]{2,1,0:T(8,128)(2,1)} %get-tuple-element.60.pair_ref, bf16[1536,3840]{1,0:T(8,128)(2,1)} %get-tuple-element.55.w_ref.gate_w.up_w.down_w, f32[512,1536]{1,0:T(8,128)} %get-tuple-element.57.hidden_ref, ...), custom_call_target="tpu_custom_call" | custom-call | flops 12884901888 | bytes 104857600 | tf_op jit(solution)/shard_map/mlp_back/pallas_call | solution.py:1325
  551.5 1.4 copy-done.3
  552.9 57.6 %out_back.1 = (bf16[4,512,1536]{2,1,0:T(8,128)(2,1)}, bf16[4,512,384]{2,1,0:T(8,128)(2,1)S(1)}, bf16[3,4,512,128]{3,2,1,0:T(8,128)(2,1)S(1)}, f32[192,1024]{1,0:T(8,128)S(1)}) custom-call(bf16[512,1536]{1,0:T(8,128)(2,1)S(1)} %copy-done.3, bf16[1536,3840]{1,0:T(8,128)(2,1)} %get-tuple-element.55.w_ref.gate_w.up_w.down_w, f32[4,512,384]{2,1,0:T(8,128)} %bitcast.139, ...), custom_call_target="tpu_custom_call" | custom-call | flops 2415919104 | bytes 104857600 | tf_op jit(solution)/shard_map/out_back/pallas_call | solution.py:1404
  610.5 7.4 fusion.5
  617.9 6.4 fusion.6
  624.4 3.2 pad_maximum_fusion.part_ref
  628.5 10.5 %convolution_convert_fusion = bf16[2048,1536]{1,0:T(8,128)(2,1)} fusion(bf16[2048,1024]{1,0:T(8,128)(2,1)S(1)} %bitcast.166, bf16[1536,3840]{1,0:T(8,128)(2,1)} %get-tuple-element.55.w_ref.gate_w.up_w.down_w), kind=kOutput, calls=%fused_computation.1 | convolution fusion | flops 6445596672 | bytes 13631488 | tf_op jit(solution)/shard_map/dot_general | solution.py:22
  639.0 216.2 %context_back.1 = (bf16[3,4,3,512,128]{4,3,2,1,0:T(8,128)(2,1)}, f32[3,4,8,512]{3,2,1,0:T(8,128)}, f32[192,1792]{1,0:T(8,128)}, bf16[512,1536]{1,0:T(8,128)(2,1)}) custom-call(bf16[3,4,512,128]{3,2,1,0:T(8,128)(2,1)} %copy-done.12, bf16[3,4,3,512,128]{4,3,2,1,0:T(8,128)(2,1)} %get-tuple-element.65.qkv_ref, f32[3,4,512,128]{3,2,1,0:T(8,128)} %get-tuple-element.66.exact_ref, ...), custom_call_target="tpu_custom_call" | custom-call | flops 32212254720 | bytes 104857600 | tf_op jit(solution)/shard_map/context_back/pallas_call | solution.py:466
  855.2 2.8 multiply_convert_fusion
  858.0 2.4 copy.117
  864.9 2.3 copy-done
  867.3 1.2 assemble.1.qkv_ref
  868.5 2.1 copy-done.1
  870.6 12.0 %convolution_convert_fusion.1.part_ref = bf16[1536,1280]{1,0:T(8,128)(2,1)} fusion(bf16[2048,1536]{1,0:T(8,128)(2,1)} %bitcast.163, bf16[2048,128]{1,0:T(8,128)(2,1)S(1)} %copy.86, bf16[2048,1152]{1,0:T(8,128)(2,1)S(1)} %bitcast.133), kind=kOutput, calls=%fused_computation.2 | convolution fusion | flops 8065515520 | bytes 15466496 | tf_op jit(solution)/shard_map/dot_general | solution.py:22
  882.6 110.4 %last.1 = (bf16[512,1536]{1,0:T(8,128)(2,1)}, f32[192,1280]{1,0:T(8,128)}, f32[8,1536]{1,0:T(8,128)}) custom-call(bf16[4,512,1152]{2,1,0:T(8,128)(2,1)} %copy-done.1, bf16[4,512,384]{2,1,0:T(8,128)(2,1)} %copy-done.11, bf16[4,512,128]{2,1,0:T(8,128)(2,1)} %bitcast.145, bf16[1536,1280]{1,0:T(8,128)(2,1)} %get-tuple-element.51.w_ref.qkv_w.forget_w, ...), custom_call_target="tpu_custom_call" | custom-call | flops 10468982784 | bytes 104857600 | tf_op jit(solution)/shard_map/last/pallas_call | solution.py:1530
  993.0 3.9 copy.116
  (144 shorter events, 22.9 us)
Async XLA Ops:
  0.6 10.8 %copy-start.25 = (bf16[192,384]{1,0:T(8,128)(2,1)S(1)}, bf16[192,384]{1,0:T(8,128)(2,1)}, u32[]{:S(2)}) copy-start(bf16[192,384]{1,0:T(8,128)(2,1)} %param.24) | copy-start | bytes 442372
  0.7 10.8 %copy-start.26 = (bf16[192,384]{1,0:T(8,128)(2,1)S(1)}, bf16[192,384]{1,0:T(8,128)(2,1)}, u32[]{:S(2)}) copy-start(bf16[192,384]{1,0:T(8,128)(2,1)} %param.23) | copy-start | bytes 442372
  0.7 12.0 %copy-start.17 = (bf16[128,4,1536]{2,1,0:T(4,128)(2,1)S(1)}, bf16[128,4,1536]{2,1,0:T(4,128)(2,1)}, u32[]{:S(2)}) copy-start(bf16[128,4,1536]{2,1,0:T(4,128)(2,1)} %param.15) | copy-start | bytes 4718596
  1.5 104.9 %copy-start.32 = (f32[6]{0:T(128)}, f32[6]{0:T(128)S(1)}, u32[]{:S(2)}) copy-start(f32[6]{0:T(128)S(1)} %convert_element_type.95) | copy-start | bytes 76
  4.1 11.4 %copy-start.29 = (f32[512]{0:T(512)}, f32[512]{0:T(512)S(1)}, u32[]{:S(2)}) copy-start(f32[512]{0:T(512)S(1)} %convert_bitcast_fusion.1) | copy-start | bytes 6148
  4.9 101.7 %copy-start.27 = (f32[4,4,128]{2,1,0:T(4,128)}, f32[4,4,128]{2,1,0:T(4,128)S(1)}, u32[]{:S(2)}) copy-start(f32[4,4,128]{2,1,0:T(4,128)S(1)} %compare_convert_fusion) | copy-start | bytes 24580
  8.2 5.8 copy-start.18
  15.8 91.1 %copy-start.4 = (bf16[512,1536]{1,0:T(8,128)(2,1)}, bf16[512,1536]{1,0:T(8,128)(2,1)S(1)}, u32[]{:S(2)}) copy-start(bf16[512,1536]{1,0:T(8,128)(2,1)S(1)} %fusion.3.rows_ref.grad_ref) | copy-start | bytes 4718596
  88.1 257.2 %copy-start.8 = (f32[1,1536]{1,0:T(1,128)}, f32[1,1536]{1,0:T(1,128)S(1)}, u32[]{:S(2)}) copy-start(f32[1,1536]{1,0:T(1,128)S(1)} %reshape_squeeze.7.gain_ref) | copy-start | bytes 18436
  90.3 15.8 %copy-start.9 = (f32[1,1536]{1,0:T(1,128)}, f32[1,1536]{1,0:T(1,128)S(1)}, u32[]{:S(2)}) copy-start(f32[1,1536]{1,0:T(1,128)S(1)} %reshape_squeeze.6.gain_ref) | copy-start | bytes 18436
  106.4 231.4 %copy-start.22 = (f32[2048,6]{0,1:T(8,128)}, f32[2048,6]{0,1:T(8,128)S(1)}, u32[]{:S(2)}) copy-start(f32[2048,6]{0,1:T(8,128)S(1)} %copy.101) | copy-start | bytes 147460
  108.3 229.6 %copy-start.35 = (bf16[4,512,1536]{2,1,0:T(8,128)(2,1)S(1)}, bf16[4,512,1536]{2,1,0:T(8,128)(2,1)}, u32[]{:S(2)}) copy-start(bf16[4,512,1536]{2,1,0:T(8,128)(2,1)} %get-tuple-element.52) | copy-start | bytes 18874372
  337.8 7.5 copy-start.5
  337.8 7.4 copy-start.14
  337.8 7.4 copy-start.15
  345.3 100.6 %slice-start = ((s8[6291456]{0:T(1024)(128)(4,1)}), s8[2097152]{0:T(1024)(128)(4,1)S(1)}, s32[]{:S(2)}) async-start(s8[6291456]{0:T(1024)(128)(4,1)} %bitcast.167), calls=%async_computation | async-start | bytes 4194304
  393.1 52.9 %slice-start.1 = ((s8[6291456]{0:T(1024)(128)(4,1)}), s8[4194304]{0:T(1024)(128)(4,1)S(1)}, s32[]{:S(2)}) async-start(s8[6291456]{0:T(1024)(128)(4,1)} %bitcast.167), calls=%async_computation.1 | async-start | bytes 8388608
  445.9 10.0 copy-start.37
  446.0 10.0 copy-start.38
  610.5 7.4 copy-start.12
  610.5 7.4 copy-start.11
  617.9 6.4 copy-start.16
  624.4 4.2 copy-start.36
  639.0 216.2 %copy-start.30 = (f32[512]{0:T(512)S(1)}, f32[512]{0:T(512)}, u32[]{:S(2)}) copy-start(f32[512]{0:T(512)} %copy-done.29) | copy-start | bytes 6148
  858.0 3.6 copy-start.23
  858.0 3.6 copy-start.28
  858.0 4.0 copy-start.31
  858.0 4.0 copy-start.34
  858.0 5.0 copy-start.19
  863.0 5.5 copy-start.24
  993.0 6.7 copy-start.20
  993.0 8.3 copy-start.21
  (9 other events, 16.3 us)

commit v6 on v5

--- a/solution.py
+++ b/solution.py
@@ -245,10 +245,12 @@
     items_ref,
     forget_ref,
     shard_ref,
+    out_shard_ref,
     rows_ref,
     back_ref,
     qkv_ref,
     full_ref,
+    full_out_ref,
     table_ref,
     exact_ref,
     lse_ref,
@@ -261,8 +263,11 @@
     tp, sibling, across, diagonal = tp_places()
     greet_all([{"tp": sibling}, {"tp": across}] + group_peers())
     me = lax.axis_index("ctx")
-    gather = WeightGather(shard_ref, full_ref, sems[9:14])
-    rows = RowGather(rows_ref, table_ref, sems[14:])
+    gathers = (
+        WeightGather(out_shard_ref, full_out_ref, sems[9:14]),
+        WeightGather(shard_ref, full_ref, sems[14:19]),
+    )
+    rows = RowGather(rows_ref, table_ref, sems[19:])
     forgets = Exchange(me, size, forget_ref, forget, sems[0:3])
     inputs = Exchange(me, size, items_ref, qkv, sems[3:6])
     results = Exchange(me, size, out, back_ref, sems[6:9])
@@ -271,7 +276,8 @@
     def _(item):
         forgets.start(item)
 
-    gather.begin()
+    for gather in gathers:
+        gather.begin()
     inputs.start(0)
     rows.begin()
 
@@ -303,7 +309,8 @@
 
             @pl.when(item == hop - 1)
             def _(hop=hop):
-                gather.advance(hop)
+                for gather in gathers:
+                    gather.advance(hop)
 
         saving = pltpu.make_async_copy(qkv.at[item], qkv_ref.at[item], save_sem)
         saving.start()
@@ -315,7 +322,8 @@
 
     rows.advance()
     for hop in range(count + 1, size):
-        gather.advance(hop)
+        for gather in gathers:
+            gather.advance(hop)
 
     @pl.loop(0, count)
     def _(item):
@@ -324,7 +332,8 @@
         results.arrive(item)
         results.drain(item)
 
-    gather.end()
+    for gather in gathers:
+        gather.end()
     rows.end()
 
 
@@ -340,7 +349,7 @@
     )
 
 
-def context(items, forget, shard, rows, f_size, head_size, ident):
+def context(items, forget, shard, out_shard, rows, f_size, head_size, ident):
     count, size, _, block, width = items.shape
     heads = width // head_size
     place = pl.BlockSpec(memory_space=pl.ANY)
@@ -352,13 +361,14 @@
             jax.ShapeDtypeStruct(exact, BF16),
             jax.ShapeDtypeStruct(items.shape, BF16),
             jax.ShapeDtypeStruct((shard.shape[0] * f_size * size, shard.shape[1]), BF16),
+            jax.ShapeDtypeStruct((shard.shape[0] * f_size * size, out_shard.shape[1]), BF16),
             jax.ShapeDtypeStruct((4,) + rows.shape, BF16),
             jax.ShapeDtypeStruct(exact, F32),
             jax.ShapeDtypeStruct(stat, F32),
             jax.ShapeDtypeStruct(stat, F32),
         ],
-        in_specs=[place] * 4,
-        out_specs=[place, place, place, place, full_block(exact), full_block(stat), full_block(stat)],
+        in_specs=[place] * 5,
+        out_specs=[place, place, place, place, place, full_block(exact), full_block(stat), full_block(stat)],
         scratch_shapes=[
             pltpu.VMEM(items.shape, BF16),
             pltpu.VMEM(forget.shape, F32),
@@ -366,13 +376,13 @@
             pltpu.SemaphoreType.DMA,
         ]
         + exchange_sems(count, size) * 3
-        + weight_sems(f_size, size)
+        + weight_sems(f_size, size) * 2
         + [pltpu.SemaphoreType.DMA((3,))] * 2
         + [pltpu.SemaphoreType.DMA],
         compiler_params=remote_params(ident, 48),
         cost_estimate=attend_cost(items, heads, 2),
         name="context",
-    )(items, forget, shard, rows)
+    )(items, forget, shard, out_shard, rows)
 
 
 def context_back_kernel(
@@ -403,16 +413,18 @@
     results = Exchange(me, size, dqkv, back_ref, sems[3:6])
     forgets = Exchange(me, size, slope, forget_ref, sems[6:9])
 
-    @pl.loop(0, count)
-    def _(item):
-        inputs.start(item)
-
+    inputs.start(0)
     weights.begin()
     rows.begin()
 
     @pl.loop(0, count)
     def _(item):
         inputs.arrive(item)
+
+        @pl.when(item + 1 < count)
+        def _():
+            inputs.start(item + 1)
+
         attend_item_back(
             qkv_ref.at[item],
             grads.at[item],
@@ -599,10 +611,8 @@
         lax.fori_loop(0, 4 * CHUNKS, body, 0)
     else:
         lax.fori_loop(0, 2 * CHUNKS, body, 0)
-        for turn in range(CHUNKS):
-            between(turn)
-            first = 2 * (CHUNKS + turn)
-            lax.fori_loop(first, first + 2, body, 0)
+        between()
+        lax.fori_loop(2 * CHUNKS, 4 * CHUNKS, body, 0)
     near.wait_send()
     for chunk in range(CHUNKS):
         far(chunk).wait_send()
@@ -663,6 +673,7 @@
         @pl.when(phase == 3)
         def _():
             near(1, chunk).wait_recv()
+
             far(chunk).wait_recv()
             finish(chunk, value + near_in[1, spot].astype(F32) + far_in[spot].astype(F32))
 
@@ -671,10 +682,10 @@
     if between is None:
         lax.fori_loop(0, 4 * CHUNKS, body, 0)
     else:
-        lax.fori_loop(0, 3 * CHUNKS, body, 0)
-        for chunk in range(CHUNKS):
-            between(chunk)
-            lax.fori_loop(3 * CHUNKS + chunk, 3 * CHUNKS + chunk + 1, body, 0)
+        lax.fori_loop(0, 2 * CHUNKS, body, 0)
+        for phase in (2, 3):
+            between(phase)
+            lax.fori_loop(phase * CHUNKS, (phase + 1) * CHUNKS, body, 0)
     for chunk in range(CHUNKS):
         near(0, chunk).wait_send()
         near(1, chunk).wait_send()
@@ -914,10 +925,13 @@
             if 1 <= n - i <= self.c_size - 1 - c:
                 self.hop(c, h, 0, self.c_size - 1 - (n - i))
 
+    def run_to(self, first, last):
+        for n in range(min(first, self.stages), min(last, self.stages)):
+            self.run(n)
+
     def run_share(self, turn, turns):
         share = -(-self.stages // turns)
-        for n in range(turn * share, min(self.stages, (turn + 1) * share)):
-            self.run(n)
+        self.run_to(turn * share, (turn + 1) * share)
 
     def end(self):
         for c in range(self.c_size):
@@ -950,6 +964,19 @@
         + [dma((f_size - 1, count))] * 2
         + [dma((2, count))] * 2
     )
+
+
+class Fetch:
+    def __init__(self, pairs, sem):
+        self.copies = [
+            pltpu.make_async_copy(source, target, sem.at[n]) for n, (source, target) in enumerate(pairs)
+        ]
+        for copy in self.copies:
+            copy.start()
+
+    def wait(self):
+        for copy in self.copies:
+            copy.wait()
 
 
 class RowGather:
@@ -1058,14 +1085,15 @@
         spot = all_ref.at[across, span(chunk)]
         return sending(spot, spot, pass_send.at[chunk], pass_recv.at[chunk], sibling)
 
-    for chunk in range(CHUNKS):
-        far(chunk).start()
     gather.begin()
+    far(0).start()
     near = sending(rows_ref, all_ref.at[me], near_send, near_recv, sibling)
     near.start()
     for turn in range(max(CHUNKS, gather.c_size - 1)):
         if turn < CHUNKS:
             far(turn).wait_recv()
+            if turn + 1 < CHUNKS:
+                far(turn + 1).start()
             passing(turn).start()
         if turn + 1 < gather.c_size:
             gather.advance(turn + 1)
@@ -1162,13 +1190,15 @@
     )(x_all, gain, full_one)
 
 
-def out_kernel(layout, x_ref, gate_ref, w_ref, gain_ref, items, *refs):
+def out_kernel(layout, x_ref, gate_ref, w_ref, gain_ref, items, shard_ref, *refs):
     seq_count, groups, width, places = layout
-    hidden_ref, normed_ref, attended_ref, mixed_ref = refs[:4]
-    buffers, sems = refs[4:8], refs[8:]
+    hidden_ref, normed_ref, attended_ref, mixed_ref, full_ref = refs[:5]
+    buffers, sems = refs[5:9], refs[9:13]
     count = items.shape[0]
     me, sibling, across, diagonal = tp_places()
-    greet((sibling, across))
+    greet_all([{"tp": sibling}, {"tp": across}] + group_peers())
+    gather = WeightGather(shard_ref, full_ref, refs[13:])
+    gather.begin()
     tp_size, rows, _ = gate_ref.shape
     local = rows // seq_count
 
@@ -1196,10 +1226,18 @@
         inverse = lax.rsqrt(jnp.mean(hidden * hidden, axis=1, keepdims=True) + epsilon)
         normed_ref[span(chunk)] = (hidden * inverse * gain_ref[...]).astype(BF16)
 
-    scatter_loop(buffers, sems, partial, finish)
-
-
-def out_project(x, gate, full_two, column, gain, items, layout, ident):
+    def between(phase):
+        if phase == 2:
+            gather.advance(1)
+        else:
+            for hop in range(2, gather.c_size):
+                gather.advance(hop)
+
+    scatter_loop(buffers, sems, partial, finish, between=between)
+    gather.end()
+
+
+def out_project(x, gate, full_out, gain, items, shard, layout, f_size, c_size, ident):
     seq_count, groups, width, places = layout
     rows, model_width = x.shape
     inner = groups * width
@@ -1212,22 +1250,32 @@
             jax.ShapeDtypeStruct(x.shape, BF16),
             jax.ShapeDtypeStruct(gate.shape, BF16),
             jax.ShapeDtypeStruct(gate.shape, BF16),
+            jax.ShapeDtypeStruct((model_width, shard.shape[1]), BF16),
         ],
         in_specs=[
             whole(x.shape),
             whole(gate.shape),
-            whole((model_width, inner), column),
+            whole((model_width, inner), 0),
             whole(gain.shape),
             whole(items.shape),
-        ],
-        out_specs=[whole(x.shape), whole(x.shape), whole(gate.shape), whole(gate.shape)],
-        scratch_shapes=scatter_buffers(rows, model_width) + SCATTER_SEMS,
+            pl.BlockSpec(memory_space=pl.ANY),
+        ],
+        out_specs=[
+            whole(x.shape),
+            whole(x.shape),
+            whole(gate.shape),
+            whole(gate.shape),
+            pl.BlockSpec(memory_space=pl.ANY),
+        ],
+        scratch_shapes=scatter_buffers(rows, model_width)
+        + SCATTER_SEMS
+        + weight_sems(f_size, c_size),
         compiler_params=remote_params(ident, 48),
         cost_estimate=pl.CostEstimate(
             flops=2 * gate.size * model_width, bytes_accessed=100 << 20, transcendentals=0
         ),
         name="out_project",
-    )(x, gate, full_two, gain, items)
+    )(x, gate, full_out, gain, items, shard)
 
 
 def mlp_kernel(normed_ref, grad_ref, gate_w, up_w, down_w, all_ref, inner_ref, pair_ref, table, own_sem, *sems):
@@ -1257,7 +1305,7 @@
     copy.wait()
 
 
-def mlp(normed, grad_all, full_two, hidden, ident):
+def mlp(normed, grad_all, full_two, full_down, hidden, ident):
     tp_size, rows, model_width = grad_all.shape
     total = tp_size * rows
     return pl.pallas_call(
@@ -1269,7 +1317,7 @@
             jax.ShapeDtypeStruct((tp_size, rows, 2 * hidden), BF16),
         ],
         in_specs=[whole(normed.shape), whole(grad_all.shape)]
-        + [whole((model_width, hidden), column) for column in range(3)],
+        + [whole((model_width, hidden), column) for column in (0, 1, 0)],
         out_specs=[
             pl.BlockSpec(memory_space=pl.ANY),
             whole((tp_size, rows, hidden)),
@@ -1281,17 +1329,29 @@
             flops=6 * total * model_width * hidden, bytes_accessed=100 << 20, transcendentals=total * hidden
         ),
         name="mlp",
-    )(normed, grad_all, full_two, full_two, full_two)
+    )(normed, grad_all, full_two, full_two, full_down)
 
 
 def mlp_back_kernel(
-    pair_ref, w_ref, hidden_ref, grad_ref, gain_ref, sums_ref, out_ref, branch_ref, part_ref, sum_ref, *refs
+    pair_hbm, w_hbm, hidden_hbm, grad_hbm, gain_ref, sums_ref, out_ref, branch_ref, part_ref, sum_ref, *refs
 ):
     buffers, sems = refs[:4], refs[4:8]
+    pair_ref, w_ref, hidden_ref, grad_ref, fetch_sem = refs[8:13]
+    columns = pl.ds(0, w_ref.shape[1])
+    fetch = Fetch(
+        [
+            (pair_hbm, pair_ref),
+            (w_hbm.at[:, columns], w_ref),
+            (hidden_hbm, hidden_ref),
+            (grad_hbm, grad_ref),
+        ],
+        fetch_sem,
+    )
     me, sibling, across, diagonal = tp_places()
     greet_all([{"tp": sibling}, {"tp": across}] + group_peers())
-    weights = WeightSum(sums_ref, 0, sum_ref, refs[8:])
+    weights = WeightSum(sums_ref, 0, sum_ref, refs[13:])
     weights.begin()
+    fetch.wait()
     part_ref[...] = jnp.zeros_like(part_ref)
     size = hidden_ref.shape[0] // CHUNKS
 
@@ -1312,15 +1372,20 @@
         out_ref[span(chunk)] = grad
         branch_ref[span(chunk)] = grad.astype(BF16)
 
-    scatter_loop(
-        buffers, sems, partial, finish, relative=True, between=lambda turn: weights.run_share(turn, CHUNKS)
-    )
+    def between(phase):
+        if phase == 2:
+            weights.run_to(0, 3)
+        else:
+            weights.run_to(3, weights.stages)
+
+    scatter_loop(buffers, sems, partial, finish, relative=True, between=between)
     weights.end()
 
 
 def mlp_back(pair, full_two, hidden_state, grad_out, gain, part, f_size, c_size, ident):
     tp_size, rows, wide = pair.shape
     model_width = hidden_state.shape[1]
+    place = pl.BlockSpec(memory_space=pl.ANY)
     total = (part.shape[0] // (f_size * c_size), part.shape[1] // 2)
     return pl.pallas_call(
         mlp_back_kernel,
@@ -1332,12 +1397,12 @@
             jax.ShapeDtypeStruct(total, F32),
         ],
         in_specs=[
-            whole(pair.shape),
-            whole((model_width, wide), 0),
-            whole(hidden_state.shape),
-            whole(grad_out.shape),
+            place,
+            place,
+            place,
+            place,
             whole(gain.shape),
-            pl.BlockSpec(memory_space=pl.ANY),
+            place,
         ],
         out_specs=[
             whole(hidden_state.shape),
@@ -1347,8 +1412,15 @@
         ],
         scratch_shapes=scatter_buffers(rows, model_width)
         + SCATTER_SEMS
+        + [
+            pltpu.VMEM(pair.shape, BF16),
+            pltpu.VMEM((model_width, wide), BF16),
+            pltpu.VMEM(hidden_state.shape, F32),
+            pltpu.VMEM(grad_out.shape, BF16),
+            pltpu.SemaphoreType.DMA((4,)),
+        ]
         + sum_scratch(f_size, c_size, *total),
-        compiler_params=remote_params(ident, 56),
+        compiler_params=remote_params(ident, 60),
         cost_estimate=pl.CostEstimate(
             flops=2 * pair.size * model_width, bytes_accessed=100 << 20, transcendentals=0
         ),
@@ -1378,7 +1450,7 @@
         attended = attended_ref[slot, spot].astype(F32)
         logit_ref[slot, spot] = (scaled * attended * (1.0 - gate)).astype(BF16)
 
-    gather_loop(table, sems, compute, between=lambda turn: weights.run_share(turn, CHUNKS))
+    gather_loop(table, sems, compute, between=lambda: weights.run_share(0, 1))
     copy = pltpu.make_async_copy(table, all_ref, own_sem)
     copy.start()
 
@@ -1394,7 +1466,7 @@
     weights.end()
 
 
-def out_back(branch, full_two, column, gate, attended, part, layout, item_count, f_size, ctx_size, ident):
+def out_back(branch, full_out, gate, attended, part, layout, item_count, f_size, ctx_size, ident):
     seq_count, groups, width, places = layout
     rows, model_width = branch.shape
     tp_size, _, inner = gate.shape
@@ -1412,7 +1484,7 @@
         ],
         in_specs=[
             whole(branch.shape),
-            whole((model_width, inner), column),
+            whole((model_width, inner), 0),
             whole(gate.shape),
             whole(attended.shape),
             pl.BlockSpec(memory_space=pl.ANY),
@@ -1426,7 +1498,7 @@
             flops=2 * gate.size * model_width, bytes_accessed=100 << 20, transcendentals=0
         ),
         name="out_back",
-    )(branch, full_two, gate, attended, part)
+    )(branch, full_out, gate, attended, part)
 
 
 def assemble_kernel(layout, items, out_ref):
@@ -1457,14 +1529,13 @@
 
 
 def last_kernel(
-    qkv_ref,
-    logit_ref,
-    forget_ref,
-    qkv_w,
-    forget_w,
-    gate_w,
-    x_ref,
-    grad_ref,
+    qkv_hbm,
+    logit_hbm,
+    forget_hbm,
+    qkv_w_hbm,
+    gate_w_hbm,
+    x_hbm,
+    grad_hbm,
     gain_ref,
     part_ref,
     extra_ref,
@@ -1474,12 +1545,28 @@
     *refs,
 ):
     buffers, sems, (mine, near_in, group_in) = refs[:4], refs[4:8], refs[8:11]
-    vector_sems, sum_refs = refs[11:15], refs[15:]
+    vector_sems = refs[11:15]
+    qkv_ref, logit_ref, forget_ref, qkv_w, gate_w, x_ref, grad_ref, fetch_sem = refs[15:23]
+    inner = gate_w.shape[1]
+    fetch = Fetch(
+        [
+            (qkv_hbm, qkv_ref),
+            (qkv_w_hbm, qkv_w),
+            (logit_hbm, logit_ref),
+            (forget_hbm, forget_ref),
+            (gate_w_hbm.at[:, pl.ds(inner, inner)], gate_w),
+            (x_hbm, x_ref),
+            (grad_hbm, grad_ref),
+        ],
+        fetch_sem,
+    )
     me, sibling, across, diagonal = tp_places()
     others = group_peers()
     greet_all([{"tp": sibling}, {"tp": across}, {"tp": diagonal}] + others)
-    weights = WeightSum(part_ref, 0, sum_ref, sum_refs)
+    weights = WeightSum(part_ref, 0, sum_ref, refs[23:])
     weights.begin()
+    fetch.wait()
+    wide = qkv_ref.shape[2]
     mine[...] = extra_ref[...]
     size = x_ref.shape[0] // CHUNKS
 
@@ -1487,9 +1574,9 @@
         return pl.ds(pl.multiple_of(chunk * size, size), size)
 
     def partial(slot, chunk):
-        value = dot(qkv_ref[slot, span(chunk)], qkv_w[...], NT)
+        value = dot(qkv_ref[slot, span(chunk)], qkv_w[:, :wide], NT)
         value = value + dot(logit_ref[slot, span(chunk)], gate_w[...], NT)
-        return value + dot(forget_ref[slot, span(chunk)], forget_w[...], NT)
+        return value + dot(forget_ref[slot, span(chunk)], qkv_w[:, wide:], NT)
 
     def finish(chunk, total):
         x = x_ref[span(chunk)].astype(F32)
@@ -1500,14 +1587,22 @@
         middle = jnp.mean(scaled * unit, axis=1, keepdims=True)
         out_ref[span(chunk)] = (grad_ref[span(chunk)] + inverse * (scaled - unit * middle)).astype(BF16)
 
-    scatter_loop(
-        buffers, sems, partial, finish, between=lambda turn: weights.run_share(turn, CHUNKS)
-    )
+    stages = weights.stages
+    late = max(3, stages - 4)
+
+    def between(phase):
+        if phase == 2:
+            weights.run_to(0, 3)
+        else:
+            weights.run_to(3, late)
+
+    scatter_loop(buffers, sems, partial, finish, between=between)
     near_send, near_recv, group_send, group_recv = vector_sems
     copies = []
     for n, peer in enumerate((sibling, across, diagonal)):
         copies.append(sending(mine, near_in.at[n], near_send.at[n], near_recv.at[n], peer))
         copies[-1].start()
+    weights.run_to(late, late + 2)
     for copy in copies:
         copy.wait()
     vector_ref[...] = mine[...] + near_in[0] + near_in[1] + near_in[2]
@@ -1516,17 +1611,19 @@
     for n, peer in enumerate(others):
         copies.append(moving(mine, group_in.at[n], group_send.at[n], group_recv.at[n], peer))
         copies[-1].start()
+    weights.run_to(late + 2, stages)
     for n, copy in enumerate(copies):
         copy.wait()
         vector_ref[...] += group_in[n]
     weights.end()
 
 
-def last(grad_qkv, grad_logit, grad_forget, full_one, full_two, column, x, grad_hidden, gain, part, extra, f_size, c_size, ident):
+def last(grad_qkv, grad_logit, grad_forget, full_one, full_out, x, grad_hidden, gain, part, extra, f_size, c_size, ident):
     rows, model_width = x.shape
     wide, inner = grad_qkv.shape[2], grad_logit.shape[2]
     shard, columns = part.shape[0] // (f_size * c_size), part.shape[1]
     dma = pltpu.SemaphoreType.DMA
+    place = pl.BlockSpec(memory_space=pl.ANY)
     return pl.pallas_call(
         last_kernel,
         grid=(1,),
@@ -1536,16 +1633,15 @@
             jax.ShapeDtypeStruct(extra.shape, F32),
         ],
         in_specs=[
-            whole(grad_qkv.shape),
-            whole(grad_logit.shape),
-            whole(grad_forget.shape),
-            whole((model_width, wide), 0),
-            whole((model_width, LANES), wide // LANES),
-            whole((model_width, inner), column),
-            whole(x.shape),
-            whole(x.shape),
+            place,
+            place,
+            place,
+            place,
+            place,
+            place,
+            place,
             whole(gain.shape),
-            pl.BlockSpec(memory_space=pl.ANY),
+            place,
             whole(extra.shape),
         ],
         out_specs=[whole(x.shape), whole((shard, columns)), whole(extra.shape)],
@@ -1558,13 +1654,23 @@
         ]
         + [dma((3,))] * 2
         + [dma((f_size * c_size - 1,))] * 2
+        + [
+            pltpu.VMEM(grad_qkv.shape, BF16),
+            pltpu.VMEM(grad_logit.shape, BF16),
+            pltpu.VMEM(grad_forget.shape, BF16),
+            pltpu.VMEM(full_one.shape, BF16),
+            pltpu.VMEM((model_width, inner), BF16),
+            pltpu.VMEM(x.shape, BF16),
+            pltpu.VMEM(x.shape, F32),
+            dma((7,)),
+        ]
         + sum_scratch(f_size, c_size, shard, columns),
         compiler_params=remote_params(ident, 60),
         cost_estimate=pl.CostEstimate(
             flops=8 * rows * model_width * (wide + inner + LANES), bytes_accessed=100 << 20, transcendentals=0
         ),
         name="last",
-    )(grad_qkv, grad_logit, grad_forget, full_one, full_one, full_two, x, grad_hidden, gain, part, extra)
+    )(grad_qkv, grad_logit, grad_forget, full_one, full_out, x, grad_hidden, gain, part, extra)
 
 
 def per_device(
@@ -1623,7 +1729,8 @@
         ],
         axis=1,
     )
-    packed_two = jnp.concatenate([w_gate, w_up, w_down, w_out, w_gate_out], axis=1)
+    packed_two = jnp.concatenate([w_gate, w_up], axis=1)
+    packed_out = jnp.concatenate([w_out, w_gate_out], axis=1)
     edge = 3 * inner_width
     input_rows = layer_input.transpose(1, 0, 2).reshape(seq_count * local_rows, model_width)
     shard_rows = model_width // shard_count
@@ -1634,7 +1741,6 @@
     )
     gain_one = gains[:, 0, :shard_rows].reshape(1, model_width)
     gain_two = gains[:, 1, :shard_rows].reshape(1, model_width)
-    out_column = 3 * hidden // inner_width
 
     def by_sequence(rows):
         return rows.transpose(1, 0, 2).reshape(seq_count * local_rows, model_width)
@@ -1665,17 +1771,25 @@
     picked = jnp.stack([cut[g, :, :, s] for s, g in places])
     picked = picked.reshape(ctx_size, item_count, pair, ctx_rows).transpose(1, 0, 2, 3)
     picked = jnp.pad(picked, ((0, 0), (0, 0), (0, 8 - pair), (0, 0)))
-    attended_items, qkv, full_two, grad_all, exact, lse, decay = context(
-        items, picked, packed_two, grad_out, fsdp_size, head_size, 7
-    )
-    down_w = full_two[:, 2 * hidden : 3 * hidden]
-    gate_out_w = full_two[:, 3 * hidden + inner_width :]
+    attended_items, qkv, full_two, full_out, grad_all, exact, lse, decay = context(
+        items, picked, packed_two, packed_out, grad_out, fsdp_size, head_size, 7
+    )
+    gate_out_w = full_out[:, inner_width:]
     gate_logit = dot(normed_flat, gate_out_w, NN)
     out_gate = jax.nn.sigmoid(gate_logit).reshape(tp_size, -1, inner_width)
-    hidden_state, normed_two, attended, mixed = out_project(
-        input_rows, out_gate, full_two, out_column, gain_two, attended_items, layout, 2
-    )
-    normed_two_all, inner_act, grad_pair = mlp(normed_two, grad_all, full_two, hidden, 3)
+    hidden_state, normed_two, attended, mixed, down_w = out_project(
+        input_rows,
+        out_gate,
+        full_out,
+        gain_two,
+        attended_items,
+        w_down,
+        layout,
+        fsdp_size,
+        ctx_size,
+        2,
+    )
+    normed_two_all, inner_act, grad_pair = mlp(normed_two, grad_all, full_two, down_w, hidden, 3)
     normed_two_flat = normed_two_all.reshape(all_rows, model_width)
     inner_flat = inner_act.reshape(all_rows, hidden)
     grad_pair_flat = grad_pair.reshape(all_rows, 2 * hidden)
@@ -1688,8 +1802,7 @@
     feedforward_part = dot(inner_flat, down_w, NT).astype(BF16)
     branch_all, grad_gate_logit, grads, up_sum = out_back(
         branch,
-        full_two,
-        out_column,
+        full_out,
         out_gate,
         attended,
         gate_up_part,
@@ -1749,8 +1862,7 @@
         grad_gate_logit,
         grad_forget_rows.reshape(tp_size, -1, LANES),
         full_one,
-        full_two,
-        out_column + 1,
+        full_out,
         input_rows,
         grad_hidden,
         gain_one,

time: 1010 us -> 955 us (0.946)
  Pallas kernels: 880 us -> 832 us
    pallas_call x1, Pallas kernels: 230 us -> 200 us  [context(): pl.pallas_call(functools.partial(context_kernel, heads, head_size), grid=...]
    pallas_call x1, Pallas kernels: 110 us -> 94 us  [last(): pl.pallas_call(last_kernel, grid=(1,), out_shape=[jax.ShapeDtypeStruct(x....]
    unnamed x102 -> x86, local copies, waits for them, and re-layouts: 20.7 us -> 16.2 us
where the time goes in v6:
time: 955 us; the launch traced here: 952 us
  Pallas kernels  832 us (87%)
  matrix products  66.3 us (7%)
  local copies, waits for them, and re-layouts  37.4 us (4%)
  other arithmetic  14.4 us (2%)
    pallas_call x1, Pallas kernels, context_back(): pl.pallas_call(functools.partial(context_back_kernel, heads, head_size),...  210 us
    pallas_call x1, Pallas kernels, context(): pl.pallas_call(functools.partial(context_kernel, heads, head_size), grid=...  200 us
    pallas_call x1, Pallas kernels, last(): pl.pallas_call(last_kernel, grid=(1,), out_shape=[jax.ShapeDtypeStruct(x....  94 us
    pallas_call x1, Pallas kernels, mlp_back(): pl.pallas_call(mlp_back_kernel, grid=(1,), out_shape=[jax.ShapeDtypeStruc...  76 us
    pallas_call x1, Pallas kernels, startup(): pl.pallas_call(startup_kernel, out_shape=[jax.ShapeDtypeStruct((4,) + row...  71.2 us
    dot_general x7, matrix products, dot(): return lax.dot_general(left, right, dims, preferred_element_type=F32)  66.3 us
    pallas_call x1, Pallas kernels, out_back(): pl.pallas_call(functools.partial(out_back_kernel, layout), grid=(1,), out...  60.8 us
    pallas_call x1, Pallas kernels, mlp(): pl.pallas_call(mlp_kernel, grid=(1,), out_shape=[jax.ShapeDtypeStruct(gra...  52.4 us

profile of v6, /device:TPU:0, one launch (start us, length us, event | category | flops | bytes accessed | tf_op | source)
XLA Modules:
  0.0 952.0 jit_solution(13835248088446065650)
XLA Ops:
  6.3 1.7 pad_maximum_fusion.2.out_shard_ref
  8.0 1.9 concatenate.18.shard_ref
  9.9 1.2 pad_maximum_fusion.1.shard_ref
  11.1 1.4 copy.58
  12.5 1.8 convert_bitcast_fusion
  15.6 71.2 %startup.1 = (bf16[4,512,1536]{2,1,0:T(8,128)(2,1)}, bf16[1536,1280]{1,0:T(8,128)(2,1)}, f32[8,8,256]{2,1,0:T(8,128)}) custom-call(bf16[512,1536]{1,0:T(8,128)(2,1)} %bitcast.136, bf16[192,1280]{1,0:T(8,128)(2,1)} %concatenate.18.shard_ref, f32[8,256]{1,0:T(8,128)} %fusion.19.gain_ref), custom_call_target="tpu_custom_call" | custom-call | tf_op jit(solution)/shard_map/startup/pallas_call | solution.py:1114
  88.0 2.1 copy-done.10
  90.1 15.9 %project.1 = (bf16[4,512,1536]{2,1,0:T(8,128)(2,1)}, f32[4,512,128]{2,1,0:T(8,128)S(1)}, bf16[3,4,3,512,128]{4,3,2,1,0:T(8,128)(2,1)}) custom-call(bf16[4,512,1536]{2,1,0:T(8,128)(2,1)} %get-tuple-element.51.x_ref, f32[1,1536]{1,0:T(1,128)S(1)} %reshape_squeeze.6.gain_ref, bf16[1536,1280]{1,0:T(8,128)(2,1)S(1)} %copy-done.10), custom_call_target="tpu_custom_call" | custom-call | flops 8053063680 | bytes 12582912 | tf_op jit(solution)/shard_map/project/pallas_call | solution.py:1167
  107.8 200.3 %context.1 = (bf16[3,4,512,128]{3,2,1,0:T(8,128)(2,1)S(1)}, bf16[3,4,3,512,128]{4,3,2,1,0:T(8,128)(2,1)}, bf16[1536,2048]{1,0:T(8,128)(2,1)}, bf16[1536,768]{1,0...) custom-call(bf16[3,4,3,512,128]{4,3,2,1,0:T(8,128)(2,1)} %get-tuple-, ...), custom_call_target="tpu_custom_call" | custom-call | flops 12884901888 | bytes 104857600 | tf_op jit(solution)/shard_map/context/pallas_call | solution.py:357
  308.1 7.3 add_divide_fusion
  315.5 50.2 %out_project.1 = (f32[512,1536]{1,0:T(8,128)}, bf16[512,1536]{1,0:T(8,128)(2,1)S(1)}, bf16[4,512,384]{2,1,0:T(8,128)(2,1)S(1)}, bf16[4,512,384]{2,1,0:T(8,128)(2,1)S(1)}, bf16[1536,1024]{1,0:T(8,128)(2,1)}) custom-call(bf16[512,1536]{1,0:T(8,128)(2,1)} %bitcast.137, f32[4,512,384]{2,1,0:T(8,128)} %bitcast.139, ...), custom_call_target="tpu_custom_call" | custom-call | flops 2415919104 | bytes 104857600 | tf_op jit(solution)/shard_map/out_project/pallas_call | solution.py:1245
  365.7 1.2 copy-done.2
  368.0 1.1 copy-done.15
  369.2 52.4 %mlp.1 = (bf16[4,512,1536]{2,1,0:T(8,128)(2,1)}, bf16[4,512,1024]{2,1,0:T(8,128)(2,1)}, bf16[4,512,2048]{2,1,0:T(8,128)(2,1)}) custom-call(bf16[512,1536]{1,0:T(8,128)(2,1)} %copy-done.15, bf16[4,512,1536]{2,1,0:T(8,128)(2,1)} %get-tuple-element.61.grad_ref, bf16[1536,2048]{1,0:T(8,128)(2,1)} %get-tuple-element.62.gate_w.up_w.w_hbm, ...), custom_call_target="tpu_custom_call" | custom-call | flops 19327352832 | bytes 104857600 | tf_op jit(solution)/shard_map/mlp/pallas_call | solution.py:1311
  421.5 11.4 %bitcast_convert_fusion.1 = bf16[1536,1024]{1,0:T(8,128)(2,1)} fusion(bf16[4,512,1536]{2,1,0:T(8,128)(2,1)} %get-tuple-element.61.grad_ref, bf16[4,512,1024]{2,1,0:T(8,128)(2,1)} %get-tuple-element.73), kind=kOutput, calls=%fused_computation.3 | convolution fusion | flops 6444023808 | bytes 13631488 | tf_op jit(solution)/shard_map/dot_general | solution.py:22
  433.0 15.9 %bitcast_convert_fusion.sums_ref = bf16[1536,2048]{1,0:T(8,128)(2,1)} fusion(bf16[4,512,1536]{2,1,0:T(8,128)(2,1)S(1)} %copy-done.32, bf16[4,512,2048]{2,1,0:T(8,128)(2,1)S(1)} %copy-done.31), kind=kOutput, calls=%fused_computation | convolution fusion | flops 12888047616 | bytes 20971520 | tf_op jit(solution)/shard_map/dot_general | solution.py:22
  448.8 76.0 %mlp_back.1 = (f32[512,1536]{1,0:T(8,128)}, bf16[512,1536]{1,0:T(8,128)(2,1)}, f32[1,1536]{1,0:T(1,128)}, f32[192,1024]{1,0:T(8,128)}) custom-call(bf16[4,512,2048]{2,1,0:T(8,128)(2,1)} %get-tuple-element.64.pair_hbm, bf16[1536,2048]{1,0:T(8,128)(2,1)} %get-tuple-element.62.gate_w.up_w.w_hbm, f32[512,1536]{1,0:T(8,128)} %get-tuple-element.59.hidden_hbm, ...), custom_call_target="tpu_custom_call" | custom-call | flops 12884901888 | bytes 104857600 | tf_op jit(solution)/shard_map/mlp_back/pallas_call | solution.py:1390
  524.9 1.4 copy-done.4
  526.3 60.8 %out_back.1 = (bf16[4,512,1536]{2,1,0:T(8,128)(2,1)}, bf16[4,512,384]{2,1,0:T(8,128)(2,1)S(1)}, bf16[3,4,512,128]{3,2,1,0:T(8,128)(2,1)S(1)}, f32[192,1024]{1,0:T(8,128)S(1)}) custom-call(bf16[512,1536]{1,0:T(8,128)(2,1)S(1)} %copy-done.4, bf16[1536,768]{1,0:T(8,128)(2,1)} %get-tuple-element.57.w_ref.gate_w_hbm, f32[4,512,384]{2,1,0:T(8,128)} %bitcast.140, ...), custom_call_target="tpu_custom_call" | custom-call | flops 2415919104 | bytes 104857600 | tf_op jit(solution)/shard_map/out_back/pallas_call | solution.py:1476
  587.2 7.4 fusion.4
  594.6 8.9 convolution_convert_fusion
  603.6 3.5 fusion.5
  607.1 2.7 pad_maximum_fusion.part_ref
  609.9 210.2 %context_back.1 = (bf16[3,4,3,512,128]{4,3,2,1,0:T(8,128)(2,1)}, f32[3,4,8,512]{3,2,1,0:T(8,128)}, f32[192,1792]{1,0:T(8,128)}, bf16[512,1536]{1,0:T(8,128)(2,1)}) custom-call(bf16[3,4,512,128]{3,2,1,0:T(8,128)(2,1)} %copy-done.14, bf16[3,4,3,512,128]{4,3,2,1,0:T(8,128)(2,1)} %get-tuple-element.69.qkv_ref, f32[3,4,512,128]{3,2,1,0:T(8,128)} %get-tuple-element.70.exact_ref, ...), custom_call_target="tpu_custom_call" | custom-call | flops 32212254720 | bytes 104857600 | tf_op jit(solution)/shard_map/context_back/pallas_call | solution.py:478
  820.0 2.8 multiply_convert_fusion
  822.8 2.4 copy.117
  830.0 2.3 copy-done
  832.3 1.2 assemble.1.qkv_hbm
  833.6 2.1 copy-done.1
  835.7 11.8 %convolution_convert_fusion.1.part_ref = bf16[1536,1280]{1,0:T(8,128)(2,1)} fusion(bf16[2048,1536]{1,0:T(8,128)(2,1)} %bitcast.164, bf16[2048,128]{1,0:T(8,128)(2,1)S(1)} %copy.86, bf16[2048,1152]{1,0:T(8,128)(2,1)S(1)} %bitcast.134), kind=kOutput, calls=%fused_computation.2 | convolution fusion | flops 8065515520 | bytes 15466496 | tf_op jit(solution)/shard_map/dot_general | solution.py:22
  847.5 94.0 %last.1 = (bf16[512,1536]{1,0:T(8,128)(2,1)}, f32[192,1280]{1,0:T(8,128)}, f32[8,1536]{1,0:T(8,128)}) custom-call(bf16[4,512,1152]{2,1,0:T(8,128)(2,1)} %copy-done.1, bf16[4,512,384]{2,1,0:T(8,128)(2,1)} %copy-done.11, bf16[4,512,128]{2,1,0:T(8,128)(2,1)} %bitcast.146, bf16[1536,1280]{1,0:T(8,128)(2,1)} %get-tuple-element.53.w_ref.qkv_w_hbm, ...), custom_call_target="tpu_custom_call" | custom-call | flops 10468982784 | bytes 104857600 | tf_op jit(solution)/shard_map/last/pallas_call | solution.py:1627
  941.5 3.9 copy.116
  (129 shorter events, 21.7 us)
Async XLA Ops:
  0.6 10.5 %copy-start.19 = (bf16[128,4,1536]{2,1,0:T(4,128)(2,1)S(1)}, bf16[128,4,1536]{2,1,0:T(4,128)(2,1)}, u32[]{:S(2)}) copy-start(bf16[128,4,1536]{2,1,0:T(4,128)(2,1)} %param.15) | copy-start | bytes 4718596
  4.1 11.3 %copy-start.24 = (f32[512]{0:T(512)}, f32[512]{0:T(512)S(1)}, u32[]{:S(2)}) copy-start(f32[512]{0:T(512)S(1)} %convert_bitcast_fusion.1) | copy-start | bytes 6148
  15.6 91.2 %copy-start.5 = (bf16[512,1536]{1,0:T(8,128)(2,1)}, bf16[512,1536]{1,0:T(8,128)(2,1)S(1)}, u32[]{:S(2)}) copy-start(bf16[512,1536]{1,0:T(8,128)(2,1)S(1)} %fusion.3.rows_ref.grad_hbm) | copy-start | bytes 4718596
  87.9 227.5 %copy-start.8 = (f32[1,1536]{1,0:T(1,128)}, f32[1,1536]{1,0:T(1,128)S(1)}, u32[]{:S(2)}) copy-start(f32[1,1536]{1,0:T(1,128)S(1)} %reshape_squeeze.7.gain_ref) | copy-start | bytes 18436
  88.0 2.1 copy-start.10
  90.1 15.9 %copy-start.9 = (f32[1,1536]{1,0:T(1,128)}, f32[1,1536]{1,0:T(1,128)S(1)}, u32[]{:S(2)}) copy-start(f32[1,1536]{1,0:T(1,128)S(1)} %reshape_squeeze.6.gain_ref) | copy-start | bytes 18436
  107.8 200.3 %copy-start.29 = (bf16[4,512,1536]{2,1,0:T(8,128)(2,1)S(1)}, bf16[4,512,1536]{2,1,0:T(8,128)(2,1)}, u32[]{:S(2)}) copy-start(bf16[4,512,1536]{2,1,0:T(8,128)(2,1)} %get-tuple-element.54) | copy-start | bytes 18874372
  308.0 7.4 copy-start.3
  308.1 7.4 copy-start.16
  308.1 7.4 copy-start.17
  308.1 7.4 copy-start.6
  365.7 1.2 copy-start.2
  421.5 11.4 %copy-start.31 = (bf16[4,512,2048]{2,1,0:T(8,128)(2,1)S(1)}, bf16[4,512,2048]{2,1,0:T(8,128)(2,1)}, u32[]{:S(2)}) copy-start(bf16[4,512,2048]{2,1,0:T(8,128)(2,1)} %get-tuple-element.64.pair_hbm) | copy-start | bytes 25165828
  421.5 11.4 %copy-start.32 = (bf16[4,512,1536]{2,1,0:T(8,128)(2,1)S(1)}, bf16[4,512,1536]{2,1,0:T(8,128)(2,1)}, u32[]{:S(2)}) copy-start(bf16[4,512,1536]{2,1,0:T(8,128)(2,1)} %get-tuple-element.65) | copy-start | bytes 18874372
  524.9 1.4 copy-start.4
  526.3 60.8 %copy-start.13 = (bf16[4,512,384]{2,1,0:T(8,128)(2,1)S(1)}, bf16[4,512,384]{2,1,0:T(8,128)(2,1)}, u32[]{:S(2)}) copy-start(bf16[4,512,384]{2,1,0:T(8,128)(2,1)} %copy-done.12) | copy-start | bytes 4718596
  587.1 7.5 copy-start.14
  587.1 16.4 %copy-start.11 = (bf16[4,512,384]{2,1,0:T(8,128)(2,1)}, bf16[4,512,384]{2,1,0:T(8,128)(2,1)S(1)}, u32[]{:S(2)}) copy-start(bf16[4,512,384]{2,1,0:T(8,128)(2,1)S(1)} %get-tuple-element.76.logit_hbm) | copy-start | bytes 4718596
  587.1 7.5 copy-start.28
  587.1 7.5 copy-start.30
  587.1 16.4 %slice-start = ((s8[6291456]{0:T(1024)(128)(4,1)}), s8[4194304]{0:T(1024)(128)(4,1)S(1)}, s32[]{:S(2)}) async-start(s8[6291456]{0:T(1024)(128)(4,1)} %bitcast.166), calls=%async_computation | async-start | bytes 8388608
  594.6 8.9 slice-start.1
  603.6 3.6 copy-start.18
  609.9 210.2 %copy-start.25 = (f32[512]{0:T(512)S(1)}, f32[512]{0:T(512)}, u32[]{:S(2)}) copy-start(f32[512]{0:T(512)} %copy-done.24) | copy-start | bytes 6148
  822.8 4.2 copy-start.26
  822.8 4.2 copy-start.27
  822.8 5.2 copy-start.20
  828.0 5.5 copy-start.23
  830.0 2.3 copy-start
  833.5 2.1 copy-start.1
  941.5 6.7 copy-start.21
  941.5 8.3 copy-start.22
  (3 other events, 3.2 us)

commit v7 on v6

--- a/solution.py
+++ b/solution.py
@@ -217,9 +217,9 @@
         )
 
     def start(self, item):
-        self.own(item).start()
         for step in range(1, self.size):
             self.copy(item, step).start()
+        self.own(item).start()
 
     def arrive(self, item):
         self.own(item).wait()
@@ -244,8 +244,10 @@
     head_size,
     items_ref,
     forget_ref,
-    shard_ref,
-    out_shard_ref,
+    gate_ref,
+    up_ref,
+    out_w_ref,
+    gate_out_ref,
     rows_ref,
     back_ref,
     qkv_ref,
@@ -264,8 +266,8 @@
     greet_all([{"tp": sibling}, {"tp": across}] + group_peers())
     me = lax.axis_index("ctx")
     gathers = (
-        WeightGather(out_shard_ref, full_out_ref, sems[9:14]),
-        WeightGather(shard_ref, full_ref, sems[14:19]),
+        WeightGather((out_w_ref, gate_out_ref), full_out_ref, sems[9:14]),
+        WeightGather((gate_ref, up_ref), full_ref, sems[14:19]),
     )
     rows = RowGather(rows_ref, table_ref, sems[19:])
     forgets = Exchange(me, size, forget_ref, forget, sems[0:3])
@@ -349,8 +351,9 @@
     )
 
 
-def context(items, forget, shard, out_shard, rows, f_size, head_size, ident):
+def context(items, forget, shards, rows, f_size, head_size, ident):
     count, size, _, block, width = items.shape
+    full = shards[0].shape[0] * f_size * size
     heads = width // head_size
     place = pl.BlockSpec(memory_space=pl.ANY)
     exact, stat = (count, size, block, width), (count, 8, size * block)
@@ -360,14 +363,16 @@
         out_shape=[
             jax.ShapeDtypeStruct(exact, BF16),
             jax.ShapeDtypeStruct(items.shape, BF16),
-            jax.ShapeDtypeStruct((shard.shape[0] * f_size * size, shard.shape[1]), BF16),
-            jax.ShapeDtypeStruct((shard.shape[0] * f_size * size, out_shard.shape[1]), BF16),
+            jax.ShapeDtypeStruct((full, 2 * shards[0].shape[1]), BF16),
+            jax.ShapeDtypeStruct((full, 2 * shards[2].shape[1]), BF16),
             jax.ShapeDtypeStruct((4,) + rows.shape, BF16),
             jax.ShapeDtypeStruct(exact, F32),
             jax.ShapeDtypeStruct(stat, F32),
             jax.ShapeDtypeStruct(stat, F32),
         ],
-        in_specs=[place] * 5,
+        in_specs=[place, place]
+        + [full_block(shard.shape) for shard in shards]
+        + [full_block(rows.shape)],
         out_specs=[place, place, place, place, place, full_block(exact), full_block(stat), full_block(stat)],
         scratch_shapes=[
             pltpu.VMEM(items.shape, BF16),
@@ -376,13 +381,13 @@
             pltpu.SemaphoreType.DMA,
         ]
         + exchange_sems(count, size) * 3
-        + weight_sems(f_size, size) * 2
+        + weight_sems(f_size, size, 2) * 2
         + [pltpu.SemaphoreType.DMA((3,))] * 2
         + [pltpu.SemaphoreType.DMA],
         compiler_params=remote_params(ident, 48),
         cost_estimate=attend_cost(items, heads, 2),
         name="context",
-    )(items, forget, shard, out_shard, rows)
+    )(items, forget, *shards, rows)
 
 
 def context_back_kernel(
@@ -393,10 +398,12 @@
     exact_ref,
     lse_ref,
     decay_ref,
+    down_ref,
     part_ref,
     table_ref,
     back_ref,
     forget_ref,
+    down_sum_ref,
     sum_ref,
     rows_ref,
     *refs,
@@ -407,14 +414,18 @@
     tp, sibling, across, diagonal = tp_places()
     greet_all([{"tp": sibling}, {"tp": across}] + group_peers())
     me = lax.axis_index("ctx")
-    weights = WeightSum(part_ref, 0, sum_ref, refs[15:23])
-    rows = RowSum(table_ref, rows_ref, refs[23:])
+    sums = (
+        WeightSum(part_ref, 0, sum_ref, refs[15:23]),
+        WeightSum(down_ref, 0, down_sum_ref, refs[23:31]),
+    )
+    rows = RowSum(table_ref, rows_ref, refs[31:])
     inputs = Exchange(me, size, items_ref, grads, sems[0:3])
     results = Exchange(me, size, dqkv, back_ref, sems[3:6])
     forgets = Exchange(me, size, slope, forget_ref, sems[6:9])
 
     inputs.start(0)
-    weights.begin()
+    for weights in sums:
+        weights.begin()
     rows.begin()
 
     @pl.loop(0, count)
@@ -451,11 +462,15 @@
 
             @pl.when(item == turn)
             def _(turn=turn):
-                weights.run_share(turn, count + 1)
+                for weights in sums:
+                    weights.run_share(turn, count + 1)
                 if turn == 0:
                     rows.advance()
 
-    weights.run_share(count, count + 1)
+    share = -(-sums[0].stages // (count + 1))
+    for n in range(count * share, sums[0].stages):
+        for weights in sums:
+            weights.run(n)
 
     @pl.loop(0, count)
     def _(item):
@@ -465,22 +480,25 @@
         forgets.arrive(item)
         forgets.drain(item)
 
-    weights.end()
+    for weights in sums:
+        weights.end()
     rows.end()
 
 
-def context_back(grads, qkv, exact, lse, decay, part, table, f_size, head_size, ident):
+def context_back(grads, qkv, exact, lse, decay, down, part, table, f_size, head_size, ident):
     count, size, _, block, width = qkv.shape
     heads = width // head_size
     place = pl.BlockSpec(memory_space=pl.ANY)
     forget = (count, size, 8, block)
     total = (part.shape[0] // (f_size * size), part.shape[1])
+    down_total = (total[0], down.shape[1])
     return pl.pallas_call(
         functools.partial(context_back_kernel, heads, head_size),
         grid=(1,),
         out_shape=[
             jax.ShapeDtypeStruct(qkv.shape, BF16),
             jax.ShapeDtypeStruct(forget, F32),
+            jax.ShapeDtypeStruct(down_total, F32),
             jax.ShapeDtypeStruct(total, F32),
             jax.ShapeDtypeStruct(table.shape[1:], BF16),
         ],
@@ -492,8 +510,15 @@
             full_block(decay.shape),
             place,
             place,
-        ],
-        out_specs=[place, place, full_block(total), full_block(table.shape[1:])],
+            place,
+        ],
+        out_specs=[
+            place,
+            place,
+            full_block(down_total),
+            full_block(total),
+            full_block(table.shape[1:]),
+        ],
         scratch_shapes=[
             pltpu.VMEM(grads.shape, BF16),
             pltpu.VMEM(qkv.shape, BF16),
@@ -504,11 +529,12 @@
         ]
         + exchange_sems(count, size) * 3
         + sum_scratch(f_size, size, *total)
+        + sum_scratch(f_size, size, *down_total)
         + row_sum_scratch(*table.shape[1:]),
         compiler_params=remote_params(ident, 60),
         cost_estimate=attend_cost(qkv, heads, 5),
         name="context_back",
-    )(grads, qkv, exact, lse, decay, part, table)
+    )(grads, qkv, exact, lse, decay, down, part, table)
 
 
 CHUNKS = 4
@@ -550,7 +576,7 @@
     return slot, chunk
 
 
-def gather_loop(table, sems, compute, own=None, relative=False, between=None):
+def gather_loop(table, sems, compute, own=None, relative=False, between=None, ready=None):
     near_send, near_recv, far_send, far_recv, pass_send, pass_recv = sems
     me, sibling, across, diagonal = tp_places()
     places = (0, 1, 2, 3) if relative else (me, sibling, across, diagonal)
@@ -585,6 +611,8 @@
     own = table.at[mine] if own is None else own
     near = sending(own, table.at[near_spot], near_send, near_recv, sibling)
     near.start()
+    if ready is not None:
+        ready()
 
     def body(step, _):
         slot, chunk = pick(step, CHUNKS, places)
@@ -682,8 +710,8 @@
     if between is None:
         lax.fori_loop(0, 4 * CHUNKS, body, 0)
     else:
-        lax.fori_loop(0, 2 * CHUNKS, body, 0)
-        for phase in (2, 3):
+        lax.fori_loop(0, CHUNKS, body, 0)
+        for phase in (1, 2, 3):
             between(phase)
             lax.fori_loop(phase * CHUNKS, (phase + 1) * CHUNKS, body, 0)
     for chunk in range(CHUNKS):
@@ -734,35 +762,30 @@
 
 
 class WeightGather:
-    def __init__(self, shard, full, sems):
-        self.shard, self.full = shard, full
+    def __init__(self, shards, full, sems):
+        self.shards, self.full = shards, full
+        widths = [shard.shape[1] for shard in shards]
+        self.columns = [pl.ds(sum(widths[:h]), width) for h, width in enumerate(widths)]
         self.f_size, self.c_size = lax.axis_size("fsdp"), lax.axis_size("ctx")
         self.f, self.c = lax.axis_index("fsdp"), lax.axis_index("ctx")
         self.sems = sems
 
-    def half(self, h):
-        wide = self.shard.shape[1] // HALVES
-        return pl.ds(h * wide, wide)
-
     def spot(self, c, h, f=None):
-        rows = self.shard.shape[0]
+        rows = self.shards[0].shape[0]
         block = (self.f if f is None else f) * self.c_size + c
-        return self.full.at[pl.ds(pl.multiple_of(block * rows, rows), rows), self.half(h)]
-
-    def own(self):
-        rows = self.shard.shape[0]
-        block = self.f * self.c_size + self.c
-        target = self.full.at[pl.ds(pl.multiple_of(block * rows, rows), rows)]
-        return pltpu.make_async_copy(self.shard, target, self.sems[4])
+        return self.full.at[pl.ds(pl.multiple_of(block * rows, rows), rows), self.columns[h]]
+
+    def own(self, h):
+        return pltpu.make_async_copy(self.shards[h], self.spot(self.c, h), self.sems[4].at[h])
 
     def along(self, c, h, hop, side, first=False):
-        source = self.shard.at[:, self.half(h)] if first else self.spot(c, h)
+        source = self.shards[h] if first else self.spot(c, h)
         peer = {"ctx": self.c + (1 if side else -1)}
         send, recv = self.sems[0].at[side, hop, h], self.sems[1].at[side, hop, h]
         return moving(source, self.spot(c, h), send, recv, peer)
 
     def over(self, c, h, step, first=False):
-        source = self.shard.at[:, self.half(h)] if first else self.spot(c, h)
+        source = self.shards[h] if first else self.spot(c, h)
         peer = {"fsdp": lax.rem(self.f + step, self.f_size)}
         send, recv = self.sems[2].at[step, c, h], self.sems[3].at[step, c, h]
         return moving(source, self.spot(c, h), send, recv, peer)
@@ -779,8 +802,7 @@
         return self.c - hop >= 0 if side else self.c + hop < self.c_size
 
     def begin(self):
-        self.own().start()
-        for h in range(HALVES):
+        for h in range(len(self.shards)):
             for side in (1, 0):
 
                 @pl.when(self.can(side))
@@ -790,8 +812,11 @@
             for step in range(1, self.f_size):
                 self.over(self.c, h, step, True).start()
 
+        for h in range(len(self.shards)):
+            self.own(h).start()
+
     def advance(self, hop):
-        for h in range(HALVES):
+        for h in range(len(self.shards)):
             for side in (1, 0):
 
                 @pl.when(self.holds(hop, side))
@@ -807,8 +832,8 @@
                         self.over(c, h, step).start()
 
     def end(self):
-        self.own().wait()
-        for h in range(HALVES):
+        for h in range(len(self.shards)):
+            self.own(h).wait()
             for step in range(1, self.f_size):
                 for c in range(self.c_size):
                     self.over_arrival(c, h, step).wait_recv()
@@ -827,9 +852,9 @@
                         self.along(c, h, hop + 1, side).wait_send()
 
 
-def weight_sems(f_size, c_size):
+def weight_sems(f_size, c_size, parts):
     dma = pltpu.SemaphoreType.DMA
-    return [dma((2, c_size + 1, HALVES))] * 2 + [dma((f_size, c_size, HALVES))] * 2 + [dma]
+    return [dma((2, c_size + 1, parts))] * 2 + [dma((f_size, c_size, parts))] * 2 + [dma((parts,))]
 
 
 class WeightSum:
@@ -874,16 +899,12 @@
             peer,
         )
 
-    def launch(self, i):
-        if i < len(self.order):
-            for step in range(1, self.f_size):
-                self.over(*self.order[i], step).start()
-
     def begin(self):
         for c, h in self.order:
+            for step in range(1, self.f_size):
+                self.over(c, h, step).start()
+        for c, h in self.order:
             self.own(c, h).start()
-        self.launch(0)
-        self.launch(1)
 
     def receive(self, i):
         c, h = self.order[i]
@@ -892,7 +913,6 @@
         value = self.stage[n].astype(F32)
         for step in range(1, self.f_size):
             self.over(c, h, step).wait_recv()
-        self.launch(i + 2)
         for step in range(1, self.f_size):
             value = value + self.total[step - 1, n].astype(F32)
         self.total[0, n] = value.astype(BF16)
@@ -993,9 +1013,9 @@
         return moving(source, self.table.at[n + 1], self.sems[0].at[n], self.sems[1].at[n], peer)
 
     def begin(self):
+        self.copy(1).start()
+        self.copy(0).start()
         self.own().start()
-        self.copy(0).start()
-        self.copy(1).start()
 
     def advance(self):
         self.copy(1).wait_recv()
@@ -1026,8 +1046,9 @@
 
     def begin(self):
         for n in range(2):
+            self.copy(n).start()
+        for n in range(2):
             self.own(n).start()
-            self.copy(n).start()
 
     def advance(self):
         self.own(0).wait()
@@ -1050,24 +1071,22 @@
     return [pltpu.VMEM(pair, BF16)] * 2 + [pltpu.VMEM(one, BF16)] * 2 + [dma((3,))] * 2 + [dma((2,))]
 
 
-def startup_kernel(rows_ref, shard_ref, gain_ref, all_ref, full_ref, gains_ref, own_sem, *sems):
+def startup_kernel(parts, rows_ref, gain_ref, *refs):
+    shards, (all_ref, full_ref, gains_ref, own_sem) = refs[:parts], refs[parts : parts + 4]
+    sems = refs[parts + 4 :]
     me, sibling, across, diagonal = tp_places()
     others = group_peers()
     greet_all([{"tp": sibling}, {"tp": across}] + others)
     near_send, near_recv, far_send, far_recv, pass_send, pass_recv = sems[:6]
-    gather = WeightGather(shard_ref, full_ref, sems[6:11])
+    gather = WeightGather(shards, full_ref, sems[6:11])
     gain_send, gain_recv, gain_own = sems[11:]
     spot = gains_ref.at[gather.f * gather.c_size + gather.c]
     gain_copies = [
         moving(gain_ref, spot, gain_send.at[n], gain_recv.at[n], peer) for n, peer in enumerate(others)
     ]
-    for copy in gain_copies:
-        copy.start()
     own_gain = pltpu.make_async_copy(gain_ref, spot, gain_own)
-    own_gain.start()
     size = rows_ref.shape[0] // CHUNKS
     own = pltpu.make_async_copy(rows_ref, all_ref.at[me], own_sem)
-    own.start()
 
     def span(chunk):
         return pl.ds(chunk * size, size)
@@ -1087,8 +1106,12 @@
 
     gather.begin()
     far(0).start()
+    for copy in gain_copies:
+        copy.start()
+    own_gain.start()
     near = sending(rows_ref, all_ref.at[me], near_send, near_recv, sibling)
     near.start()
+    own.start()
     for turn in range(max(CHUNKS, gather.c_size - 1)):
         if turn < CHUNKS:
             far(turn).wait_recv()
@@ -1108,26 +1131,28 @@
     own_gain.wait()
 
 
-def startup(rows, shard, gains, f_size, c_size, ident):
+def startup(rows, gains, shards, f_size, c_size, ident):
     place = pl.BlockSpec(memory_space=pl.ANY)
-    full = (shard.shape[0] * f_size * c_size, shard.shape[1])
+    full = (shards[0].shape[0] * f_size * c_size, sum(shard.shape[1] for shard in shards))
     return pl.pallas_call(
-        startup_kernel,
+        functools.partial(startup_kernel, len(shards)),
         out_shape=[
             jax.ShapeDtypeStruct((4,) + rows.shape, BF16),
             jax.ShapeDtypeStruct(full, BF16),
             jax.ShapeDtypeStruct((f_size * c_size,) + gains.shape, F32),
         ],
-        in_specs=[place] * 3,
+        in_specs=[pl.BlockSpec(memory_space=pltpu.VMEM)] * (2 + len(shards)),
         out_specs=[place] * 3,
         scratch_shapes=[pltpu.SemaphoreType.DMA]
         + GATHER_SEMS
-        + weight_sems(f_size, c_size)
+        + weight_sems(f_size, c_size, len(shards))
         + [pltpu.SemaphoreType.DMA((f_size * c_size - 1,))] * 2
         + [pltpu.SemaphoreType.DMA],
-        compiler_params=pltpu.CompilerParams(collective_id=ident, has_side_effects=True),
+        compiler_params=pltpu.CompilerParams(
+            collective_id=ident, has_side_effects=True, vmem_limit_bytes=32 << 20
+        ),
         name="startup",
-    )(rows, shard, gains)
+    )(rows, gains, *shards)
 
 
 def whole(shape, column=None):
@@ -1197,7 +1222,7 @@
     count = items.shape[0]
     me, sibling, across, diagonal = tp_places()
     greet_all([{"tp": sibling}, {"tp": across}] + group_peers())
-    gather = WeightGather(shard_ref, full_ref, refs[13:])
+    gather = WeightGather((shard_ref,), full_ref, refs[13:])
     gather.begin()
     tp_size, rows, _ = gate_ref.shape
     local = rows // seq_count
@@ -1227,10 +1252,10 @@
         normed_ref[span(chunk)] = (hidden * inverse * gain_ref[...]).astype(BF16)
 
     def between(phase):
-        if phase == 2:
-            gather.advance(1)
+        if phase < 3:
+            gather.advance(phase)
         else:
-            for hop in range(2, gather.c_size):
+            for hop in range(3, gather.c_size):
                 gather.advance(hop)
 
     scatter_loop(buffers, sems, partial, finish, between=between)
@@ -1258,7 +1283,7 @@
             whole((model_width, inner), 0),
             whole(gain.shape),
             whole(items.shape),
-            pl.BlockSpec(memory_space=pl.ANY),
+            whole(shard.shape),
         ],
         out_specs=[
             whole(x.shape),
@@ -1269,7 +1294,7 @@
         ],
         scratch_shapes=scatter_buffers(rows, model_width)
         + SCATTER_SEMS
-        + weight_sems(f_size, c_size),
+        + weight_sems(f_size, c_size, 1),
         compiler_params=remote_params(ident, 48),
         cost_estimate=pl.CostEstimate(
             flops=2 * gate.size * model_width, bytes_accessed=100 << 20, transcendentals=0
@@ -1278,58 +1303,80 @@
     )(x, gate, full_out, gain, items, shard)
 
 
-def mlp_kernel(normed_ref, grad_ref, gate_w, up_w, down_w, all_ref, inner_ref, pair_ref, table, own_sem, *sems):
+def mlp_kernel(
+    normed_ref, grad_hbm, gate_hbm, down_hbm, all_ref, inner_hbm, pair_hbm, table, inner_ref, pair_ref, *refs
+):
+    grad_ref, both_w, down_w, fetch_sem, out_sem = refs[:5]
+    sems = refs[5:]
+    fetch = Fetch([(gate_hbm, both_w), (grad_hbm, grad_ref), (down_hbm, down_w)], fetch_sem)
     me, sibling, across, diagonal = tp_places()
     greet((sibling, across))
     table[0] = normed_ref[...]
-    rows, hidden = table.shape[1] // CHUNKS, gate_w.shape[1]
+    rows, hidden = table.shape[1] // CHUNKS, down_w.shape[1]
     tile = min(hidden, 512)
+
+    def writing(n, slot, chunk):
+        here = (slot, pl.ds(pl.multiple_of(chunk * rows, rows), rows))
+        source, target = ((inner_ref, inner_hbm), (pair_ref, pair_hbm), (table, all_ref))[n]
+        return pltpu.make_async_copy(source.at[here], target.at[here], out_sem.at[n, slot, chunk])
 
     def compute(slot, chunk):
         spot = pl.ds(pl.multiple_of(chunk * rows, rows), rows)
         normed, grad = table[slot, spot], grad_ref[slot, spot]
         for start in range(0, hidden, tile):
             columns = pl.ds(start, tile)
-            gate = dot(normed, gate_w[:, columns], NN)
-            up = dot(normed, up_w[:, columns], NN)
+            gate = dot(normed, both_w[:, columns], NN)
+            up = dot(normed, both_w[:, pl.ds(hidden + start, tile)], NN)
             back = dot(grad, down_w[:, columns], NN)
             sig = 1.0 / (1.0 + jnp.exp(-gate))
             silu = gate * sig
             inner_ref[slot, spot, columns] = (silu * up).astype(BF16)
             pair_ref[slot, spot, columns] = (back * up * sig * (1.0 + gate * (1.0 - sig))).astype(BF16)
             pair_ref[slot, spot, pl.ds(hidden + start, tile)] = (back * silu).astype(BF16)
-
-    gather_loop(table, sems, compute, relative=True)
-    copy = pltpu.make_async_copy(table, all_ref, own_sem)
-    copy.start()
-    copy.wait()
+        for n in range(3):
+            writing(n, slot, chunk).start()
+
+    gather_loop(table, sems, compute, relative=True, ready=fetch.wait)
+    for n in range(3):
+
+        @pl.loop(0, 4 * CHUNKS)
+        def _(step):
+            writing(n, step // CHUNKS, lax.rem(step, CHUNKS)).wait()
 
 
 def mlp(normed, grad_all, full_two, full_down, hidden, ident):
     tp_size, rows, model_width = grad_all.shape
     total = tp_size * rows
+    place = pl.BlockSpec(memory_space=pl.ANY)
+    inner, pair = (tp_size, rows, hidden), (tp_size, rows, 2 * hidden)
+    dma = pltpu.SemaphoreType.DMA
     return pl.pallas_call(
         mlp_kernel,
         grid=(1,),
         out_shape=[
             jax.ShapeDtypeStruct(grad_all.shape, BF16),
-            jax.ShapeDtypeStruct((tp_size, rows, hidden), BF16),
-            jax.ShapeDtypeStruct((tp_size, rows, 2 * hidden), BF16),
-        ],
-        in_specs=[whole(normed.shape), whole(grad_all.shape)]
-        + [whole((model_width, hidden), column) for column in (0, 1, 0)],
-        out_specs=[
-            pl.BlockSpec(memory_space=pl.ANY),
-            whole((tp_size, rows, hidden)),
-            whole((tp_size, rows, 2 * hidden)),
-        ],
-        scratch_shapes=[pltpu.VMEM(grad_all.shape, BF16), pltpu.SemaphoreType.DMA] + GATHER_SEMS,
+            jax.ShapeDtypeStruct(inner, BF16),
+            jax.ShapeDtypeStruct(pair, BF16),
+        ],
+        in_specs=[whole(normed.shape), place, place, place],
+        out_specs=[place] * 3,
+        scratch_shapes=[
+            pltpu.VMEM(grad_all.shape, BF16),
+            pltpu.VMEM(inner, BF16),
+            pltpu.VMEM(pair, BF16),
+            pltpu.VMEM(grad_all.shape, BF16),
+            pltpu.VMEM((model_width, 2 * hidden), BF16),
+            pltpu.VMEM((model_width, hidden), BF16),
+            dma((3,)),
+            dma((3, tp_size, CHUNKS)),
+        ]
+        + GATHER_SEMS,
         compiler_params=remote_params(ident, 56),
         cost_estimate=pl.CostEstimate(
             flops=6 * total * model_width * hidden, bytes_accessed=100 << 20, transcendentals=total * hidden
         ),
         name="mlp",
-    )(normed, grad_all, full_two, full_two, full_down)
+    )(normed, grad_all, full_two, full_down)
 
 
 def mlp_back_kernel(
@@ -1373,10 +1420,10 @@
         branch_ref[span(chunk)] = grad.astype(BF16)
 
     def between(phase):
-        if phase == 2:
-            weights.run_to(0, 3)
+        if phase < 3:
+            weights.run_to(2 * phase - 2, 2 * phase)
         else:
-            weights.run_to(3, weights.stages)
+            weights.run_to(4, weights.stages)
 
     scatter_loop(buffers, sems, partial, finish, relative=True, between=between)
     weights.end()
@@ -1428,18 +1475,45 @@
     )(pair, full_two, hidden_state, grad_out, gain, part)
 
 
-def out_back_kernel(layout, branch_ref, w_ref, gate_ref, attended_ref, sums_ref, *refs):
+def out_back_kernel(
+    layout,
+    branch_ref,
+    w_ref,
+    gate_ref,
+    attended_ref,
+    sums_ref,
+    inner_hbm,
+    down_hbm,
+    grad_hbm,
+    all_ref,
+    logit_ref,
+    items,
+    sum_ref,
+    forward_hbm,
+    part_hbm,
+    *refs,
+):
     seq_count, groups, width, places = layout
-    all_ref, logit_ref, items, sum_ref, table, grads, own_sem = refs[:7]
-    sems = refs[7:13]
+    table, grads, own_sem = refs[:3]
+    sems = refs[3:9]
+    inner_ref, down_w, grad_ref, forward, part, fetch_sem, write_sem = refs[9:16]
     count = items.shape[0]
     me, sibling, across, diagonal = tp_places()
     greet_all([{"tp": sibling}, {"tp": across}] + group_peers())
-    weights = WeightSum(sums_ref, sum_ref.shape[1], sum_ref, refs[13:])
+    weights = WeightSum(sums_ref, sum_ref.shape[1], sum_ref, refs[16:])
     weights.begin()
     table[me] = branch_ref[...]
     tp_size, rows, _ = gate_ref.shape
     local, size = rows // seq_count, rows // CHUNKS
+    model_width, hidden = part.shape
+    tile = 2 * LANES
+    steps, tiles = 4 * CHUNKS, model_width // tile
+    fetches = []
+
+    def begin_fetch():
+        fetches.append(
+            Fetch([(inner_hbm, inner_ref), (down_hbm, down_w), (grad_hbm, grad_ref)], fetch_sem)
+        )
 
     def compute(slot, chunk):
         spot = pl.ds(pl.multiple_of(chunk * size, size), size)
@@ -1450,9 +1524,39 @@
         attended = attended_ref[slot, spot].astype(F32)
         logit_ref[slot, spot] = (scaled * attended * (1.0 - gate)).astype(BF16)
 
-    gather_loop(table, sems, compute, between=lambda: weights.run_share(0, 1))
-    copy = pltpu.make_async_copy(table, all_ref, own_sem)
-    copy.start()
+    def project_down(step, _):
+        slot, chunk = step // CHUNKS, lax.rem(step, CHUNKS)
+        spot = pl.ds(pl.multiple_of(chunk * size, size), size)
+        forward[slot, spot] = dot(inner_ref[slot, spot], down_w[...], NT).astype(BF16)
+        return 0
+
+    def down_grad(n, _):
+        columns = pl.ds(pl.multiple_of(n * tile, tile), tile)
+        left = grad_ref[:, :, columns].reshape(tp_size * rows, tile)
+        right = inner_ref[...].reshape(tp_size * rows, hidden)
+        part[columns] = dot(left, right, TN).astype(BF16)
+        return 0
+
+    last = weights.stages
+    middle = max(1, last - 4)
+
+    def stage(n):
+        weights.run(n)
+        lax.fori_loop(n * steps // last, (n + 1) * steps // last, project_down, 0)
+        lax.fori_loop(n * tiles // last, (n + 1) * tiles // last, down_grad, 0)
+
+    def between():
+        fetches[0].wait()
+        for n in range(middle):
+            stage(n)
+
+    gather_loop(table, sems, compute, between=between, ready=begin_fetch)
+    copies = [
+        pltpu.make_async_copy(table, all_ref, own_sem),
+        pltpu.make_async_copy(forward, forward_hbm, write_sem.at[0]),
+        pltpu.make_async_copy(part, part_hbm, write_sem.at[1]),
+    ]
+    copies[0].start()
 
     def deal(t, _):
         here = pl.ds(pl.multiple_of(t * local, local), local)
@@ -1462,17 +1566,26 @@
         return 0
 
     lax.fori_loop(0, tp_size, deal, 0)
-    copy.wait()
+    for n in range(middle, last):
+        stage(n)
+    for copy in copies[1:]:
+        copy.start()
+    for copy in copies:
+        copy.wait()
     weights.end()
 
 
-def out_back(branch, full_out, gate, attended, part, layout, item_count, f_size, ctx_size, ident):
+def out_back(
+    branch, full_out, gate, attended, part, inner_act, down_w, grad_all, layout, item_count, f_size, ctx_size, ident
+):
     seq_count, groups, width, places = layout
     rows, model_width = branch.shape
     tp_size, _, inner = gate.shape
     item = (item_count, ctx_size, tp_size * rows // seq_count, width)
     table = (tp_size, rows, model_width)
     total = (part.shape[0] // (f_size * ctx_size), part.shape[1] // 2)
+    place = pl.BlockSpec(memory_space=pl.ANY)
+    dma = pltpu.SemaphoreType.DMA
     return pl.pallas_call(
         functools.partial(out_back_kernel, layout),
         grid=(1,),
@@ -1481,24 +1594,38 @@
             jax.ShapeDtypeStruct(gate.shape, BF16),
             jax.ShapeDtypeStruct(item, BF16),
             jax.ShapeDtypeStruct(total, F32),
+            jax.ShapeDtypeStruct(table, BF16),
+            jax.ShapeDtypeStruct(down_w.shape, BF16),
         ],
         in_specs=[
             whole(branch.shape),
             whole((model_width, inner), 0),
             whole(gate.shape),
             whole(attended.shape),
-            pl.BlockSpec(memory_space=pl.ANY),
-        ],
-        out_specs=[pl.BlockSpec(memory_space=pl.ANY), whole(gate.shape), whole(item), whole(total)],
-        scratch_shapes=[pltpu.VMEM(table, BF16), pltpu.VMEM(gate.shape, BF16), pltpu.SemaphoreType.DMA]
+            place,
+            place,
+            place,
+            place,
+        ],
+        out_specs=[place, whole(gate.shape), whole(item), whole(total), place, place],
+        scratch_shapes=[pltpu.VMEM(table, BF16), pltpu.VMEM(gate.shape, BF16), dma]
         + GATHER_SEMS
+        + [
+            pltpu.VMEM(inner_act.shape, BF16),
+            pltpu.VMEM(down_w.shape, BF16),
+            pltpu.VMEM(table, BF16),
+            pltpu.VMEM(table, BF16),
+            pltpu.VMEM(down_w.shape, BF16),
+            dma((3,)),
+            dma((2,)),
+        ]
         + sum_scratch(f_size, ctx_size, *total),
-        compiler_params=remote_params(ident, 48),
+        compiler_params=remote_params(ident, 60),
         cost_estimate=pl.CostEstimate(
             flops=2 * gate.size * model_width, bytes_accessed=100 << 20, transcendentals=0
         ),
         name="out_back",
-    )(branch, full_out, gate, attended, part)
+    )(branch, full_out, gate, attended, part, inner_act, down_w, grad_all)
 
 
 def assemble_kernel(layout, items, out_ref):
@@ -1588,13 +1715,13 @@
         out_ref[span(chunk)] = (grad_ref[span(chunk)] + inverse * (scaled - unit * middle)).astype(BF16)
 
     stages = weights.stages
-    late = max(3, stages - 4)
+    late = max(4, stages - 4)
 
     def between(phase):
-        if phase == 2:
-            weights.run_to(0, 3)
+        if phase < 3:
+            weights.run_to(2 * phase - 2, 2 * phase)
         else:
-            weights.run_to(3, late)
+            weights.run_to(4, late)
 
     scatter_loop(buffers, sems, partial, finish, between=between)
     near_send, near_recv, group_send, group_recv = vector_sems
@@ -1719,25 +1846,14 @@
     layout = (seq_count, groups, width, places)
 
     fsdp_size = lax.axis_size("fsdp")
-    packed_one = jnp.concatenate(
-        [
-            w_query,
-            w_key,
-            w_value,
-            w_forget,
-            jnp.zeros((attn_gain.shape[0], LANES - head_count), BF16),
-        ],
-        axis=1,
-    )
-    packed_two = jnp.concatenate([w_gate, w_up], axis=1)
-    packed_out = jnp.concatenate([w_out, w_gate_out], axis=1)
+    wide_forget = jnp.pad(w_forget, ((0, 0), (0, LANES - head_count)))
     edge = 3 * inner_width
     input_rows = layer_input.transpose(1, 0, 2).reshape(seq_count * local_rows, model_width)
     shard_rows = model_width // shard_count
     own_gains = jnp.stack([attn_gain, mlp_gain]).astype(F32)
     own_gains = jnp.pad(own_gains, ((0, 6), (0, -shard_rows % LANES)))
     input_all, full_one, gains = startup(
-        input_rows, packed_one, own_gains, fsdp_size, ctx_size, 1
+        input_rows, own_gains, (w_query, w_key, w_value, wide_forget), fsdp_size, ctx_size, 1
     )
     gain_one = gains[:, 0, :shard_rows].reshape(1, model_width)
     gain_two = gains[:, 1, :shard_rows].reshape(1, model_width)
@@ -1772,7 +1888,13 @@
     picked = picked.reshape(ctx_size, item_count, pair, ctx_rows).transpose(1, 0, 2, 3)
     picked = jnp.pad(picked, ((0, 0), (0, 0), (0, 8 - pair), (0, 0)))
     attended_items, qkv, full_two, full_out, grad_all, exact, lse, decay = context(
-        items, picked, packed_two, packed_out, grad_out, fsdp_size, head_size, 7
+        items,
+        picked,
+        (w_gate, w_up, w_out, w_gate_out),
+        grad_out,
+        fsdp_size,
+        head_size,
+        7,
     )
     gate_out_w = full_out[:, inner_width:]
     gate_logit = dot(normed_flat, gate_out_w, NN)
@@ -1791,21 +1913,21 @@
     )
     normed_two_all, inner_act, grad_pair = mlp(normed_two, grad_all, full_two, down_w, hidden, 3)
     normed_two_flat = normed_two_all.reshape(all_rows, model_width)
-    inner_flat = inner_act.reshape(all_rows, hidden)
     grad_pair_flat = grad_pair.reshape(all_rows, 2 * hidden)
-    grad_flat = grad_all.reshape(all_rows, model_width)
 
     gate_up_part = dot(normed_two_flat, grad_pair_flat, TN).astype(BF16)
     grad_hidden, branch, mlp_gain_part, gate_sum = mlp_back(
         grad_pair, full_two, hidden_state, grad_out, gain_two, gate_up_part, fsdp_size, ctx_size, 4
     )
-    feedforward_part = dot(inner_flat, down_w, NT).astype(BF16)
-    branch_all, grad_gate_logit, grads, up_sum = out_back(
+    branch_all, grad_gate_logit, grads, up_sum, feedforward_part, down_part = out_back(
         branch,
         full_out,
         out_gate,
         attended,
         gate_up_part,
+        inner_act,
+        down_w,
+        grad_all,
         layout,
         item_count,
         fsdp_size,
@@ -1817,20 +1939,20 @@
 
     out_part = jnp.concatenate(
         [
-            dot(grad_flat, inner_flat, TN).astype(BF16),
             dot(branch_flat, mixed.reshape(all_rows, inner_width), TN).astype(BF16),
             dot(normed_flat, logit_flat, TN).astype(BF16),
         ],
         axis=1,
     )
-    grad_items, forget_items, out_sum, feedforward = context_back(
+    grad_items, forget_items, down_sum, out_sum, feedforward = context_back(
         grads,
         qkv,
         exact,
         lse,
         decay,
+        down_part,
         out_part,
-        feedforward_part.reshape(tp_size, -1, model_width),
+        feedforward_part,
         fsdp_size,
         head_size,
         8,
@@ -1886,12 +2008,12 @@
         qkv_sum[:, 2 * wide : 3 * wide],
         qkv_sum[:, 3 * wide : 3 * wide + head_count],
         forget_bias_grad,
-        out_sum[:, hidden + wide :],
-        out_sum[:, hidden : hidden + wide],
+        out_sum[:, wide:],
+        out_sum[:, :wide],
         mlp_gain_grad,
         gate_sum,
         up_sum,
-        out_sum[:, :hidden],
+        down_sum,
     )
 
 

time: 955 us -> 922 us (0.965)
  matrix products: 66.3 us -> 52.9 us
  Pallas kernels: 832 us -> 819 us
    pallas_call x1, Pallas kernels: 71.2 us -> 51.5 us  [startup(): pl.pallas_call(functools.partial(startup_kernel, len(shards)), out_shape=...]
    pallas_call x1, Pallas kernels: 60.8 us -> 79.9 us  [out_back(): pl.pallas_call(functools.partial(out_back_kernel, layout), grid=(1,), out...]
    dot_general x7 -> x5, matrix products: 66.3 us -> 52.9 us  [dot(): return lax.dot_general(left, right, dims, preferred_element_type=F32)]
    pallas_call x1, Pallas kernels: 52.4 us -> 40.7 us  [mlp(): pl.pallas_call(mlp_kernel, grid=(1,), out_shape=[jax.ShapeDtypeStruct(gra...]
where the time goes in v7:
time: 922 us; the launch traced here: 913 us
  Pallas kernels  819 us (89%)
  matrix products  52.9 us (6%)
  local copies, waits for them, and re-layouts  34.8 us (4%)
    pallas_call x1, Pallas kernels, context_back(): pl.pallas_call(functools.partial(context_back_kernel, heads, head_size),...  205 us
    pallas_call x1, Pallas kernels, context(): pl.pallas_call(functools.partial(context_kernel, heads, head_size), grid=...  201 us
    pallas_call x1, Pallas kernels, last(): pl.pallas_call(last_kernel, grid=(1,), out_shape=[jax.ShapeDtypeStruct(x....  102 us
    pallas_call x1, Pallas kernels, out_back(): pl.pallas_call(functools.partial(out_back_kernel, layout), grid=(1,), out...  79.9 us
    pallas_call x1, Pallas kernels, mlp_back(): pl.pallas_call(mlp_back_kernel, grid=(1,), out_shape=[jax.ShapeDtypeStruc...  71.3 us
    dot_general x5, matrix products, dot(): return lax.dot_general(left, right, dims, preferred_element_type=F32)  52.9 us
    pallas_call x1, Pallas kernels, startup(): pl.pallas_call(functools.partial(startup_kernel, len(shards)), out_shape=...  51.5 us
    pallas_call x1, Pallas kernels, out_project(): pl.pallas_call(functools.partial(out_kernel, layout), grid=(1,), out_shap...  50.2 us

profile of v7, /device:TPU:0, one launch (start us, length us, event | category | flops | bytes accessed | tf_op | source)
XLA Modules:
  0.0 913.2 jit_solution(5294467181984875236)
XLA Ops:
  0.7 1.7 copy.56
  2.7 51.5 %startup.1 = (bf16[4,512,1536]{2,1,0:T(8,128)(2,1)S(1)}, bf16[1536,1280]{1,0:T(8,128)(2,1)S(1)}, f32[8,8,256]{2,1,0:T(8,128)S(1)}) custom-call(bf16[512,1536]{1,0:T(8,128)(2,1)S(1)} %bitcast.126, f32[8,256]{1,0:T(8,128)S(1)} %fusion.19.gain_ref, bf16[192,384]{1,0:T(8,128)(2,1)S(1)} %copy-done.7, bf16[192,384]{1,0:T(8,128)(2,1)S(1)} %copy-done.8, ...), custom_call_target="tpu_custom_call" | custom-call | tf_op jit(solution)/shard_map/startup/pallas_call | solution.py:1137
  54.3 2.7 copy-done.12
  56.9 1.9 copy-done.13
  58.9 2.1 copy-done.14
  61.0 15.9 %project.1 = (bf16[4,512,1536]{2,1,0:T(8,128)(2,1)}, f32[4,512,128]{2,1,0:T(8,128)S(1)}, bf16[3,4,3,512,128]{4,3,2,1,0:T(8,128)(2,1)}) custom-call(bf16[4,512,1536]{2,1,0:T(8,128)(2,1)} %copy-done.12, f32[1,1536]{1,0:T(1,128)S(1)} %reshape_squeeze.6.gain_ref, bf16[1536,1280]{1,0:T(8,128)(2,1)S(1)} %copy-done.14), custom_call_target="tpu_custom_call" | custom-call | flops 8053063680 | bytes 12582912 | tf_op jit(solution)/shard_map/project/pallas_call | solution.py:1192
  78.8 1.0 copy.71
  81.1 201.2 %context.1 = (bf16[3,4,512,128]{3,2,1,0:T(8,128)(2,1)S(1)}, bf16[3,4,3,512,128]{4,3,2,1,0:T(8,128)(2,1)}, bf16[1536,2048]{1,0:T(8,128)(2,1)}, bf16[1536,768]{1,0...) custom-call(bf16[3,4,3,512,128]{4,3,2,1,0:T(8,128)(2,1)} %get-tuple-, ...), custom_call_target="tpu_custom_call" | custom-call | flops 12884901888 | bytes 104857600 | tf_op jit(solution)/shard_map/context/pallas_call | solution.py:360
  282.3 7.3 add_divide_fusion
  289.7 50.2 %out_project.1 = (f32[512,1536]{1,0:T(8,128)}, bf16[512,1536]{1,0:T(8,128)(2,1)S(1)}, bf16[4,512,384]{2,1,0:T(8,128)(2,1)S(1)}, bf16[4,512,384]{2,1,0:T(8,128)(2,1)S(1)}, bf16[1536,1024]{1,0:T(8,128)(2,1)}) custom-call(bf16[512,1536]{1,0:T(8,128)(2,1)} %bitcast.127, f32[4,512,384]{2,1,0:T(8,128)} %bitcast.131, ...), custom_call_target="tpu_custom_call" | custom-call | flops 2415919104 | bytes 104857600 | tf_op jit(solution)/shard_map/out_project/pallas_call | solution.py:1270
  339.9 1.2 copy-done.3
  341.0 1.1 copy-done.15
  342.2 40.7 %mlp.1 = (bf16[4,512,1536]{2,1,0:T(8,128)(2,1)}, bf16[4,512,1024]{2,1,0:T(8,128)(2,1)}, bf16[4,512,2048]{2,1,0:T(8,128)(2,1)}) custom-call(bf16[512,1536]{1,0:T(8,128)(2,1)} %copy-done.15, bf16[4,512,1536]{2,1,0:T(8,128)(2,1)} %get-tuple-element.64.grad_hbm, bf16[1536,2048]{1,0:T(8,128)(2,1)} %get-tuple-element.65.gate_hbm.w_hbm, ...), custom_call_target="tpu_custom_call" | custom-call | flops 19327352832 | bytes 104857600 | tf_op jit(solution)/shard_map/mlp/pallas_call | solution.py:1353
  382.9 19.3 %bitcast_convert_fusion.sums_ref = bf16[1536,2048]{1,0:T(8,128)(2,1)} fusion(bf16[4,512,1536]{2,1,0:T(8,128)(2,1)} %get-tuple-element.68, bf16[4,512,2048]{2,1,0:T(8,128)(2,1)} %get-tuple-element.67.pair_hbm), kind=kOutput, calls=%fused_computation | convolution fusion | flops 12888047616 | bytes 20971520 | tf_op jit(solution)/shard_map/dot_general | solution.py:22
  402.2 71.3 %mlp_back.1 = (f32[512,1536]{1,0:T(8,128)}, bf16[512,1536]{1,0:T(8,128)(2,1)}, f32[1,1536]{1,0:T(1,128)}, f32[192,1024]{1,0:T(8,128)}) custom-call(bf16[4,512,2048]{2,1,0:T(8,128)(2,1)} %get-tuple-element.67.pair_hbm, bf16[1536,2048]{1,0:T(8,128)(2,1)} %get-tuple-element.65.gate_hbm.w_hbm, f32[512,1536]{1,0:T(8,128)} %get-tuple-element.62.hidden_hbm, ...), custom_call_target="tpu_custom_call" | custom-call | flops 12884901888 | bytes 104857600 | tf_op jit(solution)/shard_map/mlp_back/pallas_call | solution.py:1437
  473.5 79.9 %out_back.1 = (bf16[4,512,1536]{2,1,0:T(8,128)(2,1)}, bf16[4,512,384]{2,1,0:T(8,128)(2,1)}, bf16[3,4,512,128]{3,2,1,0:T(8,128)(2,1)}, f32[192,1024]{1,0:T(8,128)...) custom-call(bf16[512,1536]{1,0:T(8,128)(2,1)} %get-tuple-element.69.branch_ref, ...), custom_call_target="tpu_custom_call" | custom-call | flops 2415919104 | bytes 104857600 | tf_op jit(solution)/shard_map/out_back/pallas_call | solution.py:1589
  553.4 6.4 fusion.4
  559.8 6.3 fusion.5
  566.1 1.6 pad_maximum_fusion.part_ref
  567.7 205.1 %context_back.1 = (bf16[3,4,3,512,128]{4,3,2,1,0:T(8,128)(2,1)}, f32[3,4,8,512]{3,2,1,0:T(8,128)}, f32[192,1024]{1,0:T(8,128)}, f32[192,768]{1,0:T(8,128)}, bf16[512,1536]{1,0:T(8,128)(2,1)}) custom-call(bf16[3,4,512,128]{3,2,1,0:T(8,128)(2,1)} %get-tuple-element.72.items_ref, bf16[3,4,3,512,128]{4,3,2,1,0:T(8,128)(2,1)} %get-tuple-element.73.qkv_ref, ...), custom_call_target="tpu_custom_call" | custom-call | flops 32212254720 | bytes 104857600 | tf_op jit(solution)/shard_map/context_back/pallas_call | solution.py:495
  772.8 0.9 fusion.11
  775.9 2.5 copy-done.1
  778.4 1.2 assemble.1.qkv_hbm
  779.7 13.7 %convolution_convert_fusion.part_ref = bf16[1536,1280]{1,0:T(8,128)(2,1)} fusion(bf16[2048,1536]{1,0:T(8,128)(2,1)} %bitcast.156, bf16[2048,128]{1,0:T(8,128)(2,1)S(1)} %copy.82, bf16[2048,1152]{1,0:T(8,128)(2,1)S(1)} %bitcast.129), kind=kOutput, calls=%fused_computation.1 | convolution fusion | flops 8065515520 | bytes 15466496 | tf_op jit(solution)/shard_map/dot_general | solution.py:22
  793.3 101.5 %last.1 = (bf16[512,1536]{1,0:T(8,128)(2,1)}, f32[192,1280]{1,0:T(8,128)}, f32[8,1536]{1,0:T(8,128)}) custom-call(bf16[4,512,1152]{2,1,0:T(8,128)(2,1)} %copy-done.2, bf16[4,512,384]{2,1,0:T(8,128)(2,1)} %get-tuple-element.80.logit_hbm, bf16[4,512,128]{2,1,0:T(8,128)(2,1)} %bitcast.138, bf16[1536,1280]{1,0:T(8,128)(2,1)} %copy-done.13, ...), custom_call_target="tpu_custom_call" | custom-call | flops 10468982784 | bytes 104857600 | tf_op jit(solution)/shard_map/last/pallas_call | solution.py:1754
  894.9 3.9 copy.109
  898.8 2.1 fusion.23
  900.9 0.9 slice.148
  902.5 0.9 fusion.25
  905.3 1.8 multiply_convert_fusion
  907.1 2.4 copy.110
  910.3 0.9 copy.128
  (134 shorter events, 10.5 us)
Async XLA Ops:
  0.6 1.8 copy-start.32
  0.7 2.0 copy-start.35
  0.7 2.0 copy-start.36
  0.7 2.0 copy-start.7
  0.7 2.0 copy-start.8
  0.7 2.0 copy-start.9
  2.4 74.5 %copy-start = (bf16[4,128,1536]{2,1,0:T(8,128)(2,1)}, bf16[4,128,1536]{2,1,0:T(8,128)(2,1)S(1)}, u32[]{:S(2)}) copy-start(bf16[4,128,1536]{2,1,0:T(8,128)(2,1)S(1)} %copy.56) | copy-start | bytes 4718596
  54.2 2.7 copy-start.12
  56.9 1.9 copy-start.13
  58.9 18.0 %copy-start.11 = (f32[1,1536]{1,0:T(1,128)}, f32[1,1536]{1,0:T(1,128)S(1)}, u32[]{:S(2)}) copy-start(f32[1,1536]{1,0:T(1,128)S(1)} %reshape_squeeze.6.gain_ref) | copy-start | bytes 18436
  58.9 2.1 copy-start.14
  61.0 16.3 %copy-start.37 = (bf16[6]{0:T(256)(128)(2,1)S(1)}, bf16[6]{0:T(256)(128)(2,1)}, u32[]{:S(2)}) copy-start(bf16[6]{0:T(256)(128)(2,1)} %param.22) | copy-start | bytes 40
  61.0 16.4 %copy-start.33 = (s32[4]{0:T(128)S(1)}, s32[4]{0:T(128)}, u32[]{:S(2)}) copy-start(s32[4]{0:T(128)} %param.16) | copy-start | bytes 52
  79.9 202.4 %slice-start = ((s8[6291456]{0:T(1024)(128)(4,1)}), s8[4194304]{0:T(1024)(128)(4,1)S(1)}, s32[]{:S(2)}) async-start(s8[6291456]{0:T(1024)(128)(4,1)} %bitcast.157), calls=%async_computation | async-start | bytes 8388608
  81.1 201.2 %copy-start.5 = (bf16[512,1536]{1,0:T(8,128)(2,1)}, bf16[512,1536]{1,0:T(8,128)(2,1)S(1)}, u32[]{:S(2)}) copy-start(bf16[512,1536]{1,0:T(8,128)(2,1)S(1)} %fusion.3.rows_ref.grad_hbm) | copy-start | bytes 4718596
  81.1 201.2 %slice-start.1 = ((s8[6291456]{0:T(1024)(128)(4,1)}), s8[2097152]{0:T(1024)(128)(4,1)S(1)}, s32[]{:S(2)}) async-start(s8[6291456]{0:T(1024)(128)(4,1)} %bitcast.157), calls=%async_computation.1 | async-start | bytes 4194304
  282.2 7.3 copy-start.4
  282.3 7.3 copy-start.20
  282.3 7.3 copy-start.21
  282.3 7.4 copy-start.6
  289.7 50.2 %copy-start.10 = (f32[1,1536]{1,0:T(1,128)}, f32[1,1536]{1,0:T(1,128)S(1)}, u32[]{:S(2)}) copy-start(f32[1,1536]{1,0:T(1,128)S(1)} %reshape_squeeze.7.gain_ref) | copy-start | bytes 18436
  553.4 6.4 copy-start.34
  567.7 207.2 %copy-start.31 = (f32[1,1536]{1,0:T(1,128)S(1)}, f32[1,1536]{1,0:T(1,128)}, u32[]{:S(2)}) copy-start(f32[1,1536]{1,0:T(1,128)} %get-tuple-element.86) | copy-start | bytes 18436
  775.9 3.8 copy-start.28
  775.9 2.5 copy-start.1
  779.6 13.7 %copy-start.2 = (bf16[4,512,1152]{2,1,0:T(8,128)(2,1)}, bf16[4,512,1152]{2,1,0:T(8,128)(2,1)S(1)}, u32[]{:S(2)}) copy-start(bf16[4,512,1152]{2,1,0:T(8,128)(2,1)S(1)} %assemble.1.qkv_hbm) | copy-start | bytes 14155780
  894.9 10.4 %copy-start.22 = (f32[512,1536]{1,0:T(8,128)S(1)}, f32[512,1536]{1,0:T(8,128)}, u32[]{:S(2)}) copy-start(f32[512,1536]{1,0:T(8,128)} %get-tuple-element.62.hidden_hbm) | copy-start | bytes 9437188
  894.9 10.4 %copy-start.30 = (f32[512]{0:T(512)S(1)}, f32[512]{0:T(512)}, u32[]{:S(2)}) copy-start(f32[512]{0:T(512)} %copy-done.29) | copy-start | bytes 6148
  907.1 2.4 copy-start.27
  907.1 3.2 copy-start.24
  907.1 4.1 copy-start.25
  907.1 5.0 copy-start.26
  (8 other events, 9.6 us)

commit v8 on v7

--- a/solution.py
+++ b/solution.py
@@ -249,6 +249,7 @@
     out_w_ref,
     gate_out_ref,
     rows_ref,
+    normed_hbm,
     back_ref,
     qkv_ref,
     full_ref,
@@ -257,10 +258,11 @@
     exact_ref,
     lse_ref,
     decay_ref,
+    out_gate_ref,
     *refs,
 ):
-    qkv, forget, out, save_sem = refs[:4]
-    sems = refs[4:]
+    qkv, forget, out, normed, gate_w, fetch_sem, save_sem = refs[:7]
+    sems = refs[7:]
     count, size, _, block, width = items_ref.shape
     tp, sibling, across, diagonal = tp_places()
     greet_all([{"tp": sibling}, {"tp": across}] + group_peers())
@@ -270,6 +272,7 @@
         WeightGather((gate_ref, up_ref), full_ref, sems[14:19]),
     )
     rows = RowGather(rows_ref, table_ref, sems[19:])
+    fetch = Fetch([(normed_hbm, normed)], fetch_sem)
     forgets = Exchange(me, size, forget_ref, forget, sems[0:3])
     inputs = Exchange(me, size, items_ref, qkv, sems[3:6])
     results = Exchange(me, size, out, back_ref, sems[6:9])
@@ -327,6 +330,20 @@
         for gather in gathers:
             gather.advance(hop)
 
+    gathers[0].end()
+    inner = gate_w.shape[1]
+    copy = pltpu.make_async_copy(full_out_ref.at[:, pl.ds(inner, inner)], gate_w, fetch_sem.at[1])
+    copy.start()
+    fetch.wait()
+    copy.wait()
+    step_rows = normed.shape[1] // CHUNKS
+
+    @pl.loop(0, 4 * CHUNKS)
+    def _(step):
+        spot = pl.ds(pl.multiple_of(lax.rem(step, CHUNKS) * step_rows, step_rows), step_rows)
+        logit = dot(normed[step // CHUNKS, spot], gate_w[...], NN)
+        out_gate_ref[step // CHUNKS, spot] = 1.0 / (1.0 + jnp.exp(-logit))
+
     @pl.loop(0, count)
     def _(item):
         forgets.drain(item)
@@ -334,8 +351,7 @@
         results.arrive(item)
         results.drain(item)
 
-    for gather in gathers:
-        gather.end()
+    gathers[1].end()
     rows.end()
 
 
@@ -351,9 +367,10 @@
     )
 
 
-def context(items, forget, shards, rows, f_size, head_size, ident):
+def context(items, forget, shards, rows, normed, f_size, head_size, ident):
     count, size, _, block, width = items.shape
     full = shards[0].shape[0] * f_size * size
+    gate = normed.shape[:2] + shards[3].shape[1:]
     heads = width // head_size
     place = pl.BlockSpec(memory_space=pl.ANY)
     exact, stat = (count, size, block, width), (count, 8, size * block)
@@ -369,15 +386,20 @@
             jax.ShapeDtypeStruct(exact, F32),
             jax.ShapeDtypeStruct(stat, F32),
             jax.ShapeDtypeStruct(stat, F32),
+            jax.ShapeDtypeStruct(gate, F32),
         ],
         in_specs=[place, place]
         + [full_block(shard.shape) for shard in shards]
-        + [full_block(rows.shape)],
-        out_specs=[place, place, place, place, place, full_block(exact), full_block(stat), full_block(stat)],
+        + [full_block(rows.shape), place],
+        out_specs=[place] * 5
+        + [full_block(exact), full_block(stat), full_block(stat), full_block(gate)],
         scratch_shapes=[
             pltpu.VMEM(items.shape, BF16),
             pltpu.VMEM(forget.shape, F32),
             pltpu.VMEM(exact, BF16),
+            pltpu.VMEM(normed.shape, BF16),
+            pltpu.VMEM((full, shards[3].shape[1]), BF16),
+            pltpu.SemaphoreType.DMA((2,)),
             pltpu.SemaphoreType.DMA,
         ]
         + exchange_sems(count, size) * 3
@@ -387,7 +409,7 @@
         compiler_params=remote_params(ident, 48),
         cost_estimate=attend_cost(items, heads, 2),
         name="context",
-    )(items, forget, *shards, rows)
+    )(items, forget, *shards, rows, normed)
 
 
 def context_back_kernel(
@@ -400,7 +422,8 @@
     decay_ref,
     down_ref,
     part_ref,
-    table_ref,
+    inner_hbm,
+    down_w_hbm,
     back_ref,
     forget_ref,
     down_sum_ref,
@@ -411,6 +434,8 @@
     grads, dqkv, change, slope, dq_acc, delta = refs[:6]
     sems = refs[6:15]
     count, size, block, width = items_ref.shape
+    inner, down_w, table, fetch_sem = refs[36:]
+    fetch = Fetch([(inner_hbm, inner), (down_w_hbm, down_w)], fetch_sem)
     tp, sibling, across, diagonal = tp_places()
     greet_all([{"tp": sibling}, {"tp": across}] + group_peers())
     me = lax.axis_index("ctx")
@@ -418,7 +443,7 @@
         WeightSum(part_ref, 0, sum_ref, refs[15:23]),
         WeightSum(down_ref, 0, down_sum_ref, refs[23:31]),
     )
-    rows = RowSum(table_ref, rows_ref, refs[31:])
+    rows = RowSum(table, rows_ref, refs[31:36])
     inputs = Exchange(me, size, items_ref, grads, sems[0:3])
     results = Exchange(me, size, dqkv, back_ref, sems[3:6])
     forgets = Exchange(me, size, slope, forget_ref, sems[6:9])
@@ -426,6 +451,15 @@
     inputs.start(0)
     for weights in sums:
         weights.begin()
+    fetch.wait()
+    step_rows = inner.shape[1] // CHUNKS
+
+    @pl.loop(0, 4 * CHUNKS)
+    def _(step):
+        spot = pl.ds(pl.multiple_of(lax.rem(step, CHUNKS) * step_rows, step_rows), step_rows)
+        forward = dot(inner[step // CHUNKS, spot], down_w[...], NT)
+        table[step // CHUNKS, spot] = forward.astype(BF16)
+
     rows.begin()
 
     @pl.loop(0, count)
@@ -449,7 +483,10 @@
             heads,
             head_size,
         )
-        results.start(item)
+        @pl.when(item > 0)
+        def _():
+            results.start(item)
+
         lower = triangle(False)
         after = jnp.zeros((8, 1), F32)
         for start in reversed(range(0, size * block, LANES)):
@@ -463,14 +500,14 @@
             @pl.when(item == turn)
             def _(turn=turn):
                 for weights in sums:
-                    weights.run_share(turn, count + 1)
+                    weights.run_round(turn)
                 if turn == 0:
+                    results.start(0)
                     rows.advance()
 
-    share = -(-sums[0].stages // (count + 1))
-    for n in range(count * share, sums[0].stages):
+    for n in range(count, sums[0].rounds()):
         for weights in sums:
-            weights.run(n)
+            weights.run_round(n)
 
     @pl.loop(0, count)
     def _(item):
@@ -485,13 +522,14 @@
     rows.end()
 
 
-def context_back(grads, qkv, exact, lse, decay, down, part, table, f_size, head_size, ident):
+def context_back(grads, qkv, exact, lse, decay, down, part, inner_act, down_w, f_size, head_size, ident):
     count, size, _, block, width = qkv.shape
     heads = width // head_size
     place = pl.BlockSpec(memory_space=pl.ANY)
     forget = (count, size, 8, block)
     total = (part.shape[0] // (f_size * size), part.shape[1])
     down_total = (total[0], down.shape[1])
+    table = inner_act.shape[:2] + down_w.shape[:1]
     return pl.pallas_call(
         functools.partial(context_back_kernel, heads, head_size),
         grid=(1,),
@@ -500,7 +538,7 @@
             jax.ShapeDtypeStruct(forget, F32),
             jax.ShapeDtypeStruct(down_total, F32),
             jax.ShapeDtypeStruct(total, F32),
-            jax.ShapeDtypeStruct(table.shape[1:], BF16),
+            jax.ShapeDtypeStruct(table[1:], BF16),
         ],
         in_specs=[
             place,
@@ -511,13 +549,14 @@
             place,
             place,
             place,
+            place,
         ],
         out_specs=[
             place,
             place,
             full_block(down_total),
             full_block(total),
-            full_block(table.shape[1:]),
+            full_block(table[1:]),
         ],
         scratch_shapes=[
             pltpu.VMEM(grads.shape, BF16),
@@ -530,15 +569,22 @@
         + exchange_sems(count, size) * 3
         + sum_scratch(f_size, size, *total)
         + sum_scratch(f_size, size, *down_total)
-        + row_sum_scratch(*table.shape[1:]),
-        compiler_params=remote_params(ident, 60),
+        + row_sum_scratch(*table[1:])
+        + [
+            pltpu.VMEM(inner_act.shape, BF16),
+            pltpu.VMEM(down_w.shape, BF16),
+            pltpu.VMEM(table, BF16),
+            pltpu.SemaphoreType.DMA((2,)),
+        ],
+        compiler_params=remote_params(ident, 62),
         cost_estimate=attend_cost(qkv, heads, 5),
         name="context_back",
-    )(grads, qkv, exact, lse, decay, down, part, table)
+    )(grads, qkv, exact, lse, decay, down, part, inner_act, down_w)
 
 
 CHUNKS = 4
 HALVES = 2
+SUM_CHUNKS = 2
 
 
 def tp_places():
@@ -655,7 +701,7 @@
     near_send, near_recv, far_send, far_recv = sems
     me, sibling, across, diagonal = tp_places()
     mine, near_by, far_off, corner = (0, 1, 2, 3) if relative else (me, sibling, across, diagonal)
-    rows = far_out.shape[0] // CHUNKS
+    rows = far_out.shape[0] // SUM_CHUNKS
 
     def span(chunk):
         return pl.ds(pl.multiple_of(chunk * rows, rows), rows)
@@ -679,7 +725,7 @@
         )
 
     def body(step, _):
-        phase, chunk = step // CHUNKS, lax.rem(step, CHUNKS)
+        phase, chunk = step // SUM_CHUNKS, lax.rem(step, SUM_CHUNKS)
         slot = jnp.where(
             phase == 0, corner, jnp.where(phase == 1, far_off, jnp.where(phase == 2, near_by, mine))
         )
@@ -708,19 +754,19 @@
         return 0
 
     if between is None:
-        lax.fori_loop(0, 4 * CHUNKS, body, 0)
+        lax.fori_loop(0, 4 * SUM_CHUNKS, body, 0)
     else:
-        lax.fori_loop(0, CHUNKS, body, 0)
+        lax.fori_loop(0, SUM_CHUNKS, body, 0)
         for phase in (1, 2, 3):
             between(phase)
-            lax.fori_loop(phase * CHUNKS, (phase + 1) * CHUNKS, body, 0)
-    for chunk in range(CHUNKS):
+            lax.fori_loop(phase * SUM_CHUNKS, (phase + 1) * SUM_CHUNKS, body, 0)
+    for chunk in range(SUM_CHUNKS):
         near(0, chunk).wait_send()
         near(1, chunk).wait_send()
         far(chunk).wait_send()
 
 
-SCATTER_SEMS = [pltpu.SemaphoreType.DMA((2, CHUNKS))] * 2 + [pltpu.SemaphoreType.DMA((CHUNKS,))] * 2
+SCATTER_SEMS = [pltpu.SemaphoreType.DMA((2, SUM_CHUNKS))] * 2 + [pltpu.SemaphoreType.DMA((SUM_CHUNKS,))] * 2
 
 
 def scatter_buffers(rows, width):
@@ -949,9 +995,19 @@
         for n in range(min(first, self.stages), min(last, self.stages)):
             self.run(n)
 
-    def run_share(self, turn, turns):
-        share = -(-self.stages // turns)
-        self.run_to(turn * share, (turn + 1) * share)
+    def rounds(self):
+        return self.c_size + 1
+
+    def run_round(self, n):
+        count = len(self.order)
+        for i, (c, h) in enumerate(self.order):
+            hop = n if i < 5 * count // 8 else n - 1
+            if hop == 0:
+                self.receive(i)
+            if 1 <= hop <= c:
+                self.hop(c, h, 1, hop)
+            if 1 <= hop <= self.c_size - 1 - c:
+                self.hop(c, h, 0, self.c_size - 1 - hop)
 
     def end(self):
         for c in range(self.c_size):
@@ -1031,11 +1087,8 @@
 class RowSum:
     def __init__(self, table, out, refs):
         self.table, self.out = table, out
-        self.mine, self.near, self.far_out, self.far_in, self.send, self.recv, self.own_sem = refs
+        self.near, self.far_out, self.far_in, self.send, self.recv = refs
         _, self.sibling, self.across, _ = tp_places()
-
-    def own(self, n):
-        return pltpu.make_async_copy(self.table.at[0 if n else 2], self.mine.at[n], self.own_sem.at[n])
 
     def copy(self, n):
         if n == 2:
@@ -1047,20 +1100,16 @@
     def begin(self):
         for n in range(2):
             self.copy(n).start()
-        for n in range(2):
-            self.own(n).start()
 
     def advance(self):
-        self.own(0).wait()
         self.copy(0).wait_recv()
-        self.far_out[...] = (self.mine[0].astype(F32) + self.near[0].astype(F32)).astype(BF16)
+        self.far_out[...] = (self.table[2].astype(F32) + self.near[0].astype(F32)).astype(BF16)
         self.copy(2).start()
 
     def end(self):
-        self.own(1).wait()
         self.copy(1).wait_recv()
         self.copy(2).wait_recv()
-        total = self.mine[1].astype(F32) + self.near[1].astype(F32)
+        total = self.table[0].astype(F32) + self.near[1].astype(F32)
         self.out[...] = (total + self.far_in[...].astype(F32)).astype(BF16)
         for n in range(3):
             self.copy(n).wait_send()
@@ -1068,7 +1117,7 @@
 
 def row_sum_scratch(rows, width):
     dma, pair, one = pltpu.SemaphoreType.DMA, (2, rows, width), (rows, width)
-    return [pltpu.VMEM(pair, BF16)] * 2 + [pltpu.VMEM(one, BF16)] * 2 + [dma((3,))] * 2 + [dma((2,))]
+    return [pltpu.VMEM(pair, BF16)] + [pltpu.VMEM(one, BF16)] * 2 + [dma((3,))] * 2
 
 
 def startup_kernel(parts, rows_ref, gain_ref, *refs):
@@ -1142,7 +1191,7 @@
             jax.ShapeDtypeStruct((f_size * c_size,) + gains.shape, F32),
         ],
         in_specs=[pl.BlockSpec(memory_space=pltpu.VMEM)] * (2 + len(shards)),
-        out_specs=[place] * 3,
+        out_specs=[pl.BlockSpec(memory_space=pltpu.HBM)] * 2 + [place],
         scratch_shapes=[pltpu.SemaphoreType.DMA]
         + GATHER_SEMS
         + weight_sems(f_size, c_size, len(shards))
@@ -1237,7 +1286,7 @@
         return 0
 
     lax.fori_loop(0, tp_size, mix, 0)
-    size = rows // CHUNKS
+    size = rows // SUM_CHUNKS
 
     def span(chunk):
         return pl.ds(pl.multiple_of(chunk * size, size), size)
@@ -1400,7 +1449,7 @@
     weights.begin()
     fetch.wait()
     part_ref[...] = jnp.zeros_like(part_ref)
-    size = hidden_ref.shape[0] // CHUNKS
+    size = hidden_ref.shape[0] // SUM_CHUNKS
 
     def span(chunk):
         return pl.ds(pl.multiple_of(chunk * size, size), size)
@@ -1483,36 +1532,34 @@
     attended_ref,
     sums_ref,
     inner_hbm,
-    down_hbm,
     grad_hbm,
     all_ref,
     logit_ref,
     items,
     sum_ref,
-    forward_hbm,
     part_hbm,
     *refs,
 ):
     seq_count, groups, width, places = layout
     table, grads, own_sem = refs[:3]
     sems = refs[3:9]
-    inner_ref, down_w, grad_ref, forward, part, fetch_sem, write_sem = refs[9:16]
+    inner_ref, grad_ref, part, fetch_sem, write_sem = refs[9:14]
     count = items.shape[0]
     me, sibling, across, diagonal = tp_places()
     greet_all([{"tp": sibling}, {"tp": across}] + group_peers())
-    weights = WeightSum(sums_ref, sum_ref.shape[1], sum_ref, refs[16:])
+    weights = WeightSum(sums_ref, sum_ref.shape[1], sum_ref, refs[14:])
     weights.begin()
     table[me] = branch_ref[...]
     tp_size, rows, _ = gate_ref.shape
     local, size = rows // seq_count, rows // CHUNKS
     model_width, hidden = part.shape
     tile = 2 * LANES
-    steps, tiles = 4 * CHUNKS, model_width // tile
+    tiles = model_width // tile
     fetches = []
 
     def begin_fetch():
         fetches.append(
-            Fetch([(inner_hbm, inner_ref), (down_hbm, down_w), (grad_hbm, grad_ref)], fetch_sem)
+            Fetch([(inner_hbm, inner_ref), (grad_hbm, grad_ref)], fetch_sem)
         )
 
     def compute(slot, chunk):
@@ -1524,12 +1571,6 @@
         attended = attended_ref[slot, spot].astype(F32)
         logit_ref[slot, spot] = (scaled * attended * (1.0 - gate)).astype(BF16)
 
-    def project_down(step, _):
-        slot, chunk = step // CHUNKS, lax.rem(step, CHUNKS)
-        spot = pl.ds(pl.multiple_of(chunk * size, size), size)
-        forward[slot, spot] = dot(inner_ref[slot, spot], down_w[...], NT).astype(BF16)
-        return 0
-
     def down_grad(n, _):
         columns = pl.ds(pl.multiple_of(n * tile, tile), tile)
         left = grad_ref[:, :, columns].reshape(tp_size * rows, tile)
@@ -1542,7 +1583,6 @@
 
     def stage(n):
         weights.run(n)
-        lax.fori_loop(n * steps // last, (n + 1) * steps // last, project_down, 0)
         lax.fori_loop(n * tiles // last, (n + 1) * tiles // last, down_grad, 0)
 
     def between():
@@ -1553,8 +1593,7 @@
     gather_loop(table, sems, compute, between=between, ready=begin_fetch)
     copies = [
         pltpu.make_async_copy(table, all_ref, own_sem),
-        pltpu.make_async_copy(forward, forward_hbm, write_sem.at[0]),
-        pltpu.make_async_copy(part, part_hbm, write_sem.at[1]),
+        pltpu.make_async_copy(part, part_hbm, write_sem),
     ]
     copies[0].start()
 
@@ -1576,13 +1615,14 @@
 
 
 def out_back(
-    branch, full_out, gate, attended, part, inner_act, down_w, grad_all, layout, item_count, f_size, ctx_size, ident
+    branch, full_out, gate, attended, part, inner_act, grad_all, layout, item_count, f_size, ctx_size, ident
 ):
     seq_count, groups, width, places = layout
     rows, model_width = branch.shape
     tp_size, _, inner = gate.shape
     item = (item_count, ctx_size, tp_size * rows // seq_count, width)
     table = (tp_size, rows, model_width)
+    down = (model_width, inner_act.shape[2])
     total = (part.shape[0] // (f_size * ctx_size), part.shape[1] // 2)
     place = pl.BlockSpec(memory_space=pl.ANY)
     dma = pltpu.SemaphoreType.DMA
@@ -1594,8 +1634,7 @@
             jax.ShapeDtypeStruct(gate.shape, BF16),
             jax.ShapeDtypeStruct(item, BF16),
             jax.ShapeDtypeStruct(total, F32),
-            jax.ShapeDtypeStruct(table, BF16),
-            jax.ShapeDtypeStruct(down_w.shape, BF16),
+            jax.ShapeDtypeStruct(down, BF16),
         ],
         in_specs=[
             whole(branch.shape),
@@ -1605,19 +1644,16 @@
             place,
             place,
             place,
-            place,
-        ],
-        out_specs=[place, whole(gate.shape), whole(item), whole(total), place, place],
+        ],
+        out_specs=[place, whole(gate.shape), whole(item), whole(total), place],
         scratch_shapes=[pltpu.VMEM(table, BF16), pltpu.VMEM(gate.shape, BF16), dma]
         + GATHER_SEMS
         + [
             pltpu.VMEM(inner_act.shape, BF16),
-            pltpu.VMEM(down_w.shape, BF16),
             pltpu.VMEM(table, BF16),
-            pltpu.VMEM(table, BF16),
-            pltpu.VMEM(down_w.shape, BF16),
-            dma((3,)),
+            pltpu.VMEM(down, BF16),
             dma((2,)),
+            dma,
         ]
         + sum_scratch(f_size, ctx_size, *total),
         compiler_params=remote_params(ident, 60),
@@ -1625,7 +1661,7 @@
             flops=2 * gate.size * model_width, bytes_accessed=100 << 20, transcendentals=0
         ),
         name="out_back",
-    )(branch, full_out, gate, attended, part, inner_act, down_w, grad_all)
+    )(branch, full_out, gate, attended, part, inner_act, grad_all)
 
 
 def assemble_kernel(layout, items, out_ref):
@@ -1695,7 +1731,7 @@
     fetch.wait()
     wide = qkv_ref.shape[2]
     mine[...] = extra_ref[...]
-    size = x_ref.shape[0] // CHUNKS
+    size = x_ref.shape[0] // SUM_CHUNKS
 
     def span(chunk):
         return pl.ds(pl.multiple_of(chunk * size, size), size)
@@ -1887,18 +1923,16 @@
     picked = jnp.stack([cut[g, :, :, s] for s, g in places])
     picked = picked.reshape(ctx_size, item_count, pair, ctx_rows).transpose(1, 0, 2, 3)
     picked = jnp.pad(picked, ((0, 0), (0, 0), (0, 8 - pair), (0, 0)))
-    attended_items, qkv, full_two, full_out, grad_all, exact, lse, decay = context(
+    attended_items, qkv, full_two, full_out, grad_all, exact, lse, decay, out_gate = context(
         items,
         picked,
         (w_gate, w_up, w_out, w_gate_out),
         grad_out,
+        normed_one,
         fsdp_size,
         head_size,
         7,
     )
-    gate_out_w = full_out[:, inner_width:]
-    gate_logit = dot(normed_flat, gate_out_w, NN)
-    out_gate = jax.nn.sigmoid(gate_logit).reshape(tp_size, -1, inner_width)
     hidden_state, normed_two, attended, mixed, down_w = out_project(
         input_rows,
         out_gate,
@@ -1919,14 +1953,13 @@
     grad_hidden, branch, mlp_gain_part, gate_sum = mlp_back(
         grad_pair, full_two, hidden_state, grad_out, gain_two, gate_up_part, fsdp_size, ctx_size, 4
     )
-    branch_all, grad_gate_logit, grads, up_sum, feedforward_part, down_part = out_back(
+    branch_all, grad_gate_logit, grads, up_sum, down_part = out_back(
         branch,
         full_out,
         out_gate,
         attended,
         gate_up_part,
         inner_act,
-        down_w,
         grad_all,
         layout,
         item_count,
@@ -1952,7 +1985,8 @@
         decay,
         down_part,
         out_part,
-        feedforward_part,
+        inner_act,
+        down_w,
         fsdp_size,
         head_size,
         8,

time: 922 us -> 874 us (0.948)
  Pallas kernels: 819 us -> 774 us
    pallas_call x1, Pallas kernels: 79.9 us -> 62.3 us  [out_back(): pl.pallas_call(functools.partial(out_back_kernel, layout), grid=(1,), out...]
    pallas_call x1, Pallas kernels: 102 us -> 90 us  [last(): pl.pallas_call(last_kernel, grid=(1,), out_shape=[jax.ShapeDtypeStruct(x....]
    pallas_call x1, Pallas kernels: 71.3 us -> 60.6 us  [mlp_back(): pl.pallas_call(mlp_back_kernel, grid=(1,), out_shape=[jax.ShapeDtypeStruc...]
    dot_general x5 -> x4, matrix products: 52.9 us -> 45.4 us  [dot(): return lax.dot_general(left, right, dims, preferred_element_type=F32)]
    unnamed x97 -> x89, local copies, waits for them, and re-layouts: 16.8 us -> 19.3 us
where the time goes in v8:
time: 874 us; the launch traced here: 864 us
  Pallas kernels  774 us (89%)
  matrix products  45.4 us (5%)
  local copies, waits for them, and re-layouts  37.3 us (4%)
    pallas_call x1, Pallas kernels, context(): pl.pallas_call(functools.partial(context_kernel, heads, head_size), grid=...  203 us
    pallas_call x1, Pallas kernels, context_back(): pl.pallas_call(functools.partial(context_back_kernel, heads, head_size),...  199 us
    pallas_call x1, Pallas kernels, last(): pl.pallas_call(last_kernel, grid=(1,), out_shape=[jax.ShapeDtypeStruct(x....  90 us
    pallas_call x1, Pallas kernels, out_back(): pl.pallas_call(functools.partial(out_back_kernel, layout), grid=(1,), out...  62.3 us
    pallas_call x1, Pallas kernels, mlp_back(): pl.pallas_call(mlp_back_kernel, grid=(1,), out_shape=[jax.ShapeDtypeStruc...  60.6 us
    pallas_call x1, Pallas kernels, startup(): pl.pallas_call(functools.partial(startup_kernel, len(shards)), out_shape=...  51.5 us
    pallas_call x1, Pallas kernels, out_project(): pl.pallas_call(functools.partial(out_kernel, layout), grid=(1,), out_shap...  49.8 us
    dot_general x4, matrix products, dot(): return lax.dot_general(left, right, dims, preferred_element_type=F32)  45.4 us

profile of v8, /device:TPU:0, one launch (start us, length us, event | category | flops | bytes accessed | tf_op | source)
XLA Modules:
  0.0 863.9 jit_solution(11455367060578220480)
XLA Ops:
  0.7 1.7 copy.56
  2.7 51.5 %startup.1 = (bf16[4,512,1536]{2,1,0:T(8,128)(2,1)S(1)}, bf16[1536,1280]{1,0:T(8,128)(2,1)S(1)}, f32[8,8,256]{2,1,0:T(8,128)S(1)}) custom-call(bf16[512,1536]{1,0:T(8,128)(2,1)S(1)} %bitcast.124, f32[8,256]{1,0:T(8,128)S(1)} %fusion.18.gain_ref, bf16[192,384]{1,0:T(8,128)(2,1)S(1)} %copy-done.7, bf16[192,384]{1,0:T(8,128)(2,1)S(1)} %copy-done.8, ...), custom_call_target="tpu_custom_call" | custom-call | tf_op jit(solution)/shard_map/startup/pallas_call | solution.py:1186
  54.3 2.7 copy-done.12
  56.9 1.9 copy-done.13
  58.9 2.1 copy-done.14
  61.0 15.9 %project.1 = (bf16[4,512,1536]{2,1,0:T(8,128)(2,1)}, f32[4,512,128]{2,1,0:T(8,128)S(1)}, bf16[3,4,3,512,128]{4,3,2,1,0:T(8,128)(2,1)}) custom-call(bf16[4,512,1536]{2,1,0:T(8,128)(2,1)} %copy-done.12, f32[1,1536]{1,0:T(1,128)S(1)} %reshape_squeeze.6.gain_ref, bf16[1536,1280]{1,0:T(8,128)(2,1)S(1)} %copy-done.14), custom_call_target="tpu_custom_call" | custom-call | flops 8053063680 | bytes 12582912 | tf_op jit(solution)/shard_map/project/pallas_call | solution.py:1241
  78.8 1.0 copy.71
  81.0 202.9 %context.1 = (bf16[3,4,512,128]{3,2,1,0:T(8,128)(2,1)S(1)}, bf16[3,4,3,512,128]{4,3,2,1,0:T(8,128)(2,1)}, bf16[1536,2048]{1,0:T(8,128)(2,1)}, bf16[1536,768]{1,0...) custom-call(bf16[3,4,3,512,128]{4,3,2,1,0:T(8,128)(2,1)} %get-tuple-, ...), custom_call_target="tpu_custom_call" | custom-call | flops 12884901888 | bytes 104857600 | tf_op jit(solution)/shard_map/context/pallas_call | solution.py:377
  283.9 1.1 copy-done.4
  286.5 49.8 %out_project.1 = (f32[512,1536]{1,0:T(8,128)}, bf16[512,1536]{1,0:T(8,128)(2,1)S(1)}, bf16[4,512,384]{2,1,0:T(8,128)(2,1)S(1)}, bf16[4,512,384]{2,1,0:T(8,128)(2,1)S(1)}, bf16[1536,1024]{1,0:T(8,128)(2,1)}) custom-call(bf16[512,1536]{1,0:T(8,128)(2,1)} %bitcast.125, f32[4,512,384]{2,1,0:T(8,128)} %get-tuple-element.60.gate_ref, ...), custom_call_target="tpu_custom_call" | custom-call | flops 2415919104 | bytes 104857600 | tf_op jit(solution)/shard_map/out_project/pallas_call | solution.py:1319
  336.3 1.2 copy-done.3
  337.5 1.1 copy-done.15
  338.6 40.7 %mlp.1 = (bf16[4,512,1536]{2,1,0:T(8,128)(2,1)}, bf16[4,512,1024]{2,1,0:T(8,128)(2,1)}, bf16[4,512,2048]{2,1,0:T(8,128)(2,1)}) custom-call(bf16[512,1536]{1,0:T(8,128)(2,1)} %copy-done.15, bf16[4,512,1536]{2,1,0:T(8,128)(2,1)} %get-tuple-element.65.grad_hbm, bf16[1536,2048]{1,0:T(8,128)(2,1)} %get-tuple-element.66.gate_hbm.w_hbm, ...), custom_call_target="tpu_custom_call" | custom-call | flops 19327352832 | bytes 104857600 | tf_op jit(solution)/shard_map/mlp/pallas_call | solution.py:1402
  379.3 19.1 %bitcast_convert_fusion.sums_ref = bf16[1536,2048]{1,0:T(8,128)(2,1)} fusion(bf16[4,512,1536]{2,1,0:T(8,128)(2,1)} %get-tuple-element.69, bf16[4,512,2048]{2,1,0:T(8,128)(2,1)} %get-tuple-element.68.pair_hbm), kind=kOutput, calls=%fused_computation | convolution fusion | flops 12888047616 | bytes 20971520 | tf_op jit(solution)/shard_map/dot_general | solution.py:22
  398.4 60.6 %mlp_back.1 = (f32[512,1536]{1,0:T(8,128)}, bf16[512,1536]{1,0:T(8,128)(2,1)}, f32[1,1536]{1,0:T(1,128)}, f32[192,1024]{1,0:T(8,128)}) custom-call(bf16[4,512,2048]{2,1,0:T(8,128)(2,1)} %get-tuple-element.68.pair_hbm, bf16[1536,2048]{1,0:T(8,128)(2,1)} %get-tuple-element.66.gate_hbm.w_hbm, f32[512,1536]{1,0:T(8,128)} %get-tuple-element.63.hidden_hbm, ...), custom_call_target="tpu_custom_call" | custom-call | flops 12884901888 | bytes 104857600 | tf_op jit(solution)/shard_map/mlp_back/pallas_call | solution.py:1486
  459.1 62.3 %out_back.1 = (bf16[4,512,1536]{2,1,0:T(8,128)(2,1)}, bf16[4,512,384]{2,1,0:T(8,128)(2,1)}, bf16[3,4,512,128]{3,2,1,0:T(8,128)(2,1)}, f32[192,1024]{1,0:T(8,128)}, bf16[1536,1024]{1,0:T(8,128)(2,1)}) custom-call(bf16[512,1536]{1,0:T(8,128)(2,1)} %get-tuple-element.70.branch_ref, bf16[1536,768]{1,0:T(8,128)(2,1)} %get-tuple-element.61.w_ref.gate_w_hbm, ...), custom_call_target="tpu_custom_call" | custom-call | flops 2415919104 | bytes 104857600 | tf_op jit(solution)/shard_map/out_back/pallas_call | solution.py:1629
  521.4 6.4 fusion.4
  527.8 6.3 fusion.5
  534.1 1.6 pad_maximum_fusion.part_ref
  535.7 199.5 %context_back.1 = (bf16[3,4,3,512,128]{4,3,2,1,0:T(8,128)(2,1)}, f32[3,4,8,512]{3,2,1,0:T(8,128)}, f32[192,1024]{1,0:T(8,128)}, f32[192,768]{1,0:T(8,128)}, bf16[512,1536]{1,0:T(8,128)(2,1)}) custom-call(bf16[3,4,512,128]{3,2,1,0:T(8,128)(2,1)} %get-tuple-element.73.items_ref, bf16[3,4,3,512,128]{4,3,2,1,0:T(8,128)(2,1)} %get-tuple-element.74.qkv_ref, ...), custom_call_target="tpu_custom_call" | custom-call | flops 32212254720 | bytes 104857600 | tf_op jit(solution)/shard_map/context_back/pallas_call | solution.py:533
  735.2 0.9 fusion.10
  738.3 2.5 copy-done.1
  740.8 1.2 assemble.1.qkv_hbm
  742.0 13.7 %convolution_convert_fusion.part_ref = bf16[1536,1280]{1,0:T(8,128)(2,1)} fusion(bf16[2048,1536]{1,0:T(8,128)(2,1)} %bitcast.152, bf16[2048,128]{1,0:T(8,128)(2,1)S(1)} %copy.82, bf16[2048,1152]{1,0:T(8,128)(2,1)S(1)} %bitcast.127), kind=kOutput, calls=%fused_computation.1 | convolution fusion | flops 8065515520 | bytes 15466496 | tf_op jit(solution)/shard_map/dot_general | solution.py:22
  755.7 90.0 %last.1 = (bf16[512,1536]{1,0:T(8,128)(2,1)}, f32[192,1280]{1,0:T(8,128)}, f32[8,1536]{1,0:T(8,128)}) custom-call(bf16[4,512,1152]{2,1,0:T(8,128)(2,1)} %copy-done.2, bf16[4,512,384]{2,1,0:T(8,128)(2,1)} %get-tuple-element.81.logit_hbm, bf16[4,512,128]{2,1,0:T(8,128)(2,1)} %bitcast.134, bf16[1536,1280]{1,0:T(8,128)(2,1)} %copy-done.13, ...), custom_call_target="tpu_custom_call" | custom-call | flops 10468982784 | bytes 104857600 | tf_op jit(solution)/shard_map/last/pallas_call | solution.py:1790
  845.7 3.9 copy.109
  849.6 2.1 fusion.22
  851.7 0.9 slice.144
  853.2 0.9 fusion.24
  856.0 1.8 multiply_convert_fusion
  857.9 2.4 copy.110
  861.1 0.9 copy.128
  (124 shorter events, 11.9 us)
Async XLA Ops:
  0.6 1.8 copy-start.30
  0.7 2.0 copy-start.33
  0.7 2.0 copy-start.34
  0.7 2.0 copy-start.7
  0.7 2.0 copy-start.8
  0.7 2.0 copy-start.9
  2.4 74.5 %copy-start = (bf16[4,128,1536]{2,1,0:T(8,128)(2,1)}, bf16[4,128,1536]{2,1,0:T(8,128)(2,1)S(1)}, u32[]{:S(2)}) copy-start(bf16[4,128,1536]{2,1,0:T(8,128)(2,1)S(1)} %copy.56) | copy-start | bytes 4718596
  54.2 2.7 copy-start.12
  56.9 1.9 copy-start.13
  58.9 18.0 %copy-start.11 = (f32[1,1536]{1,0:T(1,128)}, f32[1,1536]{1,0:T(1,128)S(1)}, u32[]{:S(2)}) copy-start(f32[1,1536]{1,0:T(1,128)S(1)} %reshape_squeeze.6.gain_ref) | copy-start | bytes 18436
  58.9 2.1 copy-start.14
  61.0 16.2 %copy-start.35 = (bf16[6]{0:T(256)(128)(2,1)S(1)}, bf16[6]{0:T(256)(128)(2,1)}, u32[]{:S(2)}) copy-start(bf16[6]{0:T(256)(128)(2,1)} %param.22) | copy-start | bytes 40
  61.0 16.4 %copy-start.31 = (s32[4]{0:T(128)S(1)}, s32[4]{0:T(128)}, u32[]{:S(2)}) copy-start(s32[4]{0:T(128)} %param.16) | copy-start | bytes 52
  76.9 1.4 copy-start.23
  79.8 1.1 copy-start.18
  79.8 1.2 copy-start.19
  81.0 202.9 %copy-start.5 = (bf16[512,1536]{1,0:T(8,128)(2,1)}, bf16[512,1536]{1,0:T(8,128)(2,1)S(1)}, u32[]{:S(2)}) copy-start(bf16[512,1536]{1,0:T(8,128)(2,1)S(1)} %fusion.3.rows_ref.grad_hbm) | copy-start | bytes 4718596
  81.0 205.5 %copy-start.6 = (bf16[192,1024]{1,0:T(8,128)(2,1)S(1)}, bf16[192,1024]{1,0:T(8,128)(2,1)}, u32[]{:S(2)}) copy-start(bf16[192,1024]{1,0:T(8,128)(2,1)} %shard_ref.1) | copy-start | bytes 1179652
  283.9 1.1 copy-start.4
  286.5 49.8 %copy-start.10 = (f32[1,1536]{1,0:T(1,128)}, f32[1,1536]{1,0:T(1,128)S(1)}, u32[]{:S(2)}) copy-start(f32[1,1536]{1,0:T(1,128)S(1)} %reshape_squeeze.7.gain_ref) | copy-start | bytes 18436
  336.3 1.2 copy-start.3
  337.5 1.1 copy-start.15
  521.4 6.4 copy-start.32
  535.7 201.5 %copy-start.29 = (f32[1,1536]{1,0:T(1,128)S(1)}, f32[1,1536]{1,0:T(1,128)}, u32[]{:S(2)}) copy-start(f32[1,1536]{1,0:T(1,128)} %get-tuple-element.86) | copy-start | bytes 18436
  738.2 3.8 copy-start.28
  738.2 2.5 copy-start.1
  742.0 13.7 %copy-start.2 = (bf16[4,512,1152]{2,1,0:T(8,128)(2,1)}, bf16[4,512,1152]{2,1,0:T(8,128)(2,1)S(1)}, u32[]{:S(2)}) copy-start(bf16[4,512,1152]{2,1,0:T(8,128)(2,1)S(1)} %assemble.1.qkv_hbm) | copy-start | bytes 14155780
  845.7 10.4 %copy-start.22 = (f32[512,1536]{1,0:T(8,128)S(1)}, f32[512,1536]{1,0:T(8,128)}, u32[]{:S(2)}) copy-start(f32[512,1536]{1,0:T(8,128)} %get-tuple-element.63.hidden_hbm) | copy-start | bytes 9437188
  857.9 2.4 copy-start.27
  857.9 3.2 copy-start.24
  857.9 4.1 copy-start.25
  857.9 5.0 copy-start.26
  (4 other events, 3.5 us)

commit v9 on v8

--- a/solution.py
+++ b/solution.py
@@ -1223,12 +1223,13 @@
     inner = groups * width
     rows = x.shape[0] // seq_count
     count = items_ref.shape[0]
+    product = dot(normed, w_ref[...], NN)
+    forget_ref[0] = product[:, 3 * inner :]
     for kind in range(3):
-        value = dot(normed, w_ref[:, kind * inner : (kind + 1) * inner], NN).astype(BF16)
+        value = product[:, kind * inner : (kind + 1) * inner].astype(BF16)
         for slot, (s, g) in enumerate(places):
             piece = value[s * rows : (s + 1) * rows, g * width : (g + 1) * width]
             items_ref[slot % count, slot // count, kind] = piece
-    forget_ref[0] = dot(normed, w_ref[:, 3 * inner :], NN)
 
 
 def project(x_all, gain, full_one, layout, item_count, ctx_size):

time: 874 us -> 870 us (level)
  no operation moved by 1% of the time
where the time goes in v9:
time: 870 us; the launch traced here: 861 us
  Pallas kernels  771 us (89%)
  matrix products  45.4 us (5%)
  local copies, waits for them, and re-layouts  37.3 us (4%)
    pallas_call x1, Pallas kernels, context(): pl.pallas_call(functools.partial(context_kernel, heads, head_size), grid=...  203 us
    pallas_call x1, Pallas kernels, context_back(): pl.pallas_call(functools.partial(context_back_kernel, heads, head_size),...  199 us
    pallas_call x1, Pallas kernels, last(): pl.pallas_call(last_kernel, grid=(1,), out_shape=[jax.ShapeDtypeStruct(x....  90 us
    pallas_call x1, Pallas kernels, out_back(): pl.pallas_call(functools.partial(out_back_kernel, layout), grid=(1,), out...  62.4 us
    pallas_call x1, Pallas kernels, mlp_back(): pl.pallas_call(mlp_back_kernel, grid=(1,), out_shape=[jax.ShapeDtypeStruc...  60.6 us
    pallas_call x1, Pallas kernels, startup(): pl.pallas_call(functools.partial(startup_kernel, len(shards)), out_shape=...  51.5 us
    pallas_call x1, Pallas kernels, out_project(): pl.pallas_call(functools.partial(out_kernel, layout), grid=(1,), out_shap...  49.8 us
    dot_general x4, matrix products, dot(): return lax.dot_general(left, right, dims, preferred_element_type=F32)  45.4 us

profile of v9, /device:TPU:0, one launch (start us, length us, event | category | flops | bytes accessed | tf_op | source)
XLA Modules:
  0.0 860.7 jit_solution(10666070358210296691)
XLA Ops:
  0.7 1.7 copy.56
  2.7 51.5 %startup.1 = (bf16[4,512,1536]{2,1,0:T(8,128)(2,1)S(1)}, bf16[1536,1280]{1,0:T(8,128)(2,1)S(1)}, f32[8,8,256]{2,1,0:T(8,128)S(1)}) custom-call(bf16[512,1536]{1,0:T(8,128)(2,1)S(1)} %bitcast.124, f32[8,256]{1,0:T(8,128)S(1)} %fusion.18.gain_ref, bf16[192,384]{1,0:T(8,128)(2,1)S(1)} %copy-done.7, bf16[192,384]{1,0:T(8,128)(2,1)S(1)} %copy-done.8, ...), custom_call_target="tpu_custom_call" | custom-call | tf_op jit(solution)/shard_map/startup/pallas_call | solution.py:1186
  54.3 2.7 copy-done.12
  56.9 1.9 copy-done.13
  58.9 2.1 copy-done.14
  61.0 12.6 %project.1 = (bf16[4,512,1536]{2,1,0:T(8,128)(2,1)}, f32[4,512,128]{2,1,0:T(8,128)S(1)}, bf16[3,4,3,512,128]{4,3,2,1,0:T(8,128)(2,1)}) custom-call(bf16[4,512,1536]{2,1,0:T(8,128)(2,1)} %copy-done.12, f32[1,1536]{1,0:T(1,128)S(1)} %reshape_squeeze.6.gain_ref, bf16[1536,1280]{1,0:T(8,128)(2,1)S(1)} %copy-done.14), custom_call_target="tpu_custom_call" | custom-call | flops 8053063680 | bytes 12582912 | tf_op jit(solution)/shard_map/project/pallas_call | solution.py:1242
  75.5 1.0 copy.71
  77.8 202.9 %context.1 = (bf16[3,4,512,128]{3,2,1,0:T(8,128)(2,1)S(1)}, bf16[3,4,3,512,128]{4,3,2,1,0:T(8,128)(2,1)}, bf16[1536,2048]{1,0:T(8,128)(2,1)}, bf16[1536,768]{1,0...) custom-call(bf16[3,4,3,512,128]{4,3,2,1,0:T(8,128)(2,1)} %get-tuple-, ...), custom_call_target="tpu_custom_call" | custom-call | flops 12884901888 | bytes 104857600 | tf_op jit(solution)/shard_map/context/pallas_call | solution.py:377
  280.7 1.1 copy-done.4
  283.3 49.8 %out_project.1 = (f32[512,1536]{1,0:T(8,128)}, bf16[512,1536]{1,0:T(8,128)(2,1)S(1)}, bf16[4,512,384]{2,1,0:T(8,128)(2,1)S(1)}, bf16[4,512,384]{2,1,0:T(8,128)(2,1)S(1)}, bf16[1536,1024]{1,0:T(8,128)(2,1)}) custom-call(bf16[512,1536]{1,0:T(8,128)(2,1)} %bitcast.125, f32[4,512,384]{2,1,0:T(8,128)} %get-tuple-element.60.gate_ref, ...), custom_call_target="tpu_custom_call" | custom-call | flops 2415919104 | bytes 104857600 | tf_op jit(solution)/shard_map/out_project/pallas_call | solution.py:1320
  333.1 1.2 copy-done.3
  334.2 1.1 copy-done.15
  335.4 40.8 %mlp.1 = (bf16[4,512,1536]{2,1,0:T(8,128)(2,1)}, bf16[4,512,1024]{2,1,0:T(8,128)(2,1)}, bf16[4,512,2048]{2,1,0:T(8,128)(2,1)}) custom-call(bf16[512,1536]{1,0:T(8,128)(2,1)} %copy-done.15, bf16[4,512,1536]{2,1,0:T(8,128)(2,1)} %get-tuple-element.65.grad_hbm, bf16[1536,2048]{1,0:T(8,128)(2,1)} %get-tuple-element.66.gate_hbm.w_hbm, ...), custom_call_target="tpu_custom_call" | custom-call | flops 19327352832 | bytes 104857600 | tf_op jit(solution)/shard_map/mlp/pallas_call | solution.py:1403
  376.1 19.1 %bitcast_convert_fusion.sums_ref = bf16[1536,2048]{1,0:T(8,128)(2,1)} fusion(bf16[4,512,1536]{2,1,0:T(8,128)(2,1)} %get-tuple-element.69, bf16[4,512,2048]{2,1,0:T(8,128)(2,1)} %get-tuple-element.68.pair_hbm), kind=kOutput, calls=%fused_computation | convolution fusion | flops 12888047616 | bytes 20971520 | tf_op jit(solution)/shard_map/dot_general | solution.py:22
  395.2 60.6 %mlp_back.1 = (f32[512,1536]{1,0:T(8,128)}, bf16[512,1536]{1,0:T(8,128)(2,1)}, f32[1,1536]{1,0:T(1,128)}, f32[192,1024]{1,0:T(8,128)}) custom-call(bf16[4,512,2048]{2,1,0:T(8,128)(2,1)} %get-tuple-element.68.pair_hbm, bf16[1536,2048]{1,0:T(8,128)(2,1)} %get-tuple-element.66.gate_hbm.w_hbm, f32[512,1536]{1,0:T(8,128)} %get-tuple-element.63.hidden_hbm, ...), custom_call_target="tpu_custom_call" | custom-call | flops 12884901888 | bytes 104857600 | tf_op jit(solution)/shard_map/mlp_back/pallas_call | solution.py:1487
  455.8 62.4 %out_back.1 = (bf16[4,512,1536]{2,1,0:T(8,128)(2,1)}, bf16[4,512,384]{2,1,0:T(8,128)(2,1)}, bf16[3,4,512,128]{3,2,1,0:T(8,128)(2,1)}, f32[192,1024]{1,0:T(8,128)}, bf16[1536,1024]{1,0:T(8,128)(2,1)}) custom-call(bf16[512,1536]{1,0:T(8,128)(2,1)} %get-tuple-element.70.branch_ref, bf16[1536,768]{1,0:T(8,128)(2,1)} %get-tuple-element.61.w_ref.gate_w_hbm, ...), custom_call_target="tpu_custom_call" | custom-call | flops 2415919104 | bytes 104857600 | tf_op jit(solution)/shard_map/out_back/pallas_call | solution.py:1630
  518.2 6.4 fusion.4
  524.6 6.3 fusion.5
  530.9 1.6 pad_maximum_fusion.part_ref
  532.5 199.5 %context_back.1 = (bf16[3,4,3,512,128]{4,3,2,1,0:T(8,128)(2,1)}, f32[3,4,8,512]{3,2,1,0:T(8,128)}, f32[192,1024]{1,0:T(8,128)}, f32[192,768]{1,0:T(8,128)}, bf16[512,1536]{1,0:T(8,128)(2,1)}) custom-call(bf16[3,4,512,128]{3,2,1,0:T(8,128)(2,1)} %get-tuple-element.73.items_ref, bf16[3,4,3,512,128]{4,3,2,1,0:T(8,128)(2,1)} %get-tuple-element.74.qkv_ref, ...), custom_call_target="tpu_custom_call" | custom-call | flops 32212254720 | bytes 104857600 | tf_op jit(solution)/shard_map/context_back/pallas_call | solution.py:533
  731.9 0.9 fusion.10
  735.0 2.5 copy-done.1
  737.5 1.2 assemble.1.qkv_hbm
  738.8 13.7 %convolution_convert_fusion.part_ref = bf16[1536,1280]{1,0:T(8,128)(2,1)} fusion(bf16[2048,1536]{1,0:T(8,128)(2,1)} %bitcast.152, bf16[2048,128]{1,0:T(8,128)(2,1)S(1)} %copy.82, bf16[2048,1152]{1,0:T(8,128)(2,1)S(1)} %bitcast.127), kind=kOutput, calls=%fused_computation.1 | convolution fusion | flops 8065515520 | bytes 15466496 | tf_op jit(solution)/shard_map/dot_general | solution.py:22
  752.5 90.0 %last.1 = (bf16[512,1536]{1,0:T(8,128)(2,1)}, f32[192,1280]{1,0:T(8,128)}, f32[8,1536]{1,0:T(8,128)}) custom-call(bf16[4,512,1152]{2,1,0:T(8,128)(2,1)} %copy-done.2, bf16[4,512,384]{2,1,0:T(8,128)(2,1)} %get-tuple-element.81.logit_hbm, bf16[4,512,128]{2,1,0:T(8,128)(2,1)} %bitcast.134, bf16[1536,1280]{1,0:T(8,128)(2,1)} %copy-done.13, ...), custom_call_target="tpu_custom_call" | custom-call | flops 10468982784 | bytes 104857600 | tf_op jit(solution)/shard_map/last/pallas_call | solution.py:1791
  842.4 3.9 copy.109
  846.3 2.1 fusion.22
  848.4 0.9 slice.144
  850.0 0.9 fusion.24
  852.8 1.8 multiply_convert_fusion
  854.6 2.4 copy.110
  857.8 0.9 copy.128
  (124 shorter events, 11.9 us)
Async XLA Ops:
  0.6 1.8 copy-start.30
  0.7 2.0 copy-start.33
  0.7 2.0 copy-start.34
  0.7 2.0 copy-start.7
  0.7 2.0 copy-start.8
  0.7 2.0 copy-start.9
  2.4 71.3 %copy-start = (bf16[4,128,1536]{2,1,0:T(8,128)(2,1)}, bf16[4,128,1536]{2,1,0:T(8,128)(2,1)S(1)}, u32[]{:S(2)}) copy-start(bf16[4,128,1536]{2,1,0:T(8,128)(2,1)S(1)} %copy.56) | copy-start | bytes 4718596
  54.2 2.7 copy-start.12
  56.9 1.9 copy-start.13
  58.9 14.8 %copy-start.11 = (f32[1,1536]{1,0:T(1,128)}, f32[1,1536]{1,0:T(1,128)S(1)}, u32[]{:S(2)}) copy-start(f32[1,1536]{1,0:T(1,128)S(1)} %reshape_squeeze.6.gain_ref) | copy-start | bytes 18436
  58.9 2.1 copy-start.14
  61.0 13.0 %copy-start.35 = (bf16[6]{0:T(256)(128)(2,1)S(1)}, bf16[6]{0:T(256)(128)(2,1)}, u32[]{:S(2)}) copy-start(bf16[6]{0:T(256)(128)(2,1)} %param.22) | copy-start | bytes 40
  61.0 13.1 %copy-start.31 = (s32[4]{0:T(128)S(1)}, s32[4]{0:T(128)}, u32[]{:S(2)}) copy-start(s32[4]{0:T(128)} %param.16) | copy-start | bytes 52
  73.7 1.4 copy-start.23
  76.6 1.1 copy-start.18
  76.6 1.2 copy-start.19
  77.8 202.9 %copy-start.5 = (bf16[512,1536]{1,0:T(8,128)(2,1)}, bf16[512,1536]{1,0:T(8,128)(2,1)S(1)}, u32[]{:S(2)}) copy-start(bf16[512,1536]{1,0:T(8,128)(2,1)S(1)} %fusion.3.rows_ref.grad_hbm) | copy-start | bytes 4718596
  77.8 205.5 %copy-start.6 = (bf16[192,1024]{1,0:T(8,128)(2,1)S(1)}, bf16[192,1024]{1,0:T(8,128)(2,1)}, u32[]{:S(2)}) copy-start(bf16[192,1024]{1,0:T(8,128)(2,1)} %shard_ref.1) | copy-start | bytes 1179652
  280.7 1.1 copy-start.4
  283.3 49.8 %copy-start.10 = (f32[1,1536]{1,0:T(1,128)}, f32[1,1536]{1,0:T(1,128)S(1)}, u32[]{:S(2)}) copy-start(f32[1,1536]{1,0:T(1,128)S(1)} %reshape_squeeze.7.gain_ref) | copy-start | bytes 18436
  333.1 1.2 copy-start.3
  334.2 1.1 copy-start.15
  518.2 6.4 copy-start.32
  532.5 201.5 %copy-start.29 = (f32[1,1536]{1,0:T(1,128)S(1)}, f32[1,1536]{1,0:T(1,128)}, u32[]{:S(2)}) copy-start(f32[1,1536]{1,0:T(1,128)} %get-tuple-element.86) | copy-start | bytes 18436
  735.0 3.8 copy-start.28
  735.0 2.5 copy-start.1
  738.8 13.7 %copy-start.2 = (bf16[4,512,1152]{2,1,0:T(8,128)(2,1)}, bf16[4,512,1152]{2,1,0:T(8,128)(2,1)S(1)}, u32[]{:S(2)}) copy-start(bf16[4,512,1152]{2,1,0:T(8,128)(2,1)S(1)} %assemble.1.qkv_hbm) | copy-start | bytes 14155780
  842.4 10.4 %copy-start.22 = (f32[512,1536]{1,0:T(8,128)S(1)}, f32[512,1536]{1,0:T(8,128)}, u32[]{:S(2)}) copy-start(f32[512,1536]{1,0:T(8,128)} %get-tuple-element.63.hidden_hbm) | copy-start | bytes 9437188
  854.6 2.4 copy-start.27
  854.6 3.2 copy-start.24
  854.6 4.1 copy-start.25
  854.6 5.0 copy-start.26
  (4 other events, 3.5 us)
